TPU v7x, 32 devices: a whole 2x2x4 slice. The times are simulated.
32 devices in a mesh: rep: 2 (over x), fsdp: 2 (over core), seq: 8 (over z, y).
Axes of the slice: x: 2, y: 2, z: 4, core: 2. Of those that a mesh axis runs over, the one named last changes fastest.
Arguments:
- tokens: bfloat16 [2, 4, 2048, 768], P(None, ('rep', 'fsdp'), 'seq'), may hold values from -6 to 6
- lengths: int32 [2, 4, 8], P(None, ('rep', 'fsdp')), may hold values from 1 to 1024, 2048 in all within a row
- ln1_gain: bfloat16 [768], P('fsdp'), may hold values from 0.099609375 to 1.8984375
- ln1_bias: bfloat16 [768], P('fsdp'), may hold values from -3 to 3
- qkv_weight: bfloat16 [768, 2304], P('fsdp'), may hold values from -0.21875 to 0.21875
- q_gain: bfloat16 [64], P('fsdp'), may hold values from 0.099609375 to 1.8984375
- k_gain: bfloat16 [64], P('fsdp'), may hold values from 0.099609375 to 1.8984375
- out_weight: bfloat16 [768, 768], P('fsdp'), may hold values from -1.75 to 1.75
- ln2_gain: bfloat16 [768], P('fsdp'), may hold values from 0.099609375 to 1.8984375
- ln2_bias: bfloat16 [768], P('fsdp'), may hold values from -3 to 3
- up_weight: bfloat16 [768, 3072], P('fsdp'), may hold values from -0.21875 to 0.21875
- down_weight: bfloat16 [3072, 768], P('fsdp'), may hold values from -0.109375 to 0.109375
- cotangent: bfloat16 [2, 4, 2048, 768], P(None, ('rep', 'fsdp'), 'seq'), may hold values from -6 to 6
Outputs:
- output: bfloat16 [2, 4, 2048, 768], P(None, ('rep', 'fsdp'), 'seq')
- grad_tokens: float32 [2, 4, 2048, 768], P(None, ('rep', 'fsdp'), 'seq')
- grad_ln1_gain: float32 [768], P('fsdp')
- grad_ln1_bias: float32 [768], P('fsdp')
- grad_qkv_weight: float32 [768, 2304], P('fsdp')
- grad_q_gain: float32 [64], P('fsdp')
- grad_k_gain: float32 [64], P('fsdp')
- grad_out_weight: float32 [768, 768], P('fsdp')
- grad_ln2_gain: float32 [768], P('fsdp')
- grad_ln2_bias: float32 [768], P('fsdp')
- grad_up_weight: float32 [768, 3072], P('fsdp')
- grad_down_weight: float32 [3072, 768], P('fsdp')
Inputs may be any that keep to these rules, and one draw needn't show every extreme that they name: In each row the first 7 entries are the lengths of its pictures in order and the last one is the padding at the row's end; each row's entries sum to 2048, and each row's largest entry is 1024.
All inputs are finite; a program needn't handle non-finite values.
Results may differ from a plain program's by a relative error of at most 0.014.
Values may be sent and summed in bfloat16 or wider, within the bound.
No kernel may reach another device: no remote copies, remote signals or barrier semaphores. Data moves between devices by JAX's collectives and lax.ppermute only.
A program may use at most 320 MiB of HBM per device.

v0:
```python
from functools import partial

import jax
import jax.numpy as jnp
from jax import lax
from jax.sharding import PartitionSpec as P

H = 12


EPS = 1e-06
MASKED = -1000000000.0


def layer_norm(values, gain, shift):
    center = jnp.mean(values, axis=-1, keepdims=True)
    centred = values - center
    spread = jnp.mean(centred * centred, axis=-1, keepdims=True)
    return centred * lax.rsqrt(spread + EPS) * gain + shift


def head_norm(values, gain):
    return layer_norm(values, gain, 0.0)


def gelu_exact(values):
    return jax.nn.gelu(values, approximate=False)


def picture_ids(lengths, length):
    bounds = jnp.cumsum(lengths, axis=-1)
    places = jnp.arange(length, dtype=jnp.int32)
    ident = jnp.sum((places[:, None] >= bounds[..., None, :-1]).astype(jnp.int32), axis=-1)
    return jnp.where(ident == lengths.shape[-1] - 1, -1, ident)


def split_groups(tensor):
    rows, length, width = tensor.shape
    shaped = tensor.reshape(rows, length, H // 2, 2, width // H)
    return jnp.moveaxis(shaped, 2, 0)


def join_groups(tensor):
    moved = jnp.moveaxis(tensor, 0, 2)
    return moved.reshape(moved.shape[0], moved.shape[1], -1)


def group_scores(q_group, k_group, same, scale):
    scores = (
        jnp.einsum("rqhd,rkhd->rhqk", q_group, k_group, preferred_element_type=jnp.float32) * scale
    )
    return jnp.where(same[:, None], scores, MASKED)


def attend_group(inputs, same, scale):
    q_group, k_group, v_group = inputs
    scores = group_scores(q_group, k_group, same, scale)
    top = jnp.max(scores, axis=-1, keepdims=True)
    expo = jnp.exp(scores - top)
    total = jnp.sum(expo, axis=-1, keepdims=True)
    probs = (expo / total).astype(jnp.bfloat16)
    context = jnp.einsum("rhqk,rkhd->rqhd", probs, v_group, preferred_element_type=jnp.float32)
    return (context, top[..., 0] + jnp.log(total[..., 0]))


def attend_back(inputs, same, scale):
    q_group, k_group, v_group, grad_group, logsum = inputs
    scores = group_scores(q_group, k_group, same, scale)
    probs = jnp.exp(scores - logsum[..., None])
    grad_probs = jnp.einsum(
        "rqhd,rkhd->rhqk", grad_group, v_group, preferred_element_type=jnp.float32
    )
    inner = jnp.sum(probs * grad_probs, axis=-1, keepdims=True)
    grad_scores = (probs * (grad_probs - inner)).astype(jnp.bfloat16)
    grad_q = (
        jnp.einsum("rhqk,rkhd->rqhd", grad_scores, k_group, preferred_element_type=jnp.float32)
        * scale
    )
    grad_k = (
        jnp.einsum("rhqk,rqhd->rkhd", grad_scores, q_group, preferred_element_type=jnp.float32)
        * scale
    )
    grad_v = jnp.einsum(
        "rhqk,rqhd->rkhd",
        probs.astype(jnp.bfloat16),
        grad_group,
        preferred_element_type=jnp.float32,
    )
    return (grad_q, grad_k, grad_v)


def unpack(weights):
    return tuple((member.astype(jnp.float32) if member.ndim == 1 else member for member in weights))


def on_device(
    tokens,
    lengths,
    ln1_gain,
    ln1_bias,
    qkv_weight,
    q_gain,
    k_gain,
    out_weight,
    ln2_gain,
    ln2_bias,
    up_weight,
    down_weight,
    cotangent,
):
    shards = (
        ln1_gain,
        ln1_bias,
        qkv_weight,
        q_gain,
        k_gain,
        out_weight,
        ln2_gain,
        ln2_bias,
        up_weight,
        down_weight,
    )
    micro, rows, local, width = tokens.shape
    head_dim = width // H
    scale = head_dim ** (-0.5)
    length = local * lax.axis_size("seq")
    offset = lax.axis_index("seq") * local

    def fetch():
        return unpack(
            (
                lax.all_gather(shards[0], "fsdp", axis=0, tiled=True),
                lax.all_gather(shards[1], "fsdp", axis=0, tiled=True),
                lax.all_gather(shards[2], "fsdp", axis=0, tiled=True),
                lax.all_gather(shards[3], "fsdp", axis=0, tiled=True),
                lax.all_gather(shards[4], "fsdp", axis=0, tiled=True),
                lax.all_gather(shards[5], "fsdp", axis=0, tiled=True),
                lax.all_gather(shards[6], "fsdp", axis=0, tiled=True),
                lax.all_gather(shards[7], "fsdp", axis=0, tiled=True),
                lax.all_gather(shards[8], "fsdp", axis=0, tiled=True),
                lax.all_gather(shards[9], "fsdp", axis=0, tiled=True),
            )
        )

    outputs = []
    grad_inputs = []
    running = None
    for index in range(micro):
        gathered = fetch()
        g_one, b_one, w_qkv, g_query, g_key, w_out, g_two, b_two, w_up, w_down = gathered
        x_block = tokens[index].astype(jnp.float32)
        ident = picture_ids(lengths[index], length)
        ident_local = lax.dynamic_slice_in_dim(ident, offset, local, 1)
        same = (ident_local[:, :, None] == ident[:, None, :]) & (ident[:, None, :] >= 0)
        valid = (ident_local >= 0).astype(jnp.float32)[..., None]
        norm_one, pull_one = jax.vjp(layer_norm, x_block, g_one, b_one)
        first = norm_one.astype(jnp.bfloat16)
        qkv = jnp.dot(first, w_qkv, preferred_element_type=jnp.float32)
        q_raw = qkv[..., :width].reshape(rows, local, H, head_dim)
        k_raw = qkv[..., width : 2 * width].reshape(rows, local, H, head_dim)
        q_normed, pull_query = jax.vjp(head_norm, q_raw, g_query)
        k_normed, pull_key = jax.vjp(head_norm, k_raw, g_key)
        queries = q_normed.astype(jnp.bfloat16).reshape(rows, local, width)
        keys = k_normed.astype(jnp.bfloat16).reshape(rows, local, width)
        values = qkv[..., 2 * width :].astype(jnp.bfloat16)
        keys_all, values_all = (
            lax.all_gather(keys, "seq", axis=1, tiled=True),
            lax.all_gather(values, "seq", axis=1, tiled=True),
        )
        q_groups = split_groups(queries)
        k_groups = split_groups(keys_all)
        v_groups = split_groups(values_all)
        context, logsum = lax.map(
            partial(attend_group, same=same, scale=scale), (q_groups, k_groups, v_groups)
        )
        attn = (join_groups(context) * valid).astype(jnp.bfloat16)
        middle = x_block + jnp.dot(attn, w_out, preferred_element_type=jnp.float32)
        norm_two, pull_two = jax.vjp(layer_norm, middle, g_two, b_two)
        second = norm_two.astype(jnp.bfloat16)
        upper = jnp.dot(second, w_up, preferred_element_type=jnp.float32)
        active_full, pull_active = jax.vjp(gelu_exact, upper)
        active = active_full.astype(jnp.bfloat16)
        result = middle + jnp.dot(active, w_down, preferred_element_type=jnp.float32)
        outputs.append(result.astype(jnp.bfloat16))
        again = fetch()
        w_qkv, w_out, w_up, w_down = (again[2], again[5], again[8], again[9])
        grad_y = cotangent[index]
        grad_down = jnp.einsum("rsf,rsd->fd", active, grad_y, preferred_element_type=jnp.float32)
        grad_active = jnp.einsum("rsd,fd->rsf", grad_y, w_down, preferred_element_type=jnp.float32)
        (grad_upper,) = pull_active(grad_active)
        grad_upper = grad_upper.astype(jnp.bfloat16)
        grad_up = jnp.einsum("rsd,rsf->df", second, grad_upper, preferred_element_type=jnp.float32)
        grad_second = jnp.einsum(
            "rsf,df->rsd", grad_upper, w_up, preferred_element_type=jnp.float32
        )
        grad_mid_norm, grad_g_two, grad_b_two = pull_two(grad_second)
        grad_middle = grad_y.astype(jnp.float32) + grad_mid_norm
        grad_branch = grad_middle.astype(jnp.bfloat16)
        grad_out = jnp.einsum("rsd,rse->de", attn, grad_branch, preferred_element_type=jnp.float32)
        grad_attn = (
            jnp.einsum("rse,de->rsd", grad_branch, w_out, preferred_element_type=jnp.float32)
            * valid
        ).astype(jnp.bfloat16)
        grad_qg, grad_kg, grad_vg = lax.map(
            partial(attend_back, same=same, scale=scale),
            (q_groups, k_groups, v_groups, split_groups(grad_attn), logsum),
        )
        grad_keys, grad_values = (
            lax.psum_scatter(
                join_groups(grad_kg).astype(jnp.bfloat16), "seq", scatter_dimension=1, tiled=True
            ).astype(jnp.float32),
            lax.psum_scatter(
                join_groups(grad_vg).astype(jnp.bfloat16), "seq", scatter_dimension=1, tiled=True
            ).astype(jnp.float32),
        )
        grad_q_raw, grad_g_query = pull_query(
            join_groups(grad_qg).reshape(rows, local, H, head_dim)
        )
        grad_k_raw, grad_g_key = pull_key(grad_keys.reshape(rows, local, H, head_dim))
        grad_qkv = jnp.concatenate(
            [
                grad_q_raw.reshape(rows, local, width),
                grad_k_raw.reshape(rows, local, width),
                grad_values,
            ],
            axis=-1,
        ).astype(jnp.bfloat16)
        grad_qkv_w = jnp.einsum("rsd,rse->de", first, grad_qkv, preferred_element_type=jnp.float32)
        grad_first = jnp.einsum("rse,de->rsd", grad_qkv, w_qkv, preferred_element_type=jnp.float32)
        grad_x_norm, grad_g_one, grad_b_one = pull_one(grad_first)
        grad_inputs.append(grad_middle + grad_x_norm)
        grads = (
            grad_g_one,
            grad_b_one,
            grad_qkv_w,
            grad_g_query,
            grad_g_key,
            grad_out,
            grad_g_two,
            grad_b_two,
            grad_up,
            grad_down,
        )
        running = grads if index == 0 else jax.tree.map(jnp.add, running, grads)
    owned = lax.psum_scatter(running, "fsdp", scatter_dimension=0, tiled=True)
    running = lax.psum(owned, ("rep", "seq"))
    output = jnp.stack(outputs, axis=0)
    grad_tokens = jnp.stack(grad_inputs, axis=0)
    return (
        output,
        grad_tokens,
        running[0],
        running[1],
        running[2],
        running[3],
        running[4],
        running[5],
        running[6],
        running[7],
        running[8],
        running[9],
    )


def solution(mesh):
    in_specs = (
        P(None, ("rep", "fsdp"), "seq", None),
        P(None, ("rep", "fsdp"), None),
        P("fsdp"),
        P("fsdp"),
        P("fsdp", None),
        P("fsdp"),
        P("fsdp"),
        P("fsdp", None),
        P("fsdp"),
        P("fsdp"),
        P("fsdp", None),
        P("fsdp", None),
        P(None, ("rep", "fsdp"), "seq", None),
    )
    out_specs = (
        P(None, ("rep", "fsdp"), "seq", None),
        P(None, ("rep", "fsdp"), "seq", None),
        P("fsdp"),
        P("fsdp"),
        P("fsdp", None),
        P("fsdp"),
        P("fsdp"),
        P("fsdp", None),
        P("fsdp"),
        P("fsdp"),
        P("fsdp", None),
        P("fsdp", None),
    )
    return jax.shard_map(
        on_device, mesh=mesh, in_specs=in_specs, out_specs=out_specs, check_vma=False
    )
```

profile of v0, /device:TPU:0, one launch (start us, length us, event | category | flops | bytes accessed | tf_op | source)
XLA Modules:
  0.0 1268.5 jit_solution(4192007691853410526)
XLA Ops:
  15.5 9.5 all-gather.13.cloned.1.call-done
  67.0 23.4 %all-gather.25.cloned.1.call-done = bf16[1,2048,768]{2,1,0:T(8,128)(2,1)} async-done(((bf16[1,256,768]{2,1,0:T(8,128)(2,1)}), bf16[1,2048,768]{2,1,0:T(8,128)(2,1)}) %all-gather.25.cloned.1.call-update) | async-done | bytes 3145744 | tf_op jit(solution)/shard_map/all_gather | solution.py:168
  95.3 56.6 %all-gather.27.cloned.1.call-done = bf16[1,2048,768]{2,1,0:T(8,128)(2,1)} async-done(((bf16[1,256,768]{2,1,0:T(8,128)(2,1)}), bf16[1,2048,768]{2,1,0:T(8,128)(2,1)}) %all-gather.27.cloned.1.call-update) | async-done | bytes 3145744 | tf_op jit(solution)/shard_map/all_gather | solution.py:167
  156.6 47.0 %while.57 = (s32[]{:T(128)}, f32[6,1,256,2,64]{2,4,3,1,0:T(8,128)}, f32[6,1,2,256]{3,2,1,0:T(2,128)}, bf16[6,1,2048,2,64]{2,4,3,1,0:T(8,128)(2,1)}, bf16[6,1,256...) while((s32[]{:T(128)}, f32[6,1,256,2,64]{2,4,3,1,0:T(8,128)}, ...), condition=%wide.region_25.26_spmd.clone, body=%wide.region_22.25_spmd.clone.sunk | while | flops 282066432 | bytes 15955057 | solution.py:173
  211.0 13.5 %all-gather.15.cloned.1.call-done = bf16[1,2048,768]{2,1,0:T(8,128)(2,1)} async-done(((bf16[1,256,768]{2,1,0:T(8,128)(2,1)}), bf16[1,2048,768]{2,1,0:T(8,128)(2,1)}) %all-gather.15.cloned.1.call-update) | async-done | bytes 3145744 | tf_op jit(solution)/shard_map/all_gather | solution.py:168
  229.2 56.7 %all-gather.17.cloned.1.call-done = bf16[1,2048,768]{2,1,0:T(8,128)(2,1)} async-done(((bf16[1,256,768]{2,1,0:T(8,128)(2,1)}), bf16[1,2048,768]{2,1,0:T(8,128)(2,1)}) %all-gather.17.cloned.1.call-update) | async-done | bytes 3145744 | tf_op jit(solution)/shard_map/all_gather | solution.py:167
  290.6 42.0 %while.56 = (s32[]{:T(128)}, f32[6,1,256,2,64]{2,4,3,1,0:T(8,128)}, f32[6,1,2,256]{3,2,1,0:T(2,128)}, bf16[6,1,2048,2,64]{2,4,3,1,0:T(8,128)(2,1)}, bf16[6,1,256...) while((s32[]{:T(128)}, f32[6,1,256,2,64]{2,4,3,1,0:T(8,128)}, ...), condition=%wide.region_11.12_spmd.clone, body=%wide.region_8.11_spmd.clone.sunk | while | flops 282066432 | bytes 15955057 | solution.py:173
  339.4 12.3 multiply_convert_fusion.2
  351.7 11.5 multiply_convert_fusion.3
  363.3 6.4 add_convert_fusion
  388.8 77.8 %while.59 = (s32[]{:T(128)}, f32[6,1,256,2,64]{2,4,3,1,0:T(8,128)}, bf16[6,1,2048,2,64]{2,4,3,1,0:T(8,128)(2,1)}, bf16[6,1,2048,2,64]{2,4,3,1,0:T(8,128)(2,1)}, ...) while((s32[]{:T(128)}, f32[6,1,256,2,64]{2,4,3,1,0:T(8,128)}, ...), condition=%wide.region_45.46_spmd.clone, body=%wide.region_43.45_spmd.clone.sunk | while | flops 681868800 | bytes 36608192 | solution.py:204
  481.6 59.9 %while.58 = (s32[]{:T(128)}, f32[6,1,256,2,64]{2,4,3,1,0:T(8,128)}, bf16[6,1,2048,2,64]{2,4,3,1,0:T(8,128)(2,1)}, bf16[6,1,2048,2,64]{2,4,3,1,0:T(8,128)(2,1)}, ...) while((s32[]{:T(128)}, f32[6,1,256,2,64]{2,4,3,1,0:T(8,128)}, ...), condition=%wide.region_32.33_spmd.clone, body=%wide.region_30.32_spmd.clone.sunk | while | flops 681868800 | bytes 36595848 | solution.py:204
  562.8 5.3 convolution_add_fusion.2
  572.3 5.2 convolution_add_fusion.1
  600.6 20.7 %reduce-scatter.9.cloned.1.call-done = bf16[1,256,768]{2,1,0:T(8,128)(2,1)} async-done(((bf16[1,2048,768]{2,1,0:T(8,128)(2,1)}), bf16[1,256,768]{2,1,0:T(8,128)(2,1)}) %reduce-scatter.9.cloned.1.call-update) | async-done | bytes 393232 | tf_op jit(solution)/shard_map/reduce_scatter | solution.py:209
  636.7 62.2 %reduce-scatter.11.cloned.1.call-done = bf16[1,256,768]{2,1,0:T(8,128)(2,1)} async-done(((bf16[1,2048,768]{2,1,0:T(8,128)(2,1)}), bf16[1,256,768]{2,1,0:T(8,128)(2,1)}) %reduce-scatter.11.cloned.1.call-update) | async-done | bytes 393232 | tf_op jit(solution)/shard_map/reduce_scatter | solution.py:212
  699.0 5.5 fusion.159
  707.1 69.6 %reduce-scatter.15.cloned.1.call-done = bf16[1,256,768]{2,1,0:T(8,128)(2,1)} async-done(((bf16[1,2048,768]{2,1,0:T(8,128)(2,1)}), bf16[1,256,768]{2,1,0:T(8,128)(2,1)}) %reduce-scatter.15.cloned.1.call-update) | async-done | bytes 393232 | tf_op jit(solution)/shard_map/reduce_scatter | solution.py:212
  776.7 7.4 convolution_add_fusion
  788.8 20.7 %reduce-scatter.21.cloned.1.call-done = f32[384,3072]{1,0:T(8,128)} async-done(((f32[768,3072]{1,0:T(8,128)}), f32[384,3072]{1,0:T(8,128)}) %reduce-scatter.21.cloned.1.call-update) | async-done | bytes 4718608 | tf_op jit(solution)/shard_map/reduce_scatter | solution.py:245
  809.5 20.7 %reduce-scatter.23.cloned.1.call-done = f32[1536,768]{1,0:T(8,128)} async-done(((f32[3072,768]{1,0:T(8,128)}), f32[1536,768]{1,0:T(8,128)}) %reduce-scatter.23.cloned.1.call-update) | async-done | bytes 4718608 | tf_op jit(solution)/shard_map/reduce_scatter | solution.py:245
  830.2 19.3 %reduce-scatter.17.cloned.1.call-done = f32[384,2304]{1,0:T(8,128)} async-done(((f32[768,2304]{1,0:T(8,128)}), f32[384,2304]{1,0:T(8,128)}) %reduce-scatter.17.cloned.1.call-update) | async-done | bytes 3538960 | tf_op jit(solution)/shard_map/reduce_scatter | solution.py:245
  874.9 47.1 %all-reduce.8 = (f32[384]{0:T(512)}, f32[384]{0:T(512)}, f32[32]{0:T(128)}, f32[32]{0:T(128)}, f32[384]{0:T(512)}, /*index=5*/f32[384]{0:T(512)}) all-reduce(f32[384]{0:T(512)S(1)} %dynamic-slice.3, f32[384]{0:T(512)S(1)} %dynamic-slice.5, f32[32]{0:T(128)S(1)} %dynamic-slice.7, ...), channel_id=1, replica_groups=mesh['rep'=2,'fsdp'=2,'seq'=8] {'rep','seq'}, use_global_device_ids=true, to_apply=%region_57.58 | all-reduce | flops 1600 | bytes 12800 | tf_op jit(solution)/shard_map/psum | solution.py:246
  925.4 325.2 %all-reduce.14.cloned.1.call-done = (f32[384,2304]{1,0:T(8,128)}, f32[384,768]{1,0:T(8,128)}, f32[384,3072]{1,0:T(8,128)}, f32[1536,768]{1,0:T(8,128)}) async-done(((f32[384,2304]{1,0:T(8,128)}, f32[384,768]{1,0:T(8,128)}, f32[384,3072]{1,0:T(8,128)}, f32[1536,768]{1,0:T(8,128)}), (f32[384,2304]{1,0:T(8,128)}, f32[384,768]{1,0:T(8,128)}, f32[384,3072]{1,0:T(8,128)}, ...) | async-done | bytes 14155792 | tf_op jit(solution)/shard_map/psum | solution.py:246
  (788 shorter events, 450.5 us)
Async XLA Ops:
  7.2 17.8 %all-gather.13.cloned.1.call-start = ((), (), s32[]{:S(2)}) async-start(), calls=%async_computation.8 | async-start | bytes 5308416 | tf_op jit(solution)/shard_map/all_gather | solution.py:134
  7.9 82.5 %all-gather.25.cloned.1.call-start = ((), (), s32[]{:S(2)}) async-start(), calls=%async_computation.14 | async-start | bytes 3538944 | tf_op jit(solution)/shard_map/all_gather | solution.py:168
  29.1 122.8 %all-gather.27.cloned.1.call-start = ((), (), s32[]{:S(2)}) async-start(), calls=%async_computation.15 | async-start | bytes 3538944 | tf_op jit(solution)/shard_map/all_gather | solution.py:167
  51.8 154.7 %all-gather.19.cloned.1.call-start = ((), (), s32[]{:S(2)}) async-start(), calls=%async_computation.11 | async-start | bytes 1769472 | tf_op jit(solution)/shard_map/all_gather | solution.py:137
  52.4 172.1 %all-gather.15.cloned.1.call-start = ((), (), s32[]{:S(2)}) async-start(), calls=%async_computation.9 | async-start | bytes 3538944 | tf_op jit(solution)/shard_map/all_gather | solution.py:168
  54.5 231.4 %all-gather.17.cloned.1.call-start = ((), (), s32[]{:S(2)}) async-start(), calls=%async_computation.10 | async-start | bytes 3538944 | tf_op jit(solution)/shard_map/all_gather | solution.py:167
  55.0 284.3 %all-gather.21.cloned.1.call-start = ((), (), s32[]{:S(2)}) async-start(), calls=%async_computation.12 | async-start | bytes 7077888 | tf_op jit(solution)/shard_map/all_gather | solution.py:140
  55.8 307.4 %all-gather.23.cloned.1.call-start = ((), (), s32[]{:S(2)}) async-start(), calls=%async_computation.13 | async-start | bytes 7077888 | tf_op jit(solution)/shard_map/all_gather | solution.py:141
  56.6 542.8 %reduce-scatter.13.cloned.1.call-start = ((), (), s32[]{:S(2)}) async-start(), calls=%async_computation.18 | async-start | bytes 3538944 | tf_op jit(solution)/shard_map/reduce_scatter | solution.py:209
  471.3 149.9 %reduce-scatter.9.cloned.1.call-start = ((), (), s32[]{:S(2)}) async-start(), calls=%async_computation.16 | async-start | bytes 3538944 | tf_op jit(solution)/shard_map/reduce_scatter | solution.py:209
  546.2 152.7 %reduce-scatter.11.cloned.1.call-start = ((), (), s32[]{:S(2)}) async-start(), calls=%async_computation.17 | async-start | bytes 3538944 | tf_op jit(solution)/shard_map/reduce_scatter | solution.py:212
  550.9 225.8 %reduce-scatter.15.cloned.1.call-start = ((), (), s32[]{:S(2)}) async-start(), calls=%async_computation.19 | async-start | bytes 3538944 | tf_op jit(solution)/shard_map/reduce_scatter | solution.py:212
  555.6 233.2 %reduce-scatter.19.cloned.1.call-start = ((), (), s32[]{:S(2)}) async-start(), calls=%async_computation.21 | async-start | bytes 3538944 | tf_op jit(solution)/shard_map/reduce_scatter | solution.py:245
  559.5 250.0 %reduce-scatter.21.cloned.1.call-start = ((), (), s32[]{:S(2)}) async-start(), calls=%async_computation.22 | async-start | bytes 14155776 | tf_op jit(solution)/shard_map/reduce_scatter | solution.py:245
  568.1 262.1 %reduce-scatter.23.cloned.1.call-start = ((), (), s32[]{:S(2)}) async-start(), calls=%async_computation.23 | async-start | bytes 14155776 | tf_op jit(solution)/shard_map/reduce_scatter | solution.py:245
  577.5 272.0 %reduce-scatter.17.cloned.1.call-start = ((), (), s32[]{:S(2)}) async-start(), calls=%async_computation.20 | async-start | bytes 10616832 | tf_op jit(solution)/shard_map/reduce_scatter | solution.py:245
  631.6 67.3 %copy-start.2 = (bf16[2,1,256,768]{3,2,1,0:T(8,128)(2,1)S(1)}, bf16[2,1,256,768]{3,2,1,0:T(8,128)(2,1)}, u32[]{:S(2)}) copy-start(bf16[2,1,256,768]{3,2,1,0:T(8,128)(2,1)} %param.21) | copy-start | bytes 2359300
  631.6 67.3 %copy-start.64 = (f32[768]{0:T(1024)S(1)}, f32[768]{0:T(1024)}, u32[]{:S(2)}) copy-start(f32[768]{0:T(1024)} %copy-done.63) | copy-start | bytes 9220
  631.7 67.3 %copy-start.66 = (f32[768]{0:T(1024)S(1)}, f32[768]{0:T(1024)}, u32[]{:S(2)}) copy-start(f32[768]{0:T(1024)} %copy-done.65) | copy-start | bytes 9220
  631.7 67.3 %copy-start.113 = (f32[256]{0:T(256)S(1)}, f32[256]{0:T(256)}, u32[]{:S(2)}) copy-start(f32[256]{0:T(256)} %copy-done.112) | copy-start | bytes 3076
  784.1 466.5 %all-reduce.14.cloned.1.call-start = ((), (), s32[]{:S(2)}) async-start(), calls=%async_computation.24 | async-start | bytes 28311552 | tf_op jit(solution)/shard_map/psum | solution.py:246
  866.6 55.5 %copy-start.28 = (bf16[2,1,256,768]{3,2,1,0:T(8,128)(2,1)S(1)}, bf16[2,1,256,768]{3,2,1,0:T(8,128)(2,1)}, u32[]{:S(2)}) copy-start(bf16[2,1,256,768]{3,2,1,0:T(8,128)(2,1)} %param.33) | copy-start | bytes 2359300
  866.6 55.4 %copy-start.30 = (f32[256,768]{1,0:T(8,128)S(1)}, f32[256,768]{1,0:T(8,128)}, u32[]{:S(2)}) copy-start(f32[256,768]{1,0:T(8,128)} %copy-done.29) | copy-start | bytes 2359300
  866.6 55.4 %copy-start.32 = (f32[256,768]{1,0:T(8,128)S(1)}, f32[256,768]{1,0:T(8,128)}, u32[]{:S(2)}) copy-start(f32[256,768]{1,0:T(8,128)} %copy-done.31) | copy-start | bytes 2359300
  (181 other events, 1198.5 us)
Sparse Core Ops, SparseCore 0:
  9.5 15.4 all-gather.12
  29.2 61.1 all-gather.24
  93.2 58.6 all-gather.26
  153.3 7.8 all-gather.18
  163.2 61.2 all-gather.14
  227.1 58.6 all-gather.16
  287.4 13.0 all-gather.20
  302.0 15.6 all-gather.22
  471.4 73.0 reduce-scatter.12
  547.9 73.2 reduce-scatter.8
  625.4 73.4 reduce-scatter.10
  702.9 73.7 reduce-scatter.14
  779.6 9.2 reduce-scatter.18
  791.0 18.5 reduce-scatter.20
  811.6 18.5 reduce-scatter.22
  832.4 17.0 reduce-scatter.16
  855.8 394.8 all-reduce.13
where the time goes:
time: 1280 us; the launch traced here: 1270 us
  waiting for transfers between devices  706 us (55%)
  matrix products  268 us (21%)
  local copies, waits for them, and re-layouts  131 us (10%)
  other arithmetic  81.9 us (6%)
  blocking collectives  61.2 us (5%)
  between operations  18.8 us (1%)
    psum x1, waiting for transfers between devices, on_device(): running = lax.psum(owned, ('rep', 'seq'))  325 us
    reduce_scatter x2, waiting for transfers between devices, on_device(): lax.psum_scatter(join_groups(grad_vg).astype(jnp.bfloat16), 'seq', scatte...  132 us
    all_gather x2, waiting for transfers between devices, on_device(): lax.all_gather(keys, 'seq', axis=1, tiled=True)  113 us
    reduce_scatter x4, waiting for transfers between devices, on_device(): owned = lax.psum_scatter(running, 'fsdp', scatter_dimension=0, tiled=True)  65 us
    psum x1, blocking collectives, on_device(): running = lax.psum(owned, ('rep', 'seq'))  47.1 us
    dot_general x24, matrix products, group_scores(): jnp.einsum('rqhd,rkhd->rhqk', q_group, k_group, preferred_element_type=jn...  46.2 us
    all_gather x2, waiting for transfers between devices, on_device(): lax.all_gather(values, 'seq', axis=1, tiled=True)  36.9 us
    dot_general x12, matrix products, attend_group(): jnp.einsum('rhqk,rkhd->rqhd', probs, v_group, preferred_element_type=jnp....  35.5 us
  transfers between devices with their start and end apart: 17, of which 13 were waited for; matrix products, arithmetic and copies ran while one was open for 27% of the time, Pallas kernels for 0%

commit v1 on v0

v1 whole, which is shorter than its diff:
```python
import functools

import jax
import jax.numpy as jnp
from jax import lax
from jax.experimental import pallas as pl
from jax.experimental.pallas import tpu as pltpu
from jax.sharding import PartitionSpec as P

H = 12
EPS = 1e-06
LOG2E = 1.4426950408889634
SHIFT = 512.0
BLK = 256
NN = (((1,), (0,)), ((), ()))
NT = (((1,), (1,)), ((), ()))
TN = (((0,), (0,)), ((), ()))
F32 = jnp.float32
BF16 = jnp.bfloat16


def mm(a, b, dims=NN):
    return lax.dot_general(a, b, dims, preferred_element_type=F32)


def params(**kw):
    return pltpu.CompilerParams(vmem_limit_bytes=60 * 1024 * 1024, **kw)


def norm_rows(v):
    center = jnp.mean(v, axis=-1, keepdims=True)
    centred = v - center
    inv = lax.rsqrt(jnp.mean(centred * centred, axis=-1, keepdims=True) + EPS)
    return centred * inv, inv


def norm_cols(v):
    center = jnp.mean(v, axis=0, keepdims=True)
    centred = v - center
    inv = lax.rsqrt(jnp.mean(centred * centred, axis=0, keepdims=True) + EPS)
    return centred * inv, inv


def bounds_of(len_ref, row):
    out = []
    total = jnp.int32(0)
    for j in range(len_ref.shape[1] - 1):
        total = total + len_ref[row, j]
        out.append(total)
    return out


def qkv_body(heads, hd, meta, len_ref, *refs):
    xs = refs[:8]
    w_ref, g_ref, b_ref, gq_ref, gk_ref = refs[8:13]
    qt_ref, ka_ref, kt_ref, v_ref, vt_ref, x_ref = refs[13:]
    wid = heads * hd
    spot, row = meta[0], meta[1]
    bounds = bounds_of(len_ref, row)
    for s in range(8):
        c = jnp.bitwise_xor(spot, s)
        cols = pl.ds(pl.multiple_of(c * BLK, BLK), BLK)
        x = xs[s][...]
        x_ref[cols, :] = x
        hat, _ = norm_rows(x.astype(F32))
        first = (hat * g_ref[...] + b_ref[...]).astype(BF16)
        qkv = mm(w_ref[...], first, NT)
        place = c * BLK + lax.broadcasted_iota(jnp.int32, (8, BLK), 1)
        ident = jnp.zeros((8, BLK), jnp.int32)
        place_k = c * BLK + lax.broadcasted_iota(jnp.int32, (BLK, 128), 0)
        ident_k = jnp.zeros((BLK, 128), jnp.int32)
        for bound in bounds:
            ident = ident + (place >= bound).astype(jnp.int32)
            ident_k = ident_k + (place_k >= bound).astype(jnp.int32)
        which = lax.broadcasted_iota(jnp.int32, (8, BLK), 0)
        hot = jnp.where((ident == which) & (which < len(bounds)), 16.0, 0.0)
        hot = jnp.concatenate([hot, jnp.zeros((hd - 8, BLK), F32)], axis=0)
        lane = lax.broadcasted_iota(jnp.int32, (BLK, 128), 1) - hd
        hot_k = jnp.where((ident_k == lane) & (lane < len(bounds)), SHIFT / 16.0, 0.0)
        for h in range(heads):
            q, _ = norm_cols(qkv[h * hd : (h + 1) * hd])
            k, _ = norm_cols(qkv[wid + h * hd : wid + (h + 1) * hd])
            q = (q * gq_ref[...]).astype(BF16).astype(F32) * (hd**-0.5)
            k = k * gk_ref[...]
            v = qkv[2 * wid + h * hd : 2 * wid + (h + 1) * hd]
            qt_ref[h, :, cols] = jnp.concatenate([q, hot], axis=0).astype(BF16)
            kt_ref[h, :, cols] = k.astype(BF16)
            vt_ref[h, :, cols] = v.astype(BF16)
            both = jnp.transpose(jnp.concatenate([k, v], axis=0))
            ka_ref[h, cols, :] = jnp.where(lane < 0, both, hot_k).astype(BF16)
            v_ref[h, cols, :] = both[:, hd:].astype(BF16)


def make_qkv(meta, lengths, slots, w_t, gain, bias, gq, gk, heads, hd):
    length = 8 * slots[0].shape[0]
    width = slots[0].shape[1]
    smem = pl.BlockSpec(memory_space=pltpu.SMEM)
    vmem = pl.BlockSpec(memory_space=pltpu.VMEM)
    return pl.pallas_call(
        functools.partial(qkv_body, heads, hd),
        out_shape=(
            jax.ShapeDtypeStruct((heads, 2 * hd, length), BF16),
            jax.ShapeDtypeStruct((heads, length, 2 * hd), BF16),
            jax.ShapeDtypeStruct((heads, hd, length), BF16),
            jax.ShapeDtypeStruct((heads, length, hd), BF16),
            jax.ShapeDtypeStruct((heads, hd, length), BF16),
            jax.ShapeDtypeStruct((length, width), BF16),
        ),
        in_specs=[smem, smem] + [vmem] * 13,
        out_specs=(vmem,) * 6,
        compiler_params=params(),
        name="qkv_forward",
    )(meta, lengths, *slots, w_t, gain, bias, gq, gk)


def block_range(bounds, i):
    first = i * BLK
    last = first + BLK - 1
    lo = jnp.int32(0)
    hi = bounds[-1]
    for bound in bounds:
        lo = jnp.where(first >= bound, bound, lo)
    for bound in bounds[::-1]:
        hi = jnp.where(last < bound, bound, hi)
    lo_b = lo // BLK
    hi_b = (hi + BLK - 1) // BLK
    return lo_b, jnp.where(first >= bounds[-1], lo_b, hi_b)


def attend_body(heads, hd, meta, len_ref, qt_ref, ka_ref, vt_ref, o_ref, of_ref, ls_ref):
    i = pl.program_id(0)
    bounds = bounds_of(len_ref, meta[1])
    lo, hi = block_range(bounds, i)

    def step(b, carry):
        rows = pl.ds(pl.multiple_of(b * BLK, BLK), BLK)
        out = []
        for h in range(heads):
            acc, total = carry[h]
            scores = mm(ka_ref[h, rows, :], qt_ref[h])
            expo = jnp.exp2(scores * LOG2E - SHIFT * LOG2E)
            total = total + jnp.sum(expo.reshape(BLK // 8, 8, BLK), axis=0)
            acc = acc + mm(vt_ref[h, :, rows], expo.astype(BF16))
            out.append((acc, total))
        return tuple(out)

    init = tuple((jnp.zeros((hd, BLK), F32), jnp.zeros((8, BLK), F32)) for _ in range(heads))
    done = lax.fori_loop(lo, hi, step, init)
    for h in range(heads):
        acc, total = done[h]
        total = jnp.sum(total, axis=0, keepdims=True)
        live = total > 0.0
        safe = jnp.where(live, total, 1.0)
        out = jnp.where(live, acc * (1.0 / safe), 0.0)
        o_ref[0, h * hd : (h + 1) * hd, :] = out.astype(BF16)
        of_ref[h] = out
        ls_ref[h] = jnp.log2(safe) + SHIFT * LOG2E


def attend(meta, lengths, qt, ka, vt, heads, hd):
    length = qt.shape[2]
    blocks = length // BLK
    smem = pl.BlockSpec(memory_space=pltpu.SMEM)
    return pl.pallas_call(
        functools.partial(attend_body, heads, hd),
        grid=(blocks,),
        out_shape=(
            jax.ShapeDtypeStruct((blocks, heads * hd, BLK), BF16),
            jax.ShapeDtypeStruct((heads, hd, length), F32),
            jax.ShapeDtypeStruct((heads, 1, length), F32),
        ),
        in_specs=[
            smem,
            smem,
            pl.BlockSpec((heads, 2 * hd, BLK), lambda i: (0, 0, i)),
            pl.BlockSpec((heads, length, 2 * hd), lambda i: (0, 0, 0)),
            pl.BlockSpec((heads, hd, length), lambda i: (0, 0, 0)),
        ],
        out_specs=(
            pl.BlockSpec((1, heads * hd, BLK), lambda i: (i, 0, 0)),
            pl.BlockSpec((heads, hd, BLK), lambda i: (0, 0, i)),
            pl.BlockSpec((heads, 1, BLK), lambda i: (0, 0, i)),
        ),
        compiler_params=params(),
        name="attention_forward",
    )(meta, lengths, qt, ka, vt)


def attend_back_body(
    heads, hd, meta, len_ref, qt_ref, ka_ref, kt_ref, v_ref, of_ref, ls_ref, go_ref, dq_ref, dk_ref, dv_ref
):
    i = pl.program_id(0)
    bounds = bounds_of(len_ref, meta[1])
    lo, hi = block_range(bounds, i)

    @pl.when(i == 0)
    def _():
        dk_ref[...] = jnp.zeros_like(dk_ref)
        dv_ref[...] = jnp.zeros_like(dv_ref)

    inner = []
    for h in range(heads):
        go = go_ref[0, h * hd : (h + 1) * hd, :].astype(F32)
        inner.append(jnp.sum(go * of_ref[h], axis=0, keepdims=True))

    def step(b, carry):
        rows = pl.ds(pl.multiple_of(b * BLK, BLK), BLK)
        out = []
        for h in range(heads):
            go = go_ref[0, h * hd : (h + 1) * hd, :]
            qt = qt_ref[h]
            scores = mm(ka_ref[h, rows, :], qt)
            probs = jnp.exp2(scores * LOG2E - ls_ref[h])
            grad_probs = mm(v_ref[h, rows, :], go)
            grad_scores = (probs * (grad_probs - inner[h])).astype(BF16)
            dv_ref[h, :, rows] += mm(go, probs.astype(BF16), NT)
            dk_ref[h, :, rows] += mm(qt[:hd], grad_scores, NT)
            out.append(carry[h] + mm(kt_ref[h, :, rows], grad_scores))
        return tuple(out)

    done = lax.fori_loop(lo, hi, step, tuple(jnp.zeros((hd, BLK), F32) for _ in range(heads)))
    for h in range(heads):
        dq_ref[h] = done[h] * (hd**-0.5)


def attend_back(meta, lengths, qt, ka, kt, v, of, ls, go, heads, hd):
    length = qt.shape[2]
    blocks = length // BLK
    smem = pl.BlockSpec(memory_space=pltpu.SMEM)
    whole = lambda *shape: pl.BlockSpec(shape, lambda i: (0,) * len(shape))
    return pl.pallas_call(
        functools.partial(attend_back_body, heads, hd),
        grid=(blocks,),
        out_shape=tuple(jax.ShapeDtypeStruct((heads, hd, length), F32) for _ in range(3)),
        in_specs=[
            smem,
            smem,
            pl.BlockSpec((heads, 2 * hd, BLK), lambda i: (0, 0, i)),
            whole(heads, length, 2 * hd),
            whole(heads, hd, length),
            whole(heads, length, hd),
            pl.BlockSpec((heads, hd, BLK), lambda i: (0, 0, i)),
            pl.BlockSpec((heads, 1, BLK), lambda i: (0, 0, i)),
            pl.BlockSpec((1, heads * hd, BLK), lambda i: (i, 0, 0)),
        ],
        out_specs=(
            pl.BlockSpec((heads, hd, BLK), lambda i: (0, 0, i)),
            whole(heads, hd, length),
            whole(heads, hd, length),
        ),
        compiler_params=params(),
        name="attention_backward",
    )(meta, lengths, qt, ka, kt, v, of, ls, go)


def qkv_back_body(
    heads, hd, meta, x_ref, dq_ref, dk_ref, dv_ref, w_ref, g_ref, b_ref, gq_ref, gk_ref,
    da_ref, db_ref, dw_ref, vec_ref, gain_ref, acc_ref,
):
    i = pl.program_id(0)
    wid = heads * hd

    @pl.when(i == 0)
    def _():
        acc_ref[...] = jnp.zeros_like(acc_ref)
        vec_ref[...] = jnp.zeros_like(vec_ref)
        gain_ref[...] = jnp.zeros_like(gain_ref)

    hat, _ = norm_rows(x_ref[...].astype(F32))
    first = (hat * g_ref[...] + b_ref[...]).astype(BF16)
    qk = mm(w_ref[: 2 * wid, :], first, NT)
    pieces = []
    for at, gain, grad in ((0, gq_ref, dq_ref), (1, gk_ref, dk_ref)):
        for h in range(heads):
            unit, inv = norm_cols(qk[at * wid + h * hd : at * wid + (h + 1) * hd])
            gy = grad[h]
            gain_ref[at] += gy * unit
            e = gy * gain[...]
            pieces.append(
                inv
                * (
                    e
                    - jnp.mean(e, axis=0, keepdims=True)
                    - unit * jnp.mean(e * unit, axis=0, keepdims=True)
                )
            )
    for h in range(heads):
        pieces.append(dv_ref[h])
    grad = jnp.concatenate(pieces, axis=0).astype(BF16)
    acc_ref[...] += mm(grad, first)
    back = mm(grad, w_ref[...], TN)
    vec_ref[0] += jnp.sum((back * hat).reshape(BLK // 8, 8, -1), axis=0)
    vec_ref[1] += jnp.sum(back.reshape(BLK // 8, 8, -1), axis=0)
    half = back.shape[1] // 2
    da_ref[0] = back[:, :half].astype(BF16)
    db_ref[0] = back[:, half:].astype(BF16)

    @pl.when(i == pl.num_programs(0) - 1)
    def _():
        dw_ref[...] = acc_ref[...].astype(BF16)


def qkv_back(meta, x, dq, dk, dv, w_t, gain, bias, gq, gk, heads, hd):
    length, width = x.shape
    blocks = length // BLK
    whole = lambda *shape: pl.BlockSpec(shape, lambda i, m: (0,) * len(shape))
    part = pl.BlockSpec((heads, hd, BLK), lambda i, m: (0, 0, i))
    grads = pl.BlockSpec((1, BLK, width // 2), lambda i, m: (jnp.bitwise_xor(i, m[0]), 0, 0))
    return pl.pallas_call(
        functools.partial(qkv_back_body, heads, hd),
        grid_spec=pltpu.PrefetchScalarGridSpec(
            num_scalar_prefetch=1,
            grid=(blocks,),
            in_specs=[
                pl.BlockSpec((BLK, width), lambda i, m: (i, 0)),
                part,
                part,
                part,
                whole(*w_t.shape),
                whole(1, width),
                whole(1, width),
                whole(hd, 1),
                whole(hd, 1),
            ],
            out_specs=(
                grads,
                grads,
                whole(*w_t.shape),
                whole(2, 8, width),
                whole(2, hd, BLK),
            ),
            scratch_shapes=[pltpu.VMEM(w_t.shape, F32)],
        ),
        out_shape=(
            jax.ShapeDtypeStruct((blocks, BLK, width // 2), BF16),
            jax.ShapeDtypeStruct((blocks, BLK, width // 2), BF16),
            jax.ShapeDtypeStruct(w_t.shape, BF16),
            jax.ShapeDtypeStruct((2, 8, width), F32),
            jax.ShapeDtypeStruct((2, hd, BLK), F32),
        ),
        compiler_params=params(),
        name="qkv_backward",
    )(meta, x, dq, dk, dv, w_t, gain, bias, gq, gk)


def gelu_pair(u):
    a = jnp.abs(u)
    t = 1.0 / (1.0 + (0.3275911 * 0.7071067811865476) * a)
    poly = 1.061405429 * t - 1.453152027
    poly = poly * t + 1.421413741
    poly = poly * t - 0.284496736
    poly = poly * t + 0.254829592
    bell = jnp.exp(-0.5 * (u * u))
    tail = (0.5 * poly) * t * bell
    cdf = jnp.where(u >= 0.0, 1.0 - tail, tail)
    return u * cdf, cdf + u * (bell * 0.3989422804014327)


def ffn(meta, attn_t, x, dy, valid, gain, bias, wo, wo_p, up, up_p, dn, dn_p):
    tokens, width = x.shape
    hidden = up.shape[1]
    fc = 512
    steps = hidden // fc
    near = steps // 2
    packs, _, lanes = attn_t.shape
    whole = lambda *shape: pl.BlockSpec(shape, lambda i, m: (0,) * len(shape))
    ups = pl.BlockSpec((width // 2, fc), lambda i, m: (0, lax.rem(m[2] * near + i, steps)))
    acts = pl.BlockSpec((tokens, fc), lambda i, m: (0, lax.rem(m[2] * near + i, steps)))
    half = width // 2

    def body(meta, *refs):
        (at_ref, x_ref, dy_ref, valid_ref, g_ref, b_ref, wo_own, wo_peer, up_own, up_peer, dn_own, dn_peer) = refs[:12]
        (out_ref, gm_ref, gb_ref, h2_ref, act_ref, dup_ref, da_ref, vec_ref) = refs[12:20]
        (mid_s, acc_s, own_s, peer_s, gown_s, gpeer_s) = refs[20:]
        i = pl.program_id(0)
        core = meta[2]
        zero = core == 0

        @pl.when(i == 0)
        def _():
            for p in range(packs):
                rows = pl.ds(p * lanes, lanes)
                own = at_ref[p, pl.ds(pl.multiple_of(core * half, half), half), :]
                peer = at_ref[p, pl.ds(pl.multiple_of((1 - core) * half, half), half), :]
                mid = x_ref[rows, :].astype(F32) + mm(own, wo_own[...], TN) + mm(peer, wo_peer[...], TN)
                mid_s[rows, :] = mid
                acc_s[rows, :] = mid
                hat, _ = norm_rows(mid)
                second = (hat * g_ref[...] + b_ref[...]).astype(BF16)
                h2_ref[rows, :] = second
                lo, hi = second[:, :half], second[:, half:]
                own_s[rows, :] = jnp.where(zero, lo, hi)
                peer_s[rows, :] = jnp.where(zero, hi, lo)
            gown_s[...] = jnp.zeros_like(gown_s)
            gpeer_s[...] = jnp.zeros_like(gpeer_s)

        down = jnp.where(i < near, dn_own[...], dn_peer[...])
        upper = mm(own_s[...], up_own[...]) + mm(peer_s[...], up_peer[...])
        act, slope = gelu_pair(upper)
        act = act.astype(BF16)
        grad = (mm(dy_ref[...], down, NT) * slope).astype(BF16)
        act_ref[...] = act
        dup_ref[...] = grad
        acc_s[...] += mm(act, down)
        gown_s[...] += mm(grad, up_own[...], NT)
        gpeer_s[...] += mm(grad, up_peer[...], NT)

        @pl.when(i == steps - 1)
        def _():
            out_ref[...] = acc_s[...].astype(BF16)
            vec = [jnp.zeros((8, width), F32), jnp.zeros((8, width), F32)]
            for p in range(packs):
                rows = pl.ds(p * lanes, lanes)
                hat, inv = norm_rows(mid_s[rows, :])
                a, b = gown_s[rows, :], gpeer_s[rows, :]
                gy = jnp.concatenate([jnp.where(zero, a, b), jnp.where(zero, b, a)], axis=1)
                vec[0] = vec[0] + jnp.sum((gy * hat).reshape(lanes // 8, 8, width), axis=0)
                vec[1] = vec[1] + jnp.sum(gy.reshape(lanes // 8, 8, width), axis=0)
                e = gy * g_ref[...]
                gm = dy_ref[rows, :].astype(F32) + inv * (
                    e
                    - jnp.mean(e, axis=-1, keepdims=True)
                    - hat * jnp.mean(e * hat, axis=-1, keepdims=True)
                )
                gm_ref[rows, :] = gm
                gb = gm.astype(BF16)
                gb_ref[rows, :] = gb
                ok = valid_ref[p]
                da_ref[p, pl.ds(pl.multiple_of(core * half, half), half), :] = (
                    mm(wo_own[...], gb, NT) * ok
                ).astype(BF16)
                da_ref[p, pl.ds(pl.multiple_of((1 - core) * half, half), half), :] = (
                    mm(wo_peer[...], gb, NT) * ok
                ).astype(BF16)
            vec_ref[0] = vec[0]
            vec_ref[1] = vec[1]

    return pl.pallas_call(
        body,
        grid_spec=pltpu.PrefetchScalarGridSpec(
            num_scalar_prefetch=1,
            grid=(steps,),
            in_specs=[
                whole(*attn_t.shape),
                whole(tokens, width),
                whole(tokens, width),
                whole(*valid.shape),
                whole(1, width),
                whole(1, width),
                whole(half, width),
                whole(half, width),
                ups,
                ups,
                pl.BlockSpec((fc, width), lambda i, m: (jnp.minimum(i, near - 1), 0)),
                pl.BlockSpec((fc, width), lambda i, m: (jnp.maximum(i - near, 0), 0)),
            ],
            out_specs=(
                whole(tokens, width),
                whole(tokens, width),
                whole(tokens, width),
                whole(tokens, width),
                acts,
                acts,
                whole(*attn_t.shape),
                whole(2, 8, width),
            ),
            scratch_shapes=[
                pltpu.VMEM((tokens, width), F32),
                pltpu.VMEM((tokens, width), F32),
                pltpu.VMEM((tokens, half), BF16),
                pltpu.VMEM((tokens, half), BF16),
                pltpu.VMEM((tokens, half), F32),
                pltpu.VMEM((tokens, half), F32),
            ],
        ),
        out_shape=(
            jax.ShapeDtypeStruct((tokens, width), BF16),
            jax.ShapeDtypeStruct((tokens, width), F32),
            jax.ShapeDtypeStruct((tokens, width), BF16),
            jax.ShapeDtypeStruct((tokens, width), BF16),
            jax.ShapeDtypeStruct((tokens, hidden), BF16),
            jax.ShapeDtypeStruct((tokens, hidden), BF16),
            jax.ShapeDtypeStruct(attn_t.shape, BF16),
            jax.ShapeDtypeStruct((2, 8, width), F32),
        ),
        compiler_params=params(),
        name="ffn_both_ways",
    )(meta, attn_t, x, dy, valid, gain, bias, wo, wo_p, up, up_p, dn, dn_p)


def weight_grads(meta, attn_t, gb, h2, dup, act, dy):
    tokens, width = dy.shape
    hidden = act.shape[1]
    half = width // 2
    packs, _, lanes = attn_t.shape
    n_up = hidden // width
    n_dn = hidden // 2 // half
    per = 1 + n_up + n_dn

    def body(meta, at_ref, gb_ref, h2_ref, dup_ref, act_ref, dy_ref, out_ref):
        s, j = pl.program_id(0), pl.program_id(1)
        side = jnp.where(s == 0, 1 - meta[2], meta[2])

        @pl.when(j == 0)
        def _():
            rows = pl.ds(pl.multiple_of(side * half, half), half)
            total = jnp.zeros((half, width), F32)
            for p in range(packs):
                total = total + mm(at_ref[p, rows, :], gb_ref[p * lanes : (p + 1) * lanes, :])
            out_ref[0] = total.astype(BF16)

        @pl.when((j >= 1) & (j <= n_up))
        def _():
            part = jnp.where(side == 0, h2_ref[:, :half], h2_ref[:, half:])
            out_ref[0] = mm(part, dup_ref[...], TN).astype(BF16)

        @pl.when(j > n_up)
        def _():
            out_ref[0] = mm(act_ref[...], dy_ref[...], TN).astype(BF16)

    def act_at(s, j, m):
        side = jnp.where(s == 0, 1 - m[2], m[2])
        return (0, side * n_dn + jnp.clip(j - 1 - n_up, 0, n_dn - 1))

    whole = lambda *shape: pl.BlockSpec(shape, lambda s, j, m: (0,) * len(shape))
    return pl.pallas_call(
        body,
        grid_spec=pltpu.PrefetchScalarGridSpec(
            num_scalar_prefetch=1,
            grid=(2, per),
            in_specs=[
                whole(*attn_t.shape),
                whole(tokens, width),
                whole(tokens, width),
                pl.BlockSpec((tokens, width), lambda s, j, m: (0, jnp.clip(j - 1, 0, n_up - 1))),
                pl.BlockSpec((tokens, half), act_at),
                whole(tokens, width),
            ],
            out_specs=pl.BlockSpec((1, half, width), lambda s, j, m: (s, j, 0)),
        ),
        out_shape=jax.ShapeDtypeStruct((2, per * half, width), BF16),
        compiler_params=params(),
        name="weight_gradients",
    )(meta, attn_t, gb, h2, dup, act, dy)


def finish_body(x_ref, gm_ref, back_ref, g_ref, out_ref):
    hat, inv = norm_rows(x_ref[...].astype(F32))
    e = back_ref[...].astype(F32) * g_ref[...]
    out_ref[...] = gm_ref[...] + inv * (
        e - jnp.mean(e, axis=-1, keepdims=True) - hat * jnp.mean(e * hat, axis=-1, keepdims=True)
    )


def finish(x, gm, back, gain):
    tokens, width = x.shape
    rows = pl.BlockSpec((128, width), lambda i: (i, 0))
    return pl.pallas_call(
        finish_body,
        grid=(tokens // 128,),
        in_specs=[rows, rows, rows, pl.BlockSpec((1, width), lambda i: (0, 0))],
        out_specs=rows,
        out_shape=jax.ShapeDtypeStruct((tokens, width), F32),
        compiler_params=params(),
        name="first_norm_backward",
    )(x, gm, back, gain)


def flip(value, axis, mask):
    size = lax.axis_size(axis)
    return lax.ppermute(value, axis, [(i, i ^ mask) for i in range(size)])


def bit(axis, mask):
    return (lax.axis_index(axis) // mask) % 2


def halves(value, which, axis=0):
    n = value.shape[axis] // 2
    keep = lax.dynamic_slice_in_dim(value, which * n, n, axis)
    send = lax.dynamic_slice_in_dim(value, (1 - which) * n, n, axis)
    return keep, send


def join(own, other, which, axis=0):
    return jnp.where(
        which == 0,
        jnp.concatenate([own, other], axis=axis),
        jnp.concatenate([other, own], axis=axis),
    )


def add(a, b):
    return (a.astype(F32) + b.astype(F32)).astype(BF16)


def reduce_all(value, cuts, rest):
    for axis, mask in cuts:
        keep, send = halves(value, bit(axis, mask))
        value = add(keep, flip(send, axis, mask))
    for axis, mask in rest:
        value = add(value, flip(value, axis, mask))
    for axis, mask in cuts[::-1]:
        value = join(value, flip(value, axis, mask), bit(axis, mask))
    return value


def on_device(
    tokens, lengths, ln1_gain, ln1_bias, qkv_weight, q_gain, k_gain, out_weight,
    ln2_gain, ln2_bias, up_weight, down_weight, cotangent,
):
    micro, rows, local, width = tokens.shape
    n = lax.axis_size("seq")
    length = local * n
    every = micro * rows
    team = n // every
    heads = H // team
    hd = width // H
    half = width // 2
    idx = lax.axis_index("seq")
    core = lax.axis_index("fsdp")
    row, member = idx // team, idx % team
    direct = every == 2 and team == 4
    lengths = lengths.reshape(every, lengths.shape[-1])
    mine = tokens.reshape(every, local, width)

    def swap(value):
        return flip(value, "fsdp", 1)

    vec = jnp.concatenate([ln1_gain, ln1_bias, ln2_gain, ln2_bias, q_gain, k_gain])[None]
    vec_p = swap(vec)
    ordered = jnp.where(core == 0, jnp.concatenate([vec, vec_p]), jnp.concatenate([vec_p, vec])).astype(F32)
    g1, b1, g2, b2 = (ordered[:, k * half : (k + 1) * half].reshape(1, width) for k in range(4))
    gq = ordered[:, 4 * half : 4 * half + hd // 2].reshape(hd, 1)
    gk = ordered[:, 4 * half + hd // 2 :].reshape(hd, 1)

    w_own = lax.dynamic_slice_in_dim(
        qkv_weight.reshape(half, 3, width), member * heads * hd, heads * hd, 2
    ).reshape(half, 3 * heads * hd)
    w_t = jnp.transpose(join(w_own, swap(w_own), core))

    if direct:
        near = lax.dynamic_index_in_dim(mine, row, 0, keepdims=False)
        away = lax.dynamic_index_in_dim(mine, 1 - row, 0, keepdims=False)
        far = flip(away, "seq", 4)
        cut = local // 2

        def spread(own):
            one, two = flip(own, "seq", 1), flip(own, "seq", 2)
            three = jnp.concatenate([flip(two[:cut], "seq", 1), flip(one[cut:], "seq", 2)], axis=0)
            return [own, one, two, three]

        slots = spread(near) + spread(far)
        spot = idx
    else:
        same_member = [[q * team + p for q in range(every)] for p in range(team)]
        same_row = [[q * team + p for p in range(team)] for q in range(every)]
        got = lax.all_to_all(mine, "seq", 0, 0, axis_index_groups=same_member, tiled=True)
        got = lax.all_gather(got, "seq", axis_index_groups=same_row)
        whole = jnp.swapaxes(got, 0, 1).reshape(length, width)
        slots = [whole[s * (length // 8) : (s + 1) * (length // 8)] for s in range(8)]
        spot = jnp.int32(0)
    meta = jnp.stack([spot, row, core]).astype(jnp.int32)

    out_p, up_p, down_p = swap(out_weight), swap(up_weight), swap(down_weight)

    with jax.named_scope("forward_attention"):
        qt, ka, kt, v, vt, x_row = make_qkv(meta, lengths, slots, w_t, g1, b1, gq, gk, heads, hd)
        attn, attn_f, logsum = attend(meta, lengths, qt, ka, vt, heads, hd)

    def exchange(value):
        return lax.all_to_all(value, "seq", 0, 0, tiled=True)

    packs = every * local // BLK
    if direct:
        attn_t = exchange(attn).reshape(packs, width, BLK)
    else:
        cut = jnp.moveaxis(attn.reshape(BLK * 0 + 8, heads * hd, BLK // local, local), 2, 1)
        got = exchange(cut.reshape(n, heads * hd, local))
        got = got.reshape(packs, every // packs, width, local)
        attn_t = jnp.swapaxes(got, 1, 2).reshape(packs, width, BLK)

    total = jnp.sum(lengths[:, :-1], axis=-1)
    places = idx * local + jnp.arange(local, dtype=jnp.int32)
    valid = (places[None] < total[:, None]).astype(F32).reshape(packs, 1, BLK)
    x_home = tokens.reshape(every * local, width)
    dy = cotangent.reshape(every * local, width)

    with jax.named_scope("feed_forward"):
        output, grad_mid, grad_branch, h2, act, dup, grad_attn, vec2 = ffn(
            meta, attn_t, x_home, dy, valid, g2, b2, out_weight, out_p, up_weight, up_p, down_weight, down_p
        )
    if direct:
        grad_o = exchange(grad_attn.reshape(n, heads * hd, BLK))
    else:
        cut = jnp.swapaxes(grad_attn.reshape(packs, width, every // packs, local), 1, 2)
        got = exchange(cut.reshape(n, heads * hd, local))
        got = got.reshape(8, BLK // local, heads * hd, local)
        grad_o = jnp.swapaxes(got, 1, 2).reshape(8, heads * hd, BLK)

    with jax.named_scope("weight_gradients"):
        grads = weight_grads(meta, attn_t, grad_branch, h2, dup, act, dy)
        big = add(grads[1], swap(grads[0]))
        masks = [1 << k for k in range(n.bit_length() - 1)]
        left = reduce_all(
            big[:, :half],
            [("rep", 1), ("seq", masks[0]), ("seq", masks[1])],
            [("seq", m) for m in masks[2:]],
        )
        right = reduce_all(
            big[:, half:],
            [("seq", masks[0]), ("rep", 1), ("seq", masks[1])],
            [("seq", m) for m in masks[2:]],
        )
        big = jnp.concatenate([left, right], axis=1).astype(F32)
        grad_out = big[:half]
        hidden = up_weight.shape[1]
        n_up = hidden // width
        grad_up = jnp.concatenate([big[half * (1 + k) : half * (2 + k)] for k in range(n_up)], axis=1)
        grad_down = big[half * (1 + n_up) :]

    with jax.named_scope("backward_attention"):
        dq, dk, dv = attend_back(meta, lengths, qt, ka, kt, v, attn_f, logsum, grad_o, heads, hd)
        back_a, back_b, dw_t, vec1, gains = qkv_back(
            meta, x_row, dq, dk, dv, w_t, g1, b1, gq, gk, heads, hd
        )

    if direct:

        def gather(parts):
            a = parts[0].reshape(2, 2, 2, local, half)
            b = parts[1].reshape(2, 2, 2, local, half)
            out = []
            for kind in (1, 0):
                a1 = add(a[kind, :, 0], flip(a[kind, :, 1], "seq", 1))
                b1 = add(b[kind, 0], flip(b[kind, 1], "seq", 2))
                a2 = add(a1[0], flip(a1[1], "seq", 2))
                b2 = add(b1[0], flip(b1[1], "seq", 1))
                out.append(jnp.concatenate([a2, b2], axis=1))
            return out

        far_sum, near_sum = gather((back_a, back_b))
        other = flip(far_sum, "seq", 4)
        back = jnp.where(
            row == 0, jnp.stack([near_sum, other]), jnp.stack([other, near_sum])
        ).reshape(every * local, width)
    else:
        whole = jnp.concatenate([back_a, back_b], axis=-1).reshape(every, team, local, width)
        whole = lax.psum_scatter(whole, "seq", scatter_dimension=1, axis_index_groups=same_row, tiled=True)
        got = lax.all_to_all(whole[:, 0], "seq", 0, 0, axis_index_groups=same_member, tiled=True)
        back = got.reshape(every * local, width)
    grad_tokens = finish(x_home, grad_mid, back, g1)

    with jax.named_scope("first_projection_gradient"):
        n3 = 3 * heads * hd
        keep, send = halves(dw_t, core, 1)
        piece = add(keep, swap(send))
        step_rest = [("seq", m) for m in masks if m >= team]
        piece = reduce_all(piece, [("rep", 1)], step_rest)
        parts = lax.all_gather(piece, "seq", axis_index_groups=[[q * team + p for p in range(team)] for q in range(every)])
        parts = parts.reshape(team, 3, heads * hd, half)
        grad_qkv = jnp.transpose(parts, (3, 1, 0, 2)).reshape(half, 3 * width).astype(F32)

    small = jnp.concatenate(
        [
            jnp.sum(vec1, axis=1).reshape(-1),
            jnp.sum(vec2, axis=1).reshape(-1),
            jnp.sum(gains, axis=-1).reshape(-1),
        ]
    )
    small = lax.psum(small, ("rep", "fsdp", "seq"))
    cuts = [small[k * width : (k + 1) * width] for k in range(4)]
    cuts += [small[4 * width : 4 * width + hd], small[4 * width + hd :]]
    cuts = [lax.dynamic_slice_in_dim(c, core * (c.shape[0] // 2), c.shape[0] // 2, 0) for c in cuts]
    shape = tokens.shape
    return (
        output.reshape(shape), grad_tokens.reshape(shape), cuts[0], cuts[1], grad_qkv, cuts[4], cuts[5],
        grad_out, cuts[2], cuts[3], grad_up, grad_down,
    )


def solution(mesh):
    tok = P(None, ("rep", "fsdp"), "seq", None)
    one, two = P("fsdp"), P("fsdp", None)
    in_specs = (tok, P(None, ("rep", "fsdp"), None), one, one, two, one, one, two, one, one, two, two, tok)
    out_specs = (tok, tok, one, one, two, one, one, two, one, one, two, two)
    return jax.shard_map(on_device, mesh=mesh, in_specs=in_specs, out_specs=out_specs, check_vma=False)
```

time: 1280 us -> 508 us (0.40)
  waiting for transfers between devices: 706 us -> 164 us
  matrix products: 268 us -> 0 us
  Pallas kernels: 0 us -> 130 us
  local copies, waits for them, and re-layouts: 131 us -> 39.1 us
  starting transfers between devices: 1.44 us -> 58.4 us
  other arithmetic: 81.9 us -> 38.1 us
    psum x1 -> x0, waiting for transfers between devices: 325 us -> none  [on_device(): running = lax.psum(owned, ('rep', 'seq'))]
    dot_general x108 -> x0, matrix products: 268 us -> none  [the longest x24 46.2 us: group_scores(): jnp.einsum('rqhd,rkhd->rhqk', q_group, k_group, preferred_element_type=jn...]
    reduce_scatter x8 -> x0, waiting for transfers between devices: 217 us -> none  [the longest x2 132 us: on_device(): lax.psum_scatter(join_groups(grad_vg).astype(jnp.bfloat16), 'seq', scatte...]
    all_gather x8 -> x1, waiting for transfers between devices: 160 us -> 0.01 us  [on_device(): lax.all_gather(piece, 'seq', axis_index_groups=[[q * team + p for p in ra...]
    ppermute x0 -> x42, waiting for transfers between devices: none -> 130 us  [flip(): return lax.ppermute(value, axis, [(i, i ^ mask) for i in range(size)])]
    pallas_call x0 -> x7, Pallas kernels: none -> 130 us  [the longest x1 28.2 us: attend_back(): pl.pallas_call(functools.partial(attend_back_body, heads, hd), grid=(bloc...]
    ppermute x0 -> x42, starting transfers between devices: none -> 45.2 us  [flip(): return lax.ppermute(value, axis, [(i, i ^ mask) for i in range(size)])]
    reduce_sum x37 -> x4, other arithmetic: 35.4 us -> 0.26 us  [the longest x1 0.11 us: on_device(): total = jnp.sum(lengths[:, :-1], axis=-1)]
  transfers between devices with their start and end apart: 17 -> 45, of which waited for: 13 -> 19; matrix products, arithmetic and copies ran while one was open for 27% -> 11% of each run, Pallas kernels for 0% -> 17%
where the time goes in v1:
time: 508 us; the launch traced here: 506 us
  waiting for transfers between devices  164 us (32%)
  Pallas kernels  130 us (26%)
  blocking collectives  61.7 us (12%)
  starting transfers between devices  58.4 us (11%)
  local copies, waits for them, and re-layouts  39.1 us (8%)
  other arithmetic  38.1 us (8%)
  between operations  14.8 us (3%)
    ppermute x42, waiting for transfers between devices, flip(): return lax.ppermute(value, axis, [(i, i ^ mask) for i in range(size)])  130 us
    psum x1, blocking collectives, on_device(): small = lax.psum(small, ('rep', 'fsdp', 'seq'))  61.7 us
    ppermute x42, starting transfers between devices, flip(): return lax.ppermute(value, axis, [(i, i ^ mask) for i in range(size)])  45.2 us
    all_to_all x2, waiting for transfers between devices, exchange(): return lax.all_to_all(value, 'seq', 0, 0, tiled=True)  34 us
    pallas_call x1, Pallas kernels, attend_back(): pl.pallas_call(functools.partial(attend_back_body, heads, hd), grid=(bloc...  28.2 us
    pallas_call x1, Pallas kernels, ffn(): pl.pallas_call(body, grid_spec=pltpu.PrefetchScalarGridSpec(num_scalar_pr...  25.6 us
    pallas_call x1, Pallas kernels, attend(): pl.pallas_call(functools.partial(attend_body, heads, hd), grid=(blocks,),...  22.7 us
    pallas_call x1, Pallas kernels, weight_grads(): pl.pallas_call(body, grid_spec=pltpu.PrefetchScalarGridSpec(num_scalar_pr...  19.7 us
  transfers between devices with their start and end apart: 45, of which 19 were waited for; matrix products, arithmetic and copies ran while one was open for 11% of the time, Pallas kernels for 17%

profile of v1, /device:TPU:0, one launch (start us, length us, event | category | flops | bytes accessed | tf_op | source)
XLA Modules:
  0.0 506.4 jit_solution(10842016772481766408)
XLA Ops:
  24.6 6.6 %collective-permute-done.4.refs_4_ = bf16[256,768]{1,0:T(8,128)(2,1)} collective-permute-done((bf16[256,768]{1,0:T(8,128)(2,1)}, bf16[256,768]{1,0:T(8,128)(2,1)}, u32[]{:S(2)}, u32[]{:S(2)}) %collective-permute-start.4) | collective-permute-done | bytes 393248 | tf_op jit(solution)/shard_map/ppermute | solution.py:571
  36.0 5.7 %collective-permute-done.5.refs_5_ = bf16[256,768]{1,0:T(8,128)(2,1)} collective-permute-done((bf16[256,768]{1,0:T(8,128)(2,1)}, bf16[256,768]{1,0:T(8,128)(2,1)}, u32[]{:S(2)}, u32[]{:S(2)}) %collective-permute-start.5) | collective-permute-done | bytes 393248 | tf_op jit(solution)/shard_map/ppermute | solution.py:571
  56.1 12.2 %qkv_forward.1 = (bf16[3,128,2048]{2,1,0:T(8,128)(2,1)}, bf16[3,2048,128]{2,1,0:T(8,128)(2,1)}, bf16[3,64,2048]{2,1,0:T(8,128)(2,1)}, bf16[3,2048,64]{2,1,0:T(8,...) custom-call(s32[3]{0:T(128)} %pad_add_fusion.meta, s32[2,8]{1,0:T(2,128)} %bitcast.149, ...), custom_call_target="tpu_custom_call" | custom-call | tf_op jit(solution)/shard_map/forward_attention/qkv_forward/pallas_call | solution.py:99
  68.3 22.7 %attention_forward.1 = (bf16[8,192,256]{2,1,0:T(8,128)(2,1)}, f32[3,64,2048]{2,1,0:T(8,128)}, f32[3,1,2048]{2,1,0:T(1,128)}) custom-call(s32[3]{0:T(128)} %pad_add_fusion.meta, s32[2,8]{1,0:T(2,128)} %bitcast.150, bf16[3,128,2048]{2,1,0:T(8,128)(2,1)} %get-tuple-element.37.qt_ref, bf16[3,2048,128]{2,1,0:T(8,128)(2,1)} %get-tuple-element.38.ka_ref, ...), custom_call_target="tpu_custom_call" | custom-call | tf_op jit(solution)/shard_map/forward_attention/attention_forward/pallas_call | solution.py:164
  91.0 9.4 %all-to-all-start = ((bf16[8,192,256]{2,1,0:T(8,128)(2,1)}), bf16[8,192,256]{2,1,0:T(8,128)(2,1)S(1)}, u32[]{:S(2)}, u32[]{:S(2)}) async-start(bf16[8,192,256]{2,1,0:T(8,128)(2,1)} %get-tuple-element.40), calls=%async_computation | async-start | bytes 1572864 | tf_op jit(solution)/shard_map/all_to_all | solution.py:672
  102.8 13.4 %all-to-all-done = bf16[8,192,256]{2,1,0:T(8,128)(2,1)S(1)} async-done(((bf16[8,192,256]{2,1,0:T(8,128)(2,1)}), bf16[8,192,256]{2,1,0:T(8,128)(2,1)S(1)}, u32[]{:S(2)}, u32[]{:S(2)}) %all-to-all-start) | async-done | bytes 786464 | tf_op jit(solution)/shard_map/all_to_all | solution.py:672
  117.9 25.6 %ffn_both_ways.1 = (bf16[512,768]{1,0:T(8,128)(2,1)}, f32[512,768]{1,0:T(8,128)}, bf16[512,768]{1,0:T(8,128)(2,1)}, bf16[512,768]{1,0:T(8,128)(2,1)}, bf16[512,3...) custom-call(s32[3]{0:T(128)} %pad_add_fusion.meta, ...), custom_call_target="tpu_custom_call" | custom-call | tf_op jit(solution)/shard_map/feed_forward/ffn_both_ways/pallas_call | solution.py:438
  143.5 19.7 %weight_gradients.1 = bf16[2,3456,768]{2,1,0:T(8,128)(2,1)} custom-call(s32[3]{0:T(128)} %pad_add_fusion.meta, bf16[2,768,256]{2,1,0:T(8,128)(2,1)} %bitcast.124, bf16[512,768]{1,0:T(8,128)(2,1)} %get-tuple-element.58.gb_ref, bf16[512,768]{1,0:T(8,128)(2,1)} %get-tuple-element.59.h2_ref, bf16[512,3072]{1,0:T(8,128)(2,1)} %get-tuple-element.60.dup_ref, ...), custom_call_target="tpu_custom_call" | custom-call | tf_op jit(solution)/shard_map/weight_gradients/weight_gradients/pallas_call | solution.py:526
  163.2 5.2 %slice_bitcast_fusion = bf16[3456,768]{1,0:T(8,128)(2,1)} fusion(bf16[2,3456,768]{2,1,0:T(8,128)(2,1)} %weight_gradients.1), kind=kLoop, calls=%fused_computation.2 | loop fusion | bytes 10616832 | tf_op jit(solution)/shard_map/weight_gradients/squeeze | solution.py:703
  172.3 20.6 %all-to-all-done.1.go_ref = bf16[8,192,256]{2,1,0:T(8,128)(2,1)S(1)} async-done(((bf16[8,192,256]{2,1,0:T(8,128)(2,1)}), bf16[8,192,256]{2,1,0:T(8,128)(2,1)S(1)}, u32[]{:S(2)}, u32[]{:S(2)}) %all-to-all-start.1) | async-done | bytes 786464 | tf_op jit(solution)/shard_map/all_to_all | solution.py:672
  193.8 28.2 %attention_backward.1 = (f32[3,64,2048]{2,1,0:T(8,128)}, f32[3,64,2048]{2,1,0:T(8,128)}, f32[3,64,2048]{2,1,0:T(8,128)}) custom-call(s32[3]{0:T(128)} %pad_add_fusion.meta, s32[2,8]{1,0:T(2,128)} %bitcast.151, bf16[3,128,2048]{2,1,0:T(8,128)(2,1)} %get-tuple-element.37.qt_ref, bf16[3,2048,128]{2,1,0:T(8,128)(2,1)} %get-tuple-element.38.ka_ref, ...), custom_call_target="tpu_custom_call" | custom-call | tf_op jit(solution)/shard_map/backward_attention/attention_backward/pallas_call | solution.py:231
  222.0 17.3 %qkv_backward.1 = (bf16[8,256,384]{2,1,0:T(8,128)(2,1)}, bf16[8,256,384]{2,1,0:T(8,128)(2,1)}, bf16[576,768]{1,0:T(8,128)(2,1)}, f32[2,8,768]{2,1,0:T(8,128)}, f32[2,64,256]{2,1,0:T(8,128)}) custom-call(s32[3]{0:T(128)} %pad_add_fusion.meta, bf16[2048,768]{1,0:T(8,128)(2,1)} %get-tuple-element.43.x_ref, f32[3,64,2048]{2,1,0:T(8,128)} %get-tuple-element.49.dq_ref, ...), custom_call_target="tpu_custom_call" | custom-call | tf_op jit(solution)/shard_map/backward_attention/qkv_backward/pallas_call | solution.py:309
  246.8 61.7 %psum.7 = f32[3200]{0:T(1024)S(1)} all-reduce(f32[3200]{0:T(1024)S(1)} %pad_maximum_fusion.5), channel_id=1, replica_groups=mesh['rep'=2,'fsdp'=2,'seq'=8] {'rep','fsdp','seq'}, use_global_device_ids=true, to_apply=%region_4.5 | all-reduce | flops 3200 | bytes 25600 | tf_op jit(solution)/shard_map/psum | solution.py:771
  316.8 5.4 %fusion = bf16[3456,768]{1,0:T(8,128)(2,1)S(1)} fusion(bf16[3456,768]{1,0:T(8,128)(2,1)} %collective-permute-done.27, bf16[2,3456,768]{2,1,0:T(8,128)(2,1)} %weight_gradients.1), kind=kLoop, calls=%fused_computation.1 | loop fusion | flops 10616832 | bytes 15925248 | tf_op jit(solution)/shard_map/weight_gradients/convert_element_type | solution.py:594
  327.3 33.3 %collective-permute-done.24 = bf16[288,384]{1,0:T(8,128)(2,1)S(1)} collective-permute-done((bf16[288,384]{1,0:T(8,128)(2,1)S(1)}, bf16[288,384]{1,0:T(8,128)(2,1)S(1)}, u32[]{:S(2)}, u32[]{:S(2)}) %collective-permute-start.24) | collective-permute-done | bytes 221216 | tf_op jit(solution)/shard_map/first_projection_gradient/ppermute | solution.py:571
  365.6 7.2 %collective-permute-done.25 = bf16[288,384]{1,0:T(8,128)(2,1)S(1)} collective-permute-done((bf16[288,384]{1,0:T(8,128)(2,1)S(1)}, bf16[288,384]{1,0:T(8,128)(2,1)S(1)}, u32[]{:S(2)}, u32[]{:S(2)}) %collective-permute-start.25) | collective-permute-done | bytes 221216 | tf_op jit(solution)/shard_map/first_projection_gradient/ppermute | solution.py:571
  373.1 5.1 %collective-permute-done.36 = bf16[864,384]{1,0:T(8,128)(2,1)S(1)} collective-permute-done((bf16[864,384]{1,0:T(8,128)(2,1)S(1)}, bf16[864,384]{1,0:T(8,128)(2,1)S(1)}, u32[]{:S(2)}, u32[]{:S(2)}) %collective-permute-start.36) | collective-permute-done | bytes 663584 | tf_op jit(solution)/shard_map/weight_gradients/ppermute | solution.py:571
  382.9 11.0 %collective-permute-done.37 = bf16[432,384]{1,0:T(8,128)(2,1)S(1)} collective-permute-done((bf16[432,384]{1,0:T(8,128)(2,1)S(1)}, bf16[432,384]{1,0:T(8,128)(2,1)S(1)}, u32[]{:S(2)}, u32[]{:S(2)}) %collective-permute-start.37) | collective-permute-done | bytes 331808 | tf_op jit(solution)/shard_map/weight_gradients/ppermute | solution.py:571
  397.1 9.2 %collective-permute-done.30 = bf16[432,384]{1,0:T(8,128)(2,1)S(1)} collective-permute-done((bf16[432,384]{1,0:T(8,128)(2,1)S(1)}, bf16[432,384]{1,0:T(8,128)(2,1)S(1)}, u32[]{:S(2)}, u32[]{:S(2)}) %collective-permute-start.30) | collective-permute-done | bytes 331808 | tf_op jit(solution)/shard_map/weight_gradients/ppermute | solution.py:571
  406.5 6.7 %collective-permute-done.38 = bf16[432,384]{1,0:T(8,128)(2,1)} collective-permute-done((bf16[432,384]{1,0:T(8,128)(2,1)S(1)}, bf16[432,384]{1,0:T(8,128)(2,1)}, u32[]{:S(2)}, u32[]{:S(2)}) %collective-permute-start.38) | collective-permute-done | bytes 331808 | tf_op jit(solution)/shard_map/weight_gradients/ppermute | solution.py:571
  414.3 9.7 %collective-permute-done.31 = bf16[432,384]{1,0:T(8,128)(2,1)S(1)} collective-permute-done((bf16[432,384]{1,0:T(8,128)(2,1)S(1)}, bf16[432,384]{1,0:T(8,128)(2,1)S(1)}, u32[]{:S(2)}, u32[]{:S(2)}) %collective-permute-start.31) | collective-permute-done | bytes 331808 | tf_op jit(solution)/shard_map/weight_gradients/ppermute | solution.py:571
  426.0 10.3 %collective-permute-done.39 = bf16[432,384]{1,0:T(8,128)(2,1)S(1)} collective-permute-done((bf16[432,384]{1,0:T(8,128)(2,1)S(1)}, bf16[432,384]{1,0:T(8,128)(2,1)S(1)}, u32[]{:S(2)}, u32[]{:S(2)}) %collective-permute-start.39) | collective-permute-done | bytes 331808 | tf_op jit(solution)/shard_map/weight_gradients/ppermute | solution.py:571
  453.8 8.6 %collective-permute-done.33 = bf16[864,384]{1,0:T(8,128)(2,1)S(1)} collective-permute-done((bf16[864,384]{1,0:T(8,128)(2,1)S(1)}, bf16[864,384]{1,0:T(8,128)(2,1)S(1)}, u32[]{:S(2)}, u32[]{:S(2)}) %collective-permute-start.33) | collective-permute-done | bytes 663584 | tf_op jit(solution)/shard_map/weight_gradients/ppermute | solution.py:571
  476.2 10.2 %collective-permute-done.41 = bf16[1728,384]{1,0:T(8,128)(2,1)} collective-permute-done((bf16[1728,384]{1,0:T(8,128)(2,1)}, bf16[1728,384]{1,0:T(8,128)(2,1)}, u32[]{:S(2)}, u32[]{:S(2)}) %collective-permute-start.41) | collective-permute-done | bytes 1327136 | tf_op jit(solution)/shard_map/weight_gradients/ppermute | solution.py:571
  (191 shorter events, 126.5 us)
Async XLA Ops:
  9.1 22.0 %collective-permute-start.4 = (bf16[256,768]{1,0:T(8,128)(2,1)}, bf16[256,768]{1,0:T(8,128)(2,1)}, u32[]{:S(2)}, u32[]{:S(2)}) collective-permute-start(bf16[256,768]{1,0:T(8,128)(2,1)} %get-tuple-element.125), channel_id=1, source_target_pairs={{0,4},{1,5},{2,6},{3,7},{4,0},{5,1},{6,2},{7,3},{8,12},{9,13},{10,... | collective-permute-start | bytes 1179656 | tf_op jit(solution)/shard_map/ppermute | solution.py:571
  13.2 19.5 %collective-permute-start = (bf16[256,768]{1,0:T(8,128)(2,1)S(1)}, bf16[256,768]{1,0:T(8,128)(2,1)}, u32[]{:S(2)}, u32[]{:S(2)}) collective-permute-start(bf16[256,768]{1,0:T(8,128)(2,1)S(1)} %get-tuple-element.126.refs_0_), channel_id=1, source_target_pairs={{0,1},{1,0},{2,3},{3,2},{4,5},{5,4},{6,7},{7,6},{8,9},{9,8},{10,11... | collective-permute-start | bytes 1179656 | tf_op jit(solution)/shard_map/ppermute | solution.py:571
  14.7 18.6 %collective-permute-start.1 = (bf16[256,768]{1,0:T(8,128)(2,1)S(1)}, bf16[256,768]{1,0:T(8,128)(2,1)}, u32[]{:S(2)}, u32[]{:S(2)}) collective-permute-start(bf16[256,768]{1,0:T(8,128)(2,1)S(1)} %get-tuple-element.126.refs_0_), channel_id=1, source_target_pairs={{0,2},{1,3},{2,0},{3,1},{4,6},{5,7},{6,4},{7,5},{8,10},{9,11},{10,... | collective-permute-start | bytes 1179656 | tf_op jit(solution)/shard_map/ppermute | solution.py:571
  20.5 95.6 %collective-permute-start.12 = (bf16[384,3072]{1,0:T(8,128)(2,1)}, bf16[384,3072]{1,0:T(8,128)(2,1)}, u32[]{:S(2)}, u32[]{:S(2)}) collective-permute-start(bf16[384,3072]{1,0:T(8,128)(2,1)} %refs_8_.1), channel_id=1, source_target_pairs={{0,8},{8,0},{1,9},{9,1},{2,10},{10,2},{3,11},{11,3},{4,12},{12,4},... | collective-permute-start | bytes 7077896 | tf_op jit(solution)/shard_map/ppermute | solution.py:571
  24.5 91.7 %collective-permute-start.13 = (bf16[1536,768]{1,0:T(8,128)(2,1)}, bf16[1536,768]{1,0:T(8,128)(2,1)S(1)}, u32[]{:S(2)}, u32[]{:S(2)}) collective-permute-start(bf16[1536,768]{1,0:T(8,128)(2,1)} %refs_10_.1), channel_id=1, source_target_pairs={{0,8},{8,0},{1,9},{9,1},{2,10},{10,2},{3,11},{11,3},{4,12},{12,4},... | collective-permute-start | bytes 7077896 | tf_op jit(solution)/shard_map/ppermute | solution.py:571
  91.0 25.1 %all-to-all-start = ((bf16[8,192,256]{2,1,0:T(8,128)(2,1)}), bf16[8,192,256]{2,1,0:T(8,128)(2,1)S(1)}, u32[]{:S(2)}, u32[]{:S(2)}) async-start(bf16[8,192,256]{2,1,0:T(8,128)(2,1)} %get-tuple-element.40), calls=%async_computation | async-start | bytes 1572864 | tf_op jit(solution)/shard_map/all_to_all | solution.py:672
  168.3 148.5 %collective-permute-start.27 = (bf16[3456,768]{1,0:T(8,128)(2,1)}, bf16[3456,768]{1,0:T(8,128)(2,1)}, u32[]{:S(2)}, u32[]{:S(2)}) collective-permute-start(bf16[3456,768]{1,0:T(8,128)(2,1)} %slice_bitcast_fusion), channel_id=1, source_target_pairs={{0,8},{8,0},{1,9},{9,1},{2,10},{10,2},{3,11},{11,3},{4,12},{12,4},... | collective-permute-start | bytes 15925256 | tf_op jit(solution)/shard_map/weight_gradients/ppermute | solution.py:571
  168.4 24.6 %all-to-all-start.1 = ((bf16[8,192,256]{2,1,0:T(8,128)(2,1)}), bf16[8,192,256]{2,1,0:T(8,128)(2,1)S(1)}, u32[]{:S(2)}, u32[]{:S(2)}) async-start(bf16[8,192,256]{2,1,0:T(8,128)(2,1)} %bitcast.14), calls=%async_computation.1 | async-start | bytes 1572864 | tf_op jit(solution)/shard_map/all_to_all | solution.py:672
  172.1 299.1 %all-gather.2.cloned.1.call-start = ((), (), s32[]{:S(2)}) async-start(), calls=%async_computation.2 | async-start | bytes 2211840 | tf_op jit(solution)/shard_map/first_projection_gradient/all_gather | solution.py:760
  241.6 70.8 %collective-permute-start.16 = (bf16[2,256,384]{2,1,0:T(8,128)(2,1)}, bf16[2,256,384]{2,1,0:T(8,128)(2,1)}, u32[]{:S(2)}, u32[]{:S(2)}) collective-permute-start(bf16[2,256,384]{2,1,0:T(8,128)(2,1)} %get-tuple-element.123), channel_id=1, source_target_pairs={{0,2},{1,3},{2,0},{3,1},{4,6},{5,7},{6,4},{7,5},{8,10},{9,11},{10,... | collective-permute-start | bytes 1179656 | tf_op jit(solution)/shard_map/ppermute | solution.py:571
  241.6 70.9 %collective-permute-start.20 = (bf16[2,256,384]{2,1,0:T(8,128)(2,1)}, bf16[2,256,384]{2,1,0:T(8,128)(2,1)}, u32[]{:S(2)}, u32[]{:S(2)}) collective-permute-start(bf16[2,256,384]{2,1,0:T(8,128)(2,1)} %get-tuple-element.124), channel_id=1, source_target_pairs={{0,2},{1,3},{2,0},{3,1},{4,6},{5,7},{6,4},{7,5},{8,10},{9,11},{10,... | collective-permute-start | bytes 1179656 | tf_op jit(solution)/shard_map/ppermute | solution.py:571
  244.5 78.5 %collective-permute-start.14 = (bf16[2,256,384]{2,1,0:T(8,128)(2,1)}, bf16[2,256,384]{2,1,0:T(8,128)(2,1)S(1)}, u32[]{:S(2)}, u32[]{:S(2)}) collective-permute-start(bf16[2,256,384]{2,1,0:T(8,128)(2,1)} %get-tuple-element.119), channel_id=1, source_target_pairs={{0,1},{1,0},{2,3},{3,2},{4,5},{5,4},{6,7},{7,6},{8,9},{9,8},{10,11... | collective-permute-start | bytes 1179656 | tf_op jit(solution)/shard_map/ppermute | solution.py:571
  246.0 77.1 %collective-permute-start.18 = (bf16[2,256,384]{2,1,0:T(8,128)(2,1)}, bf16[2,256,384]{2,1,0:T(8,128)(2,1)S(1)}, u32[]{:S(2)}, u32[]{:S(2)}) collective-permute-start(bf16[2,256,384]{2,1,0:T(8,128)(2,1)} %get-tuple-element.120), channel_id=1, source_target_pairs={{0,1},{1,0},{2,3},{3,2},{4,5},{5,4},{6,7},{7,6},{8,9},{9,8},{10,11... | collective-permute-start | bytes 1179656 | tf_op jit(solution)/shard_map/ppermute | solution.py:571
  314.5 124.5 %collective-permute-start.21 = (bf16[256,384]{1,0:T(8,128)(2,1)}, bf16[256,384]{1,0:T(8,128)(2,1)}, u32[]{:S(2)}, u32[]{:S(2)}) collective-permute-start(bf16[256,384]{1,0:T(8,128)(2,1)} %slice_bitcast_fusion.10), channel_id=1, source_target_pairs={{0,1},{1,0},{2,3},{3,2},{4,5},{5,4},{6,7},{7,6},{8,9},{9,8},{10,11... | collective-permute-start | bytes 589832 | tf_op jit(solution)/shard_map/ppermute | solution.py:571
  322.9 38.9 %collective-permute-start.35 = (bf16[1728,384]{1,0:T(8,128)(2,1)S(1)}, bf16[1728,384]{1,0:T(8,128)(2,1)S(1)}, u32[]{:S(2)}, u32[]{:S(2)}) collective-permute-start(bf16[1728,384]{1,0:T(8,128)(2,1)S(1)} %constant_dynamic-slice_fusion.2), channel_id=1, source_target_pairs={{0,1},{1,0},{2,3},{3,2},{4,5},{5,4},{6,7},{7,6},{8,9},{9,8},{10,11... | collective-permute-start | bytes 3981320 | tf_op jit(solution)/shard_map/weight_gradients/ppermute | solution.py:571
  324.5 38.4 %collective-permute-start.28 = (bf16[1728,384]{1,0:T(8,128)(2,1)S(1)}, bf16[1728,384]{1,0:T(8,128)(2,1)S(1)}, u32[]{:S(2)}, u32[]{:S(2)}) collective-permute-start(bf16[1728,384]{1,0:T(8,128)(2,1)S(1)} %constant_dynamic-slice_fusion.5), channel_id=1, source_target_pairs={{0,16},{16,0},{1,17},{17,1},{2,18},{18,2},{3,19},{19,3},{4,20},{20... | collective-permute-start | bytes 3981320 | tf_op jit(solution)/shard_map/weight_gradients/ppermute | solution.py:571
  325.7 34.9 %collective-permute-start.24 = (bf16[288,384]{1,0:T(8,128)(2,1)S(1)}, bf16[288,384]{1,0:T(8,128)(2,1)S(1)}, u32[]{:S(2)}, u32[]{:S(2)}) collective-permute-start(bf16[288,384]{1,0:T(8,128)(2,1)S(1)} %constant_dynamic-slice_fusion.6), channel_id=1, source_target_pairs={{0,16},{16,0},{1,17},{17,1},{2,18},{18,2},{3,19},{19,3},{4,20},{20... | collective-permute-start | bytes 663560 | tf_op jit(solution)/shard_map/first_projection_gradient/ppermute | solution.py:571
  326.9 119.4 %collective-permute-start.19 = (bf16[256,384]{1,0:T(8,128)(2,1)S(1)}, bf16[256,384]{1,0:T(8,128)(2,1)}, u32[]{:S(2)}, u32[]{:S(2)}) collective-permute-start(bf16[256,384]{1,0:T(8,128)(2,1)S(1)} %slice_bitcast_fusion.12), channel_id=1, source_target_pairs={{0,2},{1,3},{2,0},{3,1},{4,6},{5,7},{6,4},{7,5},{8,10},{9,11},{10,... | collective-permute-start | bytes 589832 | tf_op jit(solution)/shard_map/ppermute | solution.py:571
  372.8 80.1 %collective-permute-start.17 = (bf16[256,384]{1,0:T(8,128)(2,1)}, bf16[256,384]{1,0:T(8,128)(2,1)}, u32[]{:S(2)}, u32[]{:S(2)}) collective-permute-start(bf16[256,384]{1,0:T(8,128)(2,1)} %slice_bitcast_fusion.14), channel_id=1, source_target_pairs={{0,1},{1,0},{2,3},{3,2},{4,5},{5,4},{6,7},{7,6},{8,9},{9,8},{10,11... | collective-permute-start | bytes 589832 | tf_op jit(solution)/shard_map/ppermute | solution.py:571
  394.0 19.1 %collective-permute-start.38 = (bf16[432,384]{1,0:T(8,128)(2,1)S(1)}, bf16[432,384]{1,0:T(8,128)(2,1)}, u32[]{:S(2)}, u32[]{:S(2)}) collective-permute-start(bf16[432,384]{1,0:T(8,128)(2,1)S(1)} %add_convert_fusion.6), channel_id=1, source_target_pairs={{0,4},{1,5},{2,6},{3,7},{4,0},{5,1},{6,2},{7,3},{8,12},{9,13},{10,... | collective-permute-start | bytes 995336 | tf_op jit(solution)/shard_map/weight_gradients/ppermute | solution.py:571
  414.2 22.0 %collective-permute-start.39 = (bf16[432,384]{1,0:T(8,128)(2,1)S(1)}, bf16[432,384]{1,0:T(8,128)(2,1)S(1)}, u32[]{:S(2)}, u32[]{:S(2)}) collective-permute-start(bf16[432,384]{1,0:T(8,128)(2,1)S(1)} %add_convert_fusion.5), channel_id=1, source_target_pairs={{0,2},{1,3},{2,0},{3,1},{4,6},{5,7},{6,4},{7,5},{8,10},{9,11},{10,... | collective-permute-start | bytes 995336 | tf_op jit(solution)/shard_map/weight_gradients/ppermute | solution.py:571
  424.0 41.5 %collective-permute-start.15 = (bf16[256,384]{1,0:T(8,128)(2,1)S(1)}, bf16[256,384]{1,0:T(8,128)(2,1)S(1)}, u32[]{:S(2)}, u32[]{:S(2)}) collective-permute-start(bf16[256,384]{1,0:T(8,128)(2,1)S(1)} %slice_bitcast_fusion.16), channel_id=1, source_target_pairs={{0,2},{1,3},{2,0},{3,1},{4,6},{5,7},{6,4},{7,5},{8,10},{9,11},{10,... | collective-permute-start | bytes 589832 | tf_op jit(solution)/shard_map/ppermute | solution.py:571
  451.2 35.2 %collective-permute-start.41 = (bf16[1728,384]{1,0:T(8,128)(2,1)}, bf16[1728,384]{1,0:T(8,128)(2,1)}, u32[]{:S(2)}, u32[]{:S(2)}) collective-permute-start(bf16[1728,384]{1,0:T(8,128)(2,1)} %maximum_select_fusion.3), channel_id=1, source_target_pairs={{0,1},{1,0},{2,3},{3,2},{4,5},{5,4},{6,7},{7,6},{8,9},{9,8},{10,11... | collective-permute-start | bytes 3981320 | tf_op jit(solution)/shard_map/weight_gradients/ppermute | solution.py:571
  463.9 25.7 %collective-permute-start.34 = (bf16[1728,384]{1,0:T(8,128)(2,1)}, bf16[1728,384]{1,0:T(8,128)(2,1)}, u32[]{:S(2)}, u32[]{:S(2)}) collective-permute-start(bf16[1728,384]{1,0:T(8,128)(2,1)} %maximum_select_fusion.2), channel_id=1, source_target_pairs={{0,16},{16,0},{1,17},{17,1},{2,18},{18,2},{3,19},{19,3},{4,20},{20... | collective-permute-start | bytes 3981320 | tf_op jit(solution)/shard_map/weight_gradients/ppermute | solution.py:571
  (34 other events, 463.7 us)
Sparse Core Ops, SparseCore 0:
  397.3 45.0 all-gather.1

commit v2 on v1

--- a/solution.py
+++ b/solution.py
@@ -25,6 +25,10 @@
 
 def params(**kw):
     return pltpu.CompilerParams(vmem_limit_bytes=60 * 1024 * 1024, **kw)
+
+
+def cost(us):
+    return pl.CostEstimate(flops=int(us * 1.1e9), bytes_accessed=1024, transcendentals=0)
 
 
 def norm_rows(v):
@@ -109,6 +113,7 @@
         in_specs=[smem, smem] + [vmem] * 13,
         out_specs=(vmem,) * 6,
         compiler_params=params(),
+        cost_estimate=cost(12),
         name="qkv_forward",
     )(meta, lengths, *slots, w_t, gain, bias, gq, gk)
 
@@ -182,6 +187,7 @@
             pl.BlockSpec((heads, 1, BLK), lambda i: (0, 0, i)),
         ),
         compiler_params=params(),
+        cost_estimate=cost(25),
         name="attention_forward",
     )(meta, lengths, qt, ka, vt)
 
@@ -223,11 +229,12 @@
         dq_ref[h] = done[h] * (hd**-0.5)
 
 
-def attend_back(meta, lengths, qt, ka, kt, v, of, ls, go, heads, hd):
+def attend_back(meta, lengths, qt, ka, kt, v, of, ls, go, at, heads, hd):
     length = qt.shape[2]
     blocks = length // BLK
     smem = pl.BlockSpec(memory_space=pltpu.SMEM)
-    whole = lambda *shape: pl.BlockSpec(shape, lambda i: (0,) * len(shape))
+    whole = lambda *shape: pl.BlockSpec(shape, lambda i: (at, 0, 0))
+    all_out = lambda *shape: pl.BlockSpec(shape, lambda i: (0, 0, 0))
     return pl.pallas_call(
         functools.partial(attend_back_body, heads, hd),
         grid=(blocks,),
@@ -235,28 +242,30 @@
         in_specs=[
             smem,
             smem,
-            pl.BlockSpec((heads, 2 * hd, BLK), lambda i: (0, 0, i)),
+            pl.BlockSpec((heads, 2 * hd, BLK), lambda i: (at, 0, i)),
             whole(heads, length, 2 * hd),
             whole(heads, hd, length),
             whole(heads, length, hd),
-            pl.BlockSpec((heads, hd, BLK), lambda i: (0, 0, i)),
-            pl.BlockSpec((heads, 1, BLK), lambda i: (0, 0, i)),
-            pl.BlockSpec((1, heads * hd, BLK), lambda i: (i, 0, 0)),
+            pl.BlockSpec((heads, hd, BLK), lambda i: (at, 0, i)),
+            pl.BlockSpec((heads, 1, BLK), lambda i: (at, 0, i)),
+            pl.BlockSpec((1, heads * hd, BLK), lambda i: (i, at, 0)),
         ],
         out_specs=(
             pl.BlockSpec((heads, hd, BLK), lambda i: (0, 0, i)),
-            whole(heads, hd, length),
-            whole(heads, hd, length),
+            all_out(heads, hd, length),
+            all_out(heads, hd, length),
         ),
         compiler_params=params(),
+        cost_estimate=cost(11 * heads),
         name="attention_backward",
     )(meta, lengths, qt, ka, kt, v, of, ls, go)
 
 
 def qkv_back_body(
-    heads, hd, meta, x_ref, dq_ref, dk_ref, dv_ref, w_ref, g_ref, b_ref, gq_ref, gk_ref,
-    da_ref, db_ref, dw_ref, vec_ref, gain_ref, acc_ref,
+    heads, hd, meta, x_ref, *refs
 ):
+    dqs, dks, dvs = refs[:heads], refs[heads : 2 * heads], refs[2 * heads : 3 * heads]
+    w_ref, g_ref, b_ref, gq_ref, gk_ref, da_ref, db_ref, dw_ref, vec_ref, gain_ref, acc_ref = refs[3 * heads :]
     i = pl.program_id(0)
     wid = heads * hd
 
@@ -270,10 +279,10 @@
     first = (hat * g_ref[...] + b_ref[...]).astype(BF16)
     qk = mm(w_ref[: 2 * wid, :], first, NT)
     pieces = []
-    for at, gain, grad in ((0, gq_ref, dq_ref), (1, gk_ref, dk_ref)):
+    for at, gain, grad in ((0, gq_ref, dqs), (1, gk_ref, dks)):
         for h in range(heads):
             unit, inv = norm_cols(qk[at * wid + h * hd : at * wid + (h + 1) * hd])
-            gy = grad[h]
+            gy = grad[h][0]
             gain_ref[at] += gy * unit
             e = gy * gain[...]
             pieces.append(
@@ -285,7 +294,7 @@
                 )
             )
     for h in range(heads):
-        pieces.append(dv_ref[h])
+        pieces.append(dvs[h][0])
     grad = jnp.concatenate(pieces, axis=0).astype(BF16)
     acc_ref[...] += mm(grad, first)
     back = mm(grad, w_ref[...], TN)
@@ -304,7 +313,7 @@
     length, width = x.shape
     blocks = length // BLK
     whole = lambda *shape: pl.BlockSpec(shape, lambda i, m: (0,) * len(shape))
-    part = pl.BlockSpec((heads, hd, BLK), lambda i, m: (0, 0, i))
+    part = pl.BlockSpec((1, hd, BLK), lambda i, m: (0, 0, i))
     grads = pl.BlockSpec((1, BLK, width // 2), lambda i, m: (jnp.bitwise_xor(i, m[0]), 0, 0))
     return pl.pallas_call(
         functools.partial(qkv_back_body, heads, hd),
@@ -313,9 +322,7 @@
             grid=(blocks,),
             in_specs=[
                 pl.BlockSpec((BLK, width), lambda i, m: (i, 0)),
-                part,
-                part,
-                part,
+                *([part] * (3 * heads)),
                 whole(*w_t.shape),
                 whole(1, width),
                 whole(1, width),
@@ -339,8 +346,9 @@
             jax.ShapeDtypeStruct((2, hd, BLK), F32),
         ),
         compiler_params=params(),
+        cost_estimate=cost(17),
         name="qkv_backward",
-    )(meta, x, dq, dk, dv, w_t, gain, bias, gq, gk)
+    )(meta, x, *dq, *dk, *dv, w_t, gain, bias, gq, gk)
 
 
 def gelu_pair(u):
@@ -484,64 +492,81 @@
             jax.ShapeDtypeStruct((2, 8, width), F32),
         ),
         compiler_params=params(),
+        cost_estimate=cost(25),
         name="ffn_both_ways",
     )(meta, attn_t, x, dy, valid, gain, bias, wo, wo_p, up, up_p, dn, dn_p)
 
 
-def weight_grads(meta, attn_t, gb, h2, dup, act, dy):
+def down_grads(meta, own, act, dy):
     tokens, width = dy.shape
-    hidden = act.shape[1]
+    half = width // 2
+    blocks = act.shape[1] // 2 // half
+
+    def body(meta, act_ref, dy_ref, out_ref):
+        out_ref[...] = mm(act_ref[...], dy_ref[...], TN).astype(BF16)
+
+    side = (lambda m: m[2]) if own else (lambda m: 1 - m[2])
+    return pl.pallas_call(
+        body,
+        grid_spec=pltpu.PrefetchScalarGridSpec(
+            num_scalar_prefetch=1,
+            grid=(blocks,),
+            in_specs=[
+                pl.BlockSpec((tokens, half), lambda j, m: (0, side(m) * blocks + j)),
+                pl.BlockSpec((tokens, width), lambda j, m: (0, 0)),
+            ],
+            out_specs=pl.BlockSpec((half, width), lambda j, m: (j, 0)),
+        ),
+        out_shape=jax.ShapeDtypeStruct((blocks * half, width), BF16),
+        compiler_params=params(),
+        cost_estimate=cost(5),
+        name="down_gradient",
+    )(meta, act, dy)
+
+
+def up_out_grads(meta, own, attn_t, gb, h2, dup):
+    tokens, width = gb.shape
+    hidden = dup.shape[1]
     half = width // 2
     packs, _, lanes = attn_t.shape
-    n_up = hidden // width
-    n_dn = hidden // 2 // half
-    per = 1 + n_up + n_dn
-
-    def body(meta, at_ref, gb_ref, h2_ref, dup_ref, act_ref, dy_ref, out_ref):
-        s, j = pl.program_id(0), pl.program_id(1)
-        side = jnp.where(s == 0, 1 - meta[2], meta[2])
-
-        @pl.when(j == 0)
+    blocks = hidden // width
+
+    def body(meta, at_ref, gb_ref, h2_ref, dup_ref, out_ref):
+        j = pl.program_id(0)
+        side = meta[2] if own else 1 - meta[2]
+
+        @pl.when(j < blocks)
+        def _():
+            part = jnp.where(side == 0, h2_ref[:, :half], h2_ref[:, half:])
+            out_ref[...] = mm(part, dup_ref[...], TN).astype(BF16)
+
+        @pl.when(j == blocks)
         def _():
             rows = pl.ds(pl.multiple_of(side * half, half), half)
             total = jnp.zeros((half, width), F32)
             for p in range(packs):
                 total = total + mm(at_ref[p, rows, :], gb_ref[p * lanes : (p + 1) * lanes, :])
-            out_ref[0] = total.astype(BF16)
-
-        @pl.when((j >= 1) & (j <= n_up))
-        def _():
-            part = jnp.where(side == 0, h2_ref[:, :half], h2_ref[:, half:])
-            out_ref[0] = mm(part, dup_ref[...], TN).astype(BF16)
-
-        @pl.when(j > n_up)
-        def _():
-            out_ref[0] = mm(act_ref[...], dy_ref[...], TN).astype(BF16)
-
-    def act_at(s, j, m):
-        side = jnp.where(s == 0, 1 - m[2], m[2])
-        return (0, side * n_dn + jnp.clip(j - 1 - n_up, 0, n_dn - 1))
-
-    whole = lambda *shape: pl.BlockSpec(shape, lambda s, j, m: (0,) * len(shape))
+            out_ref[...] = total.astype(BF16)
+
+    whole = lambda *shape: pl.BlockSpec(shape, lambda j, m: (0,) * len(shape))
     return pl.pallas_call(
         body,
         grid_spec=pltpu.PrefetchScalarGridSpec(
             num_scalar_prefetch=1,
-            grid=(2, per),
+            grid=(blocks + 1,),
             in_specs=[
                 whole(*attn_t.shape),
                 whole(tokens, width),
                 whole(tokens, width),
-                pl.BlockSpec((tokens, width), lambda s, j, m: (0, jnp.clip(j - 1, 0, n_up - 1))),
-                pl.BlockSpec((tokens, half), act_at),
-                whole(tokens, width),
+                pl.BlockSpec((tokens, width), lambda j, m: (0, jnp.minimum(j, blocks - 1))),
             ],
-            out_specs=pl.BlockSpec((1, half, width), lambda s, j, m: (s, j, 0)),
-        ),
-        out_shape=jax.ShapeDtypeStruct((2, per * half, width), BF16),
+            out_specs=pl.BlockSpec((half, width), lambda j, m: (j, 0)),
+        ),
+        out_shape=jax.ShapeDtypeStruct(((blocks + 1) * half, width), BF16),
         compiler_params=params(),
-        name="weight_gradients",
-    )(meta, attn_t, gb, h2, dup, act, dy)
+        cost_estimate=cost(5),
+        name="up_out_gradient",
+    )(meta, attn_t, gb, h2, dup)
 
 
 def finish_body(x_ref, gm_ref, back_ref, g_ref, out_ref):
@@ -562,6 +587,7 @@
         out_specs=rows,
         out_shape=jax.ShapeDtypeStruct((tokens, width), F32),
         compiler_params=params(),
+        cost_estimate=cost(4),
         name="first_norm_backward",
     )(x, gm, back, gain)
 
@@ -698,29 +724,26 @@
         got = got.reshape(8, BLK // local, heads * hd, local)
         grad_o = jnp.swapaxes(got, 1, 2).reshape(8, heads * hd, BLK)
 
+    masks = [1 << k for k in range(n.bit_length() - 1)]
     with jax.named_scope("weight_gradients"):
-        grads = weight_grads(meta, attn_t, grad_branch, h2, dup, act, dy)
-        big = add(grads[1], swap(grads[0]))
-        masks = [1 << k for k in range(n.bit_length() - 1)]
-        left = reduce_all(
-            big[:, :half],
-            [("rep", 1), ("seq", masks[0]), ("seq", masks[1])],
-            [("seq", m) for m in masks[2:]],
-        )
-        right = reduce_all(
-            big[:, half:],
-            [("seq", masks[0]), ("rep", 1), ("seq", masks[1])],
-            [("seq", m) for m in masks[2:]],
-        )
-        big = jnp.concatenate([left, right], axis=1).astype(F32)
-        grad_out = big[:half]
+        far_d = swap(down_grads(meta, False, act, dy))
+        grad_d = add(down_grads(meta, True, act, dy), far_d)
+        far_u = swap(up_out_grads(meta, False, attn_t, grad_branch, h2, dup))
+        grad_u = add(up_out_grads(meta, True, attn_t, grad_branch, h2, dup), far_u)
+        rest = [("seq", m) for m in masks[2:]]
+        grad_d = reduce_all(grad_d, [("rep", 1), ("seq", 1), ("seq", 2)], rest)
+        grad_u = reduce_all(grad_u, [("seq", 1), ("rep", 1), ("seq", 2)], rest)
         hidden = up_weight.shape[1]
         n_up = hidden // width
-        grad_up = jnp.concatenate([big[half * (1 + k) : half * (2 + k)] for k in range(n_up)], axis=1)
-        grad_down = big[half * (1 + n_up) :]
+        grad_down = grad_d.astype(F32)
+        grad_up = jnp.concatenate([grad_u[half * k : half * (k + 1)] for k in range(n_up)], axis=1).astype(F32)
+        grad_out = grad_u[half * n_up :].astype(F32)
 
     with jax.named_scope("backward_attention"):
-        dq, dk, dv = attend_back(meta, lengths, qt, ka, kt, v, attn_f, logsum, grad_o, heads, hd)
+        parts = [
+            attend_back(meta, lengths, qt, ka, kt, v, attn_f, logsum, grad_o, h, 1, hd) for h in range(heads)
+        ]
+        dq, dk, dv = zip(*parts)
         back_a, back_b, dw_t, vec1, gains = qkv_back(
             meta, x_row, dq, dk, dv, w_t, g1, b1, gq, gk, heads, hd
         )
@@ -752,26 +775,35 @@
     grad_tokens = finish(x_home, grad_mid, back, g1)
 
     with jax.named_scope("first_projection_gradient"):
-        n3 = 3 * heads * hd
         keep, send = halves(dw_t, core, 1)
         piece = add(keep, swap(send))
-        step_rest = [("seq", m) for m in masks if m >= team]
-        piece = reduce_all(piece, [("rep", 1)], step_rest)
-        parts = lax.all_gather(piece, "seq", axis_index_groups=[[q * team + p for p in range(team)] for q in range(every)])
-        parts = parts.reshape(team, 3, heads * hd, half)
-        grad_qkv = jnp.transpose(parts, (3, 1, 0, 2)).reshape(half, 3 * width).astype(F32)
-
-    small = jnp.concatenate(
-        [
-            jnp.sum(vec1, axis=1).reshape(-1),
-            jnp.sum(vec2, axis=1).reshape(-1),
-            jnp.sum(gains, axis=-1).reshape(-1),
-        ]
-    )
-    small = lax.psum(small, ("rep", "fsdp", "seq"))
-    cuts = [small[k * width : (k + 1) * width] for k in range(4)]
-    cuts += [small[4 * width : 4 * width + hd], small[4 * width + hd :]]
-    cuts = [lax.dynamic_slice_in_dim(c, core * (c.shape[0] // 2), c.shape[0] // 2, 0) for c in cuts]
+        keep, send = halves(piece, bit("rep", 1))
+        piece = add(keep, flip(send, "rep", 1))
+        for mask in masks:
+            if mask >= team:
+                piece = add(piece, flip(piece, "seq", mask))
+        piece = piece[None]
+        for mask in masks:
+            if mask < team:
+                piece = join(piece, flip(piece, "seq", mask), bit("seq", mask))
+        piece = join(piece, flip(piece, "rep", 1), bit("rep", 1), 1)
+        piece = piece.reshape(team, 3, heads * hd, half)
+        grad_qkv = jnp.transpose(piece, (3, 1, 0, 2)).reshape(half, 3 * width).astype(F32)
+
+    with jax.named_scope("vector_gradients"):
+        small = jnp.concatenate([vec1, vec2]).sum(axis=1).reshape(4, 2, half)
+        small = jnp.concatenate(
+            [jnp.swapaxes(small, 0, 1).reshape(2, 4 * half)]
+            + [gains[k].sum(axis=-1).reshape(2, hd // 2) for k in range(2)],
+            axis=1,
+        )
+        keep, send = halves(small, core)
+        small = keep + swap(send)
+        for axis, mask in [("rep", 1)] + [("seq", m) for m in masks]:
+            small = small + flip(small, axis, mask)
+        small = small[0]
+        cuts = [small[k * half : (k + 1) * half] for k in range(4)]
+        cuts += [small[4 * half : 4 * half + hd // 2], small[4 * half + hd // 2 :]]
     shape = tokens.shape
     return (
         output.reshape(shape), grad_tokens.reshape(shape), cuts[0], cuts[1], grad_qkv, cuts[4], cuts[5],

time: 508 us -> 485 us (0.955)
  blocking collectives: 61.7 us -> 0 us
  waiting for transfers between devices: 164 us -> 218 us
  Pallas kernels: 130 us -> 164 us
  local copies, waits for them, and re-layouts: 39.1 us -> 18.6 us
  between operations: 14.8 us -> 1.49 us
  other arithmetic: 38.1 us -> 29.2 us
    ppermute x42 -> x50, waiting for transfers between devices: 130 us -> 192 us  [flip(): return lax.ppermute(value, axis, [(i, i ^ mask) for i in range(size)])]
    psum x1 -> x0, blocking collectives: 61.7 us -> none  [on_device(): small = lax.psum(small, ('rep', 'fsdp', 'seq'))]
    pallas_call x1 -> x3, Pallas kernels: 28.2 us -> 50.4 us  [attend_back(): pl.pallas_call(functools.partial(attend_back_body, heads, hd), grid=(bloc...]
    all_to_all x2, waiting for transfers between devices: 34 us -> 25.6 us  [exchange(): return lax.all_to_all(value, 'seq', 0, 0, tiled=True)]
    convert_element_type x18, other arithmetic: 12.6 us -> 5.6 us  [add(): return (a.astype(F32) + b.astype(F32)).astype(BF16)]
    pallas_call x1, Pallas kernels: 22.7 us -> 28.7 us  [attend(): pl.pallas_call(functools.partial(attend_body, heads, hd), grid=(blocks,),...]
    pallas_call x1 -> x4, Pallas kernels: 19.7 us -> 25.4 us  [the longest x2 14.2 us: up_out_grads(): pl.pallas_call(body, grid_spec=pltpu.PrefetchScalarGridSpec(num_scalar_pr...]
    all_to_all x2, starting transfers between devices: 13.1 us -> 7.96 us  [exchange(): return lax.all_to_all(value, 'seq', 0, 0, tiled=True)]
  transfers between devices with their start and end apart: 45 -> 52, of which waited for: 19 -> 25; matrix products, arithmetic and copies ran while one was open for 11% -> 8% of each run, Pallas kernels for 17% -> 29%
where the time goes in v2:
time: 485 us; the launch traced here: 486 us
  waiting for transfers between devices  218 us (45%)
  Pallas kernels  164 us (34%)
  starting transfers between devices  55 us (11%)
  other arithmetic  29.2 us (6%)
  local copies, waits for them, and re-layouts  18.6 us (4%)
    ppermute x50, waiting for transfers between devices, flip(): return lax.ppermute(value, axis, [(i, i ^ mask) for i in range(size)])  192 us
    pallas_call x3, Pallas kernels, attend_back(): pl.pallas_call(functools.partial(attend_back_body, heads, hd), grid=(bloc...  50.4 us
    ppermute x50, starting transfers between devices, flip(): return lax.ppermute(value, axis, [(i, i ^ mask) for i in range(size)])  47 us
    pallas_call x1, Pallas kernels, attend(): pl.pallas_call(functools.partial(attend_body, heads, hd), grid=(blocks,),...  28.7 us
    all_to_all x2, waiting for transfers between devices, exchange(): return lax.all_to_all(value, 'seq', 0, 0, tiled=True)  25.6 us
    pallas_call x1, Pallas kernels, ffn(): pl.pallas_call(body, grid_spec=pltpu.PrefetchScalarGridSpec(num_scalar_pr...  25.6 us
    pallas_call x1, Pallas kernels, qkv_back(): pl.pallas_call(functools.partial(qkv_back_body, heads, hd), grid_spec=plt...  17.4 us
    pallas_call x2, Pallas kernels, up_out_grads(): pl.pallas_call(body, grid_spec=pltpu.PrefetchScalarGridSpec(num_scalar_pr...  14.2 us
  transfers between devices with their start and end apart: 52, of which 25 were waited for; matrix products, arithmetic and copies ran while one was open for 8% of the time, Pallas kernels for 29%

profile of v2, /device:TPU:0, one launch (start us, length us, event | category | flops | bytes accessed | tf_op | source)
XLA Modules:
  0.0 486.4 jit_solution(17965273242362526266)
XLA Ops:
  13.9 12.4 %collective-permute-done.4.refs_4_ = bf16[256,768]{1,0:T(8,128)(2,1)} collective-permute-done((bf16[256,768]{1,0:T(8,128)(2,1)S(1)}, bf16[256,768]{1,0:T(8,128)(2,1)}, u32[]{:S(2)}, u32[]{:S(2)}) %collective-permute-start.4) | collective-permute-done | bytes 393248 | tf_op jit(solution)/shard_map/ppermute | solution.py:597
  46.8 12.2 %qkv_forward.1 = (bf16[3,128,2048]{2,1,0:T(8,128)(2,1)}, bf16[3,2048,128]{2,1,0:T(8,128)(2,1)}, bf16[3,64,2048]{2,1,0:T(8,128)(2,1)}, bf16[3,2048,64]{2,1,0:T(8,...) custom-call(s32[3]{0:T(128)} %pad_add_fusion.meta, s32[2,8]{1,0:T(2,128)} %bitcast.153, ...), custom_call_target="tpu_custom_call" | custom-call | flops 13200000000 | bytes 1024 | tf_op jit(solution)/shard_map/forward_attention/qkv_forward/pallas_call | solution.py:103
  59.1 28.7 %attention_forward.1 = (bf16[8,192,256]{2,1,0:T(8,128)(2,1)}, f32[3,64,2048]{2,1,0:T(8,128)}, f32[3,1,2048]{2,1,0:T(1,128)}) custom-call(s32[3]{0:T(128)} %pad_add_fusion.meta, s32[2,8]{1,0:T(2,128)} %bitcast.154, bf16[3,128,2048]{2,1,0:T(8,128)(2,1)} %get-tuple-element.43.qt_ref, bf16[3,2048,128]{2,1,0:T(8,128)(2,1)} %get-tuple-element.44.ka_ref, ...), custom_call_target="tpu_custom_call" | custom-call | flops 27499999232 | bytes 1024 | tf_op jit(solution)/shard_map/forward_attention/attention_forward/pallas_call | solution.py:169
  94.3 18.3 %all-to-all-done = bf16[8,192,256]{2,1,0:T(8,128)(2,1)S(1)} async-done(((bf16[8,192,256]{2,1,0:T(8,128)(2,1)}), bf16[8,192,256]{2,1,0:T(8,128)(2,1)S(1)}, u32[]{:S(2)}, u32[]{:S(2)}) %all-to-all-start) | async-done | bytes 786464 | tf_op jit(solution)/shard_map/all_to_all | solution.py:698
  113.5 25.6 %ffn_both_ways.1 = (bf16[512,768]{1,0:T(8,128)(2,1)}, f32[512,768]{1,0:T(8,128)}, bf16[512,768]{1,0:T(8,128)(2,1)}, bf16[512,768]{1,0:T(8,128)(2,1)}, bf16[512,3...) custom-call(s32[3]{0:T(128)} %pad_add_fusion.meta, ...), custom_call_target="tpu_custom_call" | custom-call | flops 27499999232 | bytes 1024 | tf_op jit(solution)/shard_map/feed_forward/ffn_both_ways/pallas_call | solution.py:446
  143.5 7.1 %up_out_gradient.3 = bf16[1920,768]{1,0:T(8,128)(2,1)} custom-call(s32[3]{0:T(128)} %pad_add_fusion.meta, bf16[2,768,256]{2,1,0:T(8,128)(2,1)} %bitcast.134, bf16[512,768]{1,0:T(8,128)(2,1)} %get-tuple-element.70.gb_ref, bf16[512,768]{1,0:T(8,128)(2,1)} %get-tuple-element.71.h2_ref, bf16[512,3072]{1,0:T(8,128)(2,1)} %get-tuple-element.72.dup_ref), custom_call_target="tpu_custom_call" | custom-call | flops 5500000256 | bytes 1024 | tf_op jit(solution)/shard_map/weight_gradients/up_out_gradient/pallas_call | solution.py:552
  150.7 5.6 %down_gradient.3 = bf16[1536,768]{1,0:T(8,128)(2,1)} custom-call(s32[3]{0:T(128)} %pad_add_fusion.meta, bf16[512,3072]{1,0:T(8,128)(2,1)} %get-tuple-element.73.act_ref, bf16[512,768]{1,0:T(8,128)(2,1)} %bitcast.151), custom_call_target="tpu_custom_call" | custom-call | flops 5500000256 | bytes 1024 | tf_op jit(solution)/shard_map/weight_gradients/down_gradient/pallas_call | solution.py:509
  156.7 7.4 %all-to-all-done.1.go_ref = bf16[8,192,256]{2,1,0:T(8,128)(2,1)} async-done(((bf16[8,192,256]{2,1,0:T(8,128)(2,1)}), bf16[8,192,256]{2,1,0:T(8,128)(2,1)}, u32[]{:S(2)}, u32[]{:S(2)}) %all-to-all-start.1) | async-done | bytes 786464 | tf_op jit(solution)/shard_map/all_to_all | solution.py:698
  164.1 16.8 %attention_backward.3 = (f32[1,64,2048]{2,1,0:T(8,128)}, f32[1,64,2048]{2,1,0:T(8,128)}, f32[1,64,2048]{2,1,0:T(8,128)}) custom-call(s32[3]{0:T(128)} %pad_add_fusion.meta, s32[2,8]{1,0:T(2,128)} %bitcast.155, bf16[3,128,2048]{2,1,0:T(8,128)(2,1)} %get-tuple-element.43.qt_ref, bf16[3,2048,128]{2,1,0:T(8,128)(2,1)} %get-tuple-element.44.ka_ref, ...), custom_call_target="tpu_custom_call" | custom-call | flops 12099999744 | bytes 1024 | tf_op jit(solution)/shard_map/backward_attention/attention_backward/pallas_call | solution.py:238
  180.8 16.8 %attention_backward.4 = (f32[1,64,2048]{2,1,0:T(8,128)}, f32[1,64,2048]{2,1,0:T(8,128)}, f32[1,64,2048]{2,1,0:T(8,128)}) custom-call(s32[3]{0:T(128)} %pad_add_fusion.meta, s32[2,8]{1,0:T(2,128)} %bitcast.156, bf16[3,128,2048]{2,1,0:T(8,128)(2,1)} %get-tuple-element.43.qt_ref, bf16[3,2048,128]{2,1,0:T(8,128)(2,1)} %get-tuple-element.44.ka_ref, ...), custom_call_target="tpu_custom_call" | custom-call | flops 12099999744 | bytes 1024 | tf_op jit(solution)/shard_map/backward_attention/attention_backward/pallas_call | solution.py:238
  197.6 16.8 %attention_backward.5 = (f32[1,64,2048]{2,1,0:T(8,128)}, f32[1,64,2048]{2,1,0:T(8,128)}, f32[1,64,2048]{2,1,0:T(8,128)}) custom-call(s32[3]{0:T(128)} %pad_add_fusion.meta, s32[2,8]{1,0:T(2,128)} %bitcast.157, bf16[3,128,2048]{2,1,0:T(8,128)(2,1)} %get-tuple-element.43.qt_ref, bf16[3,2048,128]{2,1,0:T(8,128)(2,1)} %get-tuple-element.44.ka_ref, ...), custom_call_target="tpu_custom_call" | custom-call | flops 12099999744 | bytes 1024 | tf_op jit(solution)/shard_map/backward_attention/attention_backward/pallas_call | solution.py:238
  214.5 17.4 %qkv_backward.1 = (bf16[8,256,384]{2,1,0:T(8,128)(2,1)}, bf16[8,256,384]{2,1,0:T(8,128)(2,1)}, bf16[576,768]{1,0:T(8,128)(2,1)}, f32[2,8,768]{2,1,0:T(8,128)}, f32[2,64,256]{2,1,0:T(8,128)}) custom-call(s32[3]{0:T(128)} %pad_add_fusion.meta, bf16[2048,768]{1,0:T(8,128)(2,1)} %get-tuple-element.49.x_ref, f32[1,64,2048]{2,1,0:T(8,128)} %get-tuple-element.55.refs_0_, ...), custom_call_target="tpu_custom_call" | custom-call | flops 18699999232 | bytes 1024 | tf_op jit(solution)/shard_map/backward_attention/qkv_backward/pallas_call | solution.py:318
  235.8 7.0 %up_out_gradient.2 = bf16[1920,768]{1,0:T(8,128)(2,1)} custom-call(s32[3]{0:T(128)} %pad_add_fusion.meta, bf16[2,768,256]{2,1,0:T(8,128)(2,1)} %bitcast.135, bf16[512,768]{1,0:T(8,128)(2,1)} %get-tuple-element.70.gb_ref, bf16[512,768]{1,0:T(8,128)(2,1)} %get-tuple-element.71.h2_ref, bf16[512,3072]{1,0:T(8,128)(2,1)} %get-tuple-element.72.dup_ref), custom_call_target="tpu_custom_call" | custom-call | flops 5500000256 | bytes 1024 | tf_op jit(solution)/shard_map/weight_gradients/up_out_gradient/pallas_call | solution.py:552
  242.9 5.6 %down_gradient.2 = bf16[1536,768]{1,0:T(8,128)(2,1)} custom-call(s32[3]{0:T(128)} %pad_add_fusion.meta, bf16[512,3072]{1,0:T(8,128)(2,1)} %get-tuple-element.73.act_ref, bf16[512,768]{1,0:T(8,128)(2,1)} %bitcast.152), custom_call_target="tpu_custom_call" | custom-call | flops 5500000256 | bytes 1024 | tf_op jit(solution)/shard_map/weight_gradients/down_gradient/pallas_call | solution.py:509
  254.7 15.9 %collective-permute-done.26 = f32[1,1600]{1,0:T(1,128)S(1)} collective-permute-done((f32[1,1600]{1,0:T(1,128)S(1)}, f32[1,1600]{1,0:T(1,128)S(1)}, u32[]{:S(2)}, u32[]{:S(2)}) %collective-permute-start.26) | collective-permute-done | bytes 6432 | tf_op jit(solution)/shard_map/vector_gradients/ppermute | solution.py:597
  287.2 39.1 %collective-permute-done.18 = bf16[2,256,384]{2,1,0:T(8,128)(2,1)S(1)} collective-permute-done((bf16[2,256,384]{2,1,0:T(8,128)(2,1)S(1)}, bf16[2,256,384]{2,1,0:T(8,128)(2,1)S(1)}, u32[]{:S(2)}, u32[]{:S(2)}) %collective-permute-start.18) | collective-permute-done | bytes 393248 | tf_op jit(solution)/shard_map/ppermute | solution.py:597
  331.2 9.9 %collective-permute-done.44 = bf16[384,768]{1,0:T(8,128)(2,1)S(1)} collective-permute-done((bf16[384,768]{1,0:T(8,128)(2,1)S(1)}, bf16[384,768]{1,0:T(8,128)(2,1)S(1)}, u32[]{:S(2)}, u32[]{:S(2)}) %collective-permute-start.44) | collective-permute-done | bytes 589856 | tf_op jit(solution)/shard_map/weight_gradients/ppermute | solution.py:597
  345.3 6.8 %collective-permute-done.45 = bf16[192,768]{1,0:T(8,128)(2,1)S(1)} collective-permute-done((bf16[192,768]{1,0:T(8,128)(2,1)S(1)}, bf16[192,768]{1,0:T(8,128)(2,1)S(1)}, u32[]{:S(2)}, u32[]{:S(2)}) %collective-permute-start.45) | collective-permute-done | bytes 294944 | tf_op jit(solution)/shard_map/weight_gradients/ppermute | solution.py:597
  359.7 18.3 %collective-permute-done.46 = bf16[192,768]{1,0:T(8,128)(2,1)S(1)} collective-permute-done((bf16[192,768]{1,0:T(8,128)(2,1)S(1)}, bf16[192,768]{1,0:T(8,128)(2,1)S(1)}, u32[]{:S(2)}, u32[]{:S(2)}) %collective-permute-start.46) | collective-permute-done | bytes 294944 | tf_op jit(solution)/shard_map/weight_gradients/ppermute | solution.py:597
  378.1 10.2 %collective-permute-done.38 = bf16[240,768]{1,0:T(8,128)(2,1)S(1)} collective-permute-done((bf16[240,768]{1,0:T(8,128)(2,1)S(1)}, bf16[240,768]{1,0:T(8,128)(2,1)S(1)}, u32[]{:S(2)}, u32[]{:S(2)}) %collective-permute-start.38) | collective-permute-done | bytes 368672 | tf_op jit(solution)/shard_map/weight_gradients/ppermute | solution.py:597
  392.6 6.2 %collective-permute-done.47 = bf16[192,768]{1,0:T(8,128)(2,1)S(1)} collective-permute-done((bf16[192,768]{1,0:T(8,128)(2,1)S(1)}, bf16[192,768]{1,0:T(8,128)(2,1)S(1)}, u32[]{:S(2)}, u32[]{:S(2)}) %collective-permute-start.47) | collective-permute-done | bytes 294944 | tf_op jit(solution)/shard_map/weight_gradients/ppermute | solution.py:597
  400.2 6.6 %collective-permute-done.39 = bf16[240,768]{1,0:T(8,128)(2,1)S(1)} collective-permute-done((bf16[240,768]{1,0:T(8,128)(2,1)S(1)}, bf16[240,768]{1,0:T(8,128)(2,1)S(1)}, u32[]{:S(2)}, u32[]{:S(2)}) %collective-permute-start.39) | collective-permute-done | bytes 368672 | tf_op jit(solution)/shard_map/weight_gradients/ppermute | solution.py:597
  411.6 10.3 %collective-permute-done.48 = bf16[384,768]{1,0:T(8,128)(2,1)S(1)} collective-permute-done((bf16[384,768]{1,0:T(8,128)(2,1)S(1)}, bf16[384,768]{1,0:T(8,128)(2,1)S(1)}, u32[]{:S(2)}, u32[]{:S(2)}) %collective-permute-start.48) | collective-permute-done | bytes 589856 | tf_op jit(solution)/shard_map/weight_gradients/ppermute | solution.py:597
  436.2 34.2 %collective-permute-done.33 = bf16[4,288,384]{2,1,0:T(8,128)(2,1)S(1)} collective-permute-done((bf16[4,288,384]{2,1,0:T(8,128)(2,1)S(1)}, bf16[4,288,384]{2,1,0:T(8,128)(2,1)S(1)}, u32[]{:S(2)}, u32[]{:S(2)}) %collective-permute-start.33) | collective-permute-done | bytes 884768 | tf_op jit(solution)/shard_map/first_projection_gradient/ppermute | solution.py:597
  (220 shorter events, 129.5 us)
Async XLA Ops:
  1.9 25.4 %collective-permute-start = (bf16[256,768]{1,0:T(8,128)(2,1)S(1)}, bf16[256,768]{1,0:T(8,128)(2,1)S(1)}, u32[]{:S(2)}, u32[]{:S(2)}) collective-permute-start(bf16[256,768]{1,0:T(8,128)(2,1)S(1)} %get-tuple-element.118.refs_0_), channel_id=1, source_target_pairs={{0,1},{1,0},{2,3},{3,2},{4,5},{5,4},{6,7},{7,6},{8,9},{9,8},{10,11... | collective-permute-start | bytes 1179656 | tf_op jit(solution)/shard_map/ppermute | solution.py:597
  5.0 24.0 %collective-permute-start.1 = (bf16[256,768]{1,0:T(8,128)(2,1)S(1)}, bf16[256,768]{1,0:T(8,128)(2,1)}, u32[]{:S(2)}, u32[]{:S(2)}) collective-permute-start(bf16[256,768]{1,0:T(8,128)(2,1)S(1)} %get-tuple-element.118.refs_0_), channel_id=1, source_target_pairs={{0,2},{1,3},{2,0},{3,1},{4,6},{5,7},{6,4},{7,5},{8,10},{9,11},{10,... | collective-permute-start | bytes 1179656 | tf_op jit(solution)/shard_map/ppermute | solution.py:597
  12.0 27.0 %collective-permute-start.9 = (bf16[384,576]{0,1:T(8,128)(2,1)S(1)}, bf16[384,576]{0,1:T(8,128)(2,1)S(1)}, u32[]{:S(2)}, u32[]{:S(2)}) collective-permute-start(bf16[384,576]{0,1:T(8,128)(2,1)S(1)} %bitcast.127), channel_id=1, source_target_pairs={{0,8},{8,0},{1,9},{9,1},{2,10},{10,2},{3,11},{11,3},{4,12},{12,4},... | collective-permute-start | bytes 1327112 | tf_op jit(solution)/shard_map/ppermute | solution.py:597
  35.5 77.1 %collective-permute-start.12 = (bf16[384,3072]{1,0:T(8,128)(2,1)}, bf16[384,3072]{1,0:T(8,128)(2,1)}, u32[]{:S(2)}, u32[]{:S(2)}) collective-permute-start(bf16[384,3072]{1,0:T(8,128)(2,1)} %refs_8_.1), channel_id=1, source_target_pairs={{0,8},{8,0},{1,9},{9,1},{2,10},{10,2},{3,11},{11,3},{4,12},{12,4},... | collective-permute-start | bytes 7077896 | tf_op jit(solution)/shard_map/ppermute | solution.py:597
  41.7 70.8 %collective-permute-start.13 = (bf16[1536,768]{1,0:T(8,128)(2,1)}, bf16[1536,768]{1,0:T(8,128)(2,1)}, u32[]{:S(2)}, u32[]{:S(2)}) collective-permute-start(bf16[1536,768]{1,0:T(8,128)(2,1)} %refs_10_.1), channel_id=1, source_target_pairs={{0,8},{8,0},{1,9},{9,1},{2,10},{10,2},{3,11},{11,3},{4,12},{12,4},... | collective-permute-start | bytes 7077896 | tf_op jit(solution)/shard_map/ppermute | solution.py:597
  87.8 24.8 %all-to-all-start = ((bf16[8,192,256]{2,1,0:T(8,128)(2,1)}), bf16[8,192,256]{2,1,0:T(8,128)(2,1)S(1)}, u32[]{:S(2)}, u32[]{:S(2)}) async-start(bf16[8,192,256]{2,1,0:T(8,128)(2,1)} %get-tuple-element.46), calls=%async_computation | async-start | bytes 1572864 | tf_op jit(solution)/shard_map/all_to_all | solution.py:698
  139.1 25.0 %all-to-all-start.1 = ((bf16[8,192,256]{2,1,0:T(8,128)(2,1)}), bf16[8,192,256]{2,1,0:T(8,128)(2,1)}, u32[]{:S(2)}, u32[]{:S(2)}) async-start(bf16[8,192,256]{2,1,0:T(8,128)(2,1)} %bitcast.136), calls=%async_computation.1 | async-start | bytes 1572864 | tf_op jit(solution)/shard_map/all_to_all | solution.py:698
  150.6 130.4 %collective-permute-start.34 = (bf16[1920,768]{1,0:T(8,128)(2,1)}, bf16[1920,768]{1,0:T(8,128)(2,1)S(1)}, u32[]{:S(2)}, u32[]{:S(2)}) collective-permute-start(bf16[1920,768]{1,0:T(8,128)(2,1)} %up_out_gradient.3), channel_id=1, source_target_pairs={{0,8},{8,0},{1,9},{9,1},{2,10},{10,2},{3,11},{11,3},{4,12},{12,4},... | collective-permute-start | bytes 8847368 | tf_op jit(solution)/shard_map/weight_gradients/ppermute | solution.py:597
  156.3 120.3 %collective-permute-start.42 = (bf16[1536,768]{1,0:T(8,128)(2,1)}, bf16[1536,768]{1,0:T(8,128)(2,1)}, u32[]{:S(2)}, u32[]{:S(2)}) collective-permute-start(bf16[1536,768]{1,0:T(8,128)(2,1)} %down_gradient.3), channel_id=1, source_target_pairs={{0,8},{8,0},{1,9},{9,1},{2,10},{10,2},{3,11},{11,3},{4,12},{12,4},... | collective-permute-start | bytes 7077896 | tf_op jit(solution)/shard_map/weight_gradients/ppermute | solution.py:597
  251.3 32.7 %collective-permute-start.16 = (bf16[2,256,384]{2,1,0:T(8,128)(2,1)S(1)}, bf16[2,256,384]{2,1,0:T(8,128)(2,1)S(1)}, u32[]{:S(2)}, u32[]{:S(2)}) collective-permute-start(bf16[2,256,384]{2,1,0:T(8,128)(2,1)S(1)} %get-tuple-element.115), channel_id=1, source_target_pairs={{0,2},{1,3},{2,0},{3,1},{4,6},{5,7},{6,4},{7,5},{8,10},{9,11},{10,... | collective-permute-start | bytes 1179656 | tf_op jit(solution)/shard_map/ppermute | solution.py:597
  251.3 33.4 %collective-permute-start.20 = (bf16[2,256,384]{2,1,0:T(8,128)(2,1)S(1)}, bf16[2,256,384]{2,1,0:T(8,128)(2,1)S(1)}, u32[]{:S(2)}, u32[]{:S(2)}) collective-permute-start(bf16[2,256,384]{2,1,0:T(8,128)(2,1)S(1)} %get-tuple-element.116), channel_id=1, source_target_pairs={{0,2},{1,3},{2,0},{3,1},{4,6},{5,7},{6,4},{7,5},{8,10},{9,11},{10,... | collective-permute-start | bytes 1179656 | tf_op jit(solution)/shard_map/ppermute | solution.py:597
  279.2 47.9 %collective-permute-start.43 = (bf16[768,768]{1,0:T(8,128)(2,1)S(1)}, bf16[768,768]{1,0:T(8,128)(2,1)S(1)}, u32[]{:S(2)}, u32[]{:S(2)}) collective-permute-start(bf16[768,768]{1,0:T(8,128)(2,1)S(1)} %constant_dynamic-slice_fusion.2), channel_id=1, source_target_pairs={{0,16},{16,0},{1,17},{17,1},{2,18},{18,2},{3,19},{19,3},{4,20},{20... | collective-permute-start | bytes 3538952 | tf_op jit(solution)/shard_map/weight_gradients/ppermute | solution.py:597
  282.0 46.5 %collective-permute-start.35 = (bf16[960,768]{1,0:T(8,128)(2,1)S(1)}, bf16[960,768]{1,0:T(8,128)(2,1)S(1)}, u32[]{:S(2)}, u32[]{:S(2)}) collective-permute-start(bf16[960,768]{1,0:T(8,128)(2,1)S(1)} %constant_dynamic-slice_fusion.5), channel_id=1, source_target_pairs={{0,1},{1,0},{2,3},{3,2},{4,5},{5,4},{6,7},{7,6},{8,9},{9,8},{10,11... | collective-permute-start | bytes 4423688 | tf_op jit(solution)/shard_map/weight_gradients/ppermute | solution.py:597
  283.9 42.4 %collective-permute-start.18 = (bf16[2,256,384]{2,1,0:T(8,128)(2,1)S(1)}, bf16[2,256,384]{2,1,0:T(8,128)(2,1)S(1)}, u32[]{:S(2)}, u32[]{:S(2)}) collective-permute-start(bf16[2,256,384]{2,1,0:T(8,128)(2,1)S(1)} %get-tuple-element.112), channel_id=1, source_target_pairs={{0,1},{1,0},{2,3},{3,2},{4,5},{5,4},{6,7},{7,6},{8,9},{9,8},{10,11... | collective-permute-start | bytes 1179656 | tf_op jit(solution)/shard_map/ppermute | solution.py:597
  284.7 59.7 %collective-permute-start.28 = (bf16[576,384]{1,0:T(8,128)(2,1)S(1)}, bf16[576,384]{1,0:T(8,128)(2,1)S(1)}, u32[]{:S(2)}, u32[]{:S(2)}) collective-permute-start(bf16[576,384]{1,0:T(8,128)(2,1)S(1)} %constant_dynamic-slice_fusion.7), channel_id=1, source_target_pairs={{0,8},{8,0},{1,9},{9,1},{2,10},{10,2},{3,11},{11,3},{4,12},{12,4},... | collective-permute-start | bytes 1327112 | tf_op jit(solution)/shard_map/first_projection_gradient/ppermute | solution.py:597
  286.3 102.1 %collective-permute-start.21 = (bf16[256,384]{1,0:T(8,128)(2,1)S(1)}, bf16[256,384]{1,0:T(8,128)(2,1)S(1)}, u32[]{:S(2)}, u32[]{:S(2)}) collective-permute-start(bf16[256,384]{1,0:T(8,128)(2,1)S(1)} %slice_bitcast_fusion.8), channel_id=1, source_target_pairs={{0,1},{1,0},{2,3},{3,2},{4,5},{5,4},{6,7},{7,6},{8,9},{9,8},{10,11... | collective-permute-start | bytes 589832 | tf_op jit(solution)/shard_map/ppermute | solution.py:597
  326.6 81.6 %collective-permute-start.19 = (bf16[256,384]{1,0:T(8,128)(2,1)S(1)}, bf16[256,384]{1,0:T(8,128)(2,1)S(1)}, u32[]{:S(2)}, u32[]{:S(2)}) collective-permute-start(bf16[256,384]{1,0:T(8,128)(2,1)S(1)} %slice_bitcast_fusion.10), channel_id=1, source_target_pairs={{0,2},{1,3},{2,0},{3,1},{4,6},{5,7},{6,4},{7,5},{8,10},{9,11},{10,... | collective-permute-start | bytes 589832 | tf_op jit(solution)/shard_map/ppermute | solution.py:597
  341.0 67.9 %collective-permute-start.17 = (bf16[256,384]{1,0:T(8,128)(2,1)S(1)}, bf16[256,384]{1,0:T(8,128)(2,1)S(1)}, u32[]{:S(2)}, u32[]{:S(2)}) collective-permute-start(bf16[256,384]{1,0:T(8,128)(2,1)S(1)} %slice_bitcast_fusion.12), channel_id=1, source_target_pairs={{0,1},{1,0},{2,3},{3,2},{4,5},{5,4},{6,7},{7,6},{8,9},{9,8},{10,11... | collective-permute-start | bytes 589832 | tf_op jit(solution)/shard_map/ppermute | solution.py:597
  357.9 30.3 %collective-permute-start.38 = (bf16[240,768]{1,0:T(8,128)(2,1)S(1)}, bf16[240,768]{1,0:T(8,128)(2,1)S(1)}, u32[]{:S(2)}, u32[]{:S(2)}) collective-permute-start(bf16[240,768]{1,0:T(8,128)(2,1)S(1)} %add_convert_fusion.8), channel_id=1, source_target_pairs={{0,4},{1,5},{2,6},{3,7},{4,0},{5,1},{6,2},{7,3},{8,12},{9,13},{10,... | collective-permute-start | bytes 1105928 | tf_op jit(solution)/shard_map/weight_gradients/ppermute | solution.py:597
  392.5 38.2 %collective-permute-start.15 = (bf16[256,384]{1,0:T(8,128)(2,1)S(1)}, bf16[256,384]{1,0:T(8,128)(2,1)S(1)}, u32[]{:S(2)}, u32[]{:S(2)}) collective-permute-start(bf16[256,384]{1,0:T(8,128)(2,1)S(1)} %slice_bitcast_fusion.14), channel_id=1, source_target_pairs={{0,2},{1,3},{2,0},{3,1},{4,6},{5,7},{6,4},{7,5},{8,10},{9,11},{10,... | collective-permute-start | bytes 589832 | tf_op jit(solution)/shard_map/ppermute | solution.py:597
  408.7 22.0 %collective-permute-start.22 = (bf16[256,768]{1,0:T(8,128)(2,1)S(1)}, bf16[256,768]{1,0:T(8,128)(2,1)S(1)}, u32[]{:S(2)}, u32[]{:S(2)}) collective-permute-start(bf16[256,768]{1,0:T(8,128)(2,1)S(1)} %pad_maximum_fusion.2), channel_id=1, source_target_pairs={{0,4},{1,5},{2,6},{3,7},{4,0},{5,1},{6,2},{7,3},{8,12},{9,13},{10,... | collective-permute-start | bytes 1179656 | tf_op jit(solution)/shard_map/ppermute | solution.py:597
  423.4 50.8 %collective-permute-start.49 = (bf16[768,768]{1,0:T(8,128)(2,1)}, bf16[768,768]{1,0:T(8,128)(2,1)}, u32[]{:S(2)}, u32[]{:S(2)}) collective-permute-start(bf16[768,768]{1,0:T(8,128)(2,1)} %maximum_select_fusion.4), channel_id=1, source_target_pairs={{0,16},{16,0},{1,17},{17,1},{2,18},{18,2},{3,19},{19,3},{4,20},{20... | collective-permute-start | bytes 3538952 | tf_op jit(solution)/shard_map/weight_gradients/ppermute | solution.py:597
  429.0 50.2 %collective-permute-start.41 = (bf16[960,768]{1,0:T(8,128)(2,1)}, bf16[960,768]{1,0:T(8,128)(2,1)}, u32[]{:S(2)}, u32[]{:S(2)}) collective-permute-start(bf16[960,768]{1,0:T(8,128)(2,1)} %maximum_select_fusion.3), channel_id=1, source_target_pairs={{0,1},{1,0},{2,3},{3,2},{4,5},{5,4},{6,7},{7,6},{8,9},{9,8},{10,11... | collective-permute-start | bytes 4423688 | tf_op jit(solution)/shard_map/weight_gradients/ppermute | solution.py:597
  429.8 40.7 %collective-permute-start.33 = (bf16[4,288,384]{2,1,0:T(8,128)(2,1)S(1)}, bf16[4,288,384]{2,1,0:T(8,128)(2,1)S(1)}, u32[]{:S(2)}, u32[]{:S(2)}) collective-permute-start(bf16[4,288,384]{2,1,0:T(8,128)(2,1)S(1)} %maximum_select_fusion.6), channel_id=1, source_target_pairs={{0,16},{16,0},{1,17},{17,1},{2,18},{18,2},{3,19},{19,3},{4,20},{20... | collective-permute-start | bytes 2654216 | tf_op jit(solution)/shard_map/first_projection_gradient/ppermute | solution.py:597
  (48 other events, 644.6 us)

commit v3 on v2

--- a/solution.py
+++ b/solution.py
@@ -497,76 +497,207 @@
     )(meta, attn_t, x, dy, valid, gain, bias, wo, wo_p, up, up_p, dn, dn_p)
 
 
-def down_grads(meta, own, act, dy):
-    tokens, width = dy.shape
+def up_out_grads(meta, attn_t, gb, h2, dup, far=None):
+    tokens, width = gb.shape
+    hidden = dup.shape[1]
     half = width // 2
-    blocks = act.shape[1] // 2 // half
-
-    def body(meta, act_ref, dy_ref, out_ref):
-        out_ref[...] = mm(act_ref[...], dy_ref[...], TN).astype(BF16)
-
-    side = (lambda m: m[2]) if own else (lambda m: 1 - m[2])
+    packs, _, lanes = attn_t.shape
+    n = hidden // width
+    own = far is not None
+
+    def column(j, m):
+        bit = jnp.where(j < n // 2, m[4], 1 - m[4])
+        return bit * (n // 2) + lax.rem(jnp.minimum(j, n - 1), n // 2)
+
+    def body(meta, at_ref, gb_ref, h2_ref, dup_ref, *rest):
+        j = pl.program_id(0)
+        side = meta[2] if own else 1 - meta[2]
+
+        def up():
+            part = jnp.where(side == 0, h2_ref[:, :half], h2_ref[:, half:])
+            return mm(part, dup_ref[...], TN)
+
+        def out():
+            rows = pl.ds(pl.multiple_of(side * half, half), half)
+            total = jnp.zeros((half, width), F32)
+            for p in range(packs):
+                total = total + mm(at_ref[p, rows, :], gb_ref[p * lanes : (p + 1) * lanes, :])
+            lo, hi = total[: half // 2], total[half // 2 :]
+            return jnp.where(meta[5] == 0, lo, hi), jnp.where(meta[5] == 0, hi, lo)
+
+        if own:
+            far_ref, uk_ref, us_ref, ok_ref, os_ref = rest
+
+            @pl.when(j < n // 2)
+            def _():
+                uk_ref[...] = (up() + far_ref[...].astype(F32)).astype(BF16)
+
+            @pl.when((j >= n // 2) & (j < n))
+            def _():
+                us_ref[...] = (up() + far_ref[...].astype(F32)).astype(BF16)
+
+            @pl.when(j == n)
+            def _():
+                keep, send = out()
+                ok_ref[...] = (keep + far_ref[: half // 2].astype(F32)).astype(BF16)
+                os_ref[...] = (send + far_ref[half // 2 :].astype(F32)).astype(BF16)
+        else:
+            (out_ref,) = rest
+
+            @pl.when(j < n)
+            def _():
+                out_ref[...] = up().astype(BF16)
+
+            @pl.when(j == n)
+            def _():
+                keep, send = out()
+                out_ref[: half // 2] = keep.astype(BF16)
+                out_ref[half // 2 :] = send.astype(BF16)
+
+    whole = lambda *shape: pl.BlockSpec(shape, lambda j, m: (0,) * len(shape))
+    block = lambda index: pl.BlockSpec((half, width), index)
+    if own:
+        out_specs = (
+            block(lambda j, m: (0, jnp.minimum(j, n // 2 - 1))),
+            block(lambda j, m: (0, jnp.clip(j - n // 2, 0, n // 2 - 1))),
+            whole(half // 2, width),
+            whole(half // 2, width),
+        )
+        shapes = [(half, hidden // 2)] * 2 + [(half // 2, width)] * 2
+        out_shape = tuple(jax.ShapeDtypeStruct(shape, BF16) for shape in shapes)
+    else:
+        out_specs = block(lambda j, m: (0, j))
+        out_shape = jax.ShapeDtypeStruct((half, hidden + width), BF16)
     return pl.pallas_call(
         body,
         grid_spec=pltpu.PrefetchScalarGridSpec(
             num_scalar_prefetch=1,
-            grid=(blocks,),
+            grid=(n + 1,),
             in_specs=[
-                pl.BlockSpec((tokens, half), lambda j, m: (0, side(m) * blocks + j)),
-                pl.BlockSpec((tokens, width), lambda j, m: (0, 0)),
+                whole(*attn_t.shape),
+                whole(tokens, width),
+                whole(tokens, width),
+                pl.BlockSpec((tokens, width), lambda j, m: (0, column(j, m))),
+                *([block(lambda j, m: (0, j))] if own else []),
             ],
-            out_specs=pl.BlockSpec((half, width), lambda j, m: (j, 0)),
-        ),
-        out_shape=jax.ShapeDtypeStruct((blocks * half, width), BF16),
+            out_specs=out_specs,
+        ),
+        out_shape=out_shape,
         compiler_params=params(),
-        cost_estimate=cost(5),
-        name="down_gradient",
-    )(meta, act, dy)
-
-
-def up_out_grads(meta, own, attn_t, gb, h2, dup):
-    tokens, width = gb.shape
-    hidden = dup.shape[1]
+        cost_estimate=cost(7),
+        name="up_out_gradient",
+    )(meta, attn_t, gb, h2, dup, *([far] if own else []))
+
+
+def down_grads(meta, act, dy, far=None):
+    tokens, width = dy.shape
     half = width // 2
-    packs, _, lanes = attn_t.shape
-    blocks = hidden // width
-
-    def body(meta, at_ref, gb_ref, h2_ref, dup_ref, out_ref):
-        j = pl.program_id(0)
-        side = meta[2] if own else 1 - meta[2]
-
-        @pl.when(j < blocks)
-        def _():
-            part = jnp.where(side == 0, h2_ref[:, :half], h2_ref[:, half:])
-            out_ref[...] = mm(part, dup_ref[...], TN).astype(BF16)
-
-        @pl.when(j == blocks)
-        def _():
-            rows = pl.ds(pl.multiple_of(side * half, half), half)
-            total = jnp.zeros((half, width), F32)
-            for p in range(packs):
-                total = total + mm(at_ref[p, rows, :], gb_ref[p * lanes : (p + 1) * lanes, :])
-            out_ref[...] = total.astype(BF16)
-
-    whole = lambda *shape: pl.BlockSpec(shape, lambda j, m: (0,) * len(shape))
+    n = act.shape[1] // 2 // half
+    own = far is not None
+
+    def body(meta, act_ref, dy_ref, *rest):
+        value = mm(act_ref[...], dy_ref[...], TN)
+        if own:
+            far_ref, keep_ref, send_ref = rest
+            j = pl.program_id(0)
+            value = (value + far_ref[...].astype(F32)).astype(BF16)
+
+            @pl.when(j < n // 2)
+            def _():
+                keep_ref[...] = value
+
+            @pl.when(j >= n // 2)
+            def _():
+                send_ref[...] = value
+        else:
+            (out_ref,) = rest
+            out_ref[...] = value.astype(BF16)
+
+    def column(j, m):
+        side = m[2] if own else 1 - m[2]
+        bit = jnp.where(j < n // 2, m[3], 1 - m[3])
+        return side * n + bit * (n // 2) + lax.rem(j, n // 2)
+
+    block = lambda index: pl.BlockSpec((half, width), index)
+    if own:
+        out_specs = (
+            block(lambda j, m: (jnp.minimum(j, n // 2 - 1), 0)),
+            block(lambda j, m: (jnp.maximum(j - n // 2, 0), 0)),
+        )
+        out_shape = (jax.ShapeDtypeStruct((n // 2 * half, width), BF16),) * 2
+    else:
+        out_specs = block(lambda j, m: (j, 0))
+        out_shape = jax.ShapeDtypeStruct((n * half, width), BF16)
     return pl.pallas_call(
         body,
         grid_spec=pltpu.PrefetchScalarGridSpec(
             num_scalar_prefetch=1,
-            grid=(blocks + 1,),
+            grid=(n,),
             in_specs=[
-                whole(*attn_t.shape),
-                whole(tokens, width),
-                whole(tokens, width),
-                pl.BlockSpec((tokens, width), lambda j, m: (0, jnp.minimum(j, blocks - 1))),
+                pl.BlockSpec((tokens, half), lambda j, m: (0, column(j, m))),
+                pl.BlockSpec((tokens, width), lambda j, m: (0, 0)),
+                *([block(lambda j, m: (j, 0))] if own else []),
             ],
-            out_specs=pl.BlockSpec((half, width), lambda j, m: (j, 0)),
-        ),
-        out_shape=jax.ShapeDtypeStruct(((blocks + 1) * half, width), BF16),
+            out_specs=out_specs,
+        ),
+        out_shape=out_shape,
         compiler_params=params(),
-        cost_estimate=cost(5),
-        name="up_out_gradient",
-    )(meta, attn_t, gb, h2, dup)
+        cost_estimate=cost(6),
+        name="down_gradient",
+    )(meta, act, dy, *([far] if own else []))
+
+
+def assemble(meta, downs, ups, outs):
+    half, width = outs[0].shape[0] * 2, outs[0].shape[1]
+    hidden = ups[0].shape[1] * 2
+    cut = width // 2
+
+    def body(meta, down_a, down_b, up_a, up_b, out_a, out_b, down_ref, up_ref, out_ref):
+        i = pl.program_id(0)
+
+        def place(ref, value, swapped):
+            lo, hi = value[:, :cut].astype(F32), value[:, cut:].astype(F32)
+            ref[:, :cut] = jnp.where(swapped == 0, lo, hi)
+            ref[:, cut:] = jnp.where(swapped == 0, hi, lo)
+
+        down_own = i // 2 == meta[3]
+        place(down_ref, jnp.where(down_own, down_a[...], down_b[...]), meta[5])
+        up_own = i // 2 == meta[4]
+        place(up_ref, jnp.where(up_own, up_a[...], up_b[...]), meta[3])
+
+        @pl.when(i == 0)
+        def _():
+            quarter = half // 4
+            for z in range(2):
+                for x in range(2):
+                    rows = pl.ds(pl.multiple_of(jnp.bitwise_xor(meta[3], x) * quarter, quarter), quarter)
+                    value = jnp.where(meta[5] == z, out_a[rows, :], out_b[rows, :])
+                    place(out_ref.at[pl.ds((2 * z + x) * quarter, quarter)], value, meta[4])
+
+    whole = lambda *shape: pl.BlockSpec(shape, lambda i, m: (0,) * len(shape))
+    down = pl.BlockSpec((half, width), lambda i, m: (jnp.bitwise_xor(lax.rem(i, 2), m[4]), 0))
+    up = pl.BlockSpec((half, width), lambda i, m: (0, jnp.bitwise_xor(lax.rem(i, 2), m[5])))
+    return pl.pallas_call(
+        body,
+        grid_spec=pltpu.PrefetchScalarGridSpec(
+            num_scalar_prefetch=1,
+            grid=(4,),
+            in_specs=[down, down, up, up, whole(*outs[0].shape), whole(*outs[0].shape)],
+            out_specs=(
+                pl.BlockSpec((half, width), lambda i, m: (i, 0)),
+                pl.BlockSpec((half, width), lambda i, m: (0, i)),
+                whole(half, width),
+            ),
+        ),
+        out_shape=(
+            jax.ShapeDtypeStruct((4 * half, width), F32),
+            jax.ShapeDtypeStruct((half, hidden), F32),
+            jax.ShapeDtypeStruct((half, width), F32),
+        ),
+        compiler_params=params(),
+        cost_estimate=cost(7),
+        name="weight_gradients",
+    )(meta, *downs, *ups, *outs)
 
 
 def finish_body(x_ref, gm_ref, back_ref, g_ref, out_ref):
@@ -618,17 +749,6 @@
 
 def add(a, b):
     return (a.astype(F32) + b.astype(F32)).astype(BF16)
-
-
-def reduce_all(value, cuts, rest):
-    for axis, mask in cuts:
-        keep, send = halves(value, bit(axis, mask))
-        value = add(keep, flip(send, axis, mask))
-    for axis, mask in rest:
-        value = add(value, flip(value, axis, mask))
-    for axis, mask in cuts[::-1]:
-        value = join(value, flip(value, axis, mask), bit(axis, mask))
-    return value
 
 
 def on_device(
@@ -686,7 +806,7 @@
         whole = jnp.swapaxes(got, 0, 1).reshape(length, width)
         slots = [whole[s * (length // 8) : (s + 1) * (length // 8)] for s in range(8)]
         spot = jnp.int32(0)
-    meta = jnp.stack([spot, row, core]).astype(jnp.int32)
+    meta = jnp.stack([spot, row, core, bit("rep", 1), bit("seq", 1), bit("seq", 2)]).astype(jnp.int32)
 
     out_p, up_p, down_p = swap(out_weight), swap(up_weight), swap(down_weight)
 
@@ -726,18 +846,42 @@
 
     masks = [1 << k for k in range(n.bit_length() - 1)]
     with jax.named_scope("weight_gradients"):
-        far_d = swap(down_grads(meta, False, act, dy))
-        grad_d = add(down_grads(meta, True, act, dy), far_d)
-        far_u = swap(up_out_grads(meta, False, attn_t, grad_branch, h2, dup))
-        grad_u = add(up_out_grads(meta, True, attn_t, grad_branch, h2, dup), far_u)
-        rest = [("seq", m) for m in masks[2:]]
-        grad_d = reduce_all(grad_d, [("rep", 1), ("seq", 1), ("seq", 2)], rest)
-        grad_u = reduce_all(grad_u, [("seq", 1), ("rep", 1), ("seq", 2)], rest)
-        hidden = up_weight.shape[1]
-        n_up = hidden // width
-        grad_down = grad_d.astype(F32)
-        grad_up = jnp.concatenate([grad_u[half * k : half * (k + 1)] for k in range(n_up)], axis=1).astype(F32)
-        grad_out = grad_u[half * n_up :].astype(F32)
+        far_u = swap(up_out_grads(meta, attn_t, grad_branch, h2, dup))
+        far_d = swap(down_grads(meta, act, dy))
+        up_k, up_s, out_k, out_s = up_out_grads(meta, attn_t, grad_branch, h2, dup, far_u)
+        down_k, down_s = down_grads(meta, act, dy, far_d)
+        grad_o, up_k, up_s, out_k, out_s, down_k, down_s = lax.optimization_barrier(
+            (grad_o, up_k, up_s, out_k, out_s, down_k, down_s)
+        )
+        x, y, z = ("rep", 1), ("seq", 1), ("seq", 2)
+
+        def next_half(keep, got, way, axis):
+            return halves(add(keep, got), bit(*way), axis)
+
+        down_k, down_s = next_half(down_k, flip(down_s, *x), y, 0)
+        up_k, up_s = next_half(up_k, flip(up_s, *y), z, 1)
+        out_k, out_s = next_half(out_k, flip(out_s, *z), x, 0)
+        down_k, down_s = next_half(down_k, flip(down_s, *y), z, 1)
+        up_k, up_s = next_half(up_k, flip(up_s, *z), x, 1)
+        out_k, out_s = next_half(out_k, flip(out_s, *x), y, 1)
+        down = add(down_k, flip(down_s, *z))
+        up = add(up_k, flip(up_s, *x))
+        out = add(out_k, flip(out_s, *y))
+        if masks[2:]:
+            sizes = [down.shape[0], up.shape[0]]
+            every_piece = jnp.concatenate([down, up, out])
+            for mask in masks[2:]:
+                every_piece = add(every_piece, flip(every_piece, "seq", mask))
+            down, up, out = jnp.split(every_piece, [sizes[0], sizes[0] + sizes[1]])
+        down = jnp.concatenate([down, flip(down, *z)], axis=1)
+        up = jnp.concatenate([up, flip(up, *x)], axis=1)
+        out = jnp.concatenate([out, flip(out, *y)], axis=1)
+        down = jnp.concatenate([down, flip(down, *y)], axis=0)
+        up = jnp.concatenate([up, flip(up, *z)], axis=1)
+        out = jnp.concatenate([out, flip(out, *x)], axis=0)
+        grad_down, grad_up, grad_out = assemble(
+            meta, (down, flip(down, *x)), (up, flip(up, *y)), (out, flip(out, *z))
+        )
 
     with jax.named_scope("backward_attention"):
         parts = [
@@ -797,11 +941,8 @@
             + [gains[k].sum(axis=-1).reshape(2, hd // 2) for k in range(2)],
             axis=1,
         )
-        keep, send = halves(small, core)
-        small = keep + swap(send)
-        for axis, mask in [("rep", 1)] + [("seq", m) for m in masks]:
-            small = small + flip(small, axis, mask)
-        small = small[0]
+        small = lax.all_gather(small.reshape(-1), ("rep", "fsdp", "seq")).sum(axis=0).reshape(2, -1)
+        small = jnp.where(core == 0, small[0], small[1])
         cuts = [small[k * half : (k + 1) * half] for k in range(4)]
         cuts += [small[4 * half : 4 * half + hd // 2], small[4 * half + hd // 2 :]]
     shape = tokens.shape

time: 485 us -> 531 us (1.095)
  blocking collectives: 0 us -> 67.8 us
  waiting for transfers between devices: 218 us -> 189 us
  Pallas kernels: 164 us -> 180 us
  other arithmetic: 29.2 us -> 14.2 us
    all_gather x0 -> x1, blocking collectives: none -> 67.8 us  [on_device(): lax.all_gather(small.reshape(-1), ('rep', 'fsdp', 'seq')).sum(axis=0)]
    ppermute x50, waiting for transfers between devices: 192 us -> 166 us  [flip(): return lax.ppermute(value, axis, [(i, i ^ mask) for i in range(size)])]
    pallas_call x0 -> x1, Pallas kernels: none -> 9.38 us  [assemble(): pl.pallas_call(body, grid_spec=pltpu.PrefetchScalarGridSpec(num_scalar_pr...]
    convert_element_type x2 -> x0, other arithmetic: 7.78 us -> none  [the longest x1 5.02 us: on_device(): grad_down = grad_d.astype(F32)]
    select_n x8 -> x3, other arithmetic: 7.5 us -> 0.66 us  [join(): jnp.where(which == 0, jnp.concatenate([own, other], axis=axis), jnp.conca...]
    unnamed x48 -> x55, local copies, waits for them, and re-layouts: 9.07 us -> 11.5 us
  transfers between devices with their start and end apart: 52 -> 52, of which waited for: 25 -> 21; matrix products, arithmetic and copies ran while one was open for 8% -> 6% of each run, Pallas kernels for 29% -> 16%
where the time goes in v3:
time: 531 us
  waiting for transfers between devices  189 us (36%)
  Pallas kernels  180 us (34%)
  blocking collectives  67.8 us (13%)
  starting transfers between devices  59.3 us (11%)
  local copies, waits for them, and re-layouts  19.4 us (4%)
  other arithmetic  14.2 us (3%)
    ppermute x50, waiting for transfers between devices, flip(): return lax.ppermute(value, axis, [(i, i ^ mask) for i in range(size)])  166 us
    all_gather x1, blocking collectives, on_device(): lax.all_gather(small.reshape(-1), ('rep', 'fsdp', 'seq')).sum(axis=0)  67.8 us
    pallas_call x3, Pallas kernels, attend_back(): pl.pallas_call(functools.partial(attend_back_body, heads, hd), grid=(bloc...  52.8 us
    ppermute x50, starting transfers between devices, flip(): return lax.ppermute(value, axis, [(i, i ^ mask) for i in range(size)])  51.8 us
    pallas_call x1, Pallas kernels, attend(): pl.pallas_call(functools.partial(attend_body, heads, hd), grid=(blocks,),...  30.1 us
    pallas_call x1, Pallas kernels, ffn(): pl.pallas_call(body, grid_spec=pltpu.PrefetchScalarGridSpec(num_scalar_pr...  25.6 us
    all_to_all x2, waiting for transfers between devices, exchange(): return lax.all_to_all(value, 'seq', 0, 0, tiled=True)  22.8 us
    pallas_call x1, Pallas kernels, qkv_back(): pl.pallas_call(functools.partial(qkv_back_body, heads, hd), grid_spec=plt...  17.5 us
  transfers between devices with their start and end apart: 52, of which 21 were waited for; matrix products, arithmetic and copies ran while one was open for 6% of the time, Pallas kernels for 16%

profile of v3, /device:TPU:0, one launch (start us, length us, event | category | flops | bytes accessed | tf_op | source)
XLA Modules:
  0.0 531.1 jit_solution(17165336111074480688)
XLA Ops:
  13.4 10.4 %collective-permute-done.4.refs_4_ = bf16[256,768]{1,0:T(8,128)(2,1)} collective-permute-done((bf16[256,768]{1,0:T(8,128)(2,1)S(1)}, bf16[256,768]{1,0:T(8,128)(2,1)}, u32[]{:S(2)}, u32[]{:S(2)}) %collective-permute-start.4) | collective-permute-done | bytes 393248 | tf_op jit(solution)/shard_map/ppermute | solution.py:728
  45.6 12.2 %qkv_forward.1 = (bf16[3,128,2048]{2,1,0:T(8,128)(2,1)}, bf16[3,2048,128]{2,1,0:T(8,128)(2,1)}, bf16[3,64,2048]{2,1,0:T(8,128)(2,1)}, bf16[3,2048,64]{2,1,0:T(8,...) custom-call(s32[6]{0:T(128)} %stack.41.meta, s32[2,8]{1,0:T(2,128)} %bitcast.151, ...), custom_call_target="tpu_custom_call" | custom-call | flops 13200000000 | bytes 1024 | tf_op jit(solution)/shard_map/forward_attention/qkv_forward/pallas_call | solution.py:103
  57.8 30.1 %attention_forward.1 = (bf16[8,192,256]{2,1,0:T(8,128)(2,1)}, f32[3,64,2048]{2,1,0:T(8,128)}, f32[3,1,2048]{2,1,0:T(1,128)}) custom-call(s32[6]{0:T(128)} %stack.41.meta, s32[2,8]{1,0:T(2,128)} %bitcast.152, bf16[3,128,2048]{2,1,0:T(8,128)(2,1)} %get-tuple-element.59.qt_ref, bf16[3,2048,128]{2,1,0:T(8,128)(2,1)} %get-tuple-element.60.ka_ref, ...), custom_call_target="tpu_custom_call" | custom-call | flops 27499999232 | bytes 1024 | tf_op jit(solution)/shard_map/forward_attention/attention_forward/pallas_call | solution.py:169
  93.9 18.6 %all-to-all-done = bf16[8,192,256]{2,1,0:T(8,128)(2,1)S(1)} async-done(((bf16[8,192,256]{2,1,0:T(8,128)(2,1)}), bf16[8,192,256]{2,1,0:T(8,128)(2,1)S(1)}, u32[]{:S(2)}, u32[]{:S(2)}) %all-to-all-start) | async-done | bytes 786464 | tf_op jit(solution)/shard_map/all_to_all | solution.py:818
  113.4 25.6 %ffn_both_ways.1 = (bf16[512,768]{1,0:T(8,128)(2,1)}, f32[512,768]{1,0:T(8,128)}, bf16[512,768]{1,0:T(8,128)(2,1)}, bf16[512,768]{1,0:T(8,128)(2,1)}, bf16[512,3...) custom-call(s32[6]{0:T(128)} %stack.41.meta, ...), custom_call_target="tpu_custom_call" | custom-call | flops 27499999232 | bytes 1024 | tf_op jit(solution)/shard_map/feed_forward/ffn_both_ways/pallas_call | solution.py:446
  139.1 5.7 %down_gradient.2 = bf16[1536,768]{1,0:T(8,128)(2,1)} custom-call(s32[6]{0:T(128)} %stack.41.meta, bf16[512,3072]{1,0:T(8,128)(2,1)} %get-tuple-element.78.act_ref, bf16[512,768]{1,0:T(8,128)(2,1)} %bitcast.149), custom_call_target="tpu_custom_call" | custom-call | flops 6600000000 | bytes 1024 | tf_op jit(solution)/shard_map/weight_gradients/down_gradient/pallas_call | solution.py:631
  144.8 7.2 %up_out_gradient.2 = bf16[384,3840]{1,0:T(8,128)(2,1)} custom-call(s32[6]{0:T(128)} %stack.41.meta, bf16[2,768,256]{2,1,0:T(8,128)(2,1)} %bitcast.133, bf16[512,768]{1,0:T(8,128)(2,1)} %get-tuple-element.71.gb_ref, bf16[512,768]{1,0:T(8,128)(2,1)} %get-tuple-element.72.h2_ref, bf16[512,3072]{1,0:T(8,128)(2,1)} %get-tuple-element.73.dup_ref), custom_call_target="tpu_custom_call" | custom-call | flops 7699999744 | bytes 1024 | tf_op jit(solution)/shard_map/weight_gradients/up_out_gradient/pallas_call | solution.py:571
  157.6 6.4 %down_gradient.3 = (bf16[768,768]{1,0:T(8,128)(2,1)}, bf16[768,768]{1,0:T(8,128)(2,1)}) custom-call(s32[6]{0:T(128)} %stack.41.meta, bf16[512,3072]{1,0:T(8,128)(2,1)} %get-tuple-element.78.act_ref, bf16[512,768]{1,0:T(8,128)(2,1)} %bitcast.150, bf16[1536,768]{1,0:T(8,128)(2,1)} %copy-done.19), custom_call_target="tpu_custom_call" | custom-call | flops 6600000000 | bytes 1024 | tf_op jit(solution)/shard_map/weight_gradients/down_gradient/pallas_call | solution.py:631
  164.0 8.4 %up_out_gradient.3 = (bf16[384,1536]{1,0:T(8,128)(2,1)}, bf16[384,1536]{1,0:T(8,128)(2,1)}, bf16[192,768]{1,0:T(8,128)(2,1)}, bf16[192,768]{1,0:T(8,128)(2,1)}) custom-call(s32[6]{0:T(128)} %stack.41.meta, bf16[2,768,256]{2,1,0:T(8,128)(2,1)} %bitcast.134, bf16[512,768]{1,0:T(8,128)(2,1)} %get-tuple-element.71.gb_ref, ...), custom_call_target="tpu_custom_call" | custom-call | flops 7699999744 | bytes 1024 | tf_op jit(solution)/shard_map/weight_gradients/up_out_gradient/pallas_call | solution.py:571
  177.5 17.6 %attention_backward.5 = (f32[1,64,2048]{2,1,0:T(8,128)}, f32[1,64,2048]{2,1,0:T(8,128)}, f32[1,64,2048]{2,1,0:T(8,128)}) custom-call(s32[6]{0:T(128)} %stack.41.meta, s32[2,8]{1,0:T(2,128)} %bitcast.153, bf16[3,128,2048]{2,1,0:T(8,128)(2,1)} %get-tuple-element.59.qt_ref, bf16[3,2048,128]{2,1,0:T(8,128)(2,1)} %get-tuple-element.60.ka_ref, ...), custom_call_target="tpu_custom_call" | custom-call | flops 12099999744 | bytes 1024 | tf_op jit(solution)/shard_map/backward_attention/attention_backward/pallas_call | solution.py:238
  195.1 17.6 %attention_backward.4 = (f32[1,64,2048]{2,1,0:T(8,128)}, f32[1,64,2048]{2,1,0:T(8,128)}, f32[1,64,2048]{2,1,0:T(8,128)}) custom-call(s32[6]{0:T(128)} %stack.41.meta, s32[2,8]{1,0:T(2,128)} %bitcast.154, bf16[3,128,2048]{2,1,0:T(8,128)(2,1)} %get-tuple-element.59.qt_ref, bf16[3,2048,128]{2,1,0:T(8,128)(2,1)} %get-tuple-element.60.ka_ref, ...), custom_call_target="tpu_custom_call" | custom-call | flops 12099999744 | bytes 1024 | tf_op jit(solution)/shard_map/backward_attention/attention_backward/pallas_call | solution.py:238
  212.7 17.6 %attention_backward.3 = (f32[1,64,2048]{2,1,0:T(8,128)}, f32[1,64,2048]{2,1,0:T(8,128)}, f32[1,64,2048]{2,1,0:T(8,128)}) custom-call(s32[6]{0:T(128)} %stack.41.meta, s32[2,8]{1,0:T(2,128)} %bitcast.155, bf16[3,128,2048]{2,1,0:T(8,128)(2,1)} %get-tuple-element.59.qt_ref, bf16[3,2048,128]{2,1,0:T(8,128)(2,1)} %get-tuple-element.60.ka_ref, ...), custom_call_target="tpu_custom_call" | custom-call | flops 12099999744 | bytes 1024 | tf_op jit(solution)/shard_map/backward_attention/attention_backward/pallas_call | solution.py:238
  231.9 17.5 %qkv_backward.1 = (bf16[8,256,384]{2,1,0:T(8,128)(2,1)}, bf16[8,256,384]{2,1,0:T(8,128)(2,1)}, bf16[576,768]{1,0:T(8,128)(2,1)}, f32[2,8,768]{2,1,0:T(8,128)}, f32[2,64,256]{2,1,0:T(8,128)}) custom-call(s32[6]{0:T(128)} %stack.41.meta, bf16[2048,768]{1,0:T(8,128)(2,1)} %get-tuple-element.65.x_ref, f32[1,64,2048]{2,1,0:T(8,128)} %get-tuple-element.82.refs_0_, ...), custom_call_target="tpu_custom_call" | custom-call | flops 18699999232 | bytes 1024 | tf_op jit(solution)/shard_map/backward_attention/qkv_backward/pallas_call | solution.py:318
  251.8 67.8 %all-gather = f32[32,1,3200]{2,1,0:T(1,128)S(1)} all-gather(f32[1,1,3200]{2,1,0:T(1,128)S(1)} %reshape.210), channel_id=1, replica_groups=mesh['rep'=2,'fsdp'=2,'seq'=8] {'rep','fsdp','seq'}, dimensions={0}, use_global_device_ids=true | all-gather | bytes 422400 | tf_op jit(solution)/shard_map/vector_gradients/all_gather | solution.py:944
  334.5 6.1 %collective-permute-done.16 = bf16[2,256,384]{2,1,0:T(8,128)(2,1)S(1)} collective-permute-done((bf16[2,256,384]{2,1,0:T(8,128)(2,1)S(1)}, bf16[2,256,384]{2,1,0:T(8,128)(2,1)S(1)}, u32[]{:S(2)}, u32[]{:S(2)}) %collective-permute-start.16) | collective-permute-done | bytes 393248 | tf_op jit(solution)/shard_map/ppermute | solution.py:728
  341.5 5.8 %collective-permute-done.20 = bf16[2,256,384]{2,1,0:T(8,128)(2,1)S(1)} collective-permute-done((bf16[2,256,384]{2,1,0:T(8,128)(2,1)S(1)}, bf16[2,256,384]{2,1,0:T(8,128)(2,1)S(1)}, u32[]{:S(2)}, u32[]{:S(2)}) %collective-permute-start.20) | collective-permute-done | bytes 393248 | tf_op jit(solution)/shard_map/ppermute | solution.py:728
  354.7 11.9 %collective-permute-done.32 = bf16[384,768]{1,0:T(8,128)(2,1)S(1)} collective-permute-done((bf16[384,768]{1,0:T(8,128)(2,1)S(1)}, bf16[384,768]{1,0:T(8,128)(2,1)S(1)}, u32[]{:S(2)}, u32[]{:S(2)}) %collective-permute-start.32) | collective-permute-done | bytes 589856 | tf_op jit(solution)/shard_map/weight_gradients/ppermute | solution.py:728
  379.0 6.6 %collective-permute-start.40 = (bf16[864,384]{1,0:T(8,128)(2,1)S(1)}, bf16[864,384]{1,0:T(8,128)(2,1)S(1)}, u32[]{:S(2)}, u32[]{:S(2)}) collective-permute-start(bf16[864,384]{1,0:T(8,128)(2,1)S(1)} %pad_maximum_fusion.2), channel_id=1, source_target_pairs={{0,4},{1,5},{2,6},{3,7},{4,0},{5,1},{6,2},{7,3},{8,12},{9,13},{10,... | collective-permute-start | bytes 1990664 | tf_op jit(solution)/shard_map/weight_gradients/ppermute | solution.py:728
  390.3 28.6 %collective-permute-done.40 = bf16[864,384]{1,0:T(8,128)(2,1)S(1)} collective-permute-done((bf16[864,384]{1,0:T(8,128)(2,1)S(1)}, bf16[864,384]{1,0:T(8,128)(2,1)S(1)}, u32[]{:S(2)}, u32[]{:S(2)}) %collective-permute-start.40) | collective-permute-done | bytes 663584 | tf_op jit(solution)/shard_map/weight_gradients/ppermute | solution.py:728
  420.6 11.6 %collective-permute-done.27 = bf16[288,384]{1,0:T(8,128)(2,1)S(1)} collective-permute-done((bf16[288,384]{1,0:T(8,128)(2,1)S(1)}, bf16[288,384]{1,0:T(8,128)(2,1)S(1)}, u32[]{:S(2)}, u32[]{:S(2)}) %collective-permute-start.27) | collective-permute-done | bytes 221216 | tf_op jit(solution)/shard_map/first_projection_gradient/ppermute | solution.py:728
  432.4 13.0 %collective-permute-done.41 = bf16[384,384]{1,0:T(8,128)(2,1)S(1)} collective-permute-done((bf16[384,384]{1,0:T(8,128)(2,1)S(1)}, bf16[384,384]{1,0:T(8,128)(2,1)S(1)}, u32[]{:S(2)}, u32[]{:S(2)}) %collective-permute-start.41) | collective-permute-done | bytes 294944 | tf_op jit(solution)/shard_map/weight_gradients/ppermute | solution.py:728
  449.9 11.6 %collective-permute-done.42 = bf16[384,768]{1,0:T(8,128)(2,1)S(1)} collective-permute-done((bf16[384,768]{1,0:T(8,128)(2,1)S(1)}, bf16[384,768]{1,0:T(8,128)(2,1)S(1)}, u32[]{:S(2)}, u32[]{:S(2)}) %collective-permute-start.42) | collective-permute-done | bytes 589856 | tf_op jit(solution)/shard_map/weight_gradients/ppermute | solution.py:728
  473.5 37.7 %collective-permute-done.48 = bf16[96,768]{1,0:T(8,128)(2,1)S(1)} collective-permute-done((bf16[96,768]{1,0:T(8,128)(2,1)S(1)}, bf16[96,768]{1,0:T(8,128)(2,1)S(1)}, u32[]{:S(2)}, u32[]{:S(2)}) %collective-permute-start.48) | collective-permute-done | bytes 147488 | tf_op jit(solution)/shard_map/weight_gradients/ppermute | solution.py:728
  521.6 9.4 %weight_gradients.1 = (f32[1536,768]{1,0:T(8,128)}, f32[384,3072]{1,0:T(8,128)}, f32[384,768]{1,0:T(8,128)}) custom-call(s32[6]{0:T(128)} %stack.41.meta, bf16[768,768]{1,0:T(8,128)(2,1)} %pad_maximum_fusion.down_a, bf16[768,768]{1,0:T(8,128)(2,1)} %collective-permute-done.43.down_b, bf16[384,1536]{1,0:T(8,128)(2,1)} %pad_maximum_fusion.1.up_a, ...), custom_call_target="tpu_custom_call" | custom-call | flops 7699999744 | bytes 1024 | tf_op jit(solution)/shard_map/weight_gradients/weight_gradients/pallas_call | solution.py:680
  (226 shorter events, 124.3 us)
Async XLA Ops:
  1.9 21.9 %collective-permute-start.4 = (bf16[256,768]{1,0:T(8,128)(2,1)S(1)}, bf16[256,768]{1,0:T(8,128)(2,1)}, u32[]{:S(2)}, u32[]{:S(2)}) collective-permute-start(bf16[256,768]{1,0:T(8,128)(2,1)S(1)} %get-tuple-element.152), channel_id=1, source_target_pairs={{0,4},{1,5},{2,6},{3,7},{4,0},{5,1},{6,2},{7,3},{8,12},{9,13},{10,... | collective-permute-start | bytes 1179656 | tf_op jit(solution)/shard_map/ppermute | solution.py:728
  6.1 19.8 %collective-permute-start.1 = (bf16[256,768]{1,0:T(8,128)(2,1)S(1)}, bf16[256,768]{1,0:T(8,128)(2,1)S(1)}, u32[]{:S(2)}, u32[]{:S(2)}) collective-permute-start(bf16[256,768]{1,0:T(8,128)(2,1)S(1)} %get-tuple-element.153.refs_0_), channel_id=1, source_target_pairs={{0,2},{1,3},{2,0},{3,1},{4,6},{5,7},{6,4},{7,5},{8,10},{9,11},{10,... | collective-permute-start | bytes 1179656 | tf_op jit(solution)/shard_map/ppermute | solution.py:728
  12.2 25.8 %collective-permute-start.9 = (bf16[384,576]{0,1:T(8,128)(2,1)S(1)}, bf16[384,576]{0,1:T(8,128)(2,1)S(1)}, u32[]{:S(2)}, u32[]{:S(2)}) collective-permute-start(bf16[384,576]{0,1:T(8,128)(2,1)S(1)} %bitcast.126), channel_id=1, source_target_pairs={{0,8},{8,0},{1,9},{9,1},{2,10},{10,2},{3,11},{11,3},{4,12},{12,4},... | collective-permute-start | bytes 1327112 | tf_op jit(solution)/shard_map/ppermute | solution.py:728
  36.0 57.9 %collective-permute-start.12 = (bf16[384,3072]{1,0:T(8,128)(2,1)}, bf16[384,3072]{1,0:T(8,128)(2,1)}, u32[]{:S(2)}, u32[]{:S(2)}) collective-permute-start(bf16[384,3072]{1,0:T(8,128)(2,1)} %refs_8_.1), channel_id=1, source_target_pairs={{0,8},{8,0},{1,9},{9,1},{2,10},{10,2},{3,11},{11,3},{4,12},{12,4},... | collective-permute-start | bytes 7077896 | tf_op jit(solution)/shard_map/ppermute | solution.py:728
  40.6 53.3 %collective-permute-start.13 = (bf16[1536,768]{1,0:T(8,128)(2,1)}, bf16[1536,768]{1,0:T(8,128)(2,1)}, u32[]{:S(2)}, u32[]{:S(2)}) collective-permute-start(bf16[1536,768]{1,0:T(8,128)(2,1)} %refs_10_.1), channel_id=1, source_target_pairs={{0,8},{8,0},{1,9},{9,1},{2,10},{10,2},{3,11},{11,3},{4,12},{12,4},... | collective-permute-start | bytes 7077896 | tf_op jit(solution)/shard_map/ppermute | solution.py:728
  88.0 24.6 %all-to-all-start = ((bf16[8,192,256]{2,1,0:T(8,128)(2,1)}), bf16[8,192,256]{2,1,0:T(8,128)(2,1)S(1)}, u32[]{:S(2)}, u32[]{:S(2)}) async-start(bf16[8,192,256]{2,1,0:T(8,128)(2,1)} %get-tuple-element.62), calls=%async_computation | async-start | bytes 1572864 | tf_op jit(solution)/shard_map/all_to_all | solution.py:818
  152.4 24.2 %all-to-all-start.1 = ((bf16[8,192,256]{2,1,0:T(8,128)(2,1)}), bf16[8,192,256]{2,1,0:T(8,128)(2,1)S(1)}, u32[]{:S(2)}, u32[]{:S(2)}) async-start(bf16[8,192,256]{2,1,0:T(8,128)(2,1)} %bitcast.17), calls=%async_computation.1 | async-start | bytes 1572864 | tf_op jit(solution)/shard_map/all_to_all | solution.py:818
  230.3 94.3 %collective-permute-start.37 = (bf16[192,768]{1,0:T(8,128)(2,1)}, bf16[192,768]{1,0:T(8,128)(2,1)S(1)}, u32[]{:S(2)}, u32[]{:S(2)}) collective-permute-start(bf16[192,768]{1,0:T(8,128)(2,1)} %get-tuple-element.102), channel_id=1, source_target_pairs={{0,2},{1,3},{2,0},{3,1},{4,6},{5,7},{6,4},{7,5},{8,10},{9,11},{10,... | collective-permute-start | bytes 884744 | tf_op jit(solution)/shard_map/weight_gradients/ppermute | solution.py:728
  230.6 119.4 %collective-permute-start.31 = (bf16[768,768]{1,0:T(8,128)(2,1)}, bf16[768,768]{1,0:T(8,128)(2,1)}, u32[]{:S(2)}, u32[]{:S(2)}) collective-permute-start(bf16[768,768]{1,0:T(8,128)(2,1)} %get-tuple-element.98), channel_id=1, source_target_pairs={{0,16},{16,0},{1,17},{17,1},{2,18},{18,2},{3,19},{19,3},{4,20},{20... | collective-permute-start | bytes 3538952 | tf_op jit(solution)/shard_map/weight_gradients/ppermute | solution.py:728
  230.6 121.9 %collective-permute-start.34 = (bf16[384,1536]{1,0:T(8,128)(2,1)}, bf16[384,1536]{1,0:T(8,128)(2,1)S(1)}, u32[]{:S(2)}, u32[]{:S(2)}) collective-permute-start(bf16[384,1536]{1,0:T(8,128)(2,1)} %get-tuple-element.100), channel_id=1, source_target_pairs={{0,1},{1,0},{2,3},{3,2},{4,5},{5,4},{6,7},{7,6},{8,9},{9,8},{10,11... | collective-permute-start | bytes 3538952 | tf_op jit(solution)/shard_map/weight_gradients/ppermute | solution.py:728
  324.6 25.2 %collective-permute-start.25 = (bf16[576,384]{1,0:T(8,128)(2,1)S(1)}, bf16[576,384]{1,0:T(8,128)(2,1)S(1)}, u32[]{:S(2)}, u32[]{:S(2)}) collective-permute-start(bf16[576,384]{1,0:T(8,128)(2,1)S(1)} %constant_dynamic-slice_fusion.7), channel_id=1, source_target_pairs={{0,8},{8,0},{1,9},{9,1},{2,10},{10,2},{3,11},{11,3},{4,12},{12,4},... | collective-permute-start | bytes 1327112 | tf_op jit(solution)/shard_map/first_projection_gradient/ppermute | solution.py:728
  347.3 31.7 %collective-permute-start.23 = (bf16[256,384]{1,0:T(8,128)(2,1)S(1)}, bf16[256,384]{1,0:T(8,128)(2,1)S(1)}, u32[]{:S(2)}, u32[]{:S(2)}) collective-permute-start(bf16[256,384]{1,0:T(8,128)(2,1)S(1)} %slice_bitcast_fusion.8), channel_id=1, source_target_pairs={{0,1},{1,0},{2,3},{3,2},{4,5},{5,4},{6,7},{7,6},{8,9},{9,8},{10,11... | collective-permute-start | bytes 589832 | tf_op jit(solution)/shard_map/ppermute | solution.py:728
  348.0 97.4 %collective-permute-start.19 = (bf16[256,384]{1,0:T(8,128)(2,1)S(1)}, bf16[256,384]{1,0:T(8,128)(2,1)S(1)}, u32[]{:S(2)}, u32[]{:S(2)}) collective-permute-start(bf16[256,384]{1,0:T(8,128)(2,1)S(1)} %slice_bitcast_fusion.12), channel_id=1, source_target_pairs={{0,1},{1,0},{2,3},{3,2},{4,5},{5,4},{6,7},{7,6},{8,9},{9,8},{10,11... | collective-permute-start | bytes 589832 | tf_op jit(solution)/shard_map/ppermute | solution.py:728
  349.8 35.8 %collective-permute-start.21 = (bf16[256,384]{1,0:T(8,128)(2,1)S(1)}, bf16[256,384]{1,0:T(8,128)(2,1)S(1)}, u32[]{:S(2)}, u32[]{:S(2)}) collective-permute-start(bf16[256,384]{1,0:T(8,128)(2,1)S(1)} %slice_bitcast_fusion.10), channel_id=1, source_target_pairs={{0,2},{1,3},{2,0},{3,1},{4,6},{5,7},{6,4},{7,5},{8,10},{9,11},{10,... | collective-permute-start | bytes 589832 | tf_op jit(solution)/shard_map/ppermute | solution.py:728
  374.1 73.7 %collective-permute-start.17 = (bf16[256,384]{1,0:T(8,128)(2,1)S(1)}, bf16[256,384]{1,0:T(8,128)(2,1)S(1)}, u32[]{:S(2)}, u32[]{:S(2)}) collective-permute-start(bf16[256,384]{1,0:T(8,128)(2,1)S(1)} %slice_bitcast_fusion.14), channel_id=1, source_target_pairs={{0,2},{1,3},{2,0},{3,1},{4,6},{5,7},{6,4},{7,5},{8,10},{9,11},{10,... | collective-permute-start | bytes 589832 | tf_op jit(solution)/shard_map/ppermute | solution.py:728
  379.0 39.9 %collective-permute-start.40 = (bf16[864,384]{1,0:T(8,128)(2,1)S(1)}, bf16[864,384]{1,0:T(8,128)(2,1)S(1)}, u32[]{:S(2)}, u32[]{:S(2)}) collective-permute-start(bf16[864,384]{1,0:T(8,128)(2,1)S(1)} %pad_maximum_fusion.2), channel_id=1, source_target_pairs={{0,4},{1,5},{2,6},{3,7},{4,0},{5,1},{6,2},{7,3},{8,12},{9,13},{10,... | collective-permute-start | bytes 1990664 | tf_op jit(solution)/shard_map/weight_gradients/ppermute | solution.py:728
  385.8 46.4 %collective-permute-start.27 = (bf16[288,384]{1,0:T(8,128)(2,1)S(1)}, bf16[288,384]{1,0:T(8,128)(2,1)S(1)}, u32[]{:S(2)}, u32[]{:S(2)}) collective-permute-start(bf16[288,384]{1,0:T(8,128)(2,1)S(1)} %add_convert_fusion.10), channel_id=1, source_target_pairs={{0,4},{1,5},{2,6},{3,7},{4,0},{5,1},{6,2},{7,3},{8,12},{9,13},{10,... | collective-permute-start | bytes 663560 | tf_op jit(solution)/shard_map/first_projection_gradient/ppermute | solution.py:728
  420.5 52.0 %collective-permute-start.24 = (bf16[256,768]{1,0:T(8,128)(2,1)S(1)}, bf16[256,768]{1,0:T(8,128)(2,1)S(1)}, u32[]{:S(2)}, u32[]{:S(2)}) collective-permute-start(bf16[256,768]{1,0:T(8,128)(2,1)S(1)} %pad_maximum_fusion.7), channel_id=1, source_target_pairs={{0,4},{1,5},{2,6},{3,7},{4,0},{5,1},{6,2},{7,3},{8,12},{9,13},{10,... | collective-permute-start | bytes 1179656 | tf_op jit(solution)/shard_map/ppermute | solution.py:728
  445.7 24.4 %collective-permute-start.29 = (bf16[2,288,384]{2,1,0:T(8,128)(2,1)S(1)}, bf16[2,288,384]{2,1,0:T(8,128)(2,1)S(1)}, u32[]{:S(2)}, u32[]{:S(2)}) collective-permute-start(bf16[2,288,384]{2,1,0:T(8,128)(2,1)S(1)} %maximum_select_fusion.4), channel_id=1, source_target_pairs={{0,2},{1,3},{2,0},{3,1},{4,6},{5,7},{6,4},{7,5},{8,10},{9,11},{10,... | collective-permute-start | bytes 1327112 | tf_op jit(solution)/shard_map/first_projection_gradient/ppermute | solution.py:728
  447.8 22.8 %collective-permute-start.47 = (bf16[96,384]{1,0:T(8,128)(2,1)S(1)}, bf16[96,384]{1,0:T(8,128)(2,1)S(1)}, u32[]{:S(2)}, u32[]{:S(2)}) collective-permute-start(bf16[96,384]{1,0:T(8,128)(2,1)S(1)} %split.14), channel_id=1, source_target_pairs={{0,1},{1,0},{2,3},{3,2},{4,5},{5,4},{6,7},{7,6},{8,9},{9,8},{10,11... | collective-permute-start | bytes 221192 | tf_op jit(solution)/shard_map/weight_gradients/ppermute | solution.py:728
  462.7 58.9 %collective-permute-start.43 = (bf16[768,768]{1,0:T(8,128)(2,1)}, bf16[768,768]{1,0:T(8,128)(2,1)}, u32[]{:S(2)}, u32[]{:S(2)}) collective-permute-start(bf16[768,768]{1,0:T(8,128)(2,1)} %pad_maximum_fusion.down_a), channel_id=1, source_target_pairs={{0,16},{16,0},{1,17},{17,1},{2,18},{18,2},{3,19},{19,3},{4,20},{20... | collective-permute-start | bytes 3538952 | tf_op jit(solution)/shard_map/weight_gradients/ppermute | solution.py:728
  464.1 57.5 %collective-permute-start.46 = (bf16[384,1536]{1,0:T(8,128)(2,1)}, bf16[384,1536]{1,0:T(8,128)(2,1)}, u32[]{:S(2)}, u32[]{:S(2)}) collective-permute-start(bf16[384,1536]{1,0:T(8,128)(2,1)} %pad_maximum_fusion.1.up_a), channel_id=1, source_target_pairs={{0,1},{1,0},{2,3},{3,2},{4,5},{5,4},{6,7},{7,6},{8,9},{9,8},{10,11... | collective-permute-start | bytes 3538952 | tf_op jit(solution)/shard_map/weight_gradients/ppermute | solution.py:728
  470.3 47.6 %collective-permute-start.30 = (bf16[4,288,384]{2,1,0:T(8,128)(2,1)S(1)}, bf16[4,288,384]{2,1,0:T(8,128)(2,1)S(1)}, u32[]{:S(2)}, u32[]{:S(2)}) collective-permute-start(bf16[4,288,384]{2,1,0:T(8,128)(2,1)S(1)} %maximum_select_fusion.2), channel_id=1, source_target_pairs={{0,16},{16,0},{1,17},{17,1},{2,18},{18,2},{3,19},{19,3},{4,20},{20... | collective-permute-start | bytes 2654216 | tf_op jit(solution)/shard_map/first_projection_gradient/ppermute | solution.py:728
  470.7 40.6 %collective-permute-start.48 = (bf16[96,768]{1,0:T(8,128)(2,1)S(1)}, bf16[96,768]{1,0:T(8,128)(2,1)S(1)}, u32[]{:S(2)}, u32[]{:S(2)}) collective-permute-start(bf16[96,768]{1,0:T(8,128)(2,1)S(1)} %pad_maximum_fusion.9), channel_id=1, source_target_pairs={{0,16},{16,0},{1,17},{17,1},{2,18},{18,2},{3,19},{19,3},{4,20},{20... | collective-permute-start | bytes 442376 | tf_op jit(solution)/shard_map/weight_gradients/ppermute | solution.py:728
  (51 other events, 538.6 us)

commit v4 on v3

--- a/solution.py
+++ b/solution.py
@@ -12,6 +12,7 @@
 LOG2E = 1.4426950408889634
 SHIFT = 512.0
 BLK = 256
+EXTRA = 32
 NN = (((1,), (0,)), ((), ()))
 NT = (((1,), (1,)), ((), ()))
 TN = (((0,), (0,)), ((), ()))
@@ -28,7 +29,7 @@
 
 
 def cost(us):
-    return pl.CostEstimate(flops=int(us * 1.1e9), bytes_accessed=1024, transcendentals=0)
+    return pl.CostEstimate(flops=int(us * 0.35e9), bytes_accessed=1024, transcendentals=0)
 
 
 def norm_rows(v):
@@ -265,7 +266,7 @@
     heads, hd, meta, x_ref, *refs
 ):
     dqs, dks, dvs = refs[:heads], refs[heads : 2 * heads], refs[2 * heads : 3 * heads]
-    w_ref, g_ref, b_ref, gq_ref, gk_ref, da_ref, db_ref, dw_ref, vec_ref, gain_ref, acc_ref = refs[3 * heads :]
+    w_ref, g_ref, b_ref, gq_ref, gk_ref, vec2_ref, da_ref, db_ref, dw_ref, acc_ref, vec_ref, gain_ref = refs[3 * heads :]
     i = pl.program_id(0)
     wid = heads * hd
 
@@ -306,10 +307,30 @@
 
     @pl.when(i == pl.num_programs(0) - 1)
     def _():
-        dw_ref[...] = acc_ref[...].astype(BF16)
-
-
-def qkv_back(meta, x, dq, dk, dv, w_t, gain, bias, gq, gk, heads, hd):
+        dw_ref[: 3 * wid, :] = acc_ref[...].astype(BF16)
+        lines = [jnp.sum(ref[k], axis=0, keepdims=True) for ref in (vec_ref, vec2_ref) for k in range(2)]
+        width = dw_ref.shape[1]
+        lane = lax.broadcasted_iota(jnp.int32, (hd, width), 1)
+        item = lax.broadcasted_iota(jnp.int32, (hd, width), 0)
+        spread = jnp.where(item < hd // 2, item, item - hd // 2 + width // 2)
+        line = jnp.zeros((8, width), F32)
+        for k in range(2):
+            total = lax.dot_general(
+                jnp.ones((8, BLK), F32), gain_ref[k], NT, precision=lax.Precision.HIGHEST, preferred_element_type=F32
+            )
+            pick = (lane == spread + k * (hd // 2)).astype(F32)
+            line = line + lax.dot_general(
+                total, pick, NN, precision=lax.Precision.HIGHEST, preferred_element_type=F32
+            )
+        lines.append(line[:1])
+        place = lax.broadcasted_iota(jnp.int32, (EXTRA, width), 0)
+        below = jnp.zeros((EXTRA, width), F32)
+        for k, one in enumerate(lines):
+            below = jnp.where(place == k, one, below)
+        dw_ref[3 * wid :, :] = below.astype(BF16)
+
+
+def qkv_back(meta, x, dq, dk, dv, w_t, gain, bias, gq, gk, vec2, heads, hd):
     length, width = x.shape
     blocks = length // BLK
     whole = lambda *shape: pl.BlockSpec(shape, lambda i, m: (0,) * len(shape))
@@ -328,27 +349,71 @@
                 whole(1, width),
                 whole(hd, 1),
                 whole(hd, 1),
+                whole(2, 8, width),
             ],
             out_specs=(
                 grads,
                 grads,
-                whole(*w_t.shape),
-                whole(2, 8, width),
-                whole(2, hd, BLK),
+                whole(w_t.shape[0] + EXTRA, width),
             ),
-            scratch_shapes=[pltpu.VMEM(w_t.shape, F32)],
+            scratch_shapes=[
+                pltpu.VMEM(w_t.shape, F32),
+                pltpu.VMEM((2, 8, width), F32),
+                pltpu.VMEM((2, hd, BLK), F32),
+            ],
         ),
         out_shape=(
             jax.ShapeDtypeStruct((blocks, BLK, width // 2), BF16),
             jax.ShapeDtypeStruct((blocks, BLK, width // 2), BF16),
-            jax.ShapeDtypeStruct(w_t.shape, BF16),
-            jax.ShapeDtypeStruct((2, 8, width), F32),
-            jax.ShapeDtypeStruct((2, hd, BLK), F32),
+            jax.ShapeDtypeStruct((w_t.shape[0] + EXTRA, width), BF16),
         ),
         compiler_params=params(),
         cost_estimate=cost(17),
         name="qkv_backward",
-    )(meta, x, *dq, *dk, *dv, w_t, gain, bias, gq, gk)
+    )(meta, x, *dq, *dk, *dv, w_t, gain, bias, gq, gk, vec2)
+
+
+def assemble_qkv(meta, own, other, heads, hd):
+    team, part, half = own.shape
+    wid = heads * hd
+    turned = team * wid
+
+    def body(meta, own_ref, other_ref, out_ref, vec_ref, all_s):
+        t = pl.program_id(0)
+
+        @pl.when(t == 0)
+        def _():
+            first = meta[3] == 0
+            for y in range(2):
+                for z in range(2):
+                    at = 2 * jnp.bitwise_xor(meta[4], y) + jnp.bitwise_xor(meta[5], z)
+                    a, b = own_ref[at], other_ref[at]
+                    all_s[2 * z + y, :part, :] = jnp.where(first, a, b)
+                    all_s[2 * z + y, part:, :] = jnp.where(first, b, a)
+            total = jnp.zeros((EXTRA, half), F32)
+            for p in range(team):
+                total = total + all_s[p, 3 * wid :, :].astype(F32)
+            vec_ref[...] = total
+
+        rows = pl.ds(pl.multiple_of(t * wid, wid), wid)
+        piece = jnp.concatenate([all_s[p, rows, :] for p in range(team)], axis=0)
+        out_ref[...] = jnp.transpose(piece.astype(F32))
+
+    whole = lambda *shape: pl.BlockSpec(shape, lambda i, m: (0,) * len(shape))
+    return pl.pallas_call(
+        body,
+        grid_spec=pltpu.PrefetchScalarGridSpec(
+            num_scalar_prefetch=1,
+            grid=(3,),
+            in_specs=[whole(team, part, half), whole(team, part, half)],
+            out_specs=(pl.BlockSpec((half, turned), lambda i, m: (0, i)), whole(EXTRA, half)),
+            scratch_shapes=[pltpu.VMEM((team, 2 * part, half), BF16)],
+        ),
+        out_shape=(jax.ShapeDtypeStruct((half, 3 * turned), F32), jax.ShapeDtypeStruct((EXTRA, half), F32)),
+        compiler_params=params(),
+        cost_estimate=cost(5),
+        name="first_projection_gradient",
+    )(meta, own, other)
 
 
 def gelu_pair(u):
@@ -845,28 +910,42 @@
         grad_o = jnp.swapaxes(got, 1, 2).reshape(8, heads * hd, BLK)
 
     masks = [1 << k for k in range(n.bit_length() - 1)]
+    x, y, z = ("rep", 1), ("seq", 1), ("seq", 2)
+
+    def next_half(keep, got, way, axis):
+        return halves(add(keep, got), bit(*way), axis)
+
     with jax.named_scope("weight_gradients"):
+        far_d = swap(down_grads(meta, act, dy))
         far_u = swap(up_out_grads(meta, attn_t, grad_branch, h2, dup))
-        far_d = swap(down_grads(meta, act, dy))
+        down_k, down_s = down_grads(meta, act, dy, far_d)
         up_k, up_s, out_k, out_s = up_out_grads(meta, attn_t, grad_branch, h2, dup, far_u)
-        down_k, down_s = down_grads(meta, act, dy, far_d)
         grad_o, up_k, up_s, out_k, out_s, down_k, down_s = lax.optimization_barrier(
             (grad_o, up_k, up_s, out_k, out_s, down_k, down_s)
         )
-        x, y, z = ("rep", 1), ("seq", 1), ("seq", 2)
-
-        def next_half(keep, got, way, axis):
-            return halves(add(keep, got), bit(*way), axis)
-
-        down_k, down_s = next_half(down_k, flip(down_s, *x), y, 0)
-        up_k, up_s = next_half(up_k, flip(up_s, *y), z, 1)
-        out_k, out_s = next_half(out_k, flip(out_s, *z), x, 0)
-        down_k, down_s = next_half(down_k, flip(down_s, *y), z, 1)
-        up_k, up_s = next_half(up_k, flip(up_s, *z), x, 1)
-        out_k, out_s = next_half(out_k, flip(out_s, *x), y, 1)
-        down = add(down_k, flip(down_s, *z))
-        up = add(up_k, flip(up_s, *x))
-        out = add(out_k, flip(out_s, *y))
+    got = flip(down_s, *x), flip(up_s, *y), flip(out_s, *z)
+    back = lambda h, go: attend_back(meta, lengths, qt, ka, kt, v, attn_f, logsum, go, h, 1, hd)
+    parts = [back(0, grad_o)]
+    with jax.named_scope("weight_gradients"):
+        grad_o, *got = lax.optimization_barrier((grad_o, *got))
+        down_k, down_s = next_half(down_k, got[0], y, 0)
+        up_k, up_s = next_half(up_k, got[1], z, 1)
+        out_k, out_s = next_half(out_k, got[2], x, 0)
+        got = flip(down_s, *y), flip(up_s, *z), flip(out_s, *x)
+    for h in range(1, heads - 1):
+        parts.append(back(h, grad_o))
+    with jax.named_scope("weight_gradients"):
+        grad_o, *got = lax.optimization_barrier((grad_o, *got))
+        down_k, down_s = next_half(down_k, got[0], z, 1)
+        up_k, up_s = next_half(up_k, got[1], x, 1)
+        out_k, out_s = next_half(out_k, got[2], y, 1)
+        got = flip(down_s, *z), flip(up_s, *x), flip(out_s, *y)
+    parts.append(back(heads - 1, grad_o))
+    x_row, *got = lax.optimization_barrier((x_row, *got))
+    with jax.named_scope("weight_gradients"):
+        down = add(down_k, got[0])
+        up = add(up_k, got[1])
+        out = add(out_k, got[2])
         if masks[2:]:
             sizes = [down.shape[0], up.shape[0]]
             every_piece = jnp.concatenate([down, up, out])
@@ -884,12 +963,9 @@
         )
 
     with jax.named_scope("backward_attention"):
-        parts = [
-            attend_back(meta, lengths, qt, ka, kt, v, attn_f, logsum, grad_o, h, 1, hd) for h in range(heads)
-        ]
         dq, dk, dv = zip(*parts)
-        back_a, back_b, dw_t, vec1, gains = qkv_back(
-            meta, x_row, dq, dk, dv, w_t, g1, b1, gq, gk, heads, hd
+        back_a, back_b, dw_t = qkv_back(
+            meta, x_row, dq, dk, dv, w_t, g1, b1, gq, gk, vec2, heads, hd
         )
 
     if direct:
@@ -920,31 +996,15 @@
 
     with jax.named_scope("first_projection_gradient"):
         keep, send = halves(dw_t, core, 1)
-        piece = add(keep, swap(send))
-        keep, send = halves(piece, bit("rep", 1))
-        piece = add(keep, flip(send, "rep", 1))
+        piece, send = next_half(keep, swap(send), x, 0)
+        piece = add(piece, flip(send, *x))
         for mask in masks:
             if mask >= team:
                 piece = add(piece, flip(piece, "seq", mask))
-        piece = piece[None]
-        for mask in masks:
-            if mask < team:
-                piece = join(piece, flip(piece, "seq", mask), bit("seq", mask))
-        piece = join(piece, flip(piece, "rep", 1), bit("rep", 1), 1)
-        piece = piece.reshape(team, 3, heads * hd, half)
-        grad_qkv = jnp.transpose(piece, (3, 1, 0, 2)).reshape(half, 3 * width).astype(F32)
-
-    with jax.named_scope("vector_gradients"):
-        small = jnp.concatenate([vec1, vec2]).sum(axis=1).reshape(4, 2, half)
-        small = jnp.concatenate(
-            [jnp.swapaxes(small, 0, 1).reshape(2, 4 * half)]
-            + [gains[k].sum(axis=-1).reshape(2, hd // 2) for k in range(2)],
-            axis=1,
-        )
-        small = lax.all_gather(small.reshape(-1), ("rep", "fsdp", "seq")).sum(axis=0).reshape(2, -1)
-        small = jnp.where(core == 0, small[0], small[1])
-        cuts = [small[k * half : (k + 1) * half] for k in range(4)]
-        cuts += [small[4 * half : 4 * half + hd // 2], small[4 * half + hd // 2 :]]
+        piece = jnp.stack([piece, flip(piece, *z)])
+        piece = jnp.concatenate([piece, flip(piece, *y)], axis=0)
+        grad_qkv, small = assemble_qkv(meta, piece, flip(piece, *x), heads, hd)
+        cuts = [small[0], small[1], small[2], small[3], small[4, : hd // 2], small[4, hd // 2 : hd]]
     shape = tokens.shape
     return (
         output.reshape(shape), grad_tokens.reshape(shape), cuts[0], cuts[1], grad_qkv, cuts[4], cuts[5],

time: 531 us -> 416 us (0.78); the launches traced: 531 us -> 422 us
  blocking collectives: 67.8 us -> 0 us
  waiting for transfers between devices: 189 us -> 154 us
    all_gather x1 -> x0, blocking collectives: 67.8 us -> none  [on_device(): lax.all_gather(small.reshape(-1), ('rep', 'fsdp', 'seq')).sum(axis=0)]
    ppermute x50, waiting for transfers between devices: 166 us -> 131 us  [flip(): return lax.ppermute(value, axis, [(i, i ^ mask) for i in range(size)])]
    unnamed x55 -> x62, local copies, waits for them, and re-layouts: 11.5 us -> 8.79 us
  transfers between devices with their start and end apart: 52 -> 52, of which waited for: 21 -> 21; matrix products, arithmetic and copies ran while one was open for 6% -> 5% of each run, Pallas kernels for 16% -> 29%
where the time goes in v4:
time: 416 us; the launch traced here: 422 us
  Pallas kernels  181 us (44%)
  waiting for transfers between devices  154 us (37%)
  starting transfers between devices  56.2 us (14%)
  local copies, waits for them, and re-layouts  17.7 us (4%)
  other arithmetic  10.7 us (3%)
    ppermute x50, waiting for transfers between devices, flip(): return lax.ppermute(value, axis, [(i, i ^ mask) for i in range(size)])  131 us
    pallas_call x3, Pallas kernels, attend_back(): pl.pallas_call(functools.partial(attend_back_body, heads, hd), grid=(bloc...  50.5 us
    ppermute x50, starting transfers between devices, flip(): return lax.ppermute(value, axis, [(i, i ^ mask) for i in range(size)])  48.5 us
    pallas_call x1, Pallas kernels, attend(): pl.pallas_call(functools.partial(attend_body, heads, hd), grid=(blocks,),...  28.6 us
    pallas_call x1, Pallas kernels, ffn(): pl.pallas_call(body, grid_spec=pltpu.PrefetchScalarGridSpec(num_scalar_pr...  25.6 us
    all_to_all x2, waiting for transfers between devices, exchange(): return lax.all_to_all(value, 'seq', 0, 0, tiled=True)  23.6 us
    pallas_call x1, Pallas kernels, qkv_back(): pl.pallas_call(functools.partial(qkv_back_body, heads, hd), grid_spec=plt...  17.8 us
    pallas_call x2, Pallas kernels, up_out_grads(): pl.pallas_call(body, grid_spec=pltpu.PrefetchScalarGridSpec(num_scalar_pr...  15.5 us
  transfers between devices with their start and end apart: 52, of which 21 were waited for; matrix products, arithmetic and copies ran while one was open for 5% of the time, Pallas kernels for 29%

profile of v4, /device:TPU:0, one launch (start us, length us, event | category | flops | bytes accessed | tf_op | source)
XLA Modules:
  0.0 421.8 jit_solution(9109551410100876603)
XLA Ops:
  13.4 10.4 %collective-permute-done.4.refs_4_ = bf16[256,768]{1,0:T(8,128)(2,1)} collective-permute-done((bf16[256,768]{1,0:T(8,128)(2,1)S(1)}, bf16[256,768]{1,0:T(8,128)(2,1)}, u32[]{:S(2)}, u32[]{:S(2)}) %collective-permute-start.4) | collective-permute-done | bytes 393248 | tf_op jit(solution)/shard_map/ppermute | solution.py:793
  45.6 12.2 %qkv_forward.1 = (bf16[3,128,2048]{2,1,0:T(8,128)(2,1)}, bf16[3,2048,128]{2,1,0:T(8,128)(2,1)}, bf16[3,64,2048]{2,1,0:T(8,128)(2,1)}, bf16[3,2048,64]{2,1,0:T(8,...) custom-call(s32[6]{0:T(128)} %stack.50.meta, s32[2,8]{1,0:T(2,128)} %bitcast.145, ...), custom_call_target="tpu_custom_call" | custom-call | flops 4200000000 | bytes 1024 | tf_op jit(solution)/shard_map/forward_attention/qkv_forward/pallas_call | solution.py:104
  57.8 28.6 %attention_forward.1 = (bf16[8,192,256]{2,1,0:T(8,128)(2,1)}, f32[3,64,2048]{2,1,0:T(8,128)}, f32[3,1,2048]{2,1,0:T(1,128)}) custom-call(s32[6]{0:T(128)} %stack.50.meta, s32[2,8]{1,0:T(2,128)} %bitcast.146, bf16[3,128,2048]{2,1,0:T(8,128)(2,1)} %get-tuple-element.71.qt_ref, bf16[3,2048,128]{2,1,0:T(8,128)(2,1)} %get-tuple-element.72.ka_ref, ...), custom_call_target="tpu_custom_call" | custom-call | flops 8750000128 | bytes 1024 | tf_op jit(solution)/shard_map/forward_attention/attention_forward/pallas_call | solution.py:170
  92.5 18.6 %all-to-all-done = bf16[8,192,256]{2,1,0:T(8,128)(2,1)S(1)} async-done(((bf16[8,192,256]{2,1,0:T(8,128)(2,1)}), bf16[8,192,256]{2,1,0:T(8,128)(2,1)S(1)}, u32[]{:S(2)}, u32[]{:S(2)}) %all-to-all-start) | async-done | bytes 786464 | tf_op jit(solution)/shard_map/all_to_all | solution.py:883
  111.9 25.6 %ffn_both_ways.1 = (bf16[512,768]{1,0:T(8,128)(2,1)}, f32[512,768]{1,0:T(8,128)}, bf16[512,768]{1,0:T(8,128)(2,1)}, bf16[512,768]{1,0:T(8,128)(2,1)}, bf16[512,3...) custom-call(s32[6]{0:T(128)} %stack.50.meta, ...), custom_call_target="tpu_custom_call" | custom-call | flops 8750000128 | bytes 1024 | tf_op jit(solution)/shard_map/feed_forward/ffn_both_ways/pallas_call | solution.py:511
  137.6 7.2 %up_out_gradient.2 = bf16[384,3840]{1,0:T(8,128)(2,1)} custom-call(s32[6]{0:T(128)} %stack.50.meta, bf16[2,768,256]{2,1,0:T(8,128)(2,1)} %bitcast.129, bf16[512,768]{1,0:T(8,128)(2,1)} %get-tuple-element.79.gb_ref, bf16[512,768]{1,0:T(8,128)(2,1)} %get-tuple-element.80.h2_ref, bf16[512,3072]{1,0:T(8,128)(2,1)} %get-tuple-element.81.dup_ref), custom_call_target="tpu_custom_call" | custom-call | flops 2449999872 | bytes 1024 | tf_op jit(solution)/shard_map/weight_gradients/up_out_gradient/pallas_call | solution.py:636
  144.7 5.6 %down_gradient.2 = bf16[1536,768]{1,0:T(8,128)(2,1)} custom-call(s32[6]{0:T(128)} %stack.50.meta, bf16[512,3072]{1,0:T(8,128)(2,1)} %get-tuple-element.86.act_ref, bf16[512,768]{1,0:T(8,128)(2,1)} %bitcast.143), custom_call_target="tpu_custom_call" | custom-call | flops 2100000000 | bytes 1024 | tf_op jit(solution)/shard_map/weight_gradients/down_gradient/pallas_call | solution.py:696
  155.3 6.4 %down_gradient.3 = (bf16[768,768]{1,0:T(8,128)(2,1)}, bf16[768,768]{1,0:T(8,128)(2,1)}) custom-call(s32[6]{0:T(128)} %stack.50.meta, bf16[512,3072]{1,0:T(8,128)(2,1)} %get-tuple-element.86.act_ref, bf16[512,768]{1,0:T(8,128)(2,1)} %bitcast.144, bf16[1536,768]{1,0:T(8,128)(2,1)} %collective-permute-done.15.rest_0_), custom_call_target="tpu_custom_call" | custom-call | flops 2100000000 | bytes 1024 | tf_op jit(solution)/shard_map/weight_gradients/down_gradient/pallas_call | solution.py:696
  161.7 8.4 %up_out_gradient.3 = (bf16[384,1536]{1,0:T(8,128)(2,1)}, bf16[384,1536]{1,0:T(8,128)(2,1)}, bf16[192,768]{1,0:T(8,128)(2,1)}, bf16[192,768]{1,0:T(8,128)(2,1)}) custom-call(s32[6]{0:T(128)} %stack.50.meta, bf16[2,768,256]{2,1,0:T(8,128)(2,1)} %bitcast.130, bf16[512,768]{1,0:T(8,128)(2,1)} %get-tuple-element.79.gb_ref, ...), custom_call_target="tpu_custom_call" | custom-call | flops 2449999872 | bytes 1024 | tf_op jit(solution)/shard_map/weight_gradients/up_out_gradient/pallas_call | solution.py:636
  170.1 5.0 %all-to-all-done.1.go_ref = bf16[8,192,256]{2,1,0:T(8,128)(2,1)S(1)} async-done(((bf16[8,192,256]{2,1,0:T(8,128)(2,1)}), bf16[8,192,256]{2,1,0:T(8,128)(2,1)S(1)}, u32[]{:S(2)}, u32[]{:S(2)}) %all-to-all-start.1) | async-done | bytes 786464 | tf_op jit(solution)/shard_map/all_to_all | solution.py:883
  178.7 16.9 %attention_backward.3 = (f32[1,64,2048]{2,1,0:T(8,128)}, f32[1,64,2048]{2,1,0:T(8,128)}, f32[1,64,2048]{2,1,0:T(8,128)}) custom-call(s32[6]{0:T(128)} %stack.50.meta, s32[2,8]{1,0:T(2,128)} %bitcast.147, bf16[3,128,2048]{2,1,0:T(8,128)(2,1)} %get-tuple-element.71.qt_ref, bf16[3,2048,128]{2,1,0:T(8,128)(2,1)} %get-tuple-element.72.ka_ref, ...), custom_call_target="tpu_custom_call" | custom-call | flops 3849999872 | bytes 1024 | tf_op jit(solution)/shard_map/attention_backward/pallas_call | solution.py:239
  195.6 7.3 %collective-permute-done.16 = bf16[768,768]{1,0:T(8,128)(2,1)S(1)} collective-permute-done((bf16[768,768]{1,0:T(8,128)(2,1)}, bf16[768,768]{1,0:T(8,128)(2,1)S(1)}, u32[]{:S(2)}, u32[]{:S(2)}) %collective-permute-start.16) | collective-permute-done | bytes 1179680 | tf_op jit(solution)/shard_map/ppermute | solution.py:793
  209.4 16.8 %attention_backward.4 = (f32[1,64,2048]{2,1,0:T(8,128)}, f32[1,64,2048]{2,1,0:T(8,128)}, f32[1,64,2048]{2,1,0:T(8,128)}) custom-call(s32[6]{0:T(128)} %stack.50.meta, s32[2,8]{1,0:T(2,128)} %bitcast.148, bf16[3,128,2048]{2,1,0:T(8,128)(2,1)} %get-tuple-element.71.qt_ref, bf16[3,2048,128]{2,1,0:T(8,128)(2,1)} %get-tuple-element.72.ka_ref, ...), custom_call_target="tpu_custom_call" | custom-call | flops 3849999872 | bytes 1024 | tf_op jit(solution)/shard_map/attention_backward/pallas_call | solution.py:239
  233.0 16.8 %attention_backward.5 = (f32[1,64,2048]{2,1,0:T(8,128)}, f32[1,64,2048]{2,1,0:T(8,128)}, f32[1,64,2048]{2,1,0:T(8,128)}) custom-call(s32[6]{0:T(128)} %stack.50.meta, s32[2,8]{1,0:T(2,128)} %bitcast.149, bf16[3,128,2048]{2,1,0:T(8,128)(2,1)} %get-tuple-element.71.qt_ref, bf16[3,2048,128]{2,1,0:T(8,128)(2,1)} %get-tuple-element.72.ka_ref, ...), custom_call_target="tpu_custom_call" | custom-call | flops 3849999872 | bytes 1024 | tf_op jit(solution)/shard_map/attention_backward/pallas_call | solution.py:239
  249.9 17.8 %qkv_backward.1 = (bf16[8,256,384]{2,1,0:T(8,128)(2,1)}, bf16[8,256,384]{2,1,0:T(8,128)(2,1)}, bf16[608,768]{1,0:T(8,128)(2,1)}) custom-call(s32[6]{0:T(128)} %stack.50.meta, bf16[2048,768]{1,0:T(8,128)(2,1)} %get-tuple-element.103.x_ref, f32[1,64,2048]{2,1,0:T(8,128)} %get-tuple-element.108.refs_0_, f32[1,64,2048]{2,1,0:T(8,128)} %get-tuple-element.109.refs_1_, ...), custom_call_target="tpu_custom_call" | custom-call | flops 5950000128 | bytes 1024 | tf_op jit(solution)/shard_map/backward_attention/qkv_backward/pallas_call | solution.py:339
  273.6 19.1 %collective-permute-done.27 = bf16[2,256,384]{2,1,0:T(8,128)(2,1)S(1)} collective-permute-done((bf16[2,256,384]{2,1,0:T(8,128)(2,1)S(1)}, bf16[2,256,384]{2,1,0:T(8,128)(2,1)S(1)}, u32[]{:S(2)}, u32[]{:S(2)}) %collective-permute-start.27) | collective-permute-done | bytes 393248 | tf_op jit(solution)/shard_map/ppermute | solution.py:793
  313.2 10.9 %collective-permute-done.36 = bf16[304,384]{1,0:T(8,128)(2,1)S(1)} collective-permute-done((bf16[304,384]{1,0:T(8,128)(2,1)S(1)}, bf16[304,384]{1,0:T(8,128)(2,1)S(1)}, u32[]{:S(2)}, u32[]{:S(2)}) %collective-permute-start.36) | collective-permute-done | bytes 233504 | tf_op jit(solution)/shard_map/first_projection_gradient/ppermute | solution.py:793
  327.1 5.7 %collective-permute-done.37 = bf16[304,384]{1,0:T(8,128)(2,1)S(1)} collective-permute-done((bf16[304,384]{1,0:T(8,128)(2,1)S(1)}, bf16[304,384]{1,0:T(8,128)(2,1)S(1)}, u32[]{:S(2)}, u32[]{:S(2)}) %collective-permute-start.37) | collective-permute-done | bytes 233504 | tf_op jit(solution)/shard_map/first_projection_gradient/ppermute | solution.py:793
  335.1 17.1 %collective-permute-done.47 = bf16[96,384]{1,0:T(8,128)(2,1)S(1)} collective-permute-done((bf16[96,384]{1,0:T(8,128)(2,1)S(1)}, bf16[96,384]{1,0:T(8,128)(2,1)S(1)}, u32[]{:S(2)}, u32[]{:S(2)}) %collective-permute-start.47) | collective-permute-done | bytes 73760 | tf_op jit(solution)/shard_map/weight_gradients/ppermute | solution.py:793
  362.9 7.8 %collective-permute-done.33 = bf16[256,768]{1,0:T(8,128)(2,1)S(1)} collective-permute-done((bf16[256,768]{1,0:T(8,128)(2,1)S(1)}, bf16[256,768]{1,0:T(8,128)(2,1)S(1)}, u32[]{:S(2)}, u32[]{:S(2)}) %collective-permute-start.33) | collective-permute-done | bytes 393248 | tf_op jit(solution)/shard_map/ppermute | solution.py:793
  371.7 4.5 %first_norm_backward.1 = f32[512,768]{1,0:T(8,128)} custom-call(bf16[512,768]{1,0:T(8,128)(2,1)} %bitcast.133, f32[512,768]{1,0:T(8,128)} %get-tuple-element.76.gm_ref, bf16[512,768]{1,0:T(8,128)(2,1)} %bitcast.131, f32[1,768]{1,0:T(1,128)} %bitcast.137), custom_call_target="tpu_custom_call" | custom-call | flops 1400000000 | bytes 1024 | tf_op jit(solution)/shard_map/first_norm_backward/pallas_call | solution.py:779
  376.1 27.7 %collective-permute-done.39.other_ref = bf16[4,304,384]{2,1,0:T(8,128)(2,1)} collective-permute-done((bf16[4,304,384]{2,1,0:T(8,128)(2,1)S(1)}, bf16[4,304,384]{2,1,0:T(8,128)(2,1)}, u32[]{:S(2)}, u32[]{:S(2)}) %collective-permute-start.39) | collective-permute-done | bytes 933920 | tf_op jit(solution)/shard_map/first_projection_gradient/ppermute | solution.py:793
  403.8 4.9 %first_projection_gradient.1 = (f32[384,2304]{1,0:T(8,128)}, f32[32,384]{1,0:T(8,128)}) custom-call(s32[6]{0:T(128)} %stack.50.meta, bf16[4,304,384]{2,1,0:T(8,128)(2,1)} %copy-done.7, bf16[4,304,384]{2,1,0:T(8,128)(2,1)} %collective-permute-done.39.other_ref), custom_call_target="tpu_custom_call" | custom-call | flops 1750000000 | bytes 1024 | tf_op jit(solution)/shard_map/first_projection_gradient/first_projection_gradient/pallas_call | solution.py:403
  412.2 9.4 %weight_gradients.1 = (f32[1536,768]{1,0:T(8,128)}, f32[384,3072]{1,0:T(8,128)}, f32[384,768]{1,0:T(8,128)}) custom-call(s32[6]{0:T(128)} %stack.50.meta, bf16[768,768]{1,0:T(8,128)(2,1)} %copy-done.4, bf16[768,768]{1,0:T(8,128)(2,1)} %collective-permute-done.43.down_b, bf16[384,1536]{1,0:T(8,128)(2,1)} %copy-done.5, ...), custom_call_target="tpu_custom_call" | custom-call | flops 2449999872 | bytes 1024 | tf_op jit(solution)/shard_map/weight_gradients/weight_gradients/pallas_call | solution.py:745
  (223 shorter events, 109.5 us)
Async XLA Ops:
  1.9 21.9 %collective-permute-start.4 = (bf16[256,768]{1,0:T(8,128)(2,1)S(1)}, bf16[256,768]{1,0:T(8,128)(2,1)}, u32[]{:S(2)}, u32[]{:S(2)}) collective-permute-start(bf16[256,768]{1,0:T(8,128)(2,1)S(1)} %get-tuple-element.166), channel_id=1, source_target_pairs={{0,4},{1,5},{2,6},{3,7},{4,0},{5,1},{6,2},{7,3},{8,12},{9,13},{10,... | collective-permute-start | bytes 1179656 | tf_op jit(solution)/shard_map/ppermute | solution.py:793
  12.2 25.8 %collective-permute-start.9 = (bf16[384,576]{0,1:T(8,128)(2,1)S(1)}, bf16[384,576]{0,1:T(8,128)(2,1)S(1)}, u32[]{:S(2)}, u32[]{:S(2)}) collective-permute-start(bf16[384,576]{0,1:T(8,128)(2,1)S(1)} %bitcast.120), channel_id=1, source_target_pairs={{0,8},{8,0},{1,9},{9,1},{2,10},{10,2},{3,11},{11,3},{4,12},{12,4},... | collective-permute-start | bytes 1327112 | tf_op jit(solution)/shard_map/ppermute | solution.py:793
  36.0 56.5 %collective-permute-start.12 = (bf16[384,3072]{1,0:T(8,128)(2,1)}, bf16[384,3072]{1,0:T(8,128)(2,1)}, u32[]{:S(2)}, u32[]{:S(2)}) collective-permute-start(bf16[384,3072]{1,0:T(8,128)(2,1)} %refs_8_.1), channel_id=1, source_target_pairs={{0,8},{8,0},{1,9},{9,1},{2,10},{10,2},{3,11},{11,3},{4,12},{12,4},... | collective-permute-start | bytes 7077896 | tf_op jit(solution)/shard_map/ppermute | solution.py:793
  40.6 51.8 %collective-permute-start.13 = (bf16[1536,768]{1,0:T(8,128)(2,1)}, bf16[1536,768]{1,0:T(8,128)(2,1)}, u32[]{:S(2)}, u32[]{:S(2)}) collective-permute-start(bf16[1536,768]{1,0:T(8,128)(2,1)} %refs_10_.1), channel_id=1, source_target_pairs={{0,8},{8,0},{1,9},{9,1},{2,10},{10,2},{3,11},{11,3},{4,12},{12,4},... | collective-permute-start | bytes 7077896 | tf_op jit(solution)/shard_map/ppermute | solution.py:793
  86.5 24.6 %all-to-all-start = ((bf16[8,192,256]{2,1,0:T(8,128)(2,1)}), bf16[8,192,256]{2,1,0:T(8,128)(2,1)S(1)}, u32[]{:S(2)}, u32[]{:S(2)}) async-start(bf16[8,192,256]{2,1,0:T(8,128)(2,1)} %get-tuple-element.74), calls=%async_computation | async-start | bytes 1572864 | tf_op jit(solution)/shard_map/all_to_all | solution.py:883
  150.8 24.2 %all-to-all-start.1 = ((bf16[8,192,256]{2,1,0:T(8,128)(2,1)}), bf16[8,192,256]{2,1,0:T(8,128)(2,1)S(1)}, u32[]{:S(2)}, u32[]{:S(2)}) async-start(bf16[8,192,256]{2,1,0:T(8,128)(2,1)} %bitcast.17), calls=%async_computation.1 | async-start | bytes 1572864 | tf_op jit(solution)/shard_map/all_to_all | solution.py:883
  175.1 27.8 %collective-permute-start.16 = (bf16[768,768]{1,0:T(8,128)(2,1)}, bf16[768,768]{1,0:T(8,128)(2,1)S(1)}, u32[]{:S(2)}, u32[]{:S(2)}) collective-permute-start(bf16[768,768]{1,0:T(8,128)(2,1)} %get-tuple-element.91), channel_id=1, source_target_pairs={{0,16},{16,0},{1,17},{17,1},{2,18},{18,2},{3,19},{19,3},{4,20},{20... | collective-permute-start | bytes 3538952 | tf_op jit(solution)/shard_map/ppermute | solution.py:793
  177.2 27.2 %collective-permute-start.17 = (bf16[384,1536]{1,0:T(8,128)(2,1)}, bf16[384,1536]{1,0:T(8,128)(2,1)}, u32[]{:S(2)}, u32[]{:S(2)}) collective-permute-start(bf16[384,1536]{1,0:T(8,128)(2,1)} %get-tuple-element.92), channel_id=1, source_target_pairs={{0,1},{1,0},{2,3},{3,2},{4,5},{5,4},{6,7},{7,6},{8,9},{9,8},{10,11... | collective-permute-start | bytes 3538952 | tf_op jit(solution)/shard_map/ppermute | solution.py:793
  204.8 21.4 %collective-permute-start.19 = (bf16[384,768]{1,0:T(8,128)(2,1)S(1)}, bf16[384,768]{1,0:T(8,128)(2,1)}, u32[]{:S(2)}, u32[]{:S(2)}) collective-permute-start(bf16[384,768]{1,0:T(8,128)(2,1)S(1)} %constant_dynamic-slice_fusion.7), channel_id=1, source_target_pairs={{0,1},{1,0},{2,3},{3,2},{4,5},{5,4},{6,7},{7,6},{8,9},{9,8},{10,11... | collective-permute-start | bytes 1769480 | tf_op jit(solution)/shard_map/weight_gradients/ppermute | solution.py:793
  226.3 23.5 %collective-permute-start.24 = (bf16[96,384]{1,0:T(8,128)(2,1)S(1)}, bf16[96,384]{1,0:T(8,128)(2,1)S(1)}, u32[]{:S(2)}, u32[]{:S(2)}) collective-permute-start(bf16[96,384]{1,0:T(8,128)(2,1)S(1)} %constant_dynamic-slice_fusion.2), channel_id=1, source_target_pairs={{0,1},{1,0},{2,3},{3,2},{4,5},{5,4},{6,7},{7,6},{8,9},{9,8},{10,11... | collective-permute-start | bytes 221192 | tf_op jit(solution)/shard_map/weight_gradients/ppermute | solution.py:793
  268.9 23.8 %collective-permute-start.27 = (bf16[2,256,384]{2,1,0:T(8,128)(2,1)S(1)}, bf16[2,256,384]{2,1,0:T(8,128)(2,1)S(1)}, u32[]{:S(2)}, u32[]{:S(2)}) collective-permute-start(bf16[2,256,384]{2,1,0:T(8,128)(2,1)S(1)} %get-tuple-element.164), channel_id=1, source_target_pairs={{0,2},{1,3},{2,0},{3,1},{4,6},{5,7},{6,4},{7,5},{8,10},{9,11},{10,... | collective-permute-start | bytes 1179656 | tf_op jit(solution)/shard_map/ppermute | solution.py:793
  269.9 27.7 %collective-permute-start.31 = (bf16[2,256,384]{2,1,0:T(8,128)(2,1)S(1)}, bf16[2,256,384]{2,1,0:T(8,128)(2,1)S(1)}, u32[]{:S(2)}, u32[]{:S(2)}) collective-permute-start(bf16[2,256,384]{2,1,0:T(8,128)(2,1)S(1)} %get-tuple-element.165), channel_id=1, source_target_pairs={{0,2},{1,3},{2,0},{3,1},{4,6},{5,7},{6,4},{7,5},{8,10},{9,11},{10,... | collective-permute-start | bytes 1179656 | tf_op jit(solution)/shard_map/ppermute | solution.py:793
  271.3 36.1 %collective-permute-start.40 = (bf16[864,384]{1,0:T(8,128)(2,1)S(1)}, bf16[864,384]{1,0:T(8,128)(2,1)S(1)}, u32[]{:S(2)}, u32[]{:S(2)}) collective-permute-start(bf16[864,384]{1,0:T(8,128)(2,1)S(1)} %pad_maximum_fusion.3), channel_id=1, source_target_pairs={{0,4},{1,5},{2,6},{3,7},{4,0},{5,1},{6,2},{7,3},{8,12},{9,13},{10,... | collective-permute-start | bytes 1990664 | tf_op jit(solution)/shard_map/weight_gradients/ppermute | solution.py:793
  271.4 32.9 %collective-permute-start.34 = (bf16[608,384]{1,0:T(8,128)(2,1)S(1)}, bf16[608,384]{1,0:T(8,128)(2,1)S(1)}, u32[]{:S(2)}, u32[]{:S(2)}) collective-permute-start(bf16[608,384]{1,0:T(8,128)(2,1)S(1)} %constant_dynamic-slice_fusion.1), channel_id=1, source_target_pairs={{0,8},{8,0},{1,9},{9,1},{2,10},{10,2},{3,11},{11,3},{4,12},{12,4},... | collective-permute-start | bytes 1400840 | tf_op jit(solution)/shard_map/first_projection_gradient/ppermute | solution.py:793
  272.7 25.9 %collective-permute-start.25 = (bf16[2,256,384]{2,1,0:T(8,128)(2,1)S(1)}, bf16[2,256,384]{2,1,0:T(8,128)(2,1)S(1)}, u32[]{:S(2)}, u32[]{:S(2)}) collective-permute-start(bf16[2,256,384]{2,1,0:T(8,128)(2,1)S(1)} %get-tuple-element.160), channel_id=1, source_target_pairs={{0,1},{1,0},{2,3},{3,2},{4,5},{5,4},{6,7},{7,6},{8,9},{9,8},{10,11... | collective-permute-start | bytes 1179656 | tf_op jit(solution)/shard_map/ppermute | solution.py:793
  304.3 29.3 %collective-permute-start.30 = (bf16[256,384]{1,0:T(8,128)(2,1)S(1)}, bf16[256,384]{1,0:T(8,128)(2,1)S(1)}, u32[]{:S(2)}, u32[]{:S(2)}) collective-permute-start(bf16[256,384]{1,0:T(8,128)(2,1)S(1)} %slice_bitcast_fusion.10), channel_id=1, source_target_pairs={{0,2},{1,3},{2,0},{3,1},{4,6},{5,7},{6,4},{7,5},{8,10},{9,11},{10,... | collective-permute-start | bytes 589832 | tf_op jit(solution)/shard_map/ppermute | solution.py:793
  304.3 53.2 %collective-permute-start.26 = (bf16[256,384]{1,0:T(8,128)(2,1)S(1)}, bf16[256,384]{1,0:T(8,128)(2,1)S(1)}, u32[]{:S(2)}, u32[]{:S(2)}) collective-permute-start(bf16[256,384]{1,0:T(8,128)(2,1)S(1)} %slice_bitcast_fusion.14), channel_id=1, source_target_pairs={{0,2},{1,3},{2,0},{3,1},{4,6},{5,7},{6,4},{7,5},{8,10},{9,11},{10,... | collective-permute-start | bytes 589832 | tf_op jit(solution)/shard_map/ppermute | solution.py:793
  324.3 32.4 %collective-permute-start.45 = (bf16[384,768]{1,0:T(8,128)(2,1)S(1)}, bf16[384,768]{1,0:T(8,128)(2,1)S(1)}, u32[]{:S(2)}, u32[]{:S(2)}) collective-permute-start(bf16[384,768]{1,0:T(8,128)(2,1)S(1)} %pad_maximum_fusion.5), channel_id=1, source_target_pairs={{0,2},{1,3},{2,0},{3,1},{4,6},{5,7},{6,4},{7,5},{8,10},{9,11},{10,... | collective-permute-start | bytes 1769480 | tf_op jit(solution)/shard_map/weight_gradients/ppermute | solution.py:793
  326.4 27.9 %collective-permute-start.42 = (bf16[384,768]{1,0:T(8,128)(2,1)S(1)}, bf16[384,768]{1,0:T(8,128)(2,1)S(1)}, u32[]{:S(2)}, u32[]{:S(2)}) collective-permute-start(bf16[384,768]{1,0:T(8,128)(2,1)S(1)} %pad_maximum_fusion.4), channel_id=1, source_target_pairs={{0,1},{1,0},{2,3},{3,2},{4,5},{5,4},{6,7},{7,6},{8,9},{9,8},{10,11... | collective-permute-start | bytes 1769480 | tf_op jit(solution)/shard_map/weight_gradients/ppermute | solution.py:793
  332.8 22.3 %collective-permute-start.38 = (bf16[2,304,384]{2,1,0:T(8,128)(2,1)S(1)}, bf16[2,304,384]{2,1,0:T(8,128)(2,1)S(1)}, u32[]{:S(2)}, u32[]{:S(2)}) collective-permute-start(bf16[2,304,384]{2,1,0:T(8,128)(2,1)S(1)} %pad_maximum_fusion.6), channel_id=1, source_target_pairs={{0,1},{1,0},{2,3},{3,2},{4,5},{5,4},{6,7},{7,6},{8,9},{9,8},{10,11... | collective-permute-start | bytes 1400840 | tf_op jit(solution)/shard_map/first_projection_gradient/ppermute | solution.py:793
  355.2 56.4 %collective-permute-start.43 = (bf16[768,768]{1,0:T(8,128)(2,1)S(1)}, bf16[768,768]{1,0:T(8,128)(2,1)}, u32[]{:S(2)}, u32[]{:S(2)}) collective-permute-start(bf16[768,768]{1,0:T(8,128)(2,1)S(1)} %pad_maximum_fusion.down_a), channel_id=1, source_target_pairs={{0,16},{16,0},{1,17},{17,1},{2,18},{18,2},{3,19},{19,3},{4,20},{20... | collective-permute-start | bytes 3538952 | tf_op jit(solution)/shard_map/weight_gradients/ppermute | solution.py:793
  356.7 47.2 %collective-permute-start.39 = (bf16[4,304,384]{2,1,0:T(8,128)(2,1)S(1)}, bf16[4,304,384]{2,1,0:T(8,128)(2,1)}, u32[]{:S(2)}, u32[]{:S(2)}) collective-permute-start(bf16[4,304,384]{2,1,0:T(8,128)(2,1)S(1)} %pad_maximum_fusion.2.own_ref), channel_id=1, source_target_pairs={{0,16},{16,0},{1,17},{17,1},{2,18},{18,2},{3,19},{19,3},{4,20},{20... | collective-permute-start | bytes 2801672 | tf_op jit(solution)/shard_map/first_projection_gradient/ppermute | solution.py:793
  357.6 54.0 %collective-permute-start.46 = (bf16[384,1536]{1,0:T(8,128)(2,1)S(1)}, bf16[384,1536]{1,0:T(8,128)(2,1)}, u32[]{:S(2)}, u32[]{:S(2)}) collective-permute-start(bf16[384,1536]{1,0:T(8,128)(2,1)S(1)} %pad_maximum_fusion.1.up_a), channel_id=1, source_target_pairs={{0,1},{1,0},{2,3},{3,2},{4,5},{5,4},{6,7},{7,6},{8,9},{9,8},{10,11... | collective-permute-start | bytes 3538952 | tf_op jit(solution)/shard_map/weight_gradients/ppermute | solution.py:793
  361.1 50.5 %collective-permute-start.49 = (bf16[192,768]{1,0:T(8,128)(2,1)S(1)}, bf16[192,768]{1,0:T(8,128)(2,1)S(1)}, u32[]{:S(2)}, u32[]{:S(2)}) collective-permute-start(bf16[192,768]{1,0:T(8,128)(2,1)S(1)} %pad_maximum_fusion.10.out_a), channel_id=1, source_target_pairs={{0,2},{1,3},{2,0},{3,1},{4,6},{5,7},{6,4},{7,5},{8,10},{9,11},{10,... | collective-permute-start | bytes 884744 | tf_op jit(solution)/shard_map/weight_gradients/ppermute | solution.py:793
  (56 other events, 575.9 us)

commit v5 on v4

--- a/solution.py
+++ b/solution.py
@@ -383,13 +383,12 @@
 
         @pl.when(t == 0)
         def _():
-            first = meta[3] == 0
             for y in range(2):
-                for z in range(2):
-                    at = 2 * jnp.bitwise_xor(meta[4], y) + jnp.bitwise_xor(meta[5], z)
+                for x in range(2):
+                    at = 2 * jnp.bitwise_xor(meta[4], y) + jnp.bitwise_xor(meta[3], x)
                     a, b = own_ref[at], other_ref[at]
-                    all_s[2 * z + y, :part, :] = jnp.where(first, a, b)
-                    all_s[2 * z + y, part:, :] = jnp.where(first, b, a)
+                    for z in range(2):
+                        all_s[2 * z + y, x * part : (x + 1) * part, :] = jnp.where(meta[5] == z, a, b)
             total = jnp.zeros((EXTRA, half), F32)
             for p in range(team):
                 total = total + all_s[p, 3 * wid :, :].astype(F32)
@@ -952,6 +951,14 @@
             for mask in masks[2:]:
                 every_piece = add(every_piece, flip(every_piece, "seq", mask))
             down, up, out = jnp.split(every_piece, [sizes[0], sizes[0] + sizes[1]])
+
+    with jax.named_scope("backward_attention"):
+        dq, dk, dv = zip(*parts)
+        back_a, back_b, dw_t = qkv_back(
+            meta, x_row, dq, dk, dv, w_t, g1, b1, gq, gk, vec2, heads, hd
+        )
+    back_a, back_b, dw_t, down, up, out = lax.optimization_barrier((back_a, back_b, dw_t, down, up, out))
+    with jax.named_scope("weight_gradients"):
         down = jnp.concatenate([down, flip(down, *z)], axis=1)
         up = jnp.concatenate([up, flip(up, *x)], axis=1)
         out = jnp.concatenate([out, flip(out, *y)], axis=1)
@@ -960,12 +967,6 @@
         out = jnp.concatenate([out, flip(out, *x)], axis=0)
         grad_down, grad_up, grad_out = assemble(
             meta, (down, flip(down, *x)), (up, flip(up, *y)), (out, flip(out, *z))
-        )
-
-    with jax.named_scope("backward_attention"):
-        dq, dk, dv = zip(*parts)
-        back_a, back_b, dw_t = qkv_back(
-            meta, x_row, dq, dk, dv, w_t, g1, b1, gq, gk, vec2, heads, hd
         )
 
     if direct:
@@ -1001,9 +1002,9 @@
         for mask in masks:
             if mask >= team:
                 piece = add(piece, flip(piece, "seq", mask))
-        piece = jnp.stack([piece, flip(piece, *z)])
+        piece = jnp.stack([piece, flip(piece, *x)])
         piece = jnp.concatenate([piece, flip(piece, *y)], axis=0)
-        grad_qkv, small = assemble_qkv(meta, piece, flip(piece, *x), heads, hd)
+        grad_qkv, small = assemble_qkv(meta, piece, flip(piece, *z), heads, hd)
         cuts = [small[0], small[1], small[2], small[3], small[4, : hd // 2], small[4, hd // 2 : hd]]
     shape = tokens.shape
     return (

time: 416 us -> 443 us (1.065); the launches traced: 422 us -> 441 us
  starting transfers between devices: 56.2 us -> 77.9 us
  Pallas kernels: 181 us -> 160 us
  waiting for transfers between devices: 154 us -> 174 us
    ppermute x50, waiting for transfers between devices: 131 us -> 152 us  [flip(): return lax.ppermute(value, axis, [(i, i ^ mask) for i in range(size)])]
    pallas_call x3, Pallas kernels: 50.5 us -> 37.3 us  [attend_back(): pl.pallas_call(functools.partial(attend_back_body, heads, hd), grid=(bloc...]
    ppermute x50, starting transfers between devices: 48.5 us -> 61.1 us  [flip(): return lax.ppermute(value, axis, [(i, i ^ mask) for i in range(size)])]
    all_to_all x2, starting transfers between devices: 7.64 us -> 16.8 us  [exchange(): return lax.all_to_all(value, 'seq', 0, 0, tiled=True)]
    pallas_call x1, Pallas kernels: 28.6 us -> 20.5 us  [attend(): pl.pallas_call(functools.partial(attend_body, heads, hd), grid=(blocks,),...]
  transfers between devices with their start and end apart: 52 -> 52, of which waited for: 21 -> 23; matrix products, arithmetic and copies ran while one was open for 5% -> 4% of each run, Pallas kernels for 29% -> 28%
where the time goes in v5:
time: 443 us; the launch traced here: 441 us
  waiting for transfers between devices  174 us (39%)
  Pallas kernels  160 us (36%)
  starting transfers between devices  77.9 us (18%)
  local copies, waits for them, and re-layouts  17.2 us (4%)
  other arithmetic  10.7 us (2%)
    ppermute x50, waiting for transfers between devices, flip(): return lax.ppermute(value, axis, [(i, i ^ mask) for i in range(size)])  152 us
    ppermute x50, starting transfers between devices, flip(): return lax.ppermute(value, axis, [(i, i ^ mask) for i in range(size)])  61.1 us
    pallas_call x3, Pallas kernels, attend_back(): pl.pallas_call(functools.partial(attend_back_body, heads, hd), grid=(bloc...  37.3 us
    pallas_call x1, Pallas kernels, ffn(): pl.pallas_call(body, grid_spec=pltpu.PrefetchScalarGridSpec(num_scalar_pr...  25.7 us
    all_to_all x2, waiting for transfers between devices, exchange(): return lax.all_to_all(value, 'seq', 0, 0, tiled=True)  22.5 us
    pallas_call x1, Pallas kernels, attend(): pl.pallas_call(functools.partial(attend_body, heads, hd), grid=(blocks,),...  20.5 us
    pallas_call x1, Pallas kernels, qkv_back(): pl.pallas_call(functools.partial(qkv_back_body, heads, hd), grid_spec=plt...  17.8 us
    all_to_all x2, starting transfers between devices, exchange(): return lax.all_to_all(value, 'seq', 0, 0, tiled=True)  16.8 us
  transfers between devices with their start and end apart: 52, of which 23 were waited for; matrix products, arithmetic and copies ran while one was open for 4% of the time, Pallas kernels for 28%

profile of v5, /device:TPU:0, one launch (start us, length us, event | category | flops | bytes accessed | tf_op | source)
XLA Modules:
  0.0 441.4 jit_solution(9928609624519543490)
XLA Ops:
  13.4 10.4 %collective-permute-done.4.refs_4_ = bf16[256,768]{1,0:T(8,128)(2,1)} collective-permute-done((bf16[256,768]{1,0:T(8,128)(2,1)S(1)}, bf16[256,768]{1,0:T(8,128)(2,1)}, u32[]{:S(2)}, u32[]{:S(2)}) %collective-permute-start.4) | collective-permute-done | bytes 393248 | tf_op jit(solution)/shard_map/ppermute | solution.py:792
  45.6 12.2 %qkv_forward.1 = (bf16[3,128,2048]{2,1,0:T(8,128)(2,1)}, bf16[3,2048,128]{2,1,0:T(8,128)(2,1)}, bf16[3,64,2048]{2,1,0:T(8,128)(2,1)}, bf16[3,2048,64]{2,1,0:T(8,...) custom-call(s32[6]{0:T(128)} %stack.50.meta, s32[2,8]{1,0:T(2,128)} %bitcast.145, ...), custom_call_target="tpu_custom_call" | custom-call | flops 4200000000 | bytes 1024 | tf_op jit(solution)/shard_map/forward_attention/qkv_forward/pallas_call | solution.py:104
  57.8 20.5 %attention_forward.1 = (bf16[8,192,256]{2,1,0:T(8,128)(2,1)}, f32[3,64,2048]{2,1,0:T(8,128)}, f32[3,1,2048]{2,1,0:T(1,128)}) custom-call(s32[6]{0:T(128)} %stack.50.meta, s32[2,8]{1,0:T(2,128)} %bitcast.146, bf16[3,128,2048]{2,1,0:T(8,128)(2,1)} %get-tuple-element.77.qt_ref, bf16[3,2048,128]{2,1,0:T(8,128)(2,1)} %get-tuple-element.78.ka_ref, ...), custom_call_target="tpu_custom_call" | custom-call | flops 8750000128 | bytes 1024 | tf_op jit(solution)/shard_map/forward_attention/attention_forward/pallas_call | solution.py:170
  78.3 13.0 %all-to-all-start = ((bf16[8,192,256]{2,1,0:T(8,128)(2,1)}), bf16[8,192,256]{2,1,0:T(8,128)(2,1)S(1)}, u32[]{:S(2)}, u32[]{:S(2)}) async-start(bf16[8,192,256]{2,1,0:T(8,128)(2,1)} %get-tuple-element.80), calls=%async_computation | async-start | bytes 1572864 | tf_op jit(solution)/shard_map/all_to_all | solution.py:882
  93.4 17.7 %all-to-all-done = bf16[8,192,256]{2,1,0:T(8,128)(2,1)S(1)} async-done(((bf16[8,192,256]{2,1,0:T(8,128)(2,1)}), bf16[8,192,256]{2,1,0:T(8,128)(2,1)S(1)}, u32[]{:S(2)}, u32[]{:S(2)}) %all-to-all-start) | async-done | bytes 786464 | tf_op jit(solution)/shard_map/all_to_all | solution.py:882
  112.0 25.7 %ffn_both_ways.1 = (bf16[512,768]{1,0:T(8,128)(2,1)}, f32[512,768]{1,0:T(8,128)}, bf16[512,768]{1,0:T(8,128)(2,1)}, bf16[512,768]{1,0:T(8,128)(2,1)}, bf16[512,3...) custom-call(s32[6]{0:T(128)} %stack.50.meta, ...), custom_call_target="tpu_custom_call" | custom-call | flops 8750000128 | bytes 1024 | tf_op jit(solution)/shard_map/feed_forward/ffn_both_ways/pallas_call | solution.py:510
  137.7 7.2 %up_out_gradient.2 = bf16[384,3840]{1,0:T(8,128)(2,1)} custom-call(s32[6]{0:T(128)} %stack.50.meta, bf16[2,768,256]{2,1,0:T(8,128)(2,1)} %bitcast.129, bf16[512,768]{1,0:T(8,128)(2,1)} %get-tuple-element.85.gb_ref, bf16[512,768]{1,0:T(8,128)(2,1)} %get-tuple-element.86.h2_ref, bf16[512,3072]{1,0:T(8,128)(2,1)} %get-tuple-element.87.dup_ref), custom_call_target="tpu_custom_call" | custom-call | flops 2449999872 | bytes 1024 | tf_op jit(solution)/shard_map/weight_gradients/up_out_gradient/pallas_call | solution.py:635
  155.5 6.4 %down_gradient.3 = (bf16[768,768]{1,0:T(8,128)(2,1)}, bf16[768,768]{1,0:T(8,128)(2,1)}) custom-call(s32[6]{0:T(128)} %stack.50.meta, bf16[512,3072]{1,0:T(8,128)(2,1)} %get-tuple-element.92.act_ref, bf16[512,768]{1,0:T(8,128)(2,1)} %bitcast.144, bf16[1536,768]{1,0:T(8,128)(2,1)} %collective-permute-done.15.rest_0_), custom_call_target="tpu_custom_call" | custom-call | flops 2100000000 | bytes 1024 | tf_op jit(solution)/shard_map/weight_gradients/down_gradient/pallas_call | solution.py:695
  161.9 8.4 %up_out_gradient.3 = (bf16[384,1536]{1,0:T(8,128)(2,1)}, bf16[384,1536]{1,0:T(8,128)(2,1)}, bf16[192,768]{1,0:T(8,128)(2,1)}, bf16[192,768]{1,0:T(8,128)(2,1)}) custom-call(s32[6]{0:T(128)} %stack.50.meta, bf16[2,768,256]{2,1,0:T(8,128)(2,1)} %bitcast.130, bf16[512,768]{1,0:T(8,128)(2,1)} %get-tuple-element.85.gb_ref, ...), custom_call_target="tpu_custom_call" | custom-call | flops 2449999872 | bytes 1024 | tf_op jit(solution)/shard_map/weight_gradients/up_out_gradient/pallas_call | solution.py:635
  180.3 7.7 %collective-permute-done.18 = bf16[192,768]{1,0:T(8,128)(2,1)S(1)} collective-permute-done((bf16[192,768]{1,0:T(8,128)(2,1)}, bf16[192,768]{1,0:T(8,128)(2,1)S(1)}, u32[]{:S(2)}, u32[]{:S(2)}) %collective-permute-start.18) | collective-permute-done | bytes 294944 | tf_op jit(solution)/shard_map/ppermute | solution.py:792
  188.0 16.0 %collective-permute-done.16 = bf16[768,768]{1,0:T(8,128)(2,1)S(1)} collective-permute-done((bf16[768,768]{1,0:T(8,128)(2,1)}, bf16[768,768]{1,0:T(8,128)(2,1)S(1)}, u32[]{:S(2)}, u32[]{:S(2)}) %collective-permute-start.16) | collective-permute-done | bytes 1179680 | tf_op jit(solution)/shard_map/ppermute | solution.py:792
  211.2 12.4 %attention_backward.3 = (f32[1,64,2048]{2,1,0:T(8,128)}, f32[1,64,2048]{2,1,0:T(8,128)}, f32[1,64,2048]{2,1,0:T(8,128)}) custom-call(s32[6]{0:T(128)} %stack.50.meta, s32[2,8]{1,0:T(2,128)} %bitcast.147, bf16[3,128,2048]{2,1,0:T(8,128)(2,1)} %get-tuple-element.77.qt_ref, bf16[3,2048,128]{2,1,0:T(8,128)(2,1)} %get-tuple-element.78.ka_ref, ...), custom_call_target="tpu_custom_call" | custom-call | flops 3849999872 | bytes 1024 | tf_op jit(solution)/shard_map/attention_backward/pallas_call | solution.py:239
  228.9 12.4 %attention_backward.4 = (f32[1,64,2048]{2,1,0:T(8,128)}, f32[1,64,2048]{2,1,0:T(8,128)}, f32[1,64,2048]{2,1,0:T(8,128)}) custom-call(s32[6]{0:T(128)} %stack.50.meta, s32[2,8]{1,0:T(2,128)} %bitcast.148, bf16[3,128,2048]{2,1,0:T(8,128)(2,1)} %get-tuple-element.77.qt_ref, bf16[3,2048,128]{2,1,0:T(8,128)(2,1)} %get-tuple-element.78.ka_ref, ...), custom_call_target="tpu_custom_call" | custom-call | flops 3849999872 | bytes 1024 | tf_op jit(solution)/shard_map/attention_backward/pallas_call | solution.py:239
  241.6 12.0 %collective-permute-start.25 = (bf16[864,384]{1,0:T(8,128)(2,1)S(1)}, bf16[864,384]{1,0:T(8,128)(2,1)S(1)}, u32[]{:S(2)}, u32[]{:S(2)}) collective-permute-start(bf16[864,384]{1,0:T(8,128)(2,1)S(1)} %pad_maximum_fusion.2), channel_id=1, source_target_pairs={{0,4},{1,5},{2,6},{3,7},{4,0},{5,1},{6,2},{7,3},{8,12},{9,13},{10,... | collective-permute-start | bytes 1990664 | tf_op jit(solution)/shard_map/weight_gradients/ppermute | solution.py:792
  253.6 12.4 %attention_backward.5 = (f32[1,64,2048]{2,1,0:T(8,128)}, f32[1,64,2048]{2,1,0:T(8,128)}, f32[1,64,2048]{2,1,0:T(8,128)}) custom-call(s32[6]{0:T(128)} %stack.50.meta, s32[2,8]{1,0:T(2,128)} %bitcast.149, bf16[3,128,2048]{2,1,0:T(8,128)(2,1)} %get-tuple-element.77.qt_ref, bf16[3,2048,128]{2,1,0:T(8,128)(2,1)} %get-tuple-element.78.ka_ref, ...), custom_call_target="tpu_custom_call" | custom-call | flops 3849999872 | bytes 1024 | tf_op jit(solution)/shard_map/attention_backward/pallas_call | solution.py:239
  266.1 17.8 %qkv_backward.1 = (bf16[8,256,384]{2,1,0:T(8,128)(2,1)}, bf16[8,256,384]{2,1,0:T(8,128)(2,1)}, bf16[608,768]{1,0:T(8,128)(2,1)}) custom-call(s32[6]{0:T(128)} %stack.50.meta, bf16[2048,768]{1,0:T(8,128)(2,1)} %get-tuple-element.109.x_ref, f32[1,64,2048]{2,1,0:T(8,128)} %get-tuple-element.114.refs_0_, f32[1,64,2048]{2,1,0:T(8,128)} %get-tuple-element.115.refs_1_, ...), custom_call_target="tpu_custom_call" | custom-call | flops 5950000128 | bytes 1024 | tf_op jit(solution)/shard_map/backward_attention/qkv_backward/pallas_call | solution.py:339
  291.1 8.1 %collective-permute-done.48 = bf16[96,768]{1,0:T(8,128)(2,1)S(1)} collective-permute-done((bf16[96,768]{1,0:T(8,128)(2,1)S(1)}, bf16[96,768]{1,0:T(8,128)(2,1)S(1)}, u32[]{:S(2)}, u32[]{:S(2)}) %collective-permute-start.48) | collective-permute-done | bytes 147488 | tf_op jit(solution)/shard_map/weight_gradients/ppermute | solution.py:792
  303.8 5.9 %collective-permute-done.30 = bf16[2,256,384]{2,1,0:T(8,128)(2,1)S(1)} collective-permute-done((bf16[2,256,384]{2,1,0:T(8,128)(2,1)S(1)}, bf16[2,256,384]{2,1,0:T(8,128)(2,1)S(1)}, u32[]{:S(2)}, u32[]{:S(2)}) %collective-permute-start.30) | collective-permute-done | bytes 393248 | tf_op jit(solution)/shard_map/ppermute | solution.py:792
  313.4 7.5 %collective-permute-done.32 = bf16[2,256,384]{2,1,0:T(8,128)(2,1)S(1)} collective-permute-done((bf16[2,256,384]{2,1,0:T(8,128)(2,1)S(1)}, bf16[2,256,384]{2,1,0:T(8,128)(2,1)S(1)}, u32[]{:S(2)}, u32[]{:S(2)}) %collective-permute-start.32) | collective-permute-done | bytes 393248 | tf_op jit(solution)/shard_map/ppermute | solution.py:792
  330.5 10.3 %collective-permute-done.37 = bf16[304,384]{1,0:T(8,128)(2,1)S(1)} collective-permute-done((bf16[304,384]{1,0:T(8,128)(2,1)S(1)}, bf16[304,384]{1,0:T(8,128)(2,1)S(1)}, u32[]{:S(2)}, u32[]{:S(2)}) %collective-permute-start.37) | collective-permute-done | bytes 233504 | tf_op jit(solution)/shard_map/first_projection_gradient/ppermute | solution.py:792
  356.4 31.7 %collective-permute-done.39 = bf16[2,304,384]{2,1,0:T(8,128)(2,1)S(1)} collective-permute-done((bf16[2,304,384]{2,1,0:T(8,128)(2,1)S(1)}, bf16[2,304,384]{2,1,0:T(8,128)(2,1)S(1)}, u32[]{:S(2)}, u32[]{:S(2)}) %collective-permute-start.39) | collective-permute-done | bytes 466976 | tf_op jit(solution)/shard_map/first_projection_gradient/ppermute | solution.py:792
  393.3 12.2 %collective-permute-done.34 = bf16[256,768]{1,0:T(8,128)(2,1)S(1)} collective-permute-done((bf16[256,768]{1,0:T(8,128)(2,1)S(1)}, bf16[256,768]{1,0:T(8,128)(2,1)S(1)}, u32[]{:S(2)}, u32[]{:S(2)}) %collective-permute-start.34) | collective-permute-done | bytes 393248 | tf_op jit(solution)/shard_map/ppermute | solution.py:792
  411.0 12.6 %collective-permute-done.49.out_b = bf16[192,768]{1,0:T(8,128)(2,1)S(1)} collective-permute-done((bf16[192,768]{1,0:T(8,128)(2,1)S(1)}, bf16[192,768]{1,0:T(8,128)(2,1)S(1)}, u32[]{:S(2)}, u32[]{:S(2)}) %collective-permute-start.49) | collective-permute-done | bytes 294944 | tf_op jit(solution)/shard_map/weight_gradients/ppermute | solution.py:792
  424.3 9.4 %weight_gradients.1 = (f32[1536,768]{1,0:T(8,128)}, f32[384,3072]{1,0:T(8,128)}, f32[384,768]{1,0:T(8,128)}) custom-call(s32[6]{0:T(128)} %stack.50.meta, bf16[768,768]{1,0:T(8,128)(2,1)} %copy-done.3, bf16[768,768]{1,0:T(8,128)(2,1)} %collective-permute-done.43.down_b, bf16[384,1536]{1,0:T(8,128)(2,1)} %copy-done.18, ...), custom_call_target="tpu_custom_call" | custom-call | flops 2449999872 | bytes 1024 | tf_op jit(solution)/shard_map/weight_gradients/weight_gradients/pallas_call | solution.py:744
  (229 shorter events, 130.0 us)
Async XLA Ops:
  1.9 21.9 %collective-permute-start.4 = (bf16[256,768]{1,0:T(8,128)(2,1)S(1)}, bf16[256,768]{1,0:T(8,128)(2,1)}, u32[]{:S(2)}, u32[]{:S(2)}) collective-permute-start(bf16[256,768]{1,0:T(8,128)(2,1)S(1)} %get-tuple-element.178), channel_id=1, source_target_pairs={{0,4},{1,5},{2,6},{3,7},{4,0},{5,1},{6,2},{7,3},{8,12},{9,13},{10,... | collective-permute-start | bytes 1179656 | tf_op jit(solution)/shard_map/ppermute | solution.py:792
  6.1 19.8 %collective-permute-start.1 = (bf16[256,768]{1,0:T(8,128)(2,1)S(1)}, bf16[256,768]{1,0:T(8,128)(2,1)S(1)}, u32[]{:S(2)}, u32[]{:S(2)}) collective-permute-start(bf16[256,768]{1,0:T(8,128)(2,1)S(1)} %get-tuple-element.179.refs_0_), channel_id=1, source_target_pairs={{0,2},{1,3},{2,0},{3,1},{4,6},{5,7},{6,4},{7,5},{8,10},{9,11},{10,... | collective-permute-start | bytes 1179656 | tf_op jit(solution)/shard_map/ppermute | solution.py:792
  7.6 18.8 %collective-permute-start = (bf16[256,768]{1,0:T(8,128)(2,1)S(1)}, bf16[256,768]{1,0:T(8,128)(2,1)}, u32[]{:S(2)}, u32[]{:S(2)}) collective-permute-start(bf16[256,768]{1,0:T(8,128)(2,1)S(1)} %get-tuple-element.179.refs_0_), channel_id=1, source_target_pairs={{0,1},{1,0},{2,3},{3,2},{4,5},{5,4},{6,7},{7,6},{8,9},{9,8},{10,11... | collective-permute-start | bytes 1179656 | tf_op jit(solution)/shard_map/ppermute | solution.py:792
  12.2 25.8 %collective-permute-start.9 = (bf16[384,576]{0,1:T(8,128)(2,1)S(1)}, bf16[384,576]{0,1:T(8,128)(2,1)S(1)}, u32[]{:S(2)}, u32[]{:S(2)}) collective-permute-start(bf16[384,576]{0,1:T(8,128)(2,1)S(1)} %bitcast.120), channel_id=1, source_target_pairs={{0,8},{8,0},{1,9},{9,1},{2,10},{10,2},{3,11},{11,3},{4,12},{12,4},... | collective-permute-start | bytes 1327112 | tf_op jit(solution)/shard_map/ppermute | solution.py:792
  36.0 75.1 %collective-permute-start.12 = (bf16[384,3072]{1,0:T(8,128)(2,1)}, bf16[384,3072]{1,0:T(8,128)(2,1)}, u32[]{:S(2)}, u32[]{:S(2)}) collective-permute-start(bf16[384,3072]{1,0:T(8,128)(2,1)} %refs_8_.1), channel_id=1, source_target_pairs={{0,8},{8,0},{1,9},{9,1},{2,10},{10,2},{3,11},{11,3},{4,12},{12,4},... | collective-permute-start | bytes 7077896 | tf_op jit(solution)/shard_map/ppermute | solution.py:792
  40.6 70.5 %collective-permute-start.13 = (bf16[1536,768]{1,0:T(8,128)(2,1)}, bf16[1536,768]{1,0:T(8,128)(2,1)}, u32[]{:S(2)}, u32[]{:S(2)}) collective-permute-start(bf16[1536,768]{1,0:T(8,128)(2,1)} %refs_10_.1), channel_id=1, source_target_pairs={{0,8},{8,0},{1,9},{9,1},{2,10},{10,2},{3,11},{11,3},{4,12},{12,4},... | collective-permute-start | bytes 7077896 | tf_op jit(solution)/shard_map/ppermute | solution.py:792
  78.3 32.8 %all-to-all-start = ((bf16[8,192,256]{2,1,0:T(8,128)(2,1)}), bf16[8,192,256]{2,1,0:T(8,128)(2,1)S(1)}, u32[]{:S(2)}, u32[]{:S(2)}) async-start(bf16[8,192,256]{2,1,0:T(8,128)(2,1)} %get-tuple-element.80), calls=%async_computation | async-start | bytes 1572864 | tf_op jit(solution)/shard_map/all_to_all | solution.py:882
  151.0 24.1 %all-to-all-start.1 = ((bf16[8,192,256]{2,1,0:T(8,128)(2,1)}), bf16[8,192,256]{2,1,0:T(8,128)(2,1)S(1)}, u32[]{:S(2)}, u32[]{:S(2)}) async-start(bf16[8,192,256]{2,1,0:T(8,128)(2,1)} %bitcast.17), calls=%async_computation.1 | async-start | bytes 1572864 | tf_op jit(solution)/shard_map/all_to_all | solution.py:882
  176.0 28.0 %collective-permute-start.16 = (bf16[768,768]{1,0:T(8,128)(2,1)}, bf16[768,768]{1,0:T(8,128)(2,1)S(1)}, u32[]{:S(2)}, u32[]{:S(2)}) collective-permute-start(bf16[768,768]{1,0:T(8,128)(2,1)} %get-tuple-element.97), channel_id=1, source_target_pairs={{0,16},{16,0},{1,17},{17,1},{2,18},{18,2},{3,19},{19,3},{4,20},{20... | collective-permute-start | bytes 3538952 | tf_op jit(solution)/shard_map/ppermute | solution.py:792
  178.9 26.6 %collective-permute-start.17 = (bf16[384,1536]{1,0:T(8,128)(2,1)}, bf16[384,1536]{1,0:T(8,128)(2,1)S(1)}, u32[]{:S(2)}, u32[]{:S(2)}) collective-permute-start(bf16[384,1536]{1,0:T(8,128)(2,1)} %get-tuple-element.98), channel_id=1, source_target_pairs={{0,1},{1,0},{2,3},{3,2},{4,5},{5,4},{6,7},{7,6},{8,9},{9,8},{10,11... | collective-permute-start | bytes 3538952 | tf_op jit(solution)/shard_map/ppermute | solution.py:792
  241.6 42.3 %collective-permute-start.25 = (bf16[864,384]{1,0:T(8,128)(2,1)S(1)}, bf16[864,384]{1,0:T(8,128)(2,1)S(1)}, u32[]{:S(2)}, u32[]{:S(2)}) collective-permute-start(bf16[864,384]{1,0:T(8,128)(2,1)S(1)} %pad_maximum_fusion.2), channel_id=1, source_target_pairs={{0,4},{1,5},{2,6},{3,7},{4,0},{5,1},{6,2},{7,3},{8,12},{9,13},{10,... | collective-permute-start | bytes 1990664 | tf_op jit(solution)/shard_map/weight_gradients/ppermute | solution.py:792
  284.3 17.2 %collective-permute-start.41 = (bf16[384,384]{1,0:T(8,128)(2,1)S(1)}, bf16[384,384]{1,0:T(8,128)(2,1)S(1)}, u32[]{:S(2)}, u32[]{:S(2)}) collective-permute-start(bf16[384,384]{1,0:T(8,128)(2,1)S(1)} %get-tuple-element.136), channel_id=1, source_target_pairs={{0,2},{1,3},{2,0},{3,1},{4,6},{5,7},{6,4},{7,5},{8,10},{9,11},{10,... | collective-permute-start | bytes 884744 | tf_op jit(solution)/shard_map/weight_gradients/ppermute | solution.py:792
  286.9 35.2 %collective-permute-start.35 = (bf16[608,384]{1,0:T(8,128)(2,1)S(1)}, bf16[608,384]{1,0:T(8,128)(2,1)S(1)}, u32[]{:S(2)}, u32[]{:S(2)}) collective-permute-start(bf16[608,384]{1,0:T(8,128)(2,1)S(1)} %constant_dynamic-slice_fusion.1), channel_id=1, source_target_pairs={{0,8},{8,0},{1,9},{9,1},{2,10},{10,2},{3,11},{11,3},{4,12},{12,4},... | collective-permute-start | bytes 1400840 | tf_op jit(solution)/shard_map/first_projection_gradient/ppermute | solution.py:792
  301.5 19.4 %collective-permute-start.32 = (bf16[2,256,384]{2,1,0:T(8,128)(2,1)S(1)}, bf16[2,256,384]{2,1,0:T(8,128)(2,1)S(1)}, u32[]{:S(2)}, u32[]{:S(2)}) collective-permute-start(bf16[2,256,384]{2,1,0:T(8,128)(2,1)S(1)} %get-tuple-element.177), channel_id=1, source_target_pairs={{0,2},{1,3},{2,0},{3,1},{4,6},{5,7},{6,4},{7,5},{8,10},{9,11},{10,... | collective-permute-start | bytes 1179656 | tf_op jit(solution)/shard_map/ppermute | solution.py:792
  302.8 44.3 %collective-permute-start.45 = (bf16[384,768]{1,0:T(8,128)(2,1)S(1)}, bf16[384,768]{1,0:T(8,128)(2,1)S(1)}, u32[]{:S(2)}, u32[]{:S(2)}) collective-permute-start(bf16[384,768]{1,0:T(8,128)(2,1)S(1)} %pad_maximum_fusion.3), channel_id=1, source_target_pairs={{0,2},{1,3},{2,0},{3,1},{4,6},{5,7},{6,4},{7,5},{8,10},{9,11},{10,... | collective-permute-start | bytes 1769480 | tf_op jit(solution)/shard_map/weight_gradients/ppermute | solution.py:792
  309.7 43.8 %collective-permute-start.42 = (bf16[384,768]{1,0:T(8,128)(2,1)S(1)}, bf16[384,768]{1,0:T(8,128)(2,1)S(1)}, u32[]{:S(2)}, u32[]{:S(2)}) collective-permute-start(bf16[384,768]{1,0:T(8,128)(2,1)S(1)} %constant_dynamic-update-slice_fusion), channel_id=1, source_target_pairs={{0,1},{1,0},{2,3},{3,2},{4,5},{5,4},{6,7},{7,6},{8,9},{9,8},{10,11... | collective-permute-start | bytes 1769480 | tf_op jit(solution)/shard_map/weight_gradients/ppermute | solution.py:792
  312.5 78.5 %collective-permute-start.27 = (bf16[256,384]{1,0:T(8,128)(2,1)S(1)}, bf16[256,384]{1,0:T(8,128)(2,1)S(1)}, u32[]{:S(2)}, u32[]{:S(2)}) collective-permute-start(bf16[256,384]{1,0:T(8,128)(2,1)S(1)} %slice_bitcast_fusion.14), channel_id=1, source_target_pairs={{0,2},{1,3},{2,0},{3,1},{4,6},{5,7},{6,4},{7,5},{8,10},{9,11},{10,... | collective-permute-start | bytes 589832 | tf_op jit(solution)/shard_map/ppermute | solution.py:792
  321.2 70.0 %collective-permute-start.29 = (bf16[256,384]{1,0:T(8,128)(2,1)S(1)}, bf16[256,384]{1,0:T(8,128)(2,1)S(1)}, u32[]{:S(2)}, u32[]{:S(2)}) collective-permute-start(bf16[256,384]{1,0:T(8,128)(2,1)S(1)} %slice_bitcast_fusion.12), channel_id=1, source_target_pairs={{0,1},{1,0},{2,3},{3,2},{4,5},{5,4},{6,7},{7,6},{8,9},{9,8},{10,11... | collective-permute-start | bytes 589832 | tf_op jit(solution)/shard_map/ppermute | solution.py:792
  352.5 71.1 %collective-permute-start.46 = (bf16[384,1536]{1,0:T(8,128)(2,1)S(1)}, bf16[384,1536]{1,0:T(8,128)(2,1)}, u32[]{:S(2)}, u32[]{:S(2)}) collective-permute-start(bf16[384,1536]{1,0:T(8,128)(2,1)S(1)} %constant_dynamic-update-slice_fusion.2.up_a), channel_id=1, source_target_pairs={{0,1},{1,0},{2,3},{3,2},{4,5},{5,4},{6,7},{7,6},{8,9},{9,8},{10,11... | collective-permute-start | bytes 3538952 | tf_op jit(solution)/shard_map/weight_gradients/ppermute | solution.py:792
  353.6 34.5 %collective-permute-start.39 = (bf16[2,304,384]{2,1,0:T(8,128)(2,1)S(1)}, bf16[2,304,384]{2,1,0:T(8,128)(2,1)S(1)}, u32[]{:S(2)}, u32[]{:S(2)}) collective-permute-start(bf16[2,304,384]{2,1,0:T(8,128)(2,1)S(1)} %pad_maximum_fusion.4), channel_id=1, source_target_pairs={{0,1},{1,0},{2,3},{3,2},{4,5},{5,4},{6,7},{7,6},{8,9},{9,8},{10,11... | collective-permute-start | bytes 1400840 | tf_op jit(solution)/shard_map/first_projection_gradient/ppermute | solution.py:792
  354.7 68.9 %collective-permute-start.43 = (bf16[768,768]{1,0:T(8,128)(2,1)S(1)}, bf16[768,768]{1,0:T(8,128)(2,1)}, u32[]{:S(2)}, u32[]{:S(2)}) collective-permute-start(bf16[768,768]{1,0:T(8,128)(2,1)S(1)} %pad_maximum_fusion.down_a), channel_id=1, source_target_pairs={{0,16},{16,0},{1,17},{17,1},{2,18},{18,2},{3,19},{19,3},{4,20},{20... | collective-permute-start | bytes 3538952 | tf_op jit(solution)/shard_map/weight_gradients/ppermute | solution.py:792
  388.1 17.4 %collective-permute-start.34 = (bf16[256,768]{1,0:T(8,128)(2,1)S(1)}, bf16[256,768]{1,0:T(8,128)(2,1)S(1)}, u32[]{:S(2)}, u32[]{:S(2)}) collective-permute-start(bf16[256,768]{1,0:T(8,128)(2,1)S(1)} %pad_maximum_fusion.7), channel_id=1, source_target_pairs={{0,4},{1,5},{2,6},{3,7},{4,0},{5,1},{6,2},{7,3},{8,12},{9,13},{10,... | collective-permute-start | bytes 1179656 | tf_op jit(solution)/shard_map/ppermute | solution.py:792
  391.0 42.7 %collective-permute-start.40 = (bf16[4,304,384]{2,1,0:T(8,128)(2,1)S(1)}, bf16[4,304,384]{2,1,0:T(8,128)(2,1)}, u32[]{:S(2)}, u32[]{:S(2)}) collective-permute-start(bf16[4,304,384]{2,1,0:T(8,128)(2,1)S(1)} %pad_maximum_fusion.1.own_ref), channel_id=1, source_target_pairs={{0,2},{1,3},{2,0},{3,1},{4,6},{5,7},{6,4},{7,5},{8,10},{9,11},{10,... | collective-permute-start | bytes 2801672 | tf_op jit(solution)/shard_map/first_projection_gradient/ppermute | solution.py:792
  391.2 32.4 %collective-permute-start.49 = (bf16[192,768]{1,0:T(8,128)(2,1)S(1)}, bf16[192,768]{1,0:T(8,128)(2,1)S(1)}, u32[]{:S(2)}, u32[]{:S(2)}) collective-permute-start(bf16[192,768]{1,0:T(8,128)(2,1)S(1)} %pad_maximum_fusion.8.out_a), channel_id=1, source_target_pairs={{0,2},{1,3},{2,0},{3,1},{4,6},{5,7},{6,4},{7,5},{8,10},{9,11},{10,... | collective-permute-start | bytes 884744 | tf_op jit(solution)/shard_map/weight_gradients/ppermute | solution.py:792
  (57 other events, 611.7 us)

commit v6 on v4

--- a/solution.py
+++ b/solution.py
@@ -373,23 +373,24 @@
     )(meta, x, *dq, *dk, *dv, w_t, gain, bias, gq, gk, vec2)
 
 
-def assemble_qkv(meta, own, other, heads, hd):
-    team, part, half = own.shape
+def assemble_qkv(meta, pieces, heads, hd):
+    _, part, half = pieces[0].shape
+    team = 4
     wid = heads * hd
     turned = team * wid
 
-    def body(meta, own_ref, other_ref, out_ref, vec_ref, all_s):
+    def body(meta, p00, p01, p10, p11, out_ref, vec_ref, all_s):
         t = pl.program_id(0)
 
         @pl.when(t == 0)
         def _():
-            first = meta[3] == 0
             for y in range(2):
+                at = jnp.bitwise_xor(meta[4], y)
                 for z in range(2):
-                    at = 2 * jnp.bitwise_xor(meta[4], y) + jnp.bitwise_xor(meta[5], z)
-                    a, b = own_ref[at], other_ref[at]
-                    all_s[2 * z + y, :part, :] = jnp.where(first, a, b)
-                    all_s[2 * z + y, part:, :] = jnp.where(first, b, a)
+                    own_z = meta[5] == z
+                    near, away = jnp.where(own_z, p00[at], p01[at]), jnp.where(own_z, p10[at], p11[at])
+                    for x in range(2):
+                        all_s[2 * z + y, x * part : (x + 1) * part, :] = jnp.where(meta[3] == x, near, away)
             total = jnp.zeros((EXTRA, half), F32)
             for p in range(team):
                 total = total + all_s[p, 3 * wid :, :].astype(F32)
@@ -405,7 +406,7 @@
         grid_spec=pltpu.PrefetchScalarGridSpec(
             num_scalar_prefetch=1,
             grid=(3,),
-            in_specs=[whole(team, part, half), whole(team, part, half)],
+            in_specs=[whole(2, part, half)] * 4,
             out_specs=(pl.BlockSpec((half, turned), lambda i, m: (0, i)), whole(EXTRA, half)),
             scratch_shapes=[pltpu.VMEM((team, 2 * part, half), BF16)],
         ),
@@ -413,7 +414,7 @@
         compiler_params=params(),
         cost_estimate=cost(5),
         name="first_projection_gradient",
-    )(meta, own, other)
+    )(meta, *pieces)
 
 
 def gelu_pair(u):
@@ -717,7 +718,7 @@
     hidden = ups[0].shape[1] * 2
     cut = width // 2
 
-    def body(meta, down_a, down_b, up_a, up_b, out_a, out_b, down_ref, up_ref, out_ref):
+    def body(meta, down_aa, down_ab, down_ba, down_bb, up_a, up_b, out_a, out_b, down_ref, up_ref, out_ref):
         i = pl.program_id(0)
 
         def place(ref, value, swapped):
@@ -725,8 +726,9 @@
             ref[:, :cut] = jnp.where(swapped == 0, lo, hi)
             ref[:, cut:] = jnp.where(swapped == 0, hi, lo)
 
-        down_own = i // 2 == meta[3]
-        place(down_ref, jnp.where(down_own, down_a[...], down_b[...]), meta[5])
+        down_x, down_y = i // 2 == meta[3], lax.rem(i, 2) == meta[4]
+        own_x = jnp.where(down_y, down_aa[...], down_ab[...])
+        place(down_ref, jnp.where(down_x, own_x, jnp.where(down_y, down_ba[...], down_bb[...])), meta[5])
         up_own = i // 2 == meta[4]
         place(up_ref, jnp.where(up_own, up_a[...], up_b[...]), meta[3])
 
@@ -740,14 +742,14 @@
                     place(out_ref.at[pl.ds((2 * z + x) * quarter, quarter)], value, meta[4])
 
     whole = lambda *shape: pl.BlockSpec(shape, lambda i, m: (0,) * len(shape))
-    down = pl.BlockSpec((half, width), lambda i, m: (jnp.bitwise_xor(lax.rem(i, 2), m[4]), 0))
+    down = whole(half, width)
     up = pl.BlockSpec((half, width), lambda i, m: (0, jnp.bitwise_xor(lax.rem(i, 2), m[5])))
     return pl.pallas_call(
         body,
         grid_spec=pltpu.PrefetchScalarGridSpec(
             num_scalar_prefetch=1,
             grid=(4,),
-            in_specs=[down, down, up, up, whole(*outs[0].shape), whole(*outs[0].shape)],
+            in_specs=[down, down, down, down, up, up, whole(*outs[0].shape), whole(*outs[0].shape)],
             out_specs=(
                 pl.BlockSpec((half, width), lambda i, m: (i, 0)),
                 pl.BlockSpec((half, width), lambda i, m: (0, i)),
@@ -915,96 +917,98 @@
     def next_half(keep, got, way, axis):
         return halves(add(keep, got), bit(*way), axis)
 
+    tie = lambda *values: lax.optimization_barrier(values)
     with jax.named_scope("weight_gradients"):
+        far_u = swap(up_out_grads(meta, attn_t, grad_branch, h2, dup))
         far_d = swap(down_grads(meta, act, dy))
-        far_u = swap(up_out_grads(meta, attn_t, grad_branch, h2, dup))
+        up_k, up_s, out_k, out_s = up_out_grads(meta, attn_t, grad_branch, h2, dup, far_u)
         down_k, down_s = down_grads(meta, act, dy, far_d)
-        up_k, up_s, out_k, out_s = up_out_grads(meta, attn_t, grad_branch, h2, dup, far_u)
-        grad_o, up_k, up_s, out_k, out_s, down_k, down_s = lax.optimization_barrier(
-            (grad_o, up_k, up_s, out_k, out_s, down_k, down_s)
-        )
-    got = flip(down_s, *x), flip(up_s, *y), flip(out_s, *z)
-    back = lambda h, go: attend_back(meta, lengths, qt, ka, kt, v, attn_f, logsum, go, h, 1, hd)
-    parts = [back(0, grad_o)]
+        got = flip(down_s, *x), flip(up_s, *y), flip(out_s, *z)
+    grad_o = tie(grad_o, up_k, up_s, out_k, out_s, down_k, down_s)[0]
+    head = lambda h, go: attend_back(meta, lengths, qt, ka, kt, v, attn_f, logsum, go, h, 1, hd)
+    parts = [None] * heads
+    parts[0] = head(0, grad_o)
+    grad_o, parts[0], *got = tie(grad_o, parts[0], *got)
     with jax.named_scope("weight_gradients"):
-        grad_o, *got = lax.optimization_barrier((grad_o, *got))
         down_k, down_s = next_half(down_k, got[0], y, 0)
         up_k, up_s = next_half(up_k, got[1], z, 1)
         out_k, out_s = next_half(out_k, got[2], x, 0)
         got = flip(down_s, *y), flip(up_s, *z), flip(out_s, *x)
     for h in range(1, heads - 1):
-        parts.append(back(h, grad_o))
+        parts[h] = head(h, grad_o)
+    grad_o, parts[1:-1], *got = tie(grad_o, parts[1:-1], *got)
     with jax.named_scope("weight_gradients"):
-        grad_o, *got = lax.optimization_barrier((grad_o, *got))
         down_k, down_s = next_half(down_k, got[0], z, 1)
         up_k, up_s = next_half(up_k, got[1], x, 1)
         out_k, out_s = next_half(out_k, got[2], y, 1)
         got = flip(down_s, *z), flip(up_s, *x), flip(out_s, *y)
-    parts.append(back(heads - 1, grad_o))
-    x_row, *got = lax.optimization_barrier((x_row, *got))
+    parts[-1] = head(heads - 1, grad_o)
+    parts[-1], *got = tie(parts[-1], *got)
     with jax.named_scope("weight_gradients"):
-        down = add(down_k, got[0])
-        up = add(up_k, got[1])
-        out = add(out_k, got[2])
-        if masks[2:]:
-            sizes = [down.shape[0], up.shape[0]]
-            every_piece = jnp.concatenate([down, up, out])
-            for mask in masks[2:]:
-                every_piece = add(every_piece, flip(every_piece, "seq", mask))
-            down, up, out = jnp.split(every_piece, [sizes[0], sizes[0] + sizes[1]])
-        down = jnp.concatenate([down, flip(down, *z)], axis=1)
-        up = jnp.concatenate([up, flip(up, *x)], axis=1)
-        out = jnp.concatenate([out, flip(out, *y)], axis=1)
-        down = jnp.concatenate([down, flip(down, *y)], axis=0)
-        up = jnp.concatenate([up, flip(up, *z)], axis=1)
-        out = jnp.concatenate([out, flip(out, *x)], axis=0)
-        grad_down, grad_up, grad_out = assemble(
-            meta, (down, flip(down, *x)), (up, flip(up, *y)), (out, flip(out, *z))
-        )
+        down, up, out = add(down_k, got[0]), add(up_k, got[1]), add(out_k, got[2])
+        sizes = [down.shape[0], up.shape[0]]
+        pieces = jnp.concatenate([down, up, out])
+        for mask in masks[2:]:
+            pieces = add(pieces, flip(pieces, "seq", mask))
+        down, up, out = jnp.split(pieces, [sizes[0], sizes[0] + sizes[1]])
 
     with jax.named_scope("backward_attention"):
         dq, dk, dv = zip(*parts)
-        back_a, back_b, dw_t = qkv_back(
-            meta, x_row, dq, dk, dv, w_t, g1, b1, gq, gk, vec2, heads, hd
-        )
-
-    if direct:
-
-        def gather(parts):
-            a = parts[0].reshape(2, 2, 2, local, half)
-            b = parts[1].reshape(2, 2, 2, local, half)
-            out = []
-            for kind in (1, 0):
-                a1 = add(a[kind, :, 0], flip(a[kind, :, 1], "seq", 1))
-                b1 = add(b[kind, 0], flip(b[kind, 1], "seq", 2))
-                a2 = add(a1[0], flip(a1[1], "seq", 2))
-                b2 = add(b1[0], flip(b1[1], "seq", 1))
-                out.append(jnp.concatenate([a2, b2], axis=1))
-            return out
-
-        far_sum, near_sum = gather((back_a, back_b))
-        other = flip(far_sum, "seq", 4)
-        back = jnp.where(
-            row == 0, jnp.stack([near_sum, other]), jnp.stack([other, near_sum])
-        ).reshape(every * local, width)
-    else:
-        whole = jnp.concatenate([back_a, back_b], axis=-1).reshape(every, team, local, width)
-        whole = lax.psum_scatter(whole, "seq", scatter_dimension=1, axis_index_groups=same_row, tiled=True)
-        got = lax.all_to_all(whole[:, 0], "seq", 0, 0, axis_index_groups=same_member, tiled=True)
-        back = got.reshape(every * local, width)
+        back_a, back_b, dw_t = qkv_back(meta, x_row, dq, dk, dv, w_t, g1, b1, gq, gk, vec2, heads, hd)
+    back_a, back_b, dw_t, down, up, out = tie(back_a, back_b, dw_t, down, up, out)
+
+    with jax.named_scope("first_round"):
+        keep, send = halves(dw_t, core, 1)
+        q_keep, q_send = next_half(keep, swap(send), x, 0)
+        got = [flip(down, *z), flip(up, *x), flip(out, *y), flip(q_send, *x)]
+        if direct:
+            a = back_a.reshape(2, 2, 2, local, half)
+            b = back_b.reshape(2, 2, 2, local, half)
+            got += [flip(a[:, :, 1], *y), flip(b[:, 1], *z)]
+        got = tie(*got)
+        down = jnp.concatenate([down, got[0]], axis=1)
+        up = jnp.concatenate([up, got[1]], axis=1)
+        out = jnp.concatenate([out, got[2]], axis=1)
+        piece = add(q_keep, got[3])
+        if direct:
+            a, b = add(a[:, :, 0], got[4]), add(b[:, 0], got[5])
+    with jax.named_scope("second_round"):
+        rows_at = [mask for mask in masks if mask >= team]
+        got = [flip(down, *y), flip(down, *x), flip(up, *z), flip(out, *x)]
+        got += [flip(piece, "seq", mask) for mask in rows_at[:1]]
+        if direct:
+            got += [flip(a[:, 1], *z), flip(b[:, 1], *y)]
+        got = tie(*got)
+        downs = [down, got[0], got[1]]
+        up = jnp.concatenate([up, got[2]], axis=1)
+        out = jnp.concatenate([out, got[3]], axis=0)
+        if rows_at:
+            piece = add(piece, got[4])
+        for mask in rows_at[1:]:
+            piece = add(piece, flip(piece, "seq", mask))
+        if direct:
+            a, b = add(a[:, 0], got[-2]), add(b[:, 0], got[-1])
+    with jax.named_scope("third_round"):
+        piece_y, up = tie(flip(piece, *y), up)
+        piece = jnp.stack([piece, piece_y])
+        if direct:
+            mixed = jnp.concatenate([a, b], axis=-1)
+            near, far = mixed[0], flip(mixed[1], "seq", 4)
+            back = jnp.where(row == 0, jnp.stack([near, far]), jnp.stack([far, near])).reshape(every * local, width)
+        else:
+            whole = jnp.concatenate([back_a, back_b], axis=-1).reshape(every, team, local, width)
+            whole = lax.psum_scatter(whole, "seq", scatter_dimension=1, axis_index_groups=same_row, tiled=True)
+            back = lax.all_to_all(
+                whole[:, 0], "seq", 0, 0, axis_index_groups=same_member, tiled=True
+            ).reshape(every * local, width)
+        downs.append(flip(downs[1], *x))
+        piece_z = flip(piece, *z)
+        pieces = [piece, piece_z, flip(piece, *x), flip(piece_z, *x)]
+        ups, outs = (up, flip(up, *y)), (out, flip(out, *z))
     grad_tokens = finish(x_home, grad_mid, back, g1)
-
-    with jax.named_scope("first_projection_gradient"):
-        keep, send = halves(dw_t, core, 1)
-        piece, send = next_half(keep, swap(send), x, 0)
-        piece = add(piece, flip(send, *x))
-        for mask in masks:
-            if mask >= team:
-                piece = add(piece, flip(piece, "seq", mask))
-        piece = jnp.stack([piece, flip(piece, *z)])
-        piece = jnp.concatenate([piece, flip(piece, *y)], axis=0)
-        grad_qkv, small = assemble_qkv(meta, piece, flip(piece, *x), heads, hd)
-        cuts = [small[0], small[1], small[2], small[3], small[4, : hd // 2], small[4, hd // 2 : hd]]
+    grad_qkv, small = assemble_qkv(meta, pieces, heads, hd)
+    grad_down, grad_up, grad_out = assemble(meta, downs, ups, outs)
+    cuts = [small[0], small[1], small[2], small[3], small[4, : hd // 2], small[4, hd // 2 : hd]]
     shape = tokens.shape
     return (
         output.reshape(shape), grad_tokens.reshape(shape), cuts[0], cuts[1], grad_qkv, cuts[4], cuts[5],

time: 416 us -> 402 us (0.966); the launches traced: 422 us -> 401 us
  waiting for transfers between devices: 154 us -> 120 us
  other arithmetic: 10.7 us -> 15.7 us
    ppermute x50 -> x48, waiting for transfers between devices: 131 us -> 104 us  [flip(): return lax.ppermute(value, axis, [(i, i ^ mask) for i in range(size)])]
    all_to_all x2, waiting for transfers between devices: 23.6 us -> 15.8 us  [exchange(): return lax.all_to_all(value, 'seq', 0, 0, tiled=True)]
    convert_element_type x18 -> x16, other arithmetic: 5.59 us -> 10.9 us  [add(): return (a.astype(F32) + b.astype(F32)).astype(BF16)]
    unnamed x62 -> x72, local copies, waits for them, and re-layouts: 8.79 us -> 11.2 us
    ppermute x50 -> x48, starting transfers between devices: 48.5 us -> 50.6 us  [flip(): return lax.ppermute(value, axis, [(i, i ^ mask) for i in range(size)])]
  transfers between devices with their start and end apart: 52 -> 50, of which waited for: 21 -> 19; matrix products, arithmetic and copies ran while one was open for 5% -> 6% of each run, Pallas kernels for 29% -> 36%
where the time goes in v6:
time: 402 us; the launch traced here: 401 us
  Pallas kernels  185 us (46%)
  waiting for transfers between devices  120 us (30%)
  starting transfers between devices  58.2 us (14%)
  local copies, waits for them, and re-layouts  21.5 us (5%)
  other arithmetic  15.7 us (4%)
    ppermute x48, waiting for transfers between devices, flip(): return lax.ppermute(value, axis, [(i, i ^ mask) for i in range(size)])  104 us
    pallas_call x3, Pallas kernels, attend_back(): pl.pallas_call(functools.partial(attend_back_body, heads, hd), grid=(bloc...  52.8 us
    ppermute x48, starting transfers between devices, flip(): return lax.ppermute(value, axis, [(i, i ^ mask) for i in range(size)])  50.6 us
    pallas_call x1, Pallas kernels, attend(): pl.pallas_call(functools.partial(attend_body, heads, hd), grid=(blocks,),...  30.1 us
    pallas_call x1, Pallas kernels, ffn(): pl.pallas_call(body, grid_spec=pltpu.PrefetchScalarGridSpec(num_scalar_pr...  25.6 us
    pallas_call x1, Pallas kernels, qkv_back(): pl.pallas_call(functools.partial(qkv_back_body, heads, hd), grid_spec=plt...  17.8 us
    all_to_all x2, waiting for transfers between devices, exchange(): return lax.all_to_all(value, 'seq', 0, 0, tiled=True)  15.8 us
    pallas_call x2, Pallas kernels, up_out_grads(): pl.pallas_call(body, grid_spec=pltpu.PrefetchScalarGridSpec(num_scalar_pr...  15.5 us
  transfers between devices with their start and end apart: 50, of which 19 were waited for; matrix products, arithmetic and copies ran while one was open for 6% of the time, Pallas kernels for 36%

profile of v6, /device:TPU:0, one launch (start us, length us, event | category | flops | bytes accessed | tf_op | source)
XLA Modules:
  0.0 401.3 jit_solution(3520566796896363967)
XLA Ops:
  13.4 10.4 %collective-permute-done.4.refs_4_ = bf16[256,768]{1,0:T(8,128)(2,1)} collective-permute-done((bf16[256,768]{1,0:T(8,128)(2,1)S(1)}, bf16[256,768]{1,0:T(8,128)(2,1)}, u32[]{:S(2)}, u32[]{:S(2)}) %collective-permute-start.4) | collective-permute-done | bytes 393248 | tf_op jit(solution)/shard_map/ppermute | solution.py:795
  45.6 12.2 %qkv_forward.1 = (bf16[3,128,2048]{2,1,0:T(8,128)(2,1)}, bf16[3,2048,128]{2,1,0:T(8,128)(2,1)}, bf16[3,64,2048]{2,1,0:T(8,128)(2,1)}, bf16[3,2048,64]{2,1,0:T(8,...) custom-call(s32[6]{0:T(128)} %stack.46.meta, s32[2,8]{1,0:T(2,128)} %bitcast.107, ...), custom_call_target="tpu_custom_call" | custom-call | flops 4200000000 | bytes 1024 | tf_op jit(solution)/shard_map/forward_attention/qkv_forward/pallas_call | solution.py:104
  57.8 30.1 %attention_forward.1 = (bf16[8,192,256]{2,1,0:T(8,128)(2,1)}, f32[3,64,2048]{2,1,0:T(8,128)}, f32[3,1,2048]{2,1,0:T(1,128)}) custom-call(s32[6]{0:T(128)} %stack.46.meta, s32[2,8]{1,0:T(2,128)} %bitcast.108, bf16[3,128,2048]{2,1,0:T(8,128)(2,1)} %get-tuple-element.94.qt_ref, bf16[3,2048,128]{2,1,0:T(8,128)(2,1)} %get-tuple-element.95.ka_ref, ...), custom_call_target="tpu_custom_call" | custom-call | flops 8750000128 | bytes 1024 | tf_op jit(solution)/shard_map/forward_attention/attention_forward/pallas_call | solution.py:170
  93.9 15.8 %all-to-all-done = bf16[8,192,256]{2,1,0:T(8,128)(2,1)S(1)} async-done(((bf16[8,192,256]{2,1,0:T(8,128)(2,1)}), bf16[8,192,256]{2,1,0:T(8,128)(2,1)S(1)}, u32[]{:S(2)}, u32[]{:S(2)}) %all-to-all-start) | async-done | bytes 786464 | tf_op jit(solution)/shard_map/all_to_all | solution.py:885
  110.6 25.6 %ffn_both_ways.1 = (bf16[512,768]{1,0:T(8,128)(2,1)}, f32[512,768]{1,0:T(8,128)}, bf16[512,768]{1,0:T(8,128)(2,1)}, bf16[512,768]{1,0:T(8,128)(2,1)}, bf16[512,3...) custom-call(s32[6]{0:T(128)} %stack.46.meta, ...), custom_call_target="tpu_custom_call" | custom-call | flops 8750000128 | bytes 1024 | tf_op jit(solution)/shard_map/feed_forward/ffn_both_ways/pallas_call | solution.py:512
  136.2 7.2 %up_out_gradient.2 = bf16[384,3840]{1,0:T(8,128)(2,1)} custom-call(s32[6]{0:T(128)} %stack.46.meta, bf16[2,768,256]{2,1,0:T(8,128)(2,1)} %bitcast.90, bf16[512,768]{1,0:T(8,128)(2,1)} %get-tuple-element.102.gb_ref, bf16[512,768]{1,0:T(8,128)(2,1)} %get-tuple-element.103.h2_ref, bf16[512,3072]{1,0:T(8,128)(2,1)} %get-tuple-element.104.dup_ref), custom_call_target="tpu_custom_call" | custom-call | flops 2449999872 | bytes 1024 | tf_op jit(solution)/shard_map/weight_gradients/up_out_gradient/pallas_call | solution.py:637
  143.4 5.6 %down_gradient.2 = bf16[1536,768]{1,0:T(8,128)(2,1)} custom-call(s32[6]{0:T(128)} %stack.46.meta, bf16[512,3072]{1,0:T(8,128)(2,1)} %get-tuple-element.109.act_ref, bf16[512,768]{1,0:T(8,128)(2,1)} %bitcast.105), custom_call_target="tpu_custom_call" | custom-call | flops 2100000000 | bytes 1024 | tf_op jit(solution)/shard_map/weight_gradients/down_gradient/pallas_call | solution.py:697
  154.0 6.4 %down_gradient.3 = (bf16[768,768]{1,0:T(8,128)(2,1)}, bf16[768,768]{1,0:T(8,128)(2,1)}) custom-call(s32[6]{0:T(128)} %stack.46.meta, bf16[512,3072]{1,0:T(8,128)(2,1)} %get-tuple-element.109.act_ref, bf16[512,768]{1,0:T(8,128)(2,1)} %bitcast.106, bf16[1536,768]{1,0:T(8,128)(2,1)} %collective-permute-done.15.rest_0_), custom_call_target="tpu_custom_call" | custom-call | flops 2100000000 | bytes 1024 | tf_op jit(solution)/shard_map/weight_gradients/down_gradient/pallas_call | solution.py:697
  164.6 8.4 %up_out_gradient.3 = (bf16[384,1536]{1,0:T(8,128)(2,1)}, bf16[384,1536]{1,0:T(8,128)(2,1)}, bf16[192,768]{1,0:T(8,128)(2,1)}, bf16[192,768]{1,0:T(8,128)(2,1)}) custom-call(s32[6]{0:T(128)} %stack.46.meta, bf16[2,768,256]{2,1,0:T(8,128)(2,1)} %bitcast.91, bf16[512,768]{1,0:T(8,128)(2,1)} %get-tuple-element.102.gb_ref, ...), custom_call_target="tpu_custom_call" | custom-call | flops 2449999872 | bytes 1024 | tf_op jit(solution)/shard_map/weight_gradients/up_out_gradient/pallas_call | solution.py:637
  176.6 17.7 %attention_backward.3 = (f32[1,64,2048]{2,1,0:T(8,128)}, f32[1,64,2048]{2,1,0:T(8,128)}, f32[1,64,2048]{2,1,0:T(8,128)}) custom-call(s32[6]{0:T(128)} %stack.46.meta, s32[2,8]{1,0:T(2,128)} %bitcast.109, bf16[3,128,2048]{2,1,0:T(8,128)(2,1)} %get-tuple-element.94.qt_ref, bf16[3,2048,128]{2,1,0:T(8,128)(2,1)} %get-tuple-element.95.ka_ref, ...), custom_call_target="tpu_custom_call" | custom-call | flops 3849999872 | bytes 1024 | tf_op jit(solution)/shard_map/attention_backward/pallas_call | solution.py:239
  194.3 7.1 %collective-permute-done.17 = bf16[384,1536]{1,0:T(8,128)(2,1)} collective-permute-done((bf16[384,1536]{1,0:T(8,128)(2,1)}, bf16[384,1536]{1,0:T(8,128)(2,1)}, u32[]{:S(2)}, u32[]{:S(2)}) %collective-permute-start.17) | collective-permute-done | bytes 1179680 | tf_op jit(solution)/shard_map/weight_gradients/ppermute | solution.py:795
  206.8 17.6 %attention_backward.4 = (f32[1,64,2048]{2,1,0:T(8,128)}, f32[1,64,2048]{2,1,0:T(8,128)}, f32[1,64,2048]{2,1,0:T(8,128)}) custom-call(s32[6]{0:T(128)} %stack.46.meta, s32[2,8]{1,0:T(2,128)} %bitcast.110, bf16[3,128,2048]{2,1,0:T(8,128)(2,1)} %get-tuple-element.94.qt_ref, bf16[3,2048,128]{2,1,0:T(8,128)(2,1)} %get-tuple-element.95.ka_ref, ...), custom_call_target="tpu_custom_call" | custom-call | flops 3849999872 | bytes 1024 | tf_op jit(solution)/shard_map/attention_backward/pallas_call | solution.py:239
  231.8 17.6 %attention_backward.5 = (f32[1,64,2048]{2,1,0:T(8,128)}, f32[1,64,2048]{2,1,0:T(8,128)}, f32[1,64,2048]{2,1,0:T(8,128)}) custom-call(s32[6]{0:T(128)} %stack.46.meta, s32[2,8]{1,0:T(2,128)} %bitcast.111, bf16[3,128,2048]{2,1,0:T(8,128)(2,1)} %get-tuple-element.94.qt_ref, bf16[3,2048,128]{2,1,0:T(8,128)(2,1)} %get-tuple-element.95.ka_ref, ...), custom_call_target="tpu_custom_call" | custom-call | flops 3849999872 | bytes 1024 | tf_op jit(solution)/shard_map/attention_backward/pallas_call | solution.py:239
  251.4 17.8 %qkv_backward.1 = (bf16[8,256,384]{2,1,0:T(8,128)(2,1)}, bf16[8,256,384]{2,1,0:T(8,128)(2,1)}, bf16[608,768]{1,0:T(8,128)(2,1)}) custom-call(s32[6]{0:T(128)} %stack.46.meta, bf16[2048,768]{1,0:T(8,128)(2,1)} %get-tuple-element.100.x_ref, f32[1,64,2048]{2,1,0:T(8,128)} %get-tuple-element.120.refs_0_, f32[1,64,2048]{2,1,0:T(8,128)} %get-tuple-element.128.refs_1_, ...), custom_call_target="tpu_custom_call" | custom-call | flops 5950000128 | bytes 1024 | tf_op jit(solution)/shard_map/backward_attention/qkv_backward/pallas_call | solution.py:339
  269.2 10.2 %collective-permute-done.25 = bf16[864,384]{1,0:T(8,128)(2,1)S(1)} collective-permute-done((bf16[864,384]{1,0:T(8,128)(2,1)S(1)}, bf16[864,384]{1,0:T(8,128)(2,1)S(1)}, u32[]{:S(2)}, u32[]{:S(2)}) %collective-permute-start.25) | collective-permute-done | bytes 663584 | tf_op jit(solution)/shard_map/weight_gradients/ppermute | solution.py:795
  289.8 13.7 %collective-permute-done.28 = bf16[96,384]{1,0:T(8,128)(2,1)S(1)} collective-permute-done((bf16[96,384]{1,0:T(8,128)(2,1)S(1)}, bf16[96,384]{1,0:T(8,128)(2,1)S(1)}, u32[]{:S(2)}, u32[]{:S(2)}) %collective-permute-start.28) | collective-permute-done | bytes 73760 | tf_op jit(solution)/shard_map/first_round/ppermute | solution.py:795
  304.3 5.9 %collective-permute-done.26 = bf16[384,384]{1,0:T(8,128)(2,1)S(1)} collective-permute-done((bf16[384,384]{1,0:T(8,128)(2,1)S(1)}, bf16[384,384]{1,0:T(8,128)(2,1)S(1)}, u32[]{:S(2)}, u32[]{:S(2)}) %collective-permute-start.26) | collective-permute-done | bytes 294944 | tf_op jit(solution)/shard_map/first_round/ppermute | solution.py:795
  319.6 9.1 %collective-permute-done.36 = bf16[96,768]{1,0:T(8,128)(2,1)S(1)} collective-permute-done((bf16[96,768]{1,0:T(8,128)(2,1)S(1)}, bf16[96,768]{1,0:T(8,128)(2,1)S(1)}, u32[]{:S(2)}, u32[]{:S(2)}) %collective-permute-start.36) | collective-permute-done | bytes 147488 | tf_op jit(solution)/shard_map/second_round/ppermute | solution.py:795
  330.0 7.4 %collective-permute-done.39 = bf16[2,256,384]{2,1,0:T(8,128)(2,1)S(1)} collective-permute-done((bf16[2,256,384]{2,1,0:T(8,128)(2,1)S(1)}, bf16[2,256,384]{2,1,0:T(8,128)(2,1)S(1)}, u32[]{:S(2)}, u32[]{:S(2)}) %collective-permute-start.39) | collective-permute-done | bytes 393248 | tf_op jit(solution)/shard_map/second_round/ppermute | solution.py:795
  337.4 5.7 %collective-permute-done.38 = bf16[2,256,384]{2,1,0:T(8,128)(2,1)S(1)} collective-permute-done((bf16[2,256,384]{2,1,0:T(8,128)(2,1)S(1)}, bf16[2,256,384]{2,1,0:T(8,128)(2,1)S(1)}, u32[]{:S(2)}, u32[]{:S(2)}) %collective-permute-start.38) | collective-permute-done | bytes 393248 | tf_op jit(solution)/shard_map/second_round/ppermute | solution.py:795
  345.0 5.5 %collective-permute-done.41 = bf16[304,384]{1,0:T(8,128)(2,1)S(1)} collective-permute-done((bf16[304,384]{1,0:T(8,128)(2,1)S(1)}, bf16[304,384]{1,0:T(8,128)(2,1)S(1)}, u32[]{:S(2)}, u32[]{:S(2)}) %collective-permute-start.41) | collective-permute-done | bytes 233504 | tf_op jit(solution)/shard_map/third_round/ppermute | solution.py:795
  355.6 12.0 %collective-permute-done.42.p01 = bf16[2,304,384]{2,1,0:T(8,128)(2,1)} collective-permute-done((bf16[2,304,384]{2,1,0:T(8,128)(2,1)S(1)}, bf16[2,304,384]{2,1,0:T(8,128)(2,1)}, u32[]{:S(2)}, u32[]{:S(2)}) %collective-permute-start.42) | collective-permute-done | bytes 466976 | tf_op jit(solution)/shard_map/third_round/ppermute | solution.py:795
  375.7 5.8 %collective-permute-done.44.p11 = bf16[2,304,384]{2,1,0:T(8,128)(2,1)} collective-permute-done((bf16[2,304,384]{2,1,0:T(8,128)(2,1)}, bf16[2,304,384]{2,1,0:T(8,128)(2,1)}, u32[]{:S(2)}, u32[]{:S(2)}) %collective-permute-start.44) | collective-permute-done | bytes 466976 | tf_op jit(solution)/shard_map/third_round/ppermute | solution.py:795
  392.2 8.9 %weight_gradients.1 = (f32[1536,768]{1,0:T(8,128)}, f32[384,3072]{1,0:T(8,128)}, f32[384,768]{1,0:T(8,128)}) custom-call(s32[6]{0:T(128)} %stack.46.meta, bf16[384,768]{1,0:T(8,128)(2,1)} %copy-done.15, bf16[384,768]{1,0:T(8,128)(2,1)} %copy-done.26, bf16[384,768]{1,0:T(8,128)(2,1)} %collective-permute-done.34.down_ba, bf16[384,768]{1,0:T(8,128)(2,1)} %copy-done.27, ...), custom_call_target="tpu_custom_call" | custom-call | flops 2449999872 | bytes 1024 | tf_op jit(solution)/shard_map/weight_gradients/pallas_call | solution.py:747
  (222 shorter events, 116.1 us)
Async XLA Ops:
  1.9 21.9 %collective-permute-start.4 = (bf16[256,768]{1,0:T(8,128)(2,1)S(1)}, bf16[256,768]{1,0:T(8,128)(2,1)}, u32[]{:S(2)}, u32[]{:S(2)}) collective-permute-start(bf16[256,768]{1,0:T(8,128)(2,1)S(1)} %get-tuple-element.210), channel_id=1, source_target_pairs={{0,4},{1,5},{2,6},{3,7},{4,0},{5,1},{6,2},{7,3},{8,12},{9,13},{10,... | collective-permute-start | bytes 1179656 | tf_op jit(solution)/shard_map/ppermute | solution.py:795
  12.2 25.8 %collective-permute-start.9 = (bf16[384,576]{0,1:T(8,128)(2,1)S(1)}, bf16[384,576]{0,1:T(8,128)(2,1)S(1)}, u32[]{:S(2)}, u32[]{:S(2)}) collective-permute-start(bf16[384,576]{0,1:T(8,128)(2,1)S(1)} %bitcast.84), channel_id=1, source_target_pairs={{0,8},{8,0},{1,9},{9,1},{2,10},{10,2},{3,11},{11,3},{4,12},{12,4},... | collective-permute-start | bytes 1327112 | tf_op jit(solution)/shard_map/ppermute | solution.py:795
  36.0 73.7 %collective-permute-start.12 = (bf16[384,3072]{1,0:T(8,128)(2,1)}, bf16[384,3072]{1,0:T(8,128)(2,1)}, u32[]{:S(2)}, u32[]{:S(2)}) collective-permute-start(bf16[384,3072]{1,0:T(8,128)(2,1)} %refs_8_.1), channel_id=1, source_target_pairs={{0,8},{8,0},{1,9},{9,1},{2,10},{10,2},{3,11},{11,3},{4,12},{12,4},... | collective-permute-start | bytes 7077896 | tf_op jit(solution)/shard_map/ppermute | solution.py:795
  40.6 69.1 %collective-permute-start.13 = (bf16[1536,768]{1,0:T(8,128)(2,1)}, bf16[1536,768]{1,0:T(8,128)(2,1)}, u32[]{:S(2)}, u32[]{:S(2)}) collective-permute-start(bf16[1536,768]{1,0:T(8,128)(2,1)} %refs_10_.1), channel_id=1, source_target_pairs={{0,8},{8,0},{1,9},{9,1},{2,10},{10,2},{3,11},{11,3},{4,12},{12,4},... | collective-permute-start | bytes 7077896 | tf_op jit(solution)/shard_map/ppermute | solution.py:795
  87.9 21.8 %all-to-all-start = ((bf16[8,192,256]{2,1,0:T(8,128)(2,1)}), bf16[8,192,256]{2,1,0:T(8,128)(2,1)S(1)}, u32[]{:S(2)}, u32[]{:S(2)}) async-start(bf16[8,192,256]{2,1,0:T(8,128)(2,1)} %get-tuple-element.97), calls=%async_computation | async-start | bytes 1572864 | tf_op jit(solution)/shard_map/all_to_all | solution.py:885
  143.4 21.2 %collective-permute-start.14 = (bf16[384,3840]{1,0:T(8,128)(2,1)}, bf16[384,3840]{1,0:T(8,128)(2,1)}, u32[]{:S(2)}, u32[]{:S(2)}) collective-permute-start(bf16[384,3840]{1,0:T(8,128)(2,1)} %up_out_gradient.2), channel_id=1, source_target_pairs={{0,8},{8,0},{1,9},{9,1},{2,10},{10,2},{3,11},{11,3},{4,12},{12,4},... | collective-permute-start | bytes 8847368 | tf_op jit(solution)/shard_map/weight_gradients/ppermute | solution.py:795
  149.5 26.2 %all-to-all-start.1 = ((bf16[8,192,256]{2,1,0:T(8,128)(2,1)}), bf16[8,192,256]{2,1,0:T(8,128)(2,1)S(1)}, u32[]{:S(2)}, u32[]{:S(2)}) async-start(bf16[8,192,256]{2,1,0:T(8,128)(2,1)} %bitcast.17), calls=%async_computation.1 | async-start | bytes 1572864 | tf_op jit(solution)/shard_map/all_to_all | solution.py:885
  160.4 33.9 %collective-permute-start.16 = (bf16[768,768]{1,0:T(8,128)(2,1)}, bf16[768,768]{1,0:T(8,128)(2,1)S(1)}, u32[]{:S(2)}, u32[]{:S(2)}) collective-permute-start(bf16[768,768]{1,0:T(8,128)(2,1)} %get-tuple-element.111), channel_id=1, source_target_pairs={{0,16},{16,0},{1,17},{17,1},{2,18},{18,2},{3,19},{19,3},{4,20},{20... | collective-permute-start | bytes 3538952 | tf_op jit(solution)/shard_map/weight_gradients/ppermute | solution.py:795
  173.0 28.3 %collective-permute-start.17 = (bf16[384,1536]{1,0:T(8,128)(2,1)}, bf16[384,1536]{1,0:T(8,128)(2,1)}, u32[]{:S(2)}, u32[]{:S(2)}) collective-permute-start(bf16[384,1536]{1,0:T(8,128)(2,1)} %get-tuple-element.106), channel_id=1, source_target_pairs={{0,1},{1,0},{2,3},{3,2},{4,5},{5,4},{6,7},{7,6},{8,9},{9,8},{10,11... | collective-permute-start | bytes 3538952 | tf_op jit(solution)/shard_map/weight_gradients/ppermute | solution.py:795
  203.9 20.5 %collective-permute-start.20 = (bf16[384,768]{1,0:T(8,128)(2,1)}, bf16[384,768]{1,0:T(8,128)(2,1)}, u32[]{:S(2)}, u32[]{:S(2)}) collective-permute-start(bf16[384,768]{1,0:T(8,128)(2,1)} %constant_dynamic-slice_fusion.6), channel_id=1, source_target_pairs={{0,2},{1,3},{2,0},{3,1},{4,6},{5,7},{6,4},{7,5},{8,10},{9,11},{10,... | collective-permute-start | bytes 1769480 | tf_op jit(solution)/shard_map/weight_gradients/ppermute | solution.py:795
  226.2 23.2 %collective-permute-start.24 = (bf16[96,384]{1,0:T(8,128)(2,1)}, bf16[96,384]{1,0:T(8,128)(2,1)}, u32[]{:S(2)}, u32[]{:S(2)}) collective-permute-start(bf16[96,384]{1,0:T(8,128)(2,1)} %constant_dynamic-slice_fusion.2), channel_id=1, source_target_pairs={{0,1},{1,0},{2,3},{3,2},{4,5},{5,4},{6,7},{7,6},{8,9},{9,8},{10,11... | collective-permute-start | bytes 221192 | tf_op jit(solution)/shard_map/weight_gradients/ppermute | solution.py:795
  228.8 20.7 %collective-permute-start.23 = (bf16[384,384]{1,0:T(8,128)(2,1)S(1)}, bf16[384,384]{1,0:T(8,128)(2,1)S(1)}, u32[]{:S(2)}, u32[]{:S(2)}) collective-permute-start(bf16[384,384]{1,0:T(8,128)(2,1)S(1)} %constant_dynamic-slice_fusion.3), channel_id=1, source_target_pairs={{0,16},{16,0},{1,17},{17,1},{2,18},{18,2},{3,19},{19,3},{4,20},{20... | collective-permute-start | bytes 884744 | tf_op jit(solution)/shard_map/weight_gradients/ppermute | solution.py:795
  250.6 28.7 %collective-permute-start.25 = (bf16[864,384]{1,0:T(8,128)(2,1)S(1)}, bf16[864,384]{1,0:T(8,128)(2,1)S(1)}, u32[]{:S(2)}, u32[]{:S(2)}) collective-permute-start(bf16[864,384]{1,0:T(8,128)(2,1)S(1)} %pad_maximum_fusion.1), channel_id=1, source_target_pairs={{0,4},{1,5},{2,6},{3,7},{4,0},{5,1},{6,2},{7,3},{8,12},{9,13},{10,... | collective-permute-start | bytes 1990664 | tf_op jit(solution)/shard_map/weight_gradients/ppermute | solution.py:795
  282.2 28.1 %collective-permute-start.31 = (bf16[2,2,256,384]{3,2,0,1:T(8,128)(2,1)}, bf16[2,2,256,384]{3,2,0,1:T(8,128)(2,1)}, u32[]{:S(2)}, u32[]{:S(2)}) collective-permute-start(bf16[2,2,256,384]{3,2,0,1:T(8,128)(2,1)} %bitcast.82), channel_id=1, source_target_pairs={{0,1},{1,0},{2,3},{3,2},{4,5},{5,4},{6,7},{7,6},{8,9},{9,8},{10,11... | collective-permute-start | bytes 2359304 | tf_op jit(solution)/shard_map/first_round/ppermute | solution.py:795
  284.6 25.8 %collective-permute-start.32 = (bf16[2,2,256,384]{3,2,0,1:T(8,128)(2,1)}, bf16[2,2,256,384]{3,2,0,1:T(8,128)(2,1)}, u32[]{:S(2)}, u32[]{:S(2)}) collective-permute-start(bf16[2,2,256,384]{3,2,0,1:T(8,128)(2,1)} %bitcast.81), channel_id=1, source_target_pairs={{0,2},{1,3},{2,0},{3,1},{4,6},{5,7},{6,4},{7,5},{8,10},{9,11},{10,... | collective-permute-start | bytes 2359304 | tf_op jit(solution)/shard_map/first_round/ppermute | solution.py:795
  284.6 25.7 %collective-permute-start.26 = (bf16[384,384]{1,0:T(8,128)(2,1)S(1)}, bf16[384,384]{1,0:T(8,128)(2,1)S(1)}, u32[]{:S(2)}, u32[]{:S(2)}) collective-permute-start(bf16[384,384]{1,0:T(8,128)(2,1)S(1)} %get-tuple-element.151), channel_id=1, source_target_pairs={{0,2},{1,3},{2,0},{3,1},{4,6},{5,7},{6,4},{7,5},{8,10},{9,11},{10,... | collective-permute-start | bytes 884744 | tf_op jit(solution)/shard_map/first_round/ppermute | solution.py:795
  286.6 23.7 %collective-permute-start.27 = (bf16[384,384]{1,0:T(8,128)(2,1)S(1)}, bf16[384,384]{1,0:T(8,128)(2,1)S(1)}, u32[]{:S(2)}, u32[]{:S(2)}) collective-permute-start(bf16[384,384]{1,0:T(8,128)(2,1)S(1)} %get-tuple-element.152), channel_id=1, source_target_pairs={{0,16},{16,0},{1,17},{17,1},{2,18},{18,2},{3,19},{19,3},{4,20},{20... | collective-permute-start | bytes 884744 | tf_op jit(solution)/shard_map/first_round/ppermute | solution.py:795
  310.4 32.7 %collective-permute-start.33 = (bf16[384,768]{1,0:T(8,128)(2,1)S(1)}, bf16[384,768]{1,0:T(8,128)(2,1)S(1)}, u32[]{:S(2)}, u32[]{:S(2)}) collective-permute-start(bf16[384,768]{1,0:T(8,128)(2,1)S(1)} %constant_dynamic-update-slice_fusion.down_aa), channel_id=1, source_target_pairs={{0,1},{1,0},{2,3},{3,2},{4,5},{5,4},{6,7},{7,6},{8,9},{9,8},{10,11... | collective-permute-start | bytes 1769480 | tf_op jit(solution)/shard_map/second_round/ppermute | solution.py:795
  311.7 32.2 %collective-permute-start.34 = (bf16[384,768]{1,0:T(8,128)(2,1)S(1)}, bf16[384,768]{1,0:T(8,128)(2,1)}, u32[]{:S(2)}, u32[]{:S(2)}) collective-permute-start(bf16[384,768]{1,0:T(8,128)(2,1)S(1)} %constant_dynamic-update-slice_fusion.down_aa), channel_id=1, source_target_pairs={{0,16},{16,0},{1,17},{17,1},{2,18},{18,2},{3,19},{19,3},{4,20},{20... | collective-permute-start | bytes 1769480 | tf_op jit(solution)/shard_map/second_round/ppermute | solution.py:795
  315.9 27.2 %collective-permute-start.35 = (bf16[384,768]{1,0:T(8,128)(2,1)S(1)}, bf16[384,768]{1,0:T(8,128)(2,1)S(1)}, u32[]{:S(2)}, u32[]{:S(2)}) collective-permute-start(bf16[384,768]{1,0:T(8,128)(2,1)S(1)} %pad_maximum_fusion.2), channel_id=1, source_target_pairs={{0,2},{1,3},{2,0},{3,1},{4,6},{5,7},{6,4},{7,5},{8,10},{9,11},{10,... | collective-permute-start | bytes 1769480 | tf_op jit(solution)/shard_map/second_round/ppermute | solution.py:795
  350.8 40.6 %collective-permute-start.46 = (bf16[384,1536]{1,0:T(8,128)(2,1)S(1)}, bf16[384,1536]{1,0:T(8,128)(2,1)}, u32[]{:S(2)}, u32[]{:S(2)}) collective-permute-start(bf16[384,1536]{1,0:T(8,128)(2,1)S(1)} %pad_maximum_fusion.up_a), channel_id=1, source_target_pairs={{0,1},{1,0},{2,3},{3,2},{4,5},{5,4},{6,7},{7,6},{8,9},{9,8},{10,11... | collective-permute-start | bytes 3538952 | tf_op jit(solution)/shard_map/third_round/ppermute | solution.py:795
  354.7 21.0 %collective-permute-start.43 = (bf16[2,304,384]{2,1,0:T(8,128)(2,1)S(1)}, bf16[2,304,384]{2,1,0:T(8,128)(2,1)}, u32[]{:S(2)}, u32[]{:S(2)}) collective-permute-start(bf16[2,304,384]{2,1,0:T(8,128)(2,1)S(1)} %pad_maximum_fusion.3.p00), channel_id=1, source_target_pairs={{0,16},{16,0},{1,17},{17,1},{2,18},{18,2},{3,19},{19,3},{4,20},{20... | collective-permute-start | bytes 1400840 | tf_op jit(solution)/shard_map/third_round/ppermute | solution.py:795
  369.0 20.5 %collective-permute-start.47 = (bf16[192,768]{1,0:T(8,128)(2,1)S(1)}, bf16[192,768]{1,0:T(8,128)(2,1)S(1)}, u32[]{:S(2)}, u32[]{:S(2)}) collective-permute-start(bf16[192,768]{1,0:T(8,128)(2,1)S(1)} %pad_maximum_fusion.7.out_a), channel_id=1, source_target_pairs={{0,2},{1,3},{2,0},{3,1},{4,6},{5,7},{6,4},{7,5},{8,10},{9,11},{10,... | collective-permute-start | bytes 884744 | tf_op jit(solution)/shard_map/third_round/ppermute | solution.py:795
  369.1 22.3 %collective-permute-start.45 = (bf16[384,768]{1,0:T(8,128)(2,1)}, bf16[384,768]{1,0:T(8,128)(2,1)S(1)}, u32[]{:S(2)}, u32[]{:S(2)}) collective-permute-start(bf16[384,768]{1,0:T(8,128)(2,1)} %copy-done.26), channel_id=1, source_target_pairs={{0,16},{16,0},{1,17},{17,1},{2,18},{18,2},{3,19},{19,3},{4,20},{20... | collective-permute-start | bytes 1769480 | tf_op jit(solution)/shard_map/third_round/ppermute | solution.py:795
  (57 other events, 541.0 us)

commit v7 on v6

--- a/solution.py
+++ b/solution.py
@@ -133,25 +133,31 @@
     return lo_b, jnp.where(first >= bounds[-1], lo_b, hi_b)
 
 
+def in_pairs(lo, hi, step, carry):
+    pairs = (hi - lo) // 2
+    carry = lax.fori_loop(0, pairs, lambda k, c: step([lo + 2 * k, lo + 2 * k + 1], c), carry)
+    return lax.fori_loop(lo + 2 * pairs, hi, lambda b, c: step([b], c), carry)
+
+
 def attend_body(heads, hd, meta, len_ref, qt_ref, ka_ref, vt_ref, o_ref, of_ref, ls_ref):
     i = pl.program_id(0)
     bounds = bounds_of(len_ref, meta[1])
     lo, hi = block_range(bounds, i)
 
-    def step(b, carry):
-        rows = pl.ds(pl.multiple_of(b * BLK, BLK), BLK)
-        out = []
-        for h in range(heads):
-            acc, total = carry[h]
-            scores = mm(ka_ref[h, rows, :], qt_ref[h])
-            expo = jnp.exp2(scores * LOG2E - SHIFT * LOG2E)
+    def step(blocks, carry):
+        rows = [pl.ds(pl.multiple_of(b * BLK, BLK), BLK) for b in blocks]
+        items = [(h, r) for r in rows for h in range(heads)]
+        scores = [mm(ka_ref[h, r, :], qt_ref[h]) for h, r in items]
+        expos = [jnp.exp2(one * LOG2E - SHIFT * LOG2E) for one in scores]
+        out = list(carry)
+        for expo, (h, r) in zip(expos, items):
+            acc, total = out[h]
             total = total + jnp.sum(expo.reshape(BLK // 8, 8, BLK), axis=0)
-            acc = acc + mm(vt_ref[h, :, rows], expo.astype(BF16))
-            out.append((acc, total))
+            out[h] = (acc + mm(vt_ref[h, :, r], expo.astype(BF16)), total)
         return tuple(out)
 
     init = tuple((jnp.zeros((hd, BLK), F32), jnp.zeros((8, BLK), F32)) for _ in range(heads))
-    done = lax.fori_loop(lo, hi, step, init)
+    done = in_pairs(lo, hi, step, init)
     for h in range(heads):
         acc, total = done[h]
         total = jnp.sum(total, axis=0, keepdims=True)
@@ -193,80 +199,84 @@
     )(meta, lengths, qt, ka, vt)
 
 
-def attend_back_body(
-    heads, hd, meta, len_ref, qt_ref, ka_ref, kt_ref, v_ref, of_ref, ls_ref, go_ref, dq_ref, dk_ref, dv_ref
-):
+def attend_back_body(first, heads, hd, meta, len_ref, *refs):
+    qt_ref, ka_ref, kt_ref, v_ref, of_ref, ls_ref, go_ref = refs[:7]
+    dq_ref, dk_ref, dv_ref = refs[-3:]
     i = pl.program_id(0)
     bounds = bounds_of(len_ref, meta[1])
-    lo, hi = block_range(bounds, i)
+    lo, hi = block_range(bounds, i + first)
 
     @pl.when(i == 0)
     def _():
-        dk_ref[...] = jnp.zeros_like(dk_ref)
-        dv_ref[...] = jnp.zeros_like(dv_ref)
+        if first:
+            dk_ref[...] = refs[8][...]
+            dv_ref[...] = refs[9][...]
+        else:
+            dk_ref[...] = jnp.zeros_like(dk_ref)
+            dv_ref[...] = jnp.zeros_like(dv_ref)
 
     inner = []
     for h in range(heads):
         go = go_ref[0, h * hd : (h + 1) * hd, :].astype(F32)
         inner.append(jnp.sum(go * of_ref[h], axis=0, keepdims=True))
 
-    def step(b, carry):
-        rows = pl.ds(pl.multiple_of(b * BLK, BLK), BLK)
-        out = []
-        for h in range(heads):
-            go = go_ref[0, h * hd : (h + 1) * hd, :]
-            qt = qt_ref[h]
-            scores = mm(ka_ref[h, rows, :], qt)
-            probs = jnp.exp2(scores * LOG2E - ls_ref[h])
-            grad_probs = mm(v_ref[h, rows, :], go)
-            grad_scores = (probs * (grad_probs - inner[h])).astype(BF16)
-            dv_ref[h, :, rows] += mm(go, probs.astype(BF16), NT)
-            dk_ref[h, :, rows] += mm(qt[:hd], grad_scores, NT)
-            out.append(carry[h] + mm(kt_ref[h, :, rows], grad_scores))
+    def step(blocks, carry):
+        rows = [pl.ds(pl.multiple_of(b * BLK, BLK), BLK) for b in blocks]
+        items = [(h, r) for r in rows for h in range(heads)]
+        gos = [go_ref[0, h * hd : (h + 1) * hd, :] for h in range(heads)]
+        scores = [mm(ka_ref[h, r, :], qt_ref[h]) for h, r in items]
+        grad_probs = [mm(v_ref[h, r, :], gos[h]) for h, r in items]
+        probs = [jnp.exp2(one * LOG2E - ls_ref[h]) for one, (h, _) in zip(scores, items)]
+        grads = [(p * (g - inner[h])).astype(BF16) for p, g, (h, _) in zip(probs, grad_probs, items)]
+        out = list(carry)
+        for p, g, (h, r) in zip(probs, grads, items):
+            dv_ref[h, :, r] += mm(gos[h], p.astype(BF16), NT)
+            dk_ref[h, :, r] += mm(qt_ref[h][:hd], g, NT)
+            out[h] = out[h] + mm(kt_ref[h, :, r], g)
         return tuple(out)
 
-    done = lax.fori_loop(lo, hi, step, tuple(jnp.zeros((hd, BLK), F32) for _ in range(heads)))
+    done = in_pairs(lo, hi, step, tuple(jnp.zeros((hd, BLK), F32) for _ in range(heads)))
     for h in range(heads):
         dq_ref[h] = done[h] * (hd**-0.5)
 
 
-def attend_back(meta, lengths, qt, ka, kt, v, of, ls, go, at, heads, hd):
+def attend_back(meta, lengths, qt, ka, kt, v, of, ls, go, heads, hd, before=None):
     length = qt.shape[2]
-    blocks = length // BLK
+    count = length // BLK // 2
+    first = count if before else 0
     smem = pl.BlockSpec(memory_space=pltpu.SMEM)
-    whole = lambda *shape: pl.BlockSpec(shape, lambda i: (at, 0, 0))
-    all_out = lambda *shape: pl.BlockSpec(shape, lambda i: (0, 0, 0))
+    whole = lambda *shape: pl.BlockSpec(shape, lambda i: (0, 0, 0))
+    part = lambda *shape: pl.BlockSpec(shape, lambda i: (0, 0, first + i))
+    more = [pl.BlockSpec(memory_space=pl.ANY), whole(heads, hd, length), whole(heads, hd, length)]
     return pl.pallas_call(
-        functools.partial(attend_back_body, heads, hd),
-        grid=(blocks,),
+        functools.partial(attend_back_body, first, heads, hd),
+        grid=(count,),
         out_shape=tuple(jax.ShapeDtypeStruct((heads, hd, length), F32) for _ in range(3)),
         in_specs=[
             smem,
             smem,
-            pl.BlockSpec((heads, 2 * hd, BLK), lambda i: (at, 0, i)),
+            part(heads, 2 * hd, BLK),
             whole(heads, length, 2 * hd),
             whole(heads, hd, length),
             whole(heads, length, hd),
-            pl.BlockSpec((heads, hd, BLK), lambda i: (at, 0, i)),
-            pl.BlockSpec((heads, 1, BLK), lambda i: (at, 0, i)),
-            pl.BlockSpec((1, heads * hd, BLK), lambda i: (i, at, 0)),
+            part(heads, hd, BLK),
+            part(heads, 1, BLK),
+            pl.BlockSpec((1, heads * hd, BLK), lambda i: (first + i, 0, 0)),
+            *(more if before else []),
         ],
-        out_specs=(
-            pl.BlockSpec((heads, hd, BLK), lambda i: (0, 0, i)),
-            all_out(heads, hd, length),
-            all_out(heads, hd, length),
-        ),
+        out_specs=(part(heads, hd, BLK), whole(heads, hd, length), whole(heads, hd, length)),
+        input_output_aliases={9: 0} if before else {},
         compiler_params=params(),
-        cost_estimate=cost(11 * heads),
+        cost_estimate=cost(15),
         name="attention_backward",
-    )(meta, lengths, qt, ka, kt, v, of, ls, go)
+    )(meta, lengths, qt, ka, kt, v, of, ls, go, *(before or ()))
 
 
 def qkv_back_body(
     heads, hd, meta, x_ref, *refs
 ):
-    dqs, dks, dvs = refs[:heads], refs[heads : 2 * heads], refs[2 * heads : 3 * heads]
-    w_ref, g_ref, b_ref, gq_ref, gk_ref, vec2_ref, da_ref, db_ref, dw_ref, acc_ref, vec_ref, gain_ref = refs[3 * heads :]
+    dq_ref, dk_ref, dv_ref, w_ref, g_ref, b_ref, gq_ref, gk_ref, vec2_ref = refs[:9]
+    da_ref, db_ref, dw_ref, acc_ref, vec_ref, gain_ref = refs[9:]
     i = pl.program_id(0)
     wid = heads * hd
 
@@ -280,10 +290,10 @@
     first = (hat * g_ref[...] + b_ref[...]).astype(BF16)
     qk = mm(w_ref[: 2 * wid, :], first, NT)
     pieces = []
-    for at, gain, grad in ((0, gq_ref, dqs), (1, gk_ref, dks)):
+    for at, gain, grad in ((0, gq_ref, dq_ref), (1, gk_ref, dk_ref)):
         for h in range(heads):
             unit, inv = norm_cols(qk[at * wid + h * hd : at * wid + (h + 1) * hd])
-            gy = grad[h][0]
+            gy = grad[h]
             gain_ref[at] += gy * unit
             e = gy * gain[...]
             pieces.append(
@@ -295,7 +305,7 @@
                 )
             )
     for h in range(heads):
-        pieces.append(dvs[h][0])
+        pieces.append(dv_ref[h])
     grad = jnp.concatenate(pieces, axis=0).astype(BF16)
     acc_ref[...] += mm(grad, first)
     back = mm(grad, w_ref[...], TN)
@@ -334,7 +344,7 @@
     length, width = x.shape
     blocks = length // BLK
     whole = lambda *shape: pl.BlockSpec(shape, lambda i, m: (0,) * len(shape))
-    part = pl.BlockSpec((1, hd, BLK), lambda i, m: (0, 0, i))
+    part = pl.BlockSpec((heads, hd, BLK), lambda i, m: (0, 0, i))
     grads = pl.BlockSpec((1, BLK, width // 2), lambda i, m: (jnp.bitwise_xor(i, m[0]), 0, 0))
     return pl.pallas_call(
         functools.partial(qkv_back_body, heads, hd),
@@ -343,7 +353,9 @@
             grid=(blocks,),
             in_specs=[
                 pl.BlockSpec((BLK, width), lambda i, m: (i, 0)),
-                *([part] * (3 * heads)),
+                part,
+                part,
+                part,
                 whole(*w_t.shape),
                 whole(1, width),
                 whole(1, width),
@@ -370,7 +382,7 @@
         compiler_params=params(),
         cost_estimate=cost(17),
         name="qkv_backward",
-    )(meta, x, *dq, *dk, *dv, w_t, gain, bias, gq, gk, vec2)
+    )(meta, x, dq, dk, dv, w_t, gain, bias, gq, gk, vec2)
 
 
 def assemble_qkv(meta, pieces, heads, hd):
@@ -925,25 +937,29 @@
         down_k, down_s = down_grads(meta, act, dy, far_d)
         got = flip(down_s, *x), flip(up_s, *y), flip(out_s, *z)
     grad_o = tie(grad_o, up_k, up_s, out_k, out_s, down_k, down_s)[0]
-    head = lambda h, go: attend_back(meta, lengths, qt, ka, kt, v, attn_f, logsum, go, h, 1, hd)
-    parts = [None] * heads
-    parts[0] = head(0, grad_o)
-    grad_o, parts[0], *got = tie(grad_o, parts[0], *got)
+    go_back = lambda go, before: attend_back(
+        meta, lengths, qt, ka, kt, v, attn_f, logsum, go, heads, hd, before
+    )
+    with jax.named_scope("backward_attention"):
+        parts = go_back(grad_o, None)
+    parts, *got = tie(parts, *got)
     with jax.named_scope("weight_gradients"):
         down_k, down_s = next_half(down_k, got[0], y, 0)
         up_k, up_s = next_half(up_k, got[1], z, 1)
         out_k, out_s = next_half(out_k, got[2], x, 0)
         got = flip(down_s, *y), flip(up_s, *z), flip(out_s, *x)
-    for h in range(1, heads - 1):
-        parts[h] = head(h, grad_o)
-    grad_o, parts[1:-1], *got = tie(grad_o, parts[1:-1], *got)
+    with jax.named_scope("backward_attention"):
+        parts = go_back(grad_o, parts)
+    parts, *got = tie(parts, *got)
     with jax.named_scope("weight_gradients"):
         down_k, down_s = next_half(down_k, got[0], z, 1)
         up_k, up_s = next_half(up_k, got[1], x, 1)
         out_k, out_s = next_half(out_k, got[2], y, 1)
         got = flip(down_s, *z), flip(up_s, *x), flip(out_s, *y)
-    parts[-1] = head(heads - 1, grad_o)
-    parts[-1], *got = tie(parts[-1], *got)
+    with jax.named_scope("backward_attention"):
+        dq, dk, dv = parts
+        back_a, back_b, dw_t = qkv_back(meta, x_row, dq, dk, dv, w_t, g1, b1, gq, gk, vec2, heads, hd)
+    back_a, back_b, dw_t, *got = tie(back_a, back_b, dw_t, *got)
     with jax.named_scope("weight_gradients"):
         down, up, out = add(down_k, got[0]), add(up_k, got[1]), add(out_k, got[2])
         sizes = [down.shape[0], up.shape[0]]
@@ -951,11 +967,6 @@
         for mask in masks[2:]:
             pieces = add(pieces, flip(pieces, "seq", mask))
         down, up, out = jnp.split(pieces, [sizes[0], sizes[0] + sizes[1]])
-
-    with jax.named_scope("backward_attention"):
-        dq, dk, dv = zip(*parts)
-        back_a, back_b, dw_t = qkv_back(meta, x_row, dq, dk, dv, w_t, g1, b1, gq, gk, vec2, heads, hd)
-    back_a, back_b, dw_t, down, up, out = tie(back_a, back_b, dw_t, down, up, out)
 
     with jax.named_scope("first_round"):
         keep, send = halves(dw_t, core, 1)

time: 402 us -> 372 us (0.925)
  Pallas kernels: 185 us -> 146 us
  starting transfers between devices: 58.2 us -> 62.7 us
    pallas_call x3 -> x2, Pallas kernels: 52.8 us -> 30.1 us  [attend_back(): pl.pallas_call(functools.partial(attend_back_body, first, heads, hd), gri...]
    pallas_call x1, Pallas kernels: 30.1 us -> 13.7 us  [attend(): pl.pallas_call(functools.partial(attend_body, heads, hd), grid=(blocks,),...]
  transfers between devices with their start and end apart: 50 -> 50, of which waited for: 19 -> 21; matrix products, arithmetic and copies ran while one was open for 6% -> 7% of each run, Pallas kernels for 36% -> 28%
where the time goes in v7:
time: 372 us; the launch traced here: 369 us
  Pallas kernels  146 us (39%)
  waiting for transfers between devices  122 us (33%)
  starting transfers between devices  62.7 us (17%)
  local copies, waits for them, and re-layouts  21.9 us (6%)
  other arithmetic  15.3 us (4%)
    ppermute x48, waiting for transfers between devices, flip(): return lax.ppermute(value, axis, [(i, i ^ mask) for i in range(size)])  106 us
    ppermute x48, starting transfers between devices, flip(): return lax.ppermute(value, axis, [(i, i ^ mask) for i in range(size)])  53.6 us
    pallas_call x2, Pallas kernels, attend_back(): pl.pallas_call(functools.partial(attend_back_body, first, heads, hd), gri...  30.1 us
    pallas_call x1, Pallas kernels, ffn(): pl.pallas_call(body, grid_spec=pltpu.PrefetchScalarGridSpec(num_scalar_pr...  25.7 us
    pallas_call x1, Pallas kernels, qkv_back(): pl.pallas_call(functools.partial(qkv_back_body, heads, hd), grid_spec=plt...  17.6 us
    all_to_all x2, waiting for transfers between devices, exchange(): return lax.all_to_all(value, 'seq', 0, 0, tiled=True)  16.6 us
    pallas_call x2, Pallas kernels, up_out_grads(): pl.pallas_call(body, grid_spec=pltpu.PrefetchScalarGridSpec(num_scalar_pr...  15.6 us
    pallas_call x1, Pallas kernels, attend(): pl.pallas_call(functools.partial(attend_body, heads, hd), grid=(blocks,),...  13.7 us
  transfers between devices with their start and end apart: 50, of which 21 were waited for; matrix products, arithmetic and copies ran while one was open for 7% of the time, Pallas kernels for 28%

profile of v7, /device:TPU:0, one launch (start us, length us, event | category | flops | bytes accessed | tf_op | source)
XLA Modules:
  0.0 369.3 jit_solution(7860299877855297187)
XLA Ops:
  13.4 10.4 %collective-permute-done.4.refs_4_ = bf16[256,768]{1,0:T(8,128)(2,1)} collective-permute-done((bf16[256,768]{1,0:T(8,128)(2,1)S(1)}, bf16[256,768]{1,0:T(8,128)(2,1)}, u32[]{:S(2)}, u32[]{:S(2)}) %collective-permute-start.4) | collective-permute-done | bytes 393248 | tf_op jit(solution)/shard_map/ppermute | solution.py:807
  45.6 12.2 %qkv_forward.1 = (bf16[3,128,2048]{2,1,0:T(8,128)(2,1)}, bf16[3,2048,128]{2,1,0:T(8,128)(2,1)}, bf16[3,64,2048]{2,1,0:T(8,128)(2,1)}, bf16[3,2048,64]{2,1,0:T(8,...) custom-call(s32[6]{0:T(128)} %stack.46.meta, s32[2,8]{1,0:T(2,128)} %bitcast.107, ...), custom_call_target="tpu_custom_call" | custom-call | flops 4200000000 | bytes 1024 | tf_op jit(solution)/shard_map/forward_attention/qkv_forward/pallas_call | solution.py:104
  57.8 13.7 %attention_forward.1 = (bf16[8,192,256]{2,1,0:T(8,128)(2,1)}, f32[3,64,2048]{2,1,0:T(8,128)}, f32[3,1,2048]{2,1,0:T(1,128)}) custom-call(s32[6]{0:T(128)} %stack.46.meta, s32[2,8]{1,0:T(2,128)} %bitcast.108, bf16[3,128,2048]{2,1,0:T(8,128)(2,1)} %get-tuple-element.83.qt_ref.refs_0_, bf16[3,2048,128]{2,1,0:T(8,128)(2,1)} %get-tuple-element.84.ka_ref.refs_1_, ...), custom_call_target="tpu_custom_call" | custom-call | flops 8750000128 | bytes 1024 | tf_op jit(solution)/shard_map/forward_attention/attention_forward/pallas_call | solution.py:176
  71.6 5.3 %all-to-all-start = ((bf16[8,192,256]{2,1,0:T(8,128)(2,1)}), bf16[8,192,256]{2,1,0:T(8,128)(2,1)S(1)}, u32[]{:S(2)}, u32[]{:S(2)}) async-start(bf16[8,192,256]{2,1,0:T(8,128)(2,1)} %get-tuple-element.86), calls=%async_computation | async-start | bytes 1572864 | tf_op jit(solution)/shard_map/all_to_all | solution.py:897
  79.0 15.3 %all-to-all-done = bf16[8,192,256]{2,1,0:T(8,128)(2,1)S(1)} async-done(((bf16[8,192,256]{2,1,0:T(8,128)(2,1)}), bf16[8,192,256]{2,1,0:T(8,128)(2,1)S(1)}, u32[]{:S(2)}, u32[]{:S(2)}) %all-to-all-start) | async-done | bytes 786464 | tf_op jit(solution)/shard_map/all_to_all | solution.py:897
  95.3 25.7 %ffn_both_ways.1 = (bf16[512,768]{1,0:T(8,128)(2,1)}, f32[512,768]{1,0:T(8,128)}, bf16[512,768]{1,0:T(8,128)(2,1)}, bf16[512,768]{1,0:T(8,128)(2,1)}, bf16[512,3...) custom-call(s32[6]{0:T(128)} %stack.46.meta, ...), custom_call_target="tpu_custom_call" | custom-call | flops 8750000128 | bytes 1024 | tf_op jit(solution)/shard_map/feed_forward/ffn_both_ways/pallas_call | solution.py:524
  121.0 7.2 %up_out_gradient.2 = bf16[384,3840]{1,0:T(8,128)(2,1)} custom-call(s32[6]{0:T(128)} %stack.46.meta, bf16[2,768,256]{2,1,0:T(8,128)(2,1)} %bitcast.90, bf16[512,768]{1,0:T(8,128)(2,1)} %get-tuple-element.95.gb_ref, bf16[512,768]{1,0:T(8,128)(2,1)} %get-tuple-element.96.h2_ref, bf16[512,3072]{1,0:T(8,128)(2,1)} %get-tuple-element.97.dup_ref), custom_call_target="tpu_custom_call" | custom-call | flops 2449999872 | bytes 1024 | tf_op jit(solution)/shard_map/weight_gradients/up_out_gradient/pallas_call | solution.py:649
  128.2 5.7 %down_gradient.2 = bf16[1536,768]{1,0:T(8,128)(2,1)} custom-call(s32[6]{0:T(128)} %stack.46.meta, bf16[512,3072]{1,0:T(8,128)(2,1)} %get-tuple-element.102.act_ref, bf16[512,768]{1,0:T(8,128)(2,1)} %bitcast.105), custom_call_target="tpu_custom_call" | custom-call | flops 2100000000 | bytes 1024 | tf_op jit(solution)/shard_map/weight_gradients/down_gradient/pallas_call | solution.py:709
  138.9 6.4 %down_gradient.3 = (bf16[768,768]{1,0:T(8,128)(2,1)}, bf16[768,768]{1,0:T(8,128)(2,1)}) custom-call(s32[6]{0:T(128)} %stack.46.meta, bf16[512,3072]{1,0:T(8,128)(2,1)} %get-tuple-element.102.act_ref, bf16[512,768]{1,0:T(8,128)(2,1)} %bitcast.106, bf16[1536,768]{1,0:T(8,128)(2,1)} %collective-permute-done.15.rest_0_), custom_call_target="tpu_custom_call" | custom-call | flops 2100000000 | bytes 1024 | tf_op jit(solution)/shard_map/weight_gradients/down_gradient/pallas_call | solution.py:709
  146.2 8.4 %up_out_gradient.3 = (bf16[384,1536]{1,0:T(8,128)(2,1)}, bf16[384,1536]{1,0:T(8,128)(2,1)}, bf16[192,768]{1,0:T(8,128)(2,1)}, bf16[192,768]{1,0:T(8,128)(2,1)}) custom-call(s32[6]{0:T(128)} %stack.46.meta, bf16[2,768,256]{2,1,0:T(8,128)(2,1)} %bitcast.91, bf16[512,768]{1,0:T(8,128)(2,1)} %get-tuple-element.95.gb_ref, ...), custom_call_target="tpu_custom_call" | custom-call | flops 2449999872 | bytes 1024 | tf_op jit(solution)/shard_map/weight_gradients/up_out_gradient/pallas_call | solution.py:649
  159.3 16.3 %attention_backward.2 = (f32[3,64,2048]{2,1,0:T(8,128)}, f32[3,64,2048]{2,1,0:T(8,128)}, f32[3,64,2048]{2,1,0:T(8,128)}) custom-call(s32[6]{0:T(128)} %stack.46.meta, s32[2,8]{1,0:T(2,128)} %bitcast.109, bf16[3,128,2048]{2,1,0:T(8,128)(2,1)} %get-tuple-element.83.qt_ref.refs_0_, bf16[3,2048,128]{2,1,0:T(8,128)(2,1)} %get-tuple-element.84.ka_ref.refs_1_, ...), custom_call_target="tpu_custom_call" | custom-call | flops 5249999872 | bytes 1024 | tf_op jit(solution)/shard_map/backward_attention/attention_backward/pallas_call | solution.py:251
  175.7 7.2 %collective-permute-done.17 = bf16[384,1536]{1,0:T(8,128)(2,1)} collective-permute-done((bf16[384,1536]{1,0:T(8,128)(2,1)}, bf16[384,1536]{1,0:T(8,128)(2,1)}, u32[]{:S(2)}, u32[]{:S(2)}) %collective-permute-start.17) | collective-permute-done | bytes 1179680 | tf_op jit(solution)/shard_map/weight_gradients/ppermute | solution.py:807
  189.0 13.8 %attention_backward.3 = (f32[3,64,2048]{2,1,0:T(8,128)}, f32[3,64,2048]{2,1,0:T(8,128)}, f32[3,64,2048]{2,1,0:T(8,128)}) custom-call(s32[6]{0:T(128)} %stack.46.meta, s32[2,8]{1,0:T(2,128)} %bitcast.110, bf16[3,128,2048]{2,1,0:T(8,128)(2,1)} %get-tuple-element.83.qt_ref.refs_0_, ...), custom_call_target="tpu_custom_call", output_to_operand_aliasing={{0}: (9, {})} | custom-call | flops 5249999872 | bytes 1024 | tf_op jit(solution)/shard_map/backward_attention/attention_backward/pallas_call | solution.py:251
  211.1 17.6 %qkv_backward.1 = (bf16[8,256,384]{2,1,0:T(8,128)(2,1)}, bf16[8,256,384]{2,1,0:T(8,128)(2,1)}, bf16[608,768]{1,0:T(8,128)(2,1)}) custom-call(s32[6]{0:T(128)} %stack.46.meta, bf16[2048,768]{1,0:T(8,128)(2,1)} %get-tuple-element.89.x_ref, f32[3,64,2048]{2,1,0:T(8,128)} %get-tuple-element.118.refs_0_, f32[3,64,2048]{2,1,0:T(8,128)} %get-tuple-element.119.refs_1_, ...), custom_call_target="tpu_custom_call" | custom-call | flops 5950000128 | bytes 1024 | tf_op jit(solution)/shard_map/backward_attention/qkv_backward/pallas_call | solution.py:349
  241.3 23.3 %collective-permute-done.25 = bf16[864,384]{1,0:T(8,128)(2,1)S(1)} collective-permute-done((bf16[864,384]{1,0:T(8,128)(2,1)S(1)}, bf16[864,384]{1,0:T(8,128)(2,1)S(1)}, u32[]{:S(2)}, u32[]{:S(2)}) %collective-permute-start.25) | collective-permute-done | bytes 663584 | tf_op jit(solution)/shard_map/weight_gradients/ppermute | solution.py:807
  272.4 5.2 %collective-permute-done.26 = bf16[384,384]{1,0:T(8,128)(2,1)S(1)} collective-permute-done((bf16[384,384]{1,0:T(8,128)(2,1)S(1)}, bf16[384,384]{1,0:T(8,128)(2,1)S(1)}, u32[]{:S(2)}, u32[]{:S(2)}) %collective-permute-start.26) | collective-permute-done | bytes 294944 | tf_op jit(solution)/shard_map/first_round/ppermute | solution.py:807
  288.5 7.7 %collective-permute-done.36 = bf16[96,768]{1,0:T(8,128)(2,1)S(1)} collective-permute-done((bf16[96,768]{1,0:T(8,128)(2,1)S(1)}, bf16[96,768]{1,0:T(8,128)(2,1)S(1)}, u32[]{:S(2)}, u32[]{:S(2)}) %collective-permute-start.36) | collective-permute-done | bytes 147488 | tf_op jit(solution)/shard_map/second_round/ppermute | solution.py:807
  296.9 8.6 %collective-permute-done.39 = bf16[2,256,384]{2,1,0:T(8,128)(2,1)S(1)} collective-permute-done((bf16[2,256,384]{2,1,0:T(8,128)(2,1)S(1)}, bf16[2,256,384]{2,1,0:T(8,128)(2,1)S(1)}, u32[]{:S(2)}, u32[]{:S(2)}) %collective-permute-start.39) | collective-permute-done | bytes 393248 | tf_op jit(solution)/shard_map/second_round/ppermute | solution.py:807
  305.5 6.1 %collective-permute-done.38 = bf16[2,256,384]{2,1,0:T(8,128)(2,1)S(1)} collective-permute-done((bf16[2,256,384]{2,1,0:T(8,128)(2,1)S(1)}, bf16[2,256,384]{2,1,0:T(8,128)(2,1)S(1)}, u32[]{:S(2)}, u32[]{:S(2)}) %collective-permute-start.38) | collective-permute-done | bytes 393248 | tf_op jit(solution)/shard_map/second_round/ppermute | solution.py:807
  313.6 5.5 %collective-permute-done.41 = bf16[304,384]{1,0:T(8,128)(2,1)S(1)} collective-permute-done((bf16[304,384]{1,0:T(8,128)(2,1)S(1)}, bf16[304,384]{1,0:T(8,128)(2,1)S(1)}, u32[]{:S(2)}, u32[]{:S(2)}) %collective-permute-start.41) | collective-permute-done | bytes 233504 | tf_op jit(solution)/shard_map/third_round/ppermute | solution.py:807
  325.1 11.3 %collective-permute-done.42.p01 = bf16[2,304,384]{2,1,0:T(8,128)(2,1)} collective-permute-done((bf16[2,304,384]{2,1,0:T(8,128)(2,1)S(1)}, bf16[2,304,384]{2,1,0:T(8,128)(2,1)}, u32[]{:S(2)}, u32[]{:S(2)}) %collective-permute-start.42) | collective-permute-done | bytes 466976 | tf_op jit(solution)/shard_map/third_round/ppermute | solution.py:807
  344.7 5.5 %collective-permute-done.44.p11 = bf16[2,304,384]{2,1,0:T(8,128)(2,1)} collective-permute-done((bf16[2,304,384]{2,1,0:T(8,128)(2,1)}, bf16[2,304,384]{2,1,0:T(8,128)(2,1)}, u32[]{:S(2)}, u32[]{:S(2)}) %collective-permute-start.44) | collective-permute-done | bytes 466976 | tf_op jit(solution)/shard_map/third_round/ppermute | solution.py:807
  350.3 5.2 %first_projection_gradient.1 = (f32[384,2304]{1,0:T(8,128)}, f32[32,384]{1,0:T(8,128)}) custom-call(s32[6]{0:T(128)} %stack.46.meta, bf16[2,304,384]{2,1,0:T(8,128)(2,1)} %copy-done.11, bf16[2,304,384]{2,1,0:T(8,128)(2,1)} %collective-permute-done.42.p01, bf16[2,304,384]{2,1,0:T(8,128)(2,1)} %collective-permute-done.43.p10, ...), custom_call_target="tpu_custom_call" | custom-call | flops 1750000000 | bytes 1024 | tf_op jit(solution)/shard_map/first_projection_gradient/pallas_call | solution.py:416
  360.2 8.9 %weight_gradients.1 = (f32[1536,768]{1,0:T(8,128)}, f32[384,3072]{1,0:T(8,128)}, f32[384,768]{1,0:T(8,128)}) custom-call(s32[6]{0:T(128)} %stack.46.meta, bf16[384,768]{1,0:T(8,128)(2,1)} %copy-done.8, bf16[384,768]{1,0:T(8,128)(2,1)} %copy-done.27, bf16[384,768]{1,0:T(8,128)(2,1)} %collective-permute-done.34.down_ba, bf16[384,768]{1,0:T(8,128)(2,1)} %copy-done.28, ...), custom_call_target="tpu_custom_call" | custom-call | flops 2449999872 | bytes 1024 | tf_op jit(solution)/shard_map/weight_gradients/pallas_call | solution.py:759
  (221 shorter events, 115.1 us)
Async XLA Ops:
  1.9 21.9 %collective-permute-start.4 = (bf16[256,768]{1,0:T(8,128)(2,1)S(1)}, bf16[256,768]{1,0:T(8,128)(2,1)}, u32[]{:S(2)}, u32[]{:S(2)}) collective-permute-start(bf16[256,768]{1,0:T(8,128)(2,1)S(1)} %get-tuple-element.188), channel_id=1, source_target_pairs={{0,4},{1,5},{2,6},{3,7},{4,0},{5,1},{6,2},{7,3},{8,12},{9,13},{10,... | collective-permute-start | bytes 1179656 | tf_op jit(solution)/shard_map/ppermute | solution.py:807
  6.1 19.8 %collective-permute-start.1 = (bf16[256,768]{1,0:T(8,128)(2,1)S(1)}, bf16[256,768]{1,0:T(8,128)(2,1)S(1)}, u32[]{:S(2)}, u32[]{:S(2)}) collective-permute-start(bf16[256,768]{1,0:T(8,128)(2,1)S(1)} %get-tuple-element.189.refs_0_), channel_id=1, source_target_pairs={{0,2},{1,3},{2,0},{3,1},{4,6},{5,7},{6,4},{7,5},{8,10},{9,11},{10,... | collective-permute-start | bytes 1179656 | tf_op jit(solution)/shard_map/ppermute | solution.py:807
  12.2 25.8 %collective-permute-start.9 = (bf16[384,576]{0,1:T(8,128)(2,1)S(1)}, bf16[384,576]{0,1:T(8,128)(2,1)S(1)}, u32[]{:S(2)}, u32[]{:S(2)}) collective-permute-start(bf16[384,576]{0,1:T(8,128)(2,1)S(1)} %bitcast.84), channel_id=1, source_target_pairs={{0,8},{8,0},{1,9},{9,1},{2,10},{10,2},{3,11},{11,3},{4,12},{12,4},... | collective-permute-start | bytes 1327112 | tf_op jit(solution)/shard_map/ppermute | solution.py:807
  36.0 58.3 %collective-permute-start.12 = (bf16[384,3072]{1,0:T(8,128)(2,1)}, bf16[384,3072]{1,0:T(8,128)(2,1)}, u32[]{:S(2)}, u32[]{:S(2)}) collective-permute-start(bf16[384,3072]{1,0:T(8,128)(2,1)} %refs_8_.1), channel_id=1, source_target_pairs={{0,8},{8,0},{1,9},{9,1},{2,10},{10,2},{3,11},{11,3},{4,12},{12,4},... | collective-permute-start | bytes 7077896 | tf_op jit(solution)/shard_map/ppermute | solution.py:807
  40.6 53.7 %collective-permute-start.13 = (bf16[1536,768]{1,0:T(8,128)(2,1)}, bf16[1536,768]{1,0:T(8,128)(2,1)}, u32[]{:S(2)}, u32[]{:S(2)}) collective-permute-start(bf16[1536,768]{1,0:T(8,128)(2,1)} %refs_10_.1), channel_id=1, source_target_pairs={{0,8},{8,0},{1,9},{9,1},{2,10},{10,2},{3,11},{11,3},{4,12},{12,4},... | collective-permute-start | bytes 7077896 | tf_op jit(solution)/shard_map/ppermute | solution.py:807
  71.6 22.7 %all-to-all-start = ((bf16[8,192,256]{2,1,0:T(8,128)(2,1)}), bf16[8,192,256]{2,1,0:T(8,128)(2,1)S(1)}, u32[]{:S(2)}, u32[]{:S(2)}) async-start(bf16[8,192,256]{2,1,0:T(8,128)(2,1)} %get-tuple-element.86), calls=%async_computation | async-start | bytes 1572864 | tf_op jit(solution)/shard_map/all_to_all | solution.py:897
  134.4 24.1 %all-to-all-start.1 = ((bf16[8,192,256]{2,1,0:T(8,128)(2,1)}), bf16[8,192,256]{2,1,0:T(8,128)(2,1)S(1)}, u32[]{:S(2)}, u32[]{:S(2)}) async-start(bf16[8,192,256]{2,1,0:T(8,128)(2,1)} %bitcast.17), calls=%async_computation.1 | async-start | bytes 1572864 | tf_op jit(solution)/shard_map/all_to_all | solution.py:897
  145.3 30.4 %collective-permute-start.16 = (bf16[768,768]{1,0:T(8,128)(2,1)}, bf16[768,768]{1,0:T(8,128)(2,1)S(1)}, u32[]{:S(2)}, u32[]{:S(2)}) collective-permute-start(bf16[768,768]{1,0:T(8,128)(2,1)} %get-tuple-element.104), channel_id=1, source_target_pairs={{0,16},{16,0},{1,17},{17,1},{2,18},{18,2},{3,19},{19,3},{4,20},{20... | collective-permute-start | bytes 3538952 | tf_op jit(solution)/shard_map/weight_gradients/ppermute | solution.py:807
  154.6 28.3 %collective-permute-start.17 = (bf16[384,1536]{1,0:T(8,128)(2,1)}, bf16[384,1536]{1,0:T(8,128)(2,1)}, u32[]{:S(2)}, u32[]{:S(2)}) collective-permute-start(bf16[384,1536]{1,0:T(8,128)(2,1)} %get-tuple-element.99), channel_id=1, source_target_pairs={{0,1},{1,0},{2,3},{3,2},{4,5},{5,4},{6,7},{7,6},{8,9},{9,8},{10,11... | collective-permute-start | bytes 3538952 | tf_op jit(solution)/shard_map/weight_gradients/ppermute | solution.py:807
  156.0 19.7 %collective-permute-start.18 = (bf16[192,768]{1,0:T(8,128)(2,1)}, bf16[192,768]{1,0:T(8,128)(2,1)S(1)}, u32[]{:S(2)}, u32[]{:S(2)}) collective-permute-start(bf16[192,768]{1,0:T(8,128)(2,1)} %get-tuple-element.101), channel_id=1, source_target_pairs={{0,2},{1,3},{2,0},{3,1},{4,6},{5,7},{6,4},{7,5},{8,10},{9,11},{10,... | collective-permute-start | bytes 884744 | tf_op jit(solution)/shard_map/weight_gradients/ppermute | solution.py:807
  205.2 23.4 %collective-permute-start.24 = (bf16[96,384]{1,0:T(8,128)(2,1)}, bf16[96,384]{1,0:T(8,128)(2,1)}, u32[]{:S(2)}, u32[]{:S(2)}) collective-permute-start(bf16[96,384]{1,0:T(8,128)(2,1)} %constant_dynamic-slice_fusion.2), channel_id=1, source_target_pairs={{0,1},{1,0},{2,3},{3,2},{4,5},{5,4},{6,7},{7,6},{8,9},{9,8},{10,11... | collective-permute-start | bytes 221192 | tf_op jit(solution)/shard_map/weight_gradients/ppermute | solution.py:807
  207.4 21.3 %collective-permute-start.23 = (bf16[384,384]{1,0:T(8,128)(2,1)S(1)}, bf16[384,384]{1,0:T(8,128)(2,1)S(1)}, u32[]{:S(2)}, u32[]{:S(2)}) collective-permute-start(bf16[384,384]{1,0:T(8,128)(2,1)S(1)} %constant_dynamic-slice_fusion.3), channel_id=1, source_target_pairs={{0,16},{16,0},{1,17},{17,1},{2,18},{18,2},{3,19},{19,3},{4,20},{20... | collective-permute-start | bytes 884744 | tf_op jit(solution)/shard_map/weight_gradients/ppermute | solution.py:807
  209.7 18.9 %collective-permute-start.22 = (bf16[384,384]{1,0:T(8,128)(2,1)S(1)}, bf16[384,384]{1,0:T(8,128)(2,1)S(1)}, u32[]{:S(2)}, u32[]{:S(2)}) collective-permute-start(bf16[384,384]{1,0:T(8,128)(2,1)S(1)} %constant_dynamic-slice_fusion.4), channel_id=1, source_target_pairs={{0,2},{1,3},{2,0},{3,1},{4,6},{5,7},{6,4},{7,5},{8,10},{9,11},{10,... | collective-permute-start | bytes 884744 | tf_op jit(solution)/shard_map/weight_gradients/ppermute | solution.py:807
  231.0 33.6 %collective-permute-start.25 = (bf16[864,384]{1,0:T(8,128)(2,1)S(1)}, bf16[864,384]{1,0:T(8,128)(2,1)S(1)}, u32[]{:S(2)}, u32[]{:S(2)}) collective-permute-start(bf16[864,384]{1,0:T(8,128)(2,1)S(1)} %pad_maximum_fusion.1), channel_id=1, source_target_pairs={{0,4},{1,5},{2,6},{3,7},{4,0},{5,1},{6,2},{7,3},{8,12},{9,13},{10,... | collective-permute-start | bytes 1990664 | tf_op jit(solution)/shard_map/weight_gradients/ppermute | solution.py:807
  235.8 35.3 %collective-permute-start.31 = (bf16[2,2,256,384]{3,2,0,1:T(8,128)(2,1)}, bf16[2,2,256,384]{3,2,0,1:T(8,128)(2,1)}, u32[]{:S(2)}, u32[]{:S(2)}) collective-permute-start(bf16[2,2,256,384]{3,2,0,1:T(8,128)(2,1)} %bitcast.82), channel_id=1, source_target_pairs={{0,1},{1,0},{2,3},{3,2},{4,5},{5,4},{6,7},{7,6},{8,9},{9,8},{10,11... | collective-permute-start | bytes 2359304 | tf_op jit(solution)/shard_map/first_round/ppermute | solution.py:807
  238.4 34.0 %collective-permute-start.32 = (bf16[2,2,256,384]{3,2,0,1:T(8,128)(2,1)}, bf16[2,2,256,384]{3,2,0,1:T(8,128)(2,1)}, u32[]{:S(2)}, u32[]{:S(2)}) collective-permute-start(bf16[2,2,256,384]{3,2,0,1:T(8,128)(2,1)} %bitcast.81), channel_id=1, source_target_pairs={{0,2},{1,3},{2,0},{3,1},{4,6},{5,7},{6,4},{7,5},{8,10},{9,11},{10,... | collective-permute-start | bytes 2359304 | tf_op jit(solution)/shard_map/first_round/ppermute | solution.py:807
  240.1 26.7 %collective-permute-start.30 = (bf16[304,384]{1,0:T(8,128)(2,1)S(1)}, bf16[304,384]{1,0:T(8,128)(2,1)}, u32[]{:S(2)}, u32[]{:S(2)}) collective-permute-start(bf16[304,384]{1,0:T(8,128)(2,1)S(1)} %constant_dynamic-slice_fusion), channel_id=1, source_target_pairs={{0,16},{16,0},{1,17},{17,1},{2,18},{18,2},{3,19},{19,3},{4,20},{20... | collective-permute-start | bytes 700424 | tf_op jit(solution)/shard_map/first_round/ppermute | solution.py:807
  277.6 34.0 %collective-permute-start.33 = (bf16[384,768]{1,0:T(8,128)(2,1)S(1)}, bf16[384,768]{1,0:T(8,128)(2,1)S(1)}, u32[]{:S(2)}, u32[]{:S(2)}) collective-permute-start(bf16[384,768]{1,0:T(8,128)(2,1)S(1)} %pad_maximum_fusion.2.down_aa), channel_id=1, source_target_pairs={{0,1},{1,0},{2,3},{3,2},{4,5},{5,4},{6,7},{7,6},{8,9},{9,8},{10,11... | collective-permute-start | bytes 1769480 | tf_op jit(solution)/shard_map/second_round/ppermute | solution.py:807
  278.7 33.8 %collective-permute-start.34 = (bf16[384,768]{1,0:T(8,128)(2,1)S(1)}, bf16[384,768]{1,0:T(8,128)(2,1)}, u32[]{:S(2)}, u32[]{:S(2)}) collective-permute-start(bf16[384,768]{1,0:T(8,128)(2,1)S(1)} %pad_maximum_fusion.2.down_aa), channel_id=1, source_target_pairs={{0,16},{16,0},{1,17},{17,1},{2,18},{18,2},{3,19},{19,3},{4,20},{20... | collective-permute-start | bytes 1769480 | tf_op jit(solution)/shard_map/second_round/ppermute | solution.py:807
  284.6 27.1 %collective-permute-start.35 = (bf16[384,768]{1,0:T(8,128)(2,1)S(1)}, bf16[384,768]{1,0:T(8,128)(2,1)S(1)}, u32[]{:S(2)}, u32[]{:S(2)}) collective-permute-start(bf16[384,768]{1,0:T(8,128)(2,1)S(1)} %pad_maximum_fusion.3), channel_id=1, source_target_pairs={{0,2},{1,3},{2,0},{3,1},{4,6},{5,7},{6,4},{7,5},{8,10},{9,11},{10,... | collective-permute-start | bytes 1769480 | tf_op jit(solution)/shard_map/second_round/ppermute | solution.py:807
  319.4 39.9 %collective-permute-start.46 = (bf16[384,1536]{1,0:T(8,128)(2,1)S(1)}, bf16[384,1536]{1,0:T(8,128)(2,1)}, u32[]{:S(2)}, u32[]{:S(2)}) collective-permute-start(bf16[384,1536]{1,0:T(8,128)(2,1)S(1)} %pad_maximum_fusion.up_a), channel_id=1, source_target_pairs={{0,1},{1,0},{2,3},{3,2},{4,5},{5,4},{6,7},{7,6},{8,9},{9,8},{10,11... | collective-permute-start | bytes 3538952 | tf_op jit(solution)/shard_map/third_round/ppermute | solution.py:807
  324.0 20.8 %collective-permute-start.43 = (bf16[2,304,384]{2,1,0:T(8,128)(2,1)S(1)}, bf16[2,304,384]{2,1,0:T(8,128)(2,1)}, u32[]{:S(2)}, u32[]{:S(2)}) collective-permute-start(bf16[2,304,384]{2,1,0:T(8,128)(2,1)S(1)} %pad_maximum_fusion.4.p00), channel_id=1, source_target_pairs={{0,16},{16,0},{1,17},{17,1},{2,18},{18,2},{3,19},{19,3},{4,20},{20... | collective-permute-start | bytes 1400840 | tf_op jit(solution)/shard_map/third_round/ppermute | solution.py:807
  337.7 20.6 %collective-permute-start.47 = (bf16[192,768]{1,0:T(8,128)(2,1)S(1)}, bf16[192,768]{1,0:T(8,128)(2,1)S(1)}, u32[]{:S(2)}, u32[]{:S(2)}) collective-permute-start(bf16[192,768]{1,0:T(8,128)(2,1)S(1)} %pad_maximum_fusion.8.out_a), channel_id=1, source_target_pairs={{0,2},{1,3},{2,0},{3,1},{4,6},{5,7},{6,4},{7,5},{8,10},{9,11},{10,... | collective-permute-start | bytes 884744 | tf_op jit(solution)/shard_map/third_round/ppermute | solution.py:807
  338.3 21.0 %collective-permute-start.45 = (bf16[384,768]{1,0:T(8,128)(2,1)}, bf16[384,768]{1,0:T(8,128)(2,1)S(1)}, u32[]{:S(2)}, u32[]{:S(2)}) collective-permute-start(bf16[384,768]{1,0:T(8,128)(2,1)} %copy-done.27), channel_id=1, source_target_pairs={{0,16},{16,0},{1,17},{17,1},{2,18},{18,2},{3,19},{19,3},{4,20},{20... | collective-permute-start | bytes 1769480 | tf_op jit(solution)/shard_map/third_round/ppermute | solution.py:807
  (58 other events, 566.9 us)

commit v8 on v7

--- a/solution.py
+++ b/solution.py
@@ -55,17 +55,20 @@
     return out
 
 
-def qkv_body(heads, hd, meta, len_ref, *refs):
-    xs = refs[:8]
-    w_ref, g_ref, b_ref, gq_ref, gk_ref = refs[8:13]
-    qt_ref, ka_ref, kt_ref, v_ref, vt_ref, x_ref = refs[13:]
+def qkv_body(heads, hd, cuts, meta, len_ref, *refs):
+    xs = []
+    for count in cuts:
+        xs.append(refs[:count])
+        refs = refs[count:]
+    w_ref, g_ref, b_ref, gq_ref, gk_ref = refs[:5]
+    qt_ref, ka_ref, kt_ref, v_ref, vt_ref, x_ref = refs[5:]
     wid = heads * hd
     spot, row = meta[0], meta[1]
     bounds = bounds_of(len_ref, row)
     for s in range(8):
         c = jnp.bitwise_xor(spot, s)
         cols = pl.ds(pl.multiple_of(c * BLK, BLK), BLK)
-        x = xs[s][...]
+        x = jnp.concatenate([ref[...] for ref in xs[s]], axis=0) if len(xs[s]) > 1 else xs[s][0][...]
         x_ref[cols, :] = x
         hat, _ = norm_rows(x.astype(F32))
         first = (hat * g_ref[...] + b_ref[...]).astype(BF16)
@@ -97,12 +100,13 @@
 
 
 def make_qkv(meta, lengths, slots, w_t, gain, bias, gq, gk, heads, hd):
-    length = 8 * slots[0].shape[0]
-    width = slots[0].shape[1]
+    length = 8 * sum(one.shape[0] for one in slots[0])
+    width = slots[0][0].shape[1]
+    cuts = tuple(len(one) for one in slots)
     smem = pl.BlockSpec(memory_space=pltpu.SMEM)
     vmem = pl.BlockSpec(memory_space=pltpu.VMEM)
     return pl.pallas_call(
-        functools.partial(qkv_body, heads, hd),
+        functools.partial(qkv_body, heads, hd, cuts),
         out_shape=(
             jax.ShapeDtypeStruct((heads, 2 * hd, length), BF16),
             jax.ShapeDtypeStruct((heads, length, 2 * hd), BF16),
@@ -111,12 +115,12 @@
             jax.ShapeDtypeStruct((heads, hd, length), BF16),
             jax.ShapeDtypeStruct((length, width), BF16),
         ),
-        in_specs=[smem, smem] + [vmem] * 13,
+        in_specs=[smem, smem] + [vmem] * (sum(cuts) + 5),
         out_specs=(vmem,) * 6,
         compiler_params=params(),
         cost_estimate=cost(12),
         name="qkv_forward",
-    )(meta, lengths, *slots, w_t, gain, bias, gq, gk)
+    )(meta, lengths, *sum(slots, ()), w_t, gain, bias, gq, gk)
 
 
 def block_range(bounds, i):
@@ -323,16 +327,13 @@
         lane = lax.broadcasted_iota(jnp.int32, (hd, width), 1)
         item = lax.broadcasted_iota(jnp.int32, (hd, width), 0)
         spread = jnp.where(item < hd // 2, item, item - hd // 2 + width // 2)
-        line = jnp.zeros((8, width), F32)
         for k in range(2):
             total = lax.dot_general(
                 jnp.ones((8, BLK), F32), gain_ref[k], NT, precision=lax.Precision.HIGHEST, preferred_element_type=F32
             )
-            pick = (lane == spread + k * (hd // 2)).astype(F32)
-            line = line + lax.dot_general(
-                total, pick, NN, precision=lax.Precision.HIGHEST, preferred_element_type=F32
-            )
-        lines.append(line[:1])
+            pick = (lane == spread).astype(F32)
+            line = lax.dot_general(total, pick, NN, precision=lax.Precision.HIGHEST, preferred_element_type=F32)
+            lines.append(line[:1])
         place = lax.broadcasted_iota(jnp.int32, (EXTRA, width), 0)
         below = jnp.zeros((EXTRA, width), F32)
         for k, one in enumerate(lines):
@@ -389,9 +390,11 @@
     _, part, half = pieces[0].shape
     team = 4
     wid = heads * hd
+    sizes = [half] * 4 + [hd // 2] * 2
     turned = team * wid
 
-    def body(meta, p00, p01, p10, p11, out_ref, vec_ref, all_s):
+    def body(meta, p00, p01, p10, p11, out_ref, *refs):
+        vec_refs, all_s = refs[:-1], refs[-1]
         t = pl.program_id(0)
 
         @pl.when(t == 0)
@@ -406,7 +409,8 @@
             total = jnp.zeros((EXTRA, half), F32)
             for p in range(team):
                 total = total + all_s[p, 3 * wid :, :].astype(F32)
-            vec_ref[...] = total
+            for k, ref in enumerate(vec_refs):
+                ref[...] = total[k : k + 1, : ref.shape[1]]
 
         rows = pl.ds(pl.multiple_of(t * wid, wid), wid)
         piece = jnp.concatenate([all_s[p, rows, :] for p in range(team)], axis=0)
@@ -419,10 +423,13 @@
             num_scalar_prefetch=1,
             grid=(3,),
             in_specs=[whole(2, part, half)] * 4,
-            out_specs=(pl.BlockSpec((half, turned), lambda i, m: (0, i)), whole(EXTRA, half)),
+            out_specs=(pl.BlockSpec((half, turned), lambda i, m: (0, i)), *(whole(1, k) for k in sizes)),
             scratch_shapes=[pltpu.VMEM((team, 2 * part, half), BF16)],
         ),
-        out_shape=(jax.ShapeDtypeStruct((half, 3 * turned), F32), jax.ShapeDtypeStruct((EXTRA, half), F32)),
+        out_shape=(
+            jax.ShapeDtypeStruct((half, 3 * turned), F32),
+            *(jax.ShapeDtypeStruct((1, k), F32) for k in sizes),
+        ),
         compiler_params=params(),
         cost_estimate=cost(5),
         name="first_projection_gradient",
@@ -473,7 +480,7 @@
                 acc_s[rows, :] = mid
                 hat, _ = norm_rows(mid)
                 second = (hat * g_ref[...] + b_ref[...]).astype(BF16)
-                h2_ref[rows, :] = second
+                h2_ref[:, rows] = jnp.transpose(hat * g_ref[...] + b_ref[...]).astype(BF16)
                 lo, hi = second[:, :half], second[:, half:]
                 own_s[rows, :] = jnp.where(zero, lo, hi)
                 peer_s[rows, :] = jnp.where(zero, hi, lo)
@@ -544,7 +551,7 @@
                 whole(tokens, width),
                 whole(tokens, width),
                 whole(tokens, width),
-                whole(tokens, width),
+                whole(width, tokens),
                 acts,
                 acts,
                 whole(*attn_t.shape),
@@ -563,7 +570,7 @@
             jax.ShapeDtypeStruct((tokens, width), BF16),
             jax.ShapeDtypeStruct((tokens, width), F32),
             jax.ShapeDtypeStruct((tokens, width), BF16),
-            jax.ShapeDtypeStruct((tokens, width), BF16),
+            jax.ShapeDtypeStruct((width, tokens), BF16),
             jax.ShapeDtypeStruct((tokens, hidden), BF16),
             jax.ShapeDtypeStruct((tokens, hidden), BF16),
             jax.ShapeDtypeStruct(attn_t.shape, BF16),
@@ -592,8 +599,7 @@
         side = meta[2] if own else 1 - meta[2]
 
         def up():
-            part = jnp.where(side == 0, h2_ref[:, :half], h2_ref[:, half:])
-            return mm(part, dup_ref[...], TN)
+            return mm(h2_ref[pl.ds(pl.multiple_of(side * half, half), half), :], dup_ref[...])
 
         def out():
             rows = pl.ds(pl.multiple_of(side * half, half), half)
@@ -654,7 +660,7 @@
             in_specs=[
                 whole(*attn_t.shape),
                 whole(tokens, width),
-                whole(tokens, width),
+                whole(width, tokens),
                 pl.BlockSpec((tokens, width), lambda j, m: (0, column(j, m))),
                 *([block(lambda j, m: (0, j))] if own else []),
             ],
@@ -662,7 +668,7 @@
         ),
         out_shape=out_shape,
         compiler_params=params(),
-        cost_estimate=cost(7),
+        cost_estimate=cost(0.2),
         name="up_out_gradient",
     )(meta, attn_t, gb, h2, dup, *([far] if own else []))
 
@@ -720,7 +726,7 @@
         ),
         out_shape=out_shape,
         compiler_params=params(),
-        cost_estimate=cost(6),
+        cost_estimate=cost(0.2),
         name="down_gradient",
     )(meta, act, dy, *([far] if own else []))
 
@@ -867,15 +873,15 @@
     if direct:
         near = lax.dynamic_index_in_dim(mine, row, 0, keepdims=False)
         away = lax.dynamic_index_in_dim(mine, 1 - row, 0, keepdims=False)
-        far = flip(away, "seq", 4)
         cut = local // 2
-
-        def spread(own):
-            one, two = flip(own, "seq", 1), flip(own, "seq", 2)
-            three = jnp.concatenate([flip(two[:cut], "seq", 1), flip(one[cut:], "seq", 2)], axis=0)
-            return [own, one, two, three]
-
-        slots = spread(near) + spread(far)
+        far = flip(away[:cut], "seq", 4), flip(away[cut:], "seq", 4)
+        one, two = flip(near, "seq", 1), flip(near, "seq", 2)
+        three = flip(two[:cut], "seq", 1), flip(one[cut:], "seq", 2)
+        slots = [(near,), (one,), (two,), three]
+        one = tuple(flip(part, "seq", 1) for part in far)
+        two = tuple(flip(part, "seq", 2) for part in far)
+        three = flip(two[0], "seq", 1), flip(one[1], "seq", 2)
+        slots += [far, one, two, three]
         spot = idx
     else:
         same_member = [[q * team + p for q in range(every)] for p in range(team)]
@@ -883,7 +889,7 @@
         got = lax.all_to_all(mine, "seq", 0, 0, axis_index_groups=same_member, tiled=True)
         got = lax.all_gather(got, "seq", axis_index_groups=same_row)
         whole = jnp.swapaxes(got, 0, 1).reshape(length, width)
-        slots = [whole[s * (length // 8) : (s + 1) * (length // 8)] for s in range(8)]
+        slots = [(whole[s * (length // 8) : (s + 1) * (length // 8)],) for s in range(8)]
         spot = jnp.int32(0)
     meta = jnp.stack([spot, row, core, bit("rep", 1), bit("seq", 1), bit("seq", 2)]).astype(jnp.int32)
 
@@ -956,17 +962,18 @@
         up_k, up_s = next_half(up_k, got[1], x, 1)
         out_k, out_s = next_half(out_k, got[2], y, 1)
         got = flip(down_s, *z), flip(up_s, *x), flip(out_s, *y)
-    with jax.named_scope("backward_attention"):
-        dq, dk, dv = parts
-        back_a, back_b, dw_t = qkv_back(meta, x_row, dq, dk, dv, w_t, g1, b1, gq, gk, vec2, heads, hd)
-    back_a, back_b, dw_t, *got = tie(back_a, back_b, dw_t, *got)
+    parts, *got = tie(parts, *got)
     with jax.named_scope("weight_gradients"):
         down, up, out = add(down_k, got[0]), add(up_k, got[1]), add(out_k, got[2])
         sizes = [down.shape[0], up.shape[0]]
         pieces = jnp.concatenate([down, up, out])
         for mask in masks[2:]:
             pieces = add(pieces, flip(pieces, "seq", mask))
-        down, up, out = jnp.split(pieces, [sizes[0], sizes[0] + sizes[1]])
+    with jax.named_scope("backward_attention"):
+        dq, dk, dv = parts
+        back_a, back_b, dw_t = qkv_back(meta, x_row, dq, dk, dv, w_t, g1, b1, gq, gk, vec2, heads, hd)
+    dw_t, pieces = tie(dw_t, pieces)
+    down, up, out = jnp.split(pieces, [sizes[0], sizes[0] + sizes[1]])
 
     with jax.named_scope("first_round"):
         keep, send = halves(dw_t, core, 1)
@@ -1017,9 +1024,9 @@
         pieces = [piece, piece_z, flip(piece, *x), flip(piece_z, *x)]
         ups, outs = (up, flip(up, *y)), (out, flip(out, *z))
     grad_tokens = finish(x_home, grad_mid, back, g1)
-    grad_qkv, small = assemble_qkv(meta, pieces, heads, hd)
+    grad_qkv, *cuts = assemble_qkv(meta, pieces, heads, hd)
     grad_down, grad_up, grad_out = assemble(meta, downs, ups, outs)
-    cuts = [small[0], small[1], small[2], small[3], small[4, : hd // 2], small[4, hd // 2 : hd]]
+    cuts = [one.reshape(-1) for one in cuts]
     shape = tokens.shape
     return (
         output.reshape(shape), grad_tokens.reshape(shape), cuts[0], cuts[1], grad_qkv, cuts[4], cuts[5],

time: 372 us -> 377 us (1.013)
  waiting for transfers between devices: 122 us -> 130 us
  starting transfers between devices: 62.7 us -> 57.9 us
    ppermute x48 -> x51, waiting for transfers between devices: 106 us -> 113 us  [flip(): return lax.ppermute(value, axis, [(i, i ^ mask) for i in range(size)])]
    pallas_call x0 -> x4, other arithmetic: none -> 5.09 us  [assemble_qkv(): pl.pallas_call(body, grid_spec=pltpu.PrefetchScalarGridSpec(num_scalar_pr...]
    ppermute x48 -> x51, starting transfers between devices: 53.6 us -> 49.6 us  [flip(): return lax.ppermute(value, axis, [(i, i ^ mask) for i in range(size)])]
    unnamed x72 -> x82, local copies, waits for them, and re-layouts: 11.5 us -> 11.1 us
  transfers between devices with their start and end apart: 50 -> 53, of which waited for: 21 -> 20; matrix products, arithmetic and copies ran while one was open for 7% -> 8% of each run, Pallas kernels for 28% -> 28%
where the time goes in v8:
time: 377 us; the launch traced here: 375 us
  Pallas kernels  148 us (39%)
  waiting for transfers between devices  130 us (34%)
  starting transfers between devices  57.9 us (15%)
  local copies, waits for them, and re-layouts  19.1 us (5%)
  other arithmetic  18.1 us (5%)
    ppermute x51, waiting for transfers between devices, flip(): return lax.ppermute(value, axis, [(i, i ^ mask) for i in range(size)])  113 us
    ppermute x51, starting transfers between devices, flip(): return lax.ppermute(value, axis, [(i, i ^ mask) for i in range(size)])  49.6 us
    pallas_call x2, Pallas kernels, attend_back(): pl.pallas_call(functools.partial(attend_back_body, first, heads, hd), gri...  31.2 us
    pallas_call x1, Pallas kernels, ffn(): pl.pallas_call(body, grid_spec=pltpu.PrefetchScalarGridSpec(num_scalar_pr...  25.8 us
    pallas_call x1, Pallas kernels, qkv_back(): pl.pallas_call(functools.partial(qkv_back_body, heads, hd), grid_spec=plt...  17.9 us
    all_to_all x2, waiting for transfers between devices, exchange(): return lax.all_to_all(value, 'seq', 0, 0, tiled=True)  17.1 us
    pallas_call x2, Pallas kernels, up_out_grads(): pl.pallas_call(body, grid_spec=pltpu.PrefetchScalarGridSpec(num_scalar_pr...  15.4 us
    pallas_call x1, Pallas kernels, attend(): pl.pallas_call(functools.partial(attend_body, heads, hd), grid=(blocks,),...  14.3 us
  transfers between devices with their start and end apart: 53, of which 20 were waited for; matrix products, arithmetic and copies ran while one was open for 8% of the time, Pallas kernels for 28%

profile of v8, /device:TPU:0, one launch (start us, length us, event | category | flops | bytes accessed | tf_op | source)
XLA Modules:
  0.0 374.8 jit_solution(3731386156416467902)
XLA Ops:
  13.8 13.5 %collective-permute-done.4.refs_5_ = bf16[128,768]{1,0:T(8,128)(2,1)S(1)} collective-permute-done((bf16[128,768]{1,0:T(8,128)(2,1)S(1)}, bf16[128,768]{1,0:T(8,128)(2,1)S(1)}, u32[]{:S(2)}, u32[]{:S(2)}) %collective-permute-start.4) | collective-permute-done | bytes 196640 | tf_op jit(solution)/shard_map/ppermute | solution.py:813
  35.3 7.4 %collective-permute-done.7.refs_8_ = bf16[128,768]{1,0:T(8,128)(2,1)S(1)} collective-permute-done((bf16[128,768]{1,0:T(8,128)(2,1)S(1)}, bf16[128,768]{1,0:T(8,128)(2,1)S(1)}, u32[]{:S(2)}, u32[]{:S(2)}) %collective-permute-start.7) | collective-permute-done | bytes 196640 | tf_op jit(solution)/shard_map/ppermute | solution.py:813
  51.1 12.3 %qkv_forward.1 = (bf16[3,128,2048]{2,1,0:T(8,128)(2,1)}, bf16[3,2048,128]{2,1,0:T(8,128)(2,1)}, bf16[3,64,2048]{2,1,0:T(8,128)(2,1)}, bf16[3,2048,64]{2,1,0:T(8,...) custom-call(s32[6]{0:T(128)} %stack.46.meta, s32[2,8]{1,0:T(2,128)} %bitcast.108, ...), custom_call_target="tpu_custom_call" | custom-call | flops 4200000000 | bytes 1024 | tf_op jit(solution)/shard_map/forward_attention/qkv_forward/pallas_call | solution.py:108
  63.5 14.3 %attention_forward.1 = (bf16[8,192,256]{2,1,0:T(8,128)(2,1)}, f32[3,64,2048]{2,1,0:T(8,128)}, f32[3,1,2048]{2,1,0:T(1,128)}) custom-call(s32[6]{0:T(128)} %stack.46.meta, s32[2,8]{1,0:T(2,128)} %bitcast.109, bf16[3,128,2048]{2,1,0:T(8,128)(2,1)} %get-tuple-element.90.qt_ref.refs_0_, bf16[3,2048,128]{2,1,0:T(8,128)(2,1)} %get-tuple-element.91.ka_ref.refs_1_, ...), custom_call_target="tpu_custom_call" | custom-call | flops 8750000128 | bytes 1024 | tf_op jit(solution)/shard_map/forward_attention/attention_forward/pallas_call | solution.py:180
  83.7 17.1 %all-to-all-done = bf16[8,192,256]{2,1,0:T(8,128)(2,1)S(1)} async-done(((bf16[8,192,256]{2,1,0:T(8,128)(2,1)}), bf16[8,192,256]{2,1,0:T(8,128)(2,1)S(1)}, u32[]{:S(2)}, u32[]{:S(2)}) %all-to-all-start) | async-done | bytes 786464 | tf_op jit(solution)/shard_map/all_to_all | solution.py:903
  101.7 25.8 %ffn_both_ways.1 = (bf16[512,768]{1,0:T(8,128)(2,1)}, f32[512,768]{1,0:T(8,128)}, bf16[512,768]{1,0:T(8,128)(2,1)}, bf16[768,512]{1,0:T(8,128)(2,1)}, bf16[512,3...) custom-call(s32[6]{0:T(128)} %stack.46.meta, ...), custom_call_target="tpu_custom_call" | custom-call | flops 8750000128 | bytes 1024 | tf_op jit(solution)/shard_map/feed_forward/ffn_both_ways/pallas_call | solution.py:531
  127.5 7.1 %up_out_gradient.2 = bf16[384,3840]{1,0:T(8,128)(2,1)} custom-call(s32[6]{0:T(128)} %stack.46.meta, bf16[2,768,256]{2,1,0:T(8,128)(2,1)} %bitcast.84, bf16[512,768]{1,0:T(8,128)(2,1)} %get-tuple-element.102.gb_ref, bf16[768,512]{1,0:T(8,128)(2,1)} %get-tuple-element.103.h2_ref, bf16[512,3072]{1,0:T(8,128)(2,1)} %get-tuple-element.104.dup_ref), custom_call_target="tpu_custom_call" | custom-call | flops 70000000 | bytes 1024 | tf_op jit(solution)/shard_map/weight_gradients/up_out_gradient/pallas_call | solution.py:655
  134.6 5.7 %down_gradient.2 = bf16[1536,768]{1,0:T(8,128)(2,1)} custom-call(s32[6]{0:T(128)} %stack.46.meta, bf16[512,3072]{1,0:T(8,128)(2,1)} %get-tuple-element.109.act_ref, bf16[512,768]{1,0:T(8,128)(2,1)} %bitcast.87), custom_call_target="tpu_custom_call" | custom-call | flops 70000000 | bytes 1024 | tf_op jit(solution)/shard_map/weight_gradients/down_gradient/pallas_call | solution.py:715
  145.3 6.4 %down_gradient.3 = (bf16[768,768]{1,0:T(8,128)(2,1)}, bf16[768,768]{1,0:T(8,128)(2,1)}) custom-call(s32[6]{0:T(128)} %stack.46.meta, bf16[512,3072]{1,0:T(8,128)(2,1)} %get-tuple-element.109.act_ref, bf16[512,768]{1,0:T(8,128)(2,1)} %bitcast.88, bf16[1536,768]{1,0:T(8,128)(2,1)} %collective-permute-done.18.rest_0_), custom_call_target="tpu_custom_call" | custom-call | flops 70000000 | bytes 1024 | tf_op jit(solution)/shard_map/weight_gradients/down_gradient/pallas_call | solution.py:715
  156.3 8.3 %up_out_gradient.3 = (bf16[384,1536]{1,0:T(8,128)(2,1)}, bf16[384,1536]{1,0:T(8,128)(2,1)}, bf16[192,768]{1,0:T(8,128)(2,1)}, bf16[192,768]{1,0:T(8,128)(2,1)}) custom-call(s32[6]{0:T(128)} %stack.46.meta, bf16[2,768,256]{2,1,0:T(8,128)(2,1)} %bitcast.85, bf16[512,768]{1,0:T(8,128)(2,1)} %get-tuple-element.102.gb_ref, ...), custom_call_target="tpu_custom_call" | custom-call | flops 70000000 | bytes 1024 | tf_op jit(solution)/shard_map/weight_gradients/up_out_gradient/pallas_call | solution.py:655
  167.8 15.3 %attention_backward.2 = (f32[3,64,2048]{2,1,0:T(8,128)}, f32[3,64,2048]{2,1,0:T(8,128)}, f32[3,64,2048]{2,1,0:T(8,128)}) custom-call(s32[6]{0:T(128)} %stack.46.meta, s32[2,8]{1,0:T(2,128)} %bitcast.110, bf16[3,128,2048]{2,1,0:T(8,128)(2,1)} %get-tuple-element.90.qt_ref.refs_0_, bf16[3,2048,128]{2,1,0:T(8,128)(2,1)} %get-tuple-element.91.ka_ref.refs_1_, ...), custom_call_target="tpu_custom_call" | custom-call | flops 5249999872 | bytes 1024 | tf_op jit(solution)/shard_map/backward_attention/attention_backward/pallas_call | solution.py:255
  183.1 9.8 %collective-permute-done.20 = bf16[384,1536]{1,0:T(8,128)(2,1)S(1)} collective-permute-done((bf16[384,1536]{1,0:T(8,128)(2,1)}, bf16[384,1536]{1,0:T(8,128)(2,1)S(1)}, u32[]{:S(2)}, u32[]{:S(2)}) %collective-permute-start.20) | collective-permute-done | bytes 1179680 | tf_op jit(solution)/shard_map/weight_gradients/ppermute | solution.py:813
  197.9 16.0 %attention_backward.3 = (f32[3,64,2048]{2,1,0:T(8,128)}, f32[3,64,2048]{2,1,0:T(8,128)}, f32[3,64,2048]{2,1,0:T(8,128)}) custom-call(s32[6]{0:T(128)} %stack.46.meta, s32[2,8]{1,0:T(2,128)} %bitcast.111, bf16[3,128,2048]{2,1,0:T(8,128)(2,1)} %get-tuple-element.90.qt_ref.refs_0_, ...), custom_call_target="tpu_custom_call", output_to_operand_aliasing={{0}: (9, {})} | custom-call | flops 5249999872 | bytes 1024 | tf_op jit(solution)/shard_map/backward_attention/attention_backward/pallas_call | solution.py:255
  225.4 5.3 %collective-permute-start.28 = (bf16[864,384]{1,0:T(8,128)(2,1)S(1)}, bf16[864,384]{1,0:T(8,128)(2,1)S(1)}, u32[]{:S(2)}, u32[]{:S(2)}) collective-permute-start(bf16[864,384]{1,0:T(8,128)(2,1)S(1)} %pad_maximum_fusion.1), channel_id=1, source_target_pairs={{0,4},{1,5},{2,6},{3,7},{4,0},{5,1},{6,2},{7,3},{8,12},{9,13},{10,... | collective-permute-start | bytes 1990664 | tf_op jit(solution)/shard_map/weight_gradients/ppermute | solution.py:813
  230.6 17.9 %qkv_backward.1 = (bf16[8,256,384]{2,1,0:T(8,128)(2,1)}, bf16[8,256,384]{2,1,0:T(8,128)(2,1)}, bf16[608,768]{1,0:T(8,128)(2,1)}) custom-call(s32[6]{0:T(128)} %stack.46.meta, bf16[2048,768]{1,0:T(8,128)(2,1)} %get-tuple-element.96.x_ref, f32[3,64,2048]{2,1,0:T(8,128)} %get-tuple-element.131.refs_0_, f32[3,64,2048]{2,1,0:T(8,128)} %get-tuple-element.132.refs_1_, ...), custom_call_target="tpu_custom_call" | custom-call | flops 5950000128 | bytes 1024 | tf_op jit(solution)/shard_map/backward_attention/qkv_backward/pallas_call | solution.py:350
  264.9 11.8 %collective-permute-done.35 = bf16[2,2,256,384]{3,2,0,1:T(8,128)(2,1)} collective-permute-done((bf16[2,2,256,384]{3,2,0,1:T(8,128)(2,1)}, bf16[2,2,256,384]{3,2,0,1:T(8,128)(2,1)}, u32[]{:S(2)}, u32[]{:S(2)}) %collective-permute-start.35) | collective-permute-done | bytes 786464 | tf_op jit(solution)/shard_map/first_round/ppermute | solution.py:813
  276.7 5.7 %collective-permute-done.29 = bf16[384,384]{1,0:T(8,128)(2,1)S(1)} collective-permute-done((bf16[384,384]{1,0:T(8,128)(2,1)S(1)}, bf16[384,384]{1,0:T(8,128)(2,1)S(1)}, u32[]{:S(2)}, u32[]{:S(2)}) %collective-permute-start.29) | collective-permute-done | bytes 294944 | tf_op jit(solution)/shard_map/first_round/ppermute | solution.py:813
  291.0 10.5 %collective-permute-done.39 = bf16[96,768]{1,0:T(8,128)(2,1)S(1)} collective-permute-done((bf16[96,768]{1,0:T(8,128)(2,1)S(1)}, bf16[96,768]{1,0:T(8,128)(2,1)S(1)}, u32[]{:S(2)}, u32[]{:S(2)}) %collective-permute-start.39) | collective-permute-done | bytes 147488 | tf_op jit(solution)/shard_map/second_round/ppermute | solution.py:813
  302.9 8.2 %collective-permute-done.42 = bf16[2,256,384]{2,1,0:T(8,128)(2,1)S(1)} collective-permute-done((bf16[2,256,384]{2,1,0:T(8,128)(2,1)S(1)}, bf16[2,256,384]{2,1,0:T(8,128)(2,1)S(1)}, u32[]{:S(2)}, u32[]{:S(2)}) %collective-permute-start.42) | collective-permute-done | bytes 393248 | tf_op jit(solution)/shard_map/second_round/ppermute | solution.py:813
  317.1 5.7 %collective-permute-done.44 = bf16[304,384]{1,0:T(8,128)(2,1)S(1)} collective-permute-done((bf16[304,384]{1,0:T(8,128)(2,1)S(1)}, bf16[304,384]{1,0:T(8,128)(2,1)S(1)}, u32[]{:S(2)}, u32[]{:S(2)}) %collective-permute-start.44) | collective-permute-done | bytes 233504 | tf_op jit(solution)/shard_map/third_round/ppermute | solution.py:813
  327.5 13.3 %collective-permute-done.45.p01 = bf16[2,304,384]{2,1,0:T(8,128)(2,1)} collective-permute-done((bf16[2,304,384]{2,1,0:T(8,128)(2,1)S(1)}, bf16[2,304,384]{2,1,0:T(8,128)(2,1)}, u32[]{:S(2)}, u32[]{:S(2)}) %collective-permute-start.45) | collective-permute-done | bytes 466976 | tf_op jit(solution)/shard_map/third_round/ppermute | solution.py:813
  348.5 6.2 %collective-permute-done.47.p11 = bf16[2,304,384]{2,1,0:T(8,128)(2,1)} collective-permute-done((bf16[2,304,384]{2,1,0:T(8,128)(2,1)}, bf16[2,304,384]{2,1,0:T(8,128)(2,1)}, u32[]{:S(2)}, u32[]{:S(2)}) %collective-permute-start.47) | collective-permute-done | bytes 466976 | tf_op jit(solution)/shard_map/third_round/ppermute | solution.py:813
  354.7 5.2 %first_projection_gradient.1 = (f32[384,2304]{1,0:T(8,128)}, f32[1,384]{1,0:T(1,128)}, f32[1,384]{1,0:T(1,128)}, f32[1,384]{1,0:T(1,128)}, f32[1,384]{1,0:T(1,128)}, /*index=5*/f32[1,32]{1,0:T(1,128)}, f32[1,32]{1,0:T(1,128)}) custom-call(s32[6]{0:T(128)} %stack.46.meta, bf16[2,304,384]{2,1,0:T(8,128)(2,1)} %copy-done.9, ...), custom_call_target="tpu_custom_call" | custom-call | flops 1750000000 | bytes 1024 | tf_op jit(solution)/shard_map/first_projection_gradient/pallas_call | solution.py:420
  365.7 8.9 %weight_gradients.1 = (f32[1536,768]{1,0:T(8,128)}, f32[384,3072]{1,0:T(8,128)}, f32[384,768]{1,0:T(8,128)}) custom-call(s32[6]{0:T(128)} %stack.46.meta, bf16[384,768]{1,0:T(8,128)(2,1)} %copy-done.8, bf16[384,768]{1,0:T(8,128)(2,1)} %collective-permute-done.36.down_ab, bf16[384,768]{1,0:T(8,128)(2,1)} %collective-permute-done.37.down_ba, ...), custom_call_target="tpu_custom_call" | custom-call | flops 2449999872 | bytes 1024 | tf_op jit(solution)/shard_map/weight_gradients/pallas_call | solution.py:765
  (236 shorter events, 115.6 us)
Async XLA Ops:
  1.7 29.5 %collective-permute-start.1 = (bf16[256,768]{1,0:T(8,128)(2,1)S(1)}, bf16[256,768]{1,0:T(8,128)(2,1)}, u32[]{:S(2)}, u32[]{:S(2)}) collective-permute-start(bf16[256,768]{1,0:T(8,128)(2,1)S(1)} %dynamic-slice_bitcast_fusion.refs_0_), channel_id=1, source_target_pairs={{0,2},{1,3},{2,0},{3,1},{4,6},{5,7},{6,4},{7,5},{8,10},{9,11},{10,... | collective-permute-start | bytes 1179656 | tf_op jit(solution)/shard_map/ppermute | solution.py:813
  4.8 28.9 %collective-permute-start = (bf16[256,768]{1,0:T(8,128)(2,1)S(1)}, bf16[256,768]{1,0:T(8,128)(2,1)}, u32[]{:S(2)}, u32[]{:S(2)}) collective-permute-start(bf16[256,768]{1,0:T(8,128)(2,1)S(1)} %dynamic-slice_bitcast_fusion.refs_0_), channel_id=1, source_target_pairs={{0,1},{1,0},{2,3},{3,2},{4,5},{5,4},{6,7},{7,6},{8,9},{9,8},{10,11... | collective-permute-start | bytes 1179656 | tf_op jit(solution)/shard_map/ppermute | solution.py:813
  9.3 34.0 %collective-permute-start.12 = (bf16[384,576]{0,1:T(8,128)(2,1)S(1)}, bf16[384,576]{0,1:T(8,128)(2,1)S(1)}, u32[]{:S(2)}, u32[]{:S(2)}) collective-permute-start(bf16[384,576]{0,1:T(8,128)(2,1)S(1)} %bitcast.90), channel_id=1, source_target_pairs={{0,8},{8,0},{1,9},{9,1},{2,10},{10,2},{3,11},{11,3},{4,12},{12,4},... | collective-permute-start | bytes 1327112 | tf_op jit(solution)/shard_map/ppermute | solution.py:813
  49.1 51.7 %collective-permute-start.15 = (bf16[384,3072]{1,0:T(8,128)(2,1)}, bf16[384,3072]{1,0:T(8,128)(2,1)}, u32[]{:S(2)}, u32[]{:S(2)}) collective-permute-start(bf16[384,3072]{1,0:T(8,128)(2,1)} %refs_8_.1), channel_id=1, source_target_pairs={{0,8},{8,0},{1,9},{9,1},{2,10},{10,2},{3,11},{11,3},{4,12},{12,4},... | collective-permute-start | bytes 7077896 | tf_op jit(solution)/shard_map/ppermute | solution.py:813
  49.1 51.7 %collective-permute-start.16 = (bf16[1536,768]{1,0:T(8,128)(2,1)}, bf16[1536,768]{1,0:T(8,128)(2,1)}, u32[]{:S(2)}, u32[]{:S(2)}) collective-permute-start(bf16[1536,768]{1,0:T(8,128)(2,1)} %refs_10_.1), channel_id=1, source_target_pairs={{0,8},{8,0},{1,9},{9,1},{2,10},{10,2},{3,11},{11,3},{4,12},{12,4},... | collective-permute-start | bytes 7077896 | tf_op jit(solution)/shard_map/ppermute | solution.py:813
  77.8 23.1 %all-to-all-start = ((bf16[8,192,256]{2,1,0:T(8,128)(2,1)}), bf16[8,192,256]{2,1,0:T(8,128)(2,1)S(1)}, u32[]{:S(2)}, u32[]{:S(2)}) async-start(bf16[8,192,256]{2,1,0:T(8,128)(2,1)} %get-tuple-element.93), calls=%async_computation | async-start | bytes 1572864 | tf_op jit(solution)/shard_map/all_to_all | solution.py:903
  134.6 20.1 %collective-permute-start.17 = (bf16[384,3840]{1,0:T(8,128)(2,1)}, bf16[384,3840]{1,0:T(8,128)(2,1)S(1)}, u32[]{:S(2)}, u32[]{:S(2)}) collective-permute-start(bf16[384,3840]{1,0:T(8,128)(2,1)} %up_out_gradient.2), channel_id=1, source_target_pairs={{0,8},{8,0},{1,9},{9,1},{2,10},{10,2},{3,11},{11,3},{4,12},{12,4},... | collective-permute-start | bytes 8847368 | tf_op jit(solution)/shard_map/weight_gradients/ppermute | solution.py:813
  140.8 26.9 %all-to-all-start.1 = ((bf16[8,192,256]{2,1,0:T(8,128)(2,1)}), bf16[8,192,256]{2,1,0:T(8,128)(2,1)}, u32[]{:S(2)}, u32[]{:S(2)}) async-start(bf16[8,192,256]{2,1,0:T(8,128)(2,1)} %bitcast.95), calls=%async_computation.1 | async-start | bytes 1572864 | tf_op jit(solution)/shard_map/all_to_all | solution.py:903
  151.7 31.4 %collective-permute-start.19 = (bf16[768,768]{1,0:T(8,128)(2,1)}, bf16[768,768]{1,0:T(8,128)(2,1)}, u32[]{:S(2)}, u32[]{:S(2)}) collective-permute-start(bf16[768,768]{1,0:T(8,128)(2,1)} %get-tuple-element.111), channel_id=1, source_target_pairs={{0,16},{16,0},{1,17},{17,1},{2,18},{18,2},{3,19},{19,3},{4,20},{20... | collective-permute-start | bytes 3538952 | tf_op jit(solution)/shard_map/weight_gradients/ppermute | solution.py:813
  164.6 28.2 %collective-permute-start.20 = (bf16[384,1536]{1,0:T(8,128)(2,1)}, bf16[384,1536]{1,0:T(8,128)(2,1)S(1)}, u32[]{:S(2)}, u32[]{:S(2)}) collective-permute-start(bf16[384,1536]{1,0:T(8,128)(2,1)} %get-tuple-element.106), channel_id=1, source_target_pairs={{0,1},{1,0},{2,3},{3,2},{4,5},{5,4},{6,7},{7,6},{8,9},{9,8},{10,11... | collective-permute-start | bytes 3538952 | tf_op jit(solution)/shard_map/weight_gradients/ppermute | solution.py:813
  193.3 20.6 %collective-permute-start.23 = (bf16[384,768]{1,0:T(8,128)(2,1)S(1)}, bf16[384,768]{1,0:T(8,128)(2,1)}, u32[]{:S(2)}, u32[]{:S(2)}) collective-permute-start(bf16[384,768]{1,0:T(8,128)(2,1)S(1)} %constant_dynamic-slice_fusion.6), channel_id=1, source_target_pairs={{0,2},{1,3},{2,0},{3,1},{4,6},{5,7},{6,4},{7,5},{8,10},{9,11},{10,... | collective-permute-start | bytes 1769480 | tf_op jit(solution)/shard_map/weight_gradients/ppermute | solution.py:813
  196.0 17.9 %collective-permute-start.22 = (bf16[384,768]{1,0:T(8,128)(2,1)S(1)}, bf16[384,768]{1,0:T(8,128)(2,1)}, u32[]{:S(2)}, u32[]{:S(2)}) collective-permute-start(bf16[384,768]{1,0:T(8,128)(2,1)S(1)} %constant_dynamic-slice_fusion.7), channel_id=1, source_target_pairs={{0,1},{1,0},{2,3},{3,2},{4,5},{5,4},{6,7},{7,6},{8,9},{9,8},{10,11... | collective-permute-start | bytes 1769480 | tf_op jit(solution)/shard_map/weight_gradients/ppermute | solution.py:813
  225.4 29.1 %collective-permute-start.28 = (bf16[864,384]{1,0:T(8,128)(2,1)S(1)}, bf16[864,384]{1,0:T(8,128)(2,1)S(1)}, u32[]{:S(2)}, u32[]{:S(2)}) collective-permute-start(bf16[864,384]{1,0:T(8,128)(2,1)S(1)} %pad_maximum_fusion.1), channel_id=1, source_target_pairs={{0,4},{1,5},{2,6},{3,7},{4,0},{5,1},{6,2},{7,3},{8,12},{9,13},{10,... | collective-permute-start | bytes 1990664 | tf_op jit(solution)/shard_map/weight_gradients/ppermute | solution.py:813
  256.0 20.7 %collective-permute-start.35 = (bf16[2,2,256,384]{3,2,0,1:T(8,128)(2,1)}, bf16[2,2,256,384]{3,2,0,1:T(8,128)(2,1)}, u32[]{:S(2)}, u32[]{:S(2)}) collective-permute-start(bf16[2,2,256,384]{3,2,0,1:T(8,128)(2,1)} %bitcast.81), channel_id=1, source_target_pairs={{0,2},{1,3},{2,0},{3,1},{4,6},{5,7},{6,4},{7,5},{8,10},{9,11},{10,... | collective-permute-start | bytes 2359304 | tf_op jit(solution)/shard_map/first_round/ppermute | solution.py:813
  256.1 26.4 %collective-permute-start.29 = (bf16[384,384]{1,0:T(8,128)(2,1)S(1)}, bf16[384,384]{1,0:T(8,128)(2,1)S(1)}, u32[]{:S(2)}, u32[]{:S(2)}) collective-permute-start(bf16[384,384]{1,0:T(8,128)(2,1)S(1)} %get-tuple-element.201), channel_id=1, source_target_pairs={{0,2},{1,3},{2,0},{3,1},{4,6},{5,7},{6,4},{7,5},{8,10},{9,11},{10,... | collective-permute-start | bytes 884744 | tf_op jit(solution)/shard_map/first_round/ppermute | solution.py:813
  258.1 24.3 %collective-permute-start.30 = (bf16[384,384]{1,0:T(8,128)(2,1)S(1)}, bf16[384,384]{1,0:T(8,128)(2,1)S(1)}, u32[]{:S(2)}, u32[]{:S(2)}) collective-permute-start(bf16[384,384]{1,0:T(8,128)(2,1)S(1)} %get-tuple-element.200), channel_id=1, source_target_pairs={{0,16},{16,0},{1,17},{17,1},{2,18},{18,2},{3,19},{19,3},{4,20},{20... | collective-permute-start | bytes 884744 | tf_op jit(solution)/shard_map/first_round/ppermute | solution.py:813
  282.5 33.3 %collective-permute-start.36 = (bf16[384,768]{1,0:T(8,128)(2,1)S(1)}, bf16[384,768]{1,0:T(8,128)(2,1)}, u32[]{:S(2)}, u32[]{:S(2)}) collective-permute-start(bf16[384,768]{1,0:T(8,128)(2,1)S(1)} %pad_maximum_fusion.2.down_aa), channel_id=1, source_target_pairs={{0,1},{1,0},{2,3},{3,2},{4,5},{5,4},{6,7},{7,6},{8,9},{9,8},{10,11... | collective-permute-start | bytes 1769480 | tf_op jit(solution)/shard_map/second_round/ppermute | solution.py:813
  283.7 32.1 %collective-permute-start.37 = (bf16[384,768]{1,0:T(8,128)(2,1)S(1)}, bf16[384,768]{1,0:T(8,128)(2,1)}, u32[]{:S(2)}, u32[]{:S(2)}) collective-permute-start(bf16[384,768]{1,0:T(8,128)(2,1)S(1)} %pad_maximum_fusion.2.down_aa), channel_id=1, source_target_pairs={{0,16},{16,0},{1,17},{17,1},{2,18},{18,2},{3,19},{19,3},{4,20},{20... | collective-permute-start | bytes 1769480 | tf_op jit(solution)/shard_map/second_round/ppermute | solution.py:813
  288.4 27.4 %collective-permute-start.38 = (bf16[384,768]{1,0:T(8,128)(2,1)S(1)}, bf16[384,768]{1,0:T(8,128)(2,1)S(1)}, u32[]{:S(2)}, u32[]{:S(2)}) collective-permute-start(bf16[384,768]{1,0:T(8,128)(2,1)S(1)} %pad_maximum_fusion.3), channel_id=1, source_target_pairs={{0,2},{1,3},{2,0},{3,1},{4,6},{5,7},{6,4},{7,5},{8,10},{9,11},{10,... | collective-permute-start | bytes 1769480 | tf_op jit(solution)/shard_map/second_round/ppermute | solution.py:813
  322.7 42.3 %collective-permute-start.49 = (bf16[384,1536]{1,0:T(8,128)(2,1)S(1)}, bf16[384,1536]{1,0:T(8,128)(2,1)}, u32[]{:S(2)}, u32[]{:S(2)}) collective-permute-start(bf16[384,1536]{1,0:T(8,128)(2,1)S(1)} %pad_maximum_fusion.up_a), channel_id=1, source_target_pairs={{0,1},{1,0},{2,3},{3,2},{4,5},{5,4},{6,7},{7,6},{8,9},{9,8},{10,11... | collective-permute-start | bytes 3538952 | tf_op jit(solution)/shard_map/third_round/ppermute | solution.py:813
  324.0 18.9 %collective-permute-start.43 = (bf16[256,768]{1,0:T(8,128)(2,1)S(1)}, bf16[256,768]{1,0:T(8,128)(2,1)S(1)}, u32[]{:S(2)}, u32[]{:S(2)}) collective-permute-start(bf16[256,768]{1,0:T(8,128)(2,1)S(1)} %get-tuple-element.197), channel_id=1, source_target_pairs={{0,4},{1,5},{2,6},{3,7},{4,0},{5,1},{6,2},{7,3},{8,12},{9,13},{10,... | collective-permute-start | bytes 1179656 | tf_op jit(solution)/shard_map/third_round/ppermute | solution.py:813
  326.8 21.7 %collective-permute-start.46 = (bf16[2,304,384]{2,1,0:T(8,128)(2,1)S(1)}, bf16[2,304,384]{2,1,0:T(8,128)(2,1)}, u32[]{:S(2)}, u32[]{:S(2)}) collective-permute-start(bf16[2,304,384]{2,1,0:T(8,128)(2,1)S(1)} %pad_maximum_fusion.4.p00), channel_id=1, source_target_pairs={{0,16},{16,0},{1,17},{17,1},{2,18},{18,2},{3,19},{19,3},{4,20},{20... | collective-permute-start | bytes 1400840 | tf_op jit(solution)/shard_map/third_round/ppermute | solution.py:813
  341.3 23.7 %collective-permute-start.48 = (bf16[384,768]{1,0:T(8,128)(2,1)}, bf16[384,768]{1,0:T(8,128)(2,1)}, u32[]{:S(2)}, u32[]{:S(2)}) collective-permute-start(bf16[384,768]{1,0:T(8,128)(2,1)} %collective-permute-done.36.down_ab), channel_id=1, source_target_pairs={{0,16},{16,0},{1,17},{17,1},{2,18},{18,2},{3,19},{19,3},{4,20},{20... | collective-permute-start | bytes 1769480 | tf_op jit(solution)/shard_map/third_round/ppermute | solution.py:813
  342.9 22.1 %collective-permute-start.50 = (bf16[192,768]{1,0:T(8,128)(2,1)S(1)}, bf16[192,768]{1,0:T(8,128)(2,1)S(1)}, u32[]{:S(2)}, u32[]{:S(2)}) collective-permute-start(bf16[192,768]{1,0:T(8,128)(2,1)S(1)} %pad_maximum_fusion.6.out_a), channel_id=1, source_target_pairs={{0,2},{1,3},{2,0},{3,1},{4,6},{5,7},{6,4},{7,5},{8,10},{9,11},{10,... | collective-permute-start | bytes 884744 | tf_op jit(solution)/shard_map/third_round/ppermute | solution.py:813
  (66 other events, 621.5 us)

commit v9 on v8

--- a/solution.py
+++ b/solution.py
@@ -390,11 +390,9 @@
     _, part, half = pieces[0].shape
     team = 4
     wid = heads * hd
-    sizes = [half] * 4 + [hd // 2] * 2
     turned = team * wid
 
-    def body(meta, p00, p01, p10, p11, out_ref, *refs):
-        vec_refs, all_s = refs[:-1], refs[-1]
+    def body(meta, p00, p01, p10, p11, out_ref, vec_ref, all_s):
         t = pl.program_id(0)
 
         @pl.when(t == 0)
@@ -409,8 +407,7 @@
             total = jnp.zeros((EXTRA, half), F32)
             for p in range(team):
                 total = total + all_s[p, 3 * wid :, :].astype(F32)
-            for k, ref in enumerate(vec_refs):
-                ref[...] = total[k : k + 1, : ref.shape[1]]
+            vec_ref[...] = total
 
         rows = pl.ds(pl.multiple_of(t * wid, wid), wid)
         piece = jnp.concatenate([all_s[p, rows, :] for p in range(team)], axis=0)
@@ -423,13 +420,10 @@
             num_scalar_prefetch=1,
             grid=(3,),
             in_specs=[whole(2, part, half)] * 4,
-            out_specs=(pl.BlockSpec((half, turned), lambda i, m: (0, i)), *(whole(1, k) for k in sizes)),
+            out_specs=(pl.BlockSpec((half, turned), lambda i, m: (0, i)), whole(EXTRA, half)),
             scratch_shapes=[pltpu.VMEM((team, 2 * part, half), BF16)],
         ),
-        out_shape=(
-            jax.ShapeDtypeStruct((half, 3 * turned), F32),
-            *(jax.ShapeDtypeStruct((1, k), F32) for k in sizes),
-        ),
+        out_shape=(jax.ShapeDtypeStruct((half, 3 * turned), F32), jax.ShapeDtypeStruct((EXTRA, half), F32)),
         compiler_params=params(),
         cost_estimate=cost(5),
         name="first_projection_gradient",
@@ -582,85 +576,42 @@
     )(meta, attn_t, x, dy, valid, gain, bias, wo, wo_p, up, up_p, dn, dn_p)
 
 
-def up_out_grads(meta, attn_t, gb, h2, dup, far=None):
-    tokens, width = gb.shape
+def up_grads(meta, h2, dup, far=None):
+    width, tokens = h2.shape
     hidden = dup.shape[1]
     half = width // 2
-    packs, _, lanes = attn_t.shape
     n = hidden // width
     own = far is not None
 
-    def column(j, m):
-        bit = jnp.where(j < n // 2, m[4], 1 - m[4])
-        return bit * (n // 2) + lax.rem(jnp.minimum(j, n - 1), n // 2)
-
-    def body(meta, at_ref, gb_ref, h2_ref, dup_ref, *rest):
+    def body(meta, h2_ref, dup_ref, *rest):
         j = pl.program_id(0)
         side = meta[2] if own else 1 - meta[2]
-
-        def up():
-            return mm(h2_ref[pl.ds(pl.multiple_of(side * half, half), half), :], dup_ref[...])
-
-        def out():
-            rows = pl.ds(pl.multiple_of(side * half, half), half)
-            total = jnp.zeros((half, width), F32)
-            for p in range(packs):
-                total = total + mm(at_ref[p, rows, :], gb_ref[p * lanes : (p + 1) * lanes, :])
-            lo, hi = total[: half // 2], total[half // 2 :]
-            return jnp.where(meta[5] == 0, lo, hi), jnp.where(meta[5] == 0, hi, lo)
-
+        value = mm(h2_ref[pl.ds(pl.multiple_of(side * half, half), half), :], dup_ref[...])
         if own:
-            far_ref, uk_ref, us_ref, ok_ref, os_ref = rest
-
-            @pl.when(j < n // 2)
-            def _():
-                uk_ref[...] = (up() + far_ref[...].astype(F32)).astype(BF16)
-
-            @pl.when((j >= n // 2) & (j < n))
-            def _():
-                us_ref[...] = (up() + far_ref[...].astype(F32)).astype(BF16)
-
-            @pl.when(j == n)
-            def _():
-                keep, send = out()
-                ok_ref[...] = (keep + far_ref[: half // 2].astype(F32)).astype(BF16)
-                os_ref[...] = (send + far_ref[half // 2 :].astype(F32)).astype(BF16)
+            store_halves(j, n, value, *rest)
         else:
-            (out_ref,) = rest
-
-            @pl.when(j < n)
-            def _():
-                out_ref[...] = up().astype(BF16)
-
-            @pl.when(j == n)
-            def _():
-                keep, send = out()
-                out_ref[: half // 2] = keep.astype(BF16)
-                out_ref[half // 2 :] = send.astype(BF16)
-
-    whole = lambda *shape: pl.BlockSpec(shape, lambda j, m: (0,) * len(shape))
+            rest[0][...] = value.astype(BF16)
+
+    def column(j, m):
+        return jnp.where(j < n // 2, m[4], 1 - m[4]) * (n // 2) + lax.rem(j, n // 2)
+
     block = lambda index: pl.BlockSpec((half, width), index)
     if own:
         out_specs = (
             block(lambda j, m: (0, jnp.minimum(j, n // 2 - 1))),
-            block(lambda j, m: (0, jnp.clip(j - n // 2, 0, n // 2 - 1))),
-            whole(half // 2, width),
-            whole(half // 2, width),
+            block(lambda j, m: (0, jnp.maximum(j - n // 2, 0))),
         )
-        shapes = [(half, hidden // 2)] * 2 + [(half // 2, width)] * 2
-        out_shape = tuple(jax.ShapeDtypeStruct(shape, BF16) for shape in shapes)
+        out_shape = (jax.ShapeDtypeStruct((half, hidden // 2), BF16),) * 2
     else:
         out_specs = block(lambda j, m: (0, j))
-        out_shape = jax.ShapeDtypeStruct((half, hidden + width), BF16)
+        out_shape = jax.ShapeDtypeStruct((half, hidden), BF16)
     return pl.pallas_call(
         body,
         grid_spec=pltpu.PrefetchScalarGridSpec(
             num_scalar_prefetch=1,
-            grid=(n + 1,),
+            grid=(n,),
             in_specs=[
-                whole(*attn_t.shape),
-                whole(tokens, width),
-                whole(width, tokens),
+                pl.BlockSpec((width, tokens), lambda j, m: (0, 0)),
                 pl.BlockSpec((tokens, width), lambda j, m: (0, column(j, m))),
                 *([block(lambda j, m: (0, j))] if own else []),
             ],
@@ -669,49 +620,61 @@
         out_shape=out_shape,
         compiler_params=params(),
         cost_estimate=cost(0.2),
-        name="up_out_gradient",
-    )(meta, attn_t, gb, h2, dup, *([far] if own else []))
-
-
-def down_grads(meta, act, dy, far=None):
+        name="up_gradient",
+    )(meta, h2, dup, *([far] if own else []))
+
+
+def store_halves(j, n, value, far_ref, keep_ref, send_ref):
+    value = (value + far_ref[...].astype(F32)).astype(BF16)
+
+    @pl.when(j < n // 2)
+    def _():
+        keep_ref[...] = value
+
+    @pl.when(j >= n // 2)
+    def _():
+        send_ref[...] = value
+
+
+def down_out_grads(meta, act, dy, attn_t, gb, far=None):
     tokens, width = dy.shape
     half = width // 2
+    packs, _, lanes = attn_t.shape
     n = act.shape[1] // 2 // half
+    quarter = half // n
+    rows = half + quarter
     own = far is not None
 
-    def body(meta, act_ref, dy_ref, *rest):
-        value = mm(act_ref[...], dy_ref[...], TN)
+    def block_at(j, m):
+        return jnp.where(j < n // 2, m[3], 1 - m[3]) * (n // 2) + lax.rem(j, n // 2)
+
+    def body(meta, act_ref, dy_ref, at_ref, gb_ref, *rest):
+        j = pl.program_id(0)
+        side = meta[2] if own else 1 - meta[2]
+        at = pl.ds(pl.multiple_of(side * half + block_at(j, meta) * quarter, quarter), quarter)
+        total = jnp.zeros((quarter, width), F32)
+        for p in range(packs):
+            total = total + mm(at_ref[p, at, :], gb_ref[p * lanes : (p + 1) * lanes, :])
+        value = jnp.concatenate([mm(act_ref[...], dy_ref[...], TN), total], axis=0)
         if own:
-            far_ref, keep_ref, send_ref = rest
-            j = pl.program_id(0)
-            value = (value + far_ref[...].astype(F32)).astype(BF16)
-
-            @pl.when(j < n // 2)
-            def _():
-                keep_ref[...] = value
-
-            @pl.when(j >= n // 2)
-            def _():
-                send_ref[...] = value
+            store_halves(j, n, value, *rest)
         else:
-            (out_ref,) = rest
-            out_ref[...] = value.astype(BF16)
+            rest[0][...] = value.astype(BF16)
 
     def column(j, m):
-        side = m[2] if own else 1 - m[2]
-        bit = jnp.where(j < n // 2, m[3], 1 - m[3])
-        return side * n + bit * (n // 2) + lax.rem(j, n // 2)
-
-    block = lambda index: pl.BlockSpec((half, width), index)
+        return (m[2] if own else 1 - m[2]) * n + block_at(j, m)
+
+    whole = lambda *shape: pl.BlockSpec(shape, lambda j, m: (0,) * len(shape))
+    block = lambda index: pl.BlockSpec((rows, width), index)
     if own:
         out_specs = (
             block(lambda j, m: (jnp.minimum(j, n // 2 - 1), 0)),
             block(lambda j, m: (jnp.maximum(j - n // 2, 0), 0)),
         )
-        out_shape = (jax.ShapeDtypeStruct((n // 2 * half, width), BF16),) * 2
+        out_shape = (jax.ShapeDtypeStruct((n // 2 * rows, width), BF16),) * 2
     else:
         out_specs = block(lambda j, m: (j, 0))
-        out_shape = jax.ShapeDtypeStruct((n * half, width), BF16)
+        out_shape = jax.ShapeDtypeStruct((n * rows, width), BF16)
     return pl.pallas_call(
         body,
         grid_spec=pltpu.PrefetchScalarGridSpec(
@@ -719,7 +682,9 @@
             grid=(n,),
             in_specs=[
                 pl.BlockSpec((tokens, half), lambda j, m: (0, column(j, m))),
-                pl.BlockSpec((tokens, width), lambda j, m: (0, 0)),
+                whole(tokens, width),
+                whole(*attn_t.shape),
+                whole(tokens, width),
                 *([block(lambda j, m: (j, 0))] if own else []),
             ],
             out_specs=out_specs,
@@ -727,51 +692,43 @@
         out_shape=out_shape,
         compiler_params=params(),
         cost_estimate=cost(0.2),
-        name="down_gradient",
-    )(meta, act, dy, *([far] if own else []))
-
-
-def assemble(meta, downs, ups, outs):
-    half, width = outs[0].shape[0] * 2, outs[0].shape[1]
+        name="down_out_gradient",
+    )(meta, act, dy, attn_t, gb, *([far] if own else []))
+
+
+def assemble(meta, downs, ups):
+    rows, width = downs[0].shape
+    half = width // 2
+    quarter = rows - half
     hidden = ups[0].shape[1] * 2
-    cut = width // 2
-
-    def body(meta, down_aa, down_ab, down_ba, down_bb, up_a, up_b, out_a, out_b, down_ref, up_ref, out_ref):
+
+    def body(meta, down_aa, down_ab, down_ba, down_bb, up_a, up_b, down_ref, up_ref, out_ref):
         i = pl.program_id(0)
 
         def place(ref, value, swapped):
-            lo, hi = value[:, :cut].astype(F32), value[:, cut:].astype(F32)
-            ref[:, :cut] = jnp.where(swapped == 0, lo, hi)
-            ref[:, cut:] = jnp.where(swapped == 0, hi, lo)
+            lo, hi = value[:, :half].astype(F32), value[:, half:].astype(F32)
+            ref[:, :half] = jnp.where(swapped == 0, lo, hi)
+            ref[:, half:] = jnp.where(swapped == 0, hi, lo)
 
         down_x, down_y = i // 2 == meta[3], lax.rem(i, 2) == meta[4]
         own_x = jnp.where(down_y, down_aa[...], down_ab[...])
-        place(down_ref, jnp.where(down_x, own_x, jnp.where(down_y, down_ba[...], down_bb[...])), meta[5])
-        up_own = i // 2 == meta[4]
-        place(up_ref, jnp.where(up_own, up_a[...], up_b[...]), meta[3])
-
-        @pl.when(i == 0)
-        def _():
-            quarter = half // 4
-            for z in range(2):
-                for x in range(2):
-                    rows = pl.ds(pl.multiple_of(jnp.bitwise_xor(meta[3], x) * quarter, quarter), quarter)
-                    value = jnp.where(meta[5] == z, out_a[rows, :], out_b[rows, :])
-                    place(out_ref.at[pl.ds((2 * z + x) * quarter, quarter)], value, meta[4])
-
-    whole = lambda *shape: pl.BlockSpec(shape, lambda i, m: (0,) * len(shape))
-    down = whole(half, width)
+        down = jnp.where(down_x, own_x, jnp.where(down_y, down_ba[...], down_bb[...]))
+        place(down_ref, down[:half], meta[5])
+        place(out_ref, down[half:], meta[5])
+        place(up_ref, jnp.where(i // 2 == meta[4], up_a[...], up_b[...]), meta[3])
+
+    down = pl.BlockSpec((rows, width), lambda i, m: (0, 0))
     up = pl.BlockSpec((half, width), lambda i, m: (0, jnp.bitwise_xor(lax.rem(i, 2), m[5])))
     return pl.pallas_call(
         body,
         grid_spec=pltpu.PrefetchScalarGridSpec(
             num_scalar_prefetch=1,
             grid=(4,),
-            in_specs=[down, down, down, down, up, up, whole(*outs[0].shape), whole(*outs[0].shape)],
+            in_specs=[down, down, down, down, up, up],
             out_specs=(
                 pl.BlockSpec((half, width), lambda i, m: (i, 0)),
                 pl.BlockSpec((half, width), lambda i, m: (0, i)),
-                whole(half, width),
+                pl.BlockSpec((quarter, width), lambda i, m: (i, 0)),
             ),
         ),
         out_shape=(
@@ -782,7 +739,7 @@
         compiler_params=params(),
         cost_estimate=cost(7),
         name="weight_gradients",
-    )(meta, *downs, *ups, *outs)
+    )(meta, *downs, *ups)
 
 
 def finish_body(x_ref, gm_ref, back_ref, g_ref, out_ref):
@@ -875,9 +832,11 @@
         away = lax.dynamic_index_in_dim(mine, 1 - row, 0, keepdims=False)
         cut = local // 2
         far = flip(away[:cut], "seq", 4), flip(away[cut:], "seq", 4)
-        one, two = flip(near, "seq", 1), flip(near, "seq", 2)
-        three = flip(two[:cut], "seq", 1), flip(one[cut:], "seq", 2)
-        slots = [(near,), (one,), (two,), three]
+        one = flip(near, "seq", 1)
+        later, start = lax.optimization_barrier((near, far[0]))
+        far = start, far[1]
+        two = flip(later, "seq", 2)
+        slots = [(near,), (one,), (two,), (flip(two, "seq", 1),)]
         one = tuple(flip(part, "seq", 1) for part in far)
         two = tuple(flip(part, "seq", 2) for part in far)
         three = flip(two[0], "seq", 1), flip(one[1], "seq", 2)
@@ -937,12 +896,12 @@
 
     tie = lambda *values: lax.optimization_barrier(values)
     with jax.named_scope("weight_gradients"):
-        far_u = swap(up_out_grads(meta, attn_t, grad_branch, h2, dup))
-        far_d = swap(down_grads(meta, act, dy))
-        up_k, up_s, out_k, out_s = up_out_grads(meta, attn_t, grad_branch, h2, dup, far_u)
-        down_k, down_s = down_grads(meta, act, dy, far_d)
-        got = flip(down_s, *x), flip(up_s, *y), flip(out_s, *z)
-    grad_o = tie(grad_o, up_k, up_s, out_k, out_s, down_k, down_s)[0]
+        far_d = swap(down_out_grads(meta, act, dy, attn_t, grad_branch))
+        far_u = swap(up_grads(meta, h2, dup))
+        down_k, down_s = down_out_grads(meta, act, dy, attn_t, grad_branch, far_d)
+        up_k, up_s = up_grads(meta, h2, dup, far_u)
+        got = flip(down_s, *x), flip(up_s, *y)
+    grad_o = tie(grad_o, up_k, up_s, down_k, down_s)[0]
     go_back = lambda go, before: attend_back(
         meta, lengths, qt, ka, kt, v, attn_f, logsum, go, heads, hd, before
     )
@@ -952,33 +911,30 @@
     with jax.named_scope("weight_gradients"):
         down_k, down_s = next_half(down_k, got[0], y, 0)
         up_k, up_s = next_half(up_k, got[1], z, 1)
-        out_k, out_s = next_half(out_k, got[2], x, 0)
-        got = flip(down_s, *y), flip(up_s, *z), flip(out_s, *x)
+        got = flip(down_s, *y), flip(up_s, *z)
     with jax.named_scope("backward_attention"):
         parts = go_back(grad_o, parts)
     parts, *got = tie(parts, *got)
     with jax.named_scope("weight_gradients"):
         down_k, down_s = next_half(down_k, got[0], z, 1)
         up_k, up_s = next_half(up_k, got[1], x, 1)
-        out_k, out_s = next_half(out_k, got[2], y, 1)
-        got = flip(down_s, *z), flip(up_s, *x), flip(out_s, *y)
+        got = flip(down_s, *z), flip(up_s, *x)
     parts, *got = tie(parts, *got)
     with jax.named_scope("weight_gradients"):
-        down, up, out = add(down_k, got[0]), add(up_k, got[1]), add(out_k, got[2])
-        sizes = [down.shape[0], up.shape[0]]
-        pieces = jnp.concatenate([down, up, out])
+        down, up = add(down_k, got[0]), add(up_k, got[1])
+        pieces = jnp.concatenate([down, up])
         for mask in masks[2:]:
             pieces = add(pieces, flip(pieces, "seq", mask))
     with jax.named_scope("backward_attention"):
         dq, dk, dv = parts
         back_a, back_b, dw_t = qkv_back(meta, x_row, dq, dk, dv, w_t, g1, b1, gq, gk, vec2, heads, hd)
     dw_t, pieces = tie(dw_t, pieces)
-    down, up, out = jnp.split(pieces, [sizes[0], sizes[0] + sizes[1]])
+    down, up = jnp.split(pieces, [down.shape[0]])
 
     with jax.named_scope("first_round"):
         keep, send = halves(dw_t, core, 1)
         q_keep, q_send = next_half(keep, swap(send), x, 0)
-        got = [flip(down, *z), flip(up, *x), flip(out, *y), flip(q_send, *x)]
+        got = [flip(down, *z), flip(up, *x), flip(q_send, *x)]
         if direct:
             a = back_a.reshape(2, 2, 2, local, half)
             b = back_b.reshape(2, 2, 2, local, half)
@@ -986,22 +942,20 @@
         got = tie(*got)
         down = jnp.concatenate([down, got[0]], axis=1)
         up = jnp.concatenate([up, got[1]], axis=1)
-        out = jnp.concatenate([out, got[2]], axis=1)
-        piece = add(q_keep, got[3])
+        piece = add(q_keep, got[2])
         if direct:
-            a, b = add(a[:, :, 0], got[4]), add(b[:, 0], got[5])
+            a, b = add(a[:, :, 0], got[3]), add(b[:, 0], got[4])
     with jax.named_scope("second_round"):
         rows_at = [mask for mask in masks if mask >= team]
-        got = [flip(down, *y), flip(down, *x), flip(up, *z), flip(out, *x)]
+        got = [flip(down, *y), flip(down, *x), flip(up, *z)]
         got += [flip(piece, "seq", mask) for mask in rows_at[:1]]
         if direct:
             got += [flip(a[:, 1], *z), flip(b[:, 1], *y)]
         got = tie(*got)
         downs = [down, got[0], got[1]]
         up = jnp.concatenate([up, got[2]], axis=1)
-        out = jnp.concatenate([out, got[3]], axis=0)
         if rows_at:
-            piece = add(piece, got[4])
+            piece = add(piece, got[3])
         for mask in rows_at[1:]:
             piece = add(piece, flip(piece, "seq", mask))
         if direct:
@@ -1022,11 +976,11 @@
         downs.append(flip(downs[1], *x))
         piece_z = flip(piece, *z)
         pieces = [piece, piece_z, flip(piece, *x), flip(piece_z, *x)]
-        ups, outs = (up, flip(up, *y)), (out, flip(out, *z))
+        ups = (up, flip(up, *y))
     grad_tokens = finish(x_home, grad_mid, back, g1)
-    grad_qkv, *cuts = assemble_qkv(meta, pieces, heads, hd)
-    grad_down, grad_up, grad_out = assemble(meta, downs, ups, outs)
-    cuts = [one.reshape(-1) for one in cuts]
+    grad_qkv, small = assemble_qkv(meta, pieces, heads, hd)
+    grad_down, grad_up, grad_out = assemble(meta, downs, ups)
+    cuts = [small[k] for k in range(4)] + [small[4, : hd // 2], small[5, : hd // 2]]
     shape = tokens.shape
     return (
         output.reshape(shape), grad_tokens.reshape(shape), cuts[0], cuts[1], grad_qkv, cuts[4], cuts[5],

time: 377 us -> 394 us (1.045)
  waiting for transfers between devices: 130 us -> 144 us
  local copies, waits for them, and re-layouts: 19.1 us -> 26.2 us
  Pallas kernels: 148 us -> 144 us
    ppermute x51 -> x44, waiting for transfers between devices: 113 us -> 129 us  [flip(): return lax.ppermute(value, axis, [(i, i ^ mask) for i in range(size)])]
    pallas_call x4 -> x0, other arithmetic: 5.09 us -> none  [assemble_qkv(): pl.pallas_call(body, grid_spec=pltpu.PrefetchScalarGridSpec(num_scalar_pr...]
    unnamed x82 -> x64, local copies, waits for them, and re-layouts: 11.1 us -> 13.8 us
    ppermute x51 -> x44, starting transfers between devices: 49.6 us -> 47.4 us  [flip(): return lax.ppermute(value, axis, [(i, i ^ mask) for i in range(size)])]
    convert_element_type x16 -> x13, other arithmetic: 9.69 us -> 11.4 us  [add(): return (a.astype(F32) + b.astype(F32)).astype(BF16)]
  transfers between devices with their start and end apart: 53 -> 46, of which waited for: 20 -> 20; matrix products, arithmetic and copies ran while one was open for 8% -> 7% of each run, Pallas kernels for 28% -> 27%
where the time goes in v9:
time: 394 us; the launch traced here: 389 us
  waiting for transfers between devices  144 us (37%)
  Pallas kernels  144 us (37%)
  starting transfers between devices  57.7 us (15%)
  local copies, waits for them, and re-layouts  26.2 us (7%)
  other arithmetic  15.7 us (4%)
    ppermute x44, waiting for transfers between devices, flip(): return lax.ppermute(value, axis, [(i, i ^ mask) for i in range(size)])  129 us
    ppermute x44, starting transfers between devices, flip(): return lax.ppermute(value, axis, [(i, i ^ mask) for i in range(size)])  47.4 us
    pallas_call x2, Pallas kernels, attend_back(): pl.pallas_call(functools.partial(attend_back_body, first, heads, hd), gri...  29.9 us
    pallas_call x1, Pallas kernels, ffn(): pl.pallas_call(body, grid_spec=pltpu.PrefetchScalarGridSpec(num_scalar_pr...  25.8 us
    pallas_call x1, Pallas kernels, qkv_back(): pl.pallas_call(functools.partial(qkv_back_body, heads, hd), grid_spec=plt...  17.9 us
    all_to_all x2, waiting for transfers between devices, exchange(): return lax.all_to_all(value, 'seq', 0, 0, tiled=True)  15 us
    unnamed x64, local copies, waits for them, and re-layouts  13.8 us
    pallas_call x2, Pallas kernels, down_out_grads(): pl.pallas_call(body, grid_spec=pltpu.PrefetchScalarGridSpec(num_scalar_pr...  13.7 us
  transfers between devices with their start and end apart: 46, of which 20 were waited for; matrix products, arithmetic and copies ran while one was open for 7% of the time, Pallas kernels for 27%

profile of v9, /device:TPU:0, one launch (start us, length us, event | category | flops | bytes accessed | tf_op | source)
XLA Modules:
  0.0 388.8 jit_solution(15271544263042978900)
XLA Ops:
  7.0 13.1 %collective-permute-done.1.refs_4_ = bf16[128,768]{1,0:T(8,128)(2,1)S(1)} collective-permute-done((bf16[128,768]{1,0:T(8,128)(2,1)S(1)}, bf16[128,768]{1,0:T(8,128)(2,1)S(1)}, u32[]{:S(2)}, u32[]{:S(2)}) %collective-permute-start.1) | collective-permute-done | bytes 196640 | tf_op jit(solution)/shard_map/ppermute | solution.py:770
  28.3 8.0 %collective-permute-done.8.refs_9_ = bf16[128,768]{1,0:T(8,128)(2,1)S(1)} collective-permute-done((bf16[128,768]{1,0:T(8,128)(2,1)S(1)}, bf16[128,768]{1,0:T(8,128)(2,1)S(1)}, u32[]{:S(2)}, u32[]{:S(2)}) %collective-permute-start.8) | collective-permute-done | bytes 196640 | tf_op jit(solution)/shard_map/ppermute | solution.py:770
  38.3 5.8 %collective-permute-done.6.refs_7_ = bf16[128,768]{1,0:T(8,128)(2,1)} collective-permute-done((bf16[128,768]{1,0:T(8,128)(2,1)S(1)}, bf16[128,768]{1,0:T(8,128)(2,1)}, u32[]{:S(2)}, u32[]{:S(2)}) %collective-permute-start.6) | collective-permute-done | bytes 196640 | tf_op jit(solution)/shard_map/ppermute | solution.py:770
  50.1 6.6 %collective-permute-done.5.refs_6_ = bf16[128,768]{1,0:T(8,128)(2,1)S(1)} collective-permute-done((bf16[128,768]{1,0:T(8,128)(2,1)S(1)}, bf16[128,768]{1,0:T(8,128)(2,1)S(1)}, u32[]{:S(2)}, u32[]{:S(2)}) %collective-permute-start.5) | collective-permute-done | bytes 196640 | tf_op jit(solution)/shard_map/ppermute | solution.py:770
  59.8 12.6 %qkv_forward.1 = (bf16[3,128,2048]{2,1,0:T(8,128)(2,1)}, bf16[3,2048,128]{2,1,0:T(8,128)(2,1)}, bf16[3,64,2048]{2,1,0:T(8,128)(2,1)}, bf16[3,2048,64]{2,1,0:T(8,...) custom-call(s32[6]{0:T(128)} %stack.46.meta, s32[2,8]{1,0:T(2,128)} %bitcast.110, ...), custom_call_target="tpu_custom_call" | custom-call | flops 4200000000 | bytes 1024 | tf_op jit(solution)/shard_map/forward_attention/qkv_forward/pallas_call | solution.py:108
  72.4 13.4 %attention_forward.1 = (bf16[8,192,256]{2,1,0:T(8,128)(2,1)}, f32[3,64,2048]{2,1,0:T(8,128)}, f32[3,1,2048]{2,1,0:T(1,128)}) custom-call(s32[6]{0:T(128)} %stack.46.meta, s32[2,8]{1,0:T(2,128)} %bitcast.111, bf16[3,128,2048]{2,1,0:T(8,128)(2,1)} %get-tuple-element.82.qt_ref.refs_0_, bf16[3,2048,128]{2,1,0:T(8,128)(2,1)} %get-tuple-element.83.ka_ref.refs_1_, ...), custom_call_target="tpu_custom_call" | custom-call | flops 8750000128 | bytes 1024 | tf_op jit(solution)/shard_map/forward_attention/attention_forward/pallas_call | solution.py:180
  85.9 5.9 %all-to-all-start = ((bf16[8,192,256]{2,1,0:T(8,128)(2,1)}), bf16[8,192,256]{2,1,0:T(8,128)(2,1)S(1)}, u32[]{:S(2)}, u32[]{:S(2)}) async-start(bf16[8,192,256]{2,1,0:T(8,128)(2,1)} %get-tuple-element.85), calls=%async_computation | async-start | bytes 1572864 | tf_op jit(solution)/shard_map/all_to_all | solution.py:862
  94.1 15.0 %all-to-all-done = bf16[8,192,256]{2,1,0:T(8,128)(2,1)S(1)} async-done(((bf16[8,192,256]{2,1,0:T(8,128)(2,1)}), bf16[8,192,256]{2,1,0:T(8,128)(2,1)S(1)}, u32[]{:S(2)}, u32[]{:S(2)}) %all-to-all-start) | async-done | bytes 786464 | tf_op jit(solution)/shard_map/all_to_all | solution.py:862
  110.0 25.8 %ffn_both_ways.1 = (bf16[512,768]{1,0:T(8,128)(2,1)}, f32[512,768]{1,0:T(8,128)}, bf16[512,768]{1,0:T(8,128)(2,1)}, bf16[768,512]{1,0:T(8,128)(2,1)}, bf16[512,3...) custom-call(s32[6]{0:T(128)} %stack.46.meta, ...), custom_call_target="tpu_custom_call" | custom-call | flops 8750000128 | bytes 1024 | tf_op jit(solution)/shard_map/feed_forward/ffn_both_ways/pallas_call | solution.py:525
  135.8 6.4 %down_out_gradient.2 = bf16[1920,768]{1,0:T(8,128)(2,1)} custom-call(s32[6]{0:T(128)} %stack.46.meta, bf16[512,3072]{1,0:T(8,128)(2,1)} %get-tuple-element.98.act_ref, bf16[512,768]{1,0:T(8,128)(2,1)} %bitcast.89, bf16[2,768,256]{2,1,0:T(8,128)(2,1)} %bitcast.86, bf16[512,768]{1,0:T(8,128)(2,1)} %get-tuple-element.99.gb_ref), custom_call_target="tpu_custom_call" | custom-call | flops 70000000 | bytes 1024 | tf_op jit(solution)/shard_map/weight_gradients/down_out_gradient/pallas_call | solution.py:678
  142.2 6.0 %up_gradient.2 = bf16[384,3072]{1,0:T(8,128)(2,1)} custom-call(s32[6]{0:T(128)} %stack.46.meta, bf16[768,512]{1,0:T(8,128)(2,1)} %get-tuple-element.94.h2_ref, bf16[512,3072]{1,0:T(8,128)(2,1)} %get-tuple-element.95.dup_ref), custom_call_target="tpu_custom_call" | custom-call | flops 70000000 | bytes 1024 | tf_op jit(solution)/shard_map/weight_gradients/up_gradient/pallas_call | solution.py:608
  154.8 7.3 %down_out_gradient.3 = (bf16[960,768]{1,0:T(8,128)(2,1)}, bf16[960,768]{1,0:T(8,128)(2,1)}) custom-call(s32[6]{0:T(128)} %stack.46.meta, bf16[512,3072]{1,0:T(8,128)(2,1)} %get-tuple-element.98.act_ref, bf16[512,768]{1,0:T(8,128)(2,1)} %bitcast.90, bf16[2,768,256]{2,1,0:T(8,128)(2,1)} %bitcast.87, bf16[512,768]{1,0:T(8,128)(2,1)} %get-tuple-element.99.gb_ref, ...), custom_call_target="tpu_custom_call" | custom-call | flops 70000000 | bytes 1024 | tf_op jit(solution)/shard_map/weight_gradients/down_out_gradient/pallas_call | solution.py:678
  166.5 6.6 %up_gradient.3 = (bf16[384,1536]{1,0:T(8,128)(2,1)}, bf16[384,1536]{1,0:T(8,128)(2,1)}) custom-call(s32[6]{0:T(128)} %stack.46.meta, bf16[768,512]{1,0:T(8,128)(2,1)} %get-tuple-element.94.h2_ref, bf16[512,3072]{1,0:T(8,128)(2,1)} %get-tuple-element.95.dup_ref, bf16[384,3072]{1,0:T(8,128)(2,1)} %collective-permute-done.16.rest_0_), custom_call_target="tpu_custom_call" | custom-call | flops 70000000 | bytes 1024 | tf_op jit(solution)/shard_map/weight_gradients/up_gradient/pallas_call | solution.py:608
  174.8 14.0 %attention_backward.2 = (f32[3,64,2048]{2,1,0:T(8,128)}, f32[3,64,2048]{2,1,0:T(8,128)}, f32[3,64,2048]{2,1,0:T(8,128)}) custom-call(s32[6]{0:T(128)} %stack.46.meta, s32[2,8]{1,0:T(2,128)} %bitcast.112, bf16[3,128,2048]{2,1,0:T(8,128)(2,1)} %get-tuple-element.82.qt_ref.refs_0_, bf16[3,2048,128]{2,1,0:T(8,128)(2,1)} %get-tuple-element.83.ka_ref.refs_1_, ...), custom_call_target="tpu_custom_call" | custom-call | flops 5249999872 | bytes 1024 | tf_op jit(solution)/shard_map/backward_attention/attention_backward/pallas_call | solution.py:255
  188.8 12.3 %collective-permute-done.19 = bf16[384,1536]{1,0:T(8,128)(2,1)} collective-permute-done((bf16[384,1536]{1,0:T(8,128)(2,1)}, bf16[384,1536]{1,0:T(8,128)(2,1)}, u32[]{:S(2)}, u32[]{:S(2)}) %collective-permute-start.19) | collective-permute-done | bytes 1179680 | tf_op jit(solution)/shard_map/weight_gradients/ppermute | solution.py:770
  210.2 16.0 %attention_backward.3 = (f32[3,64,2048]{2,1,0:T(8,128)}, f32[3,64,2048]{2,1,0:T(8,128)}, f32[3,64,2048]{2,1,0:T(8,128)}) custom-call(s32[6]{0:T(128)} %stack.46.meta, s32[2,8]{1,0:T(2,128)} %bitcast.113, bf16[3,128,2048]{2,1,0:T(8,128)(2,1)} %get-tuple-element.82.qt_ref.refs_0_, ...), custom_call_target="tpu_custom_call", output_to_operand_aliasing={{0}: (9, {})} | custom-call | flops 5249999872 | bytes 1024 | tf_op jit(solution)/shard_map/backward_attention/attention_backward/pallas_call | solution.py:255
  230.3 6.7 %collective-permute-done.23 = bf16[384,384]{1,0:T(8,128)(2,1)S(1)} collective-permute-done((bf16[384,384]{1,0:T(8,128)(2,1)S(1)}, bf16[384,384]{1,0:T(8,128)(2,1)S(1)}, u32[]{:S(2)}, u32[]{:S(2)}) %collective-permute-start.23) | collective-permute-done | bytes 294944 | tf_op jit(solution)/shard_map/weight_gradients/ppermute | solution.py:770
  241.5 17.9 %qkv_backward.1 = (bf16[8,256,384]{2,1,0:T(8,128)(2,1)}, bf16[8,256,384]{2,1,0:T(8,128)(2,1)}, bf16[608,768]{1,0:T(8,128)(2,1)}) custom-call(s32[6]{0:T(128)} %stack.46.meta, bf16[2048,768]{1,0:T(8,128)(2,1)} %get-tuple-element.88.x_ref, f32[3,64,2048]{2,1,0:T(8,128)} %get-tuple-element.119.refs_0_, f32[3,64,2048]{2,1,0:T(8,128)} %get-tuple-element.120.refs_1_, ...), custom_call_target="tpu_custom_call" | custom-call | flops 5950000128 | bytes 1024 | tf_op jit(solution)/shard_map/backward_attention/qkv_backward/pallas_call | solution.py:350
  276.0 13.3 %collective-permute-done.30 = bf16[2,2,256,384]{3,2,0,1:T(8,128)(2,1)} collective-permute-done((bf16[2,2,256,384]{3,2,0,1:T(8,128)(2,1)}, bf16[2,2,256,384]{3,2,0,1:T(8,128)(2,1)}, u32[]{:S(2)}, u32[]{:S(2)}) %collective-permute-start.30) | collective-permute-done | bytes 786464 | tf_op jit(solution)/shard_map/first_round/ppermute | solution.py:770
  289.3 7.4 %collective-permute-done.25 = bf16[480,384]{1,0:T(8,128)(2,1)} collective-permute-done((bf16[480,384]{1,0:T(8,128)(2,1)S(1)}, bf16[480,384]{1,0:T(8,128)(2,1)}, u32[]{:S(2)}, u32[]{:S(2)}) %collective-permute-start.25) | collective-permute-done | bytes 368672 | tf_op jit(solution)/shard_map/first_round/ppermute | solution.py:770
  307.9 7.4 %collective-permute-done.34 = bf16[304,384]{1,0:T(8,128)(2,1)S(1)} collective-permute-done((bf16[304,384]{1,0:T(8,128)(2,1)S(1)}, bf16[304,384]{1,0:T(8,128)(2,1)S(1)}, u32[]{:S(2)}, u32[]{:S(2)}) %collective-permute-start.34) | collective-permute-done | bytes 233504 | tf_op jit(solution)/shard_map/second_round/ppermute | solution.py:770
  315.3 11.9 %collective-permute-done.36 = bf16[2,256,384]{2,1,0:T(8,128)(2,1)S(1)} collective-permute-done((bf16[2,256,384]{2,1,0:T(8,128)(2,1)S(1)}, bf16[2,256,384]{2,1,0:T(8,128)(2,1)S(1)}, u32[]{:S(2)}, u32[]{:S(2)}) %collective-permute-start.36) | collective-permute-done | bytes 393248 | tf_op jit(solution)/shard_map/second_round/ppermute | solution.py:770
  345.2 12.0 %collective-permute-done.39.p01 = bf16[2,304,384]{2,1,0:T(8,128)(2,1)} collective-permute-done((bf16[2,304,384]{2,1,0:T(8,128)(2,1)S(1)}, bf16[2,304,384]{2,1,0:T(8,128)(2,1)}, u32[]{:S(2)}, u32[]{:S(2)}) %collective-permute-start.39) | collective-permute-done | bytes 466976 | tf_op jit(solution)/shard_map/third_round/ppermute | solution.py:770
  380.5 8.3 %weight_gradients.1 = (f32[1536,768]{1,0:T(8,128)}, f32[384,3072]{1,0:T(8,128)}, f32[384,768]{1,0:T(8,128)}) custom-call(s32[6]{0:T(128)} %stack.46.meta, bf16[480,768]{1,0:T(8,128)(2,1)} %copy-done.9, bf16[480,768]{1,0:T(8,128)(2,1)} %copy-done.21, bf16[480,768]{1,0:T(8,128)(2,1)} %copy-done.20, bf16[480,768]{1,0:T(8,128)(2,1)} %collective-permute-done.42.down_bb, ...), custom_call_target="tpu_custom_call" | custom-call | flops 2449999872 | bytes 1024 | tf_op jit(solution)/shard_map/weight_gradients/pallas_call | solution.py:722
  (193 shorter events, 127.8 us)
Async XLA Ops:
  5.9 20.3 %collective-permute-start.4 = (bf16[128,768]{1,0:T(8,128)(2,1)S(1)}, bf16[128,768]{1,0:T(8,128)(2,1)S(1)}, u32[]{:S(2)}, u32[]{:S(2)}) collective-permute-start(bf16[128,768]{1,0:T(8,128)(2,1)S(1)} %get-tuple-element.182), channel_id=1, source_target_pairs={{0,4},{1,5},{2,6},{3,7},{4,0},{5,1},{6,2},{7,3},{8,12},{9,13},{10,... | collective-permute-start | bytes 589832 | tf_op jit(solution)/shard_map/ppermute | solution.py:770
  20.1 37.3 %collective-permute-start = (bf16[256,768]{1,0:T(8,128)(2,1)S(1)}, bf16[256,768]{1,0:T(8,128)(2,1)}, u32[]{:S(2)}, u32[]{:S(2)}) collective-permute-start(bf16[256,768]{1,0:T(8,128)(2,1)S(1)} %dynamic-slice_bitcast_fusion.refs_0_), channel_id=1, source_target_pairs={{0,1},{1,0},{2,3},{3,2},{4,5},{5,4},{6,7},{7,6},{8,9},{9,8},{10,11... | collective-permute-start | bytes 1179656 | tf_op jit(solution)/shard_map/ppermute | solution.py:770
  25.0 21.0 %collective-permute-start.11 = (bf16[384,576]{0,1:T(8,128)(2,1)S(1)}, bf16[384,576]{0,1:T(8,128)(2,1)S(1)}, u32[]{:S(2)}, u32[]{:S(2)}) collective-permute-start(bf16[384,576]{0,1:T(8,128)(2,1)S(1)} %bitcast.92), channel_id=1, source_target_pairs={{0,8},{8,0},{1,9},{9,1},{2,10},{10,2},{3,11},{11,3},{4,12},{12,4},... | collective-permute-start | bytes 1327112 | tf_op jit(solution)/shard_map/ppermute | solution.py:770
  38.1 21.6 %collective-permute-start.3 = (bf16[256,768]{1,0:T(8,128)(2,1)}, bf16[256,768]{1,0:T(8,128)(2,1)}, u32[]{:S(2)}, u32[]{:S(2)}) collective-permute-start(bf16[256,768]{1,0:T(8,128)(2,1)} %collective-permute-done.2.refs_2_), channel_id=1, source_target_pairs={{0,1},{1,0},{2,3},{3,2},{4,5},{5,4},{6,7},{7,6},{8,9},{9,8},{10,11... | collective-permute-start | bytes 1179656 | tf_op jit(solution)/shard_map/ppermute | solution.py:770
  56.7 37.4 %collective-permute-start.14 = (bf16[384,3072]{1,0:T(8,128)(2,1)}, bf16[384,3072]{1,0:T(8,128)(2,1)}, u32[]{:S(2)}, u32[]{:S(2)}) collective-permute-start(bf16[384,3072]{1,0:T(8,128)(2,1)} %refs_8_.1), channel_id=1, source_target_pairs={{0,8},{8,0},{1,9},{9,1},{2,10},{10,2},{3,11},{11,3},{4,12},{12,4},... | collective-permute-start | bytes 7077896 | tf_op jit(solution)/shard_map/ppermute | solution.py:770
  57.4 36.7 %collective-permute-start.15 = (bf16[1536,768]{1,0:T(8,128)(2,1)}, bf16[1536,768]{1,0:T(8,128)(2,1)S(1)}, u32[]{:S(2)}, u32[]{:S(2)}) collective-permute-start(bf16[1536,768]{1,0:T(8,128)(2,1)} %refs_10_.1), channel_id=1, source_target_pairs={{0,8},{8,0},{1,9},{9,1},{2,10},{10,2},{3,11},{11,3},{4,12},{12,4},... | collective-permute-start | bytes 7077896 | tf_op jit(solution)/shard_map/ppermute | solution.py:770
  85.9 23.3 %all-to-all-start = ((bf16[8,192,256]{2,1,0:T(8,128)(2,1)}), bf16[8,192,256]{2,1,0:T(8,128)(2,1)S(1)}, u32[]{:S(2)}, u32[]{:S(2)}) async-start(bf16[8,192,256]{2,1,0:T(8,128)(2,1)} %get-tuple-element.85), calls=%async_computation | async-start | bytes 1572864 | tf_op jit(solution)/shard_map/all_to_all | solution.py:862
  148.7 26.1 %all-to-all-start.1 = ((bf16[8,192,256]{2,1,0:T(8,128)(2,1)}), bf16[8,192,256]{2,1,0:T(8,128)(2,1)}, u32[]{:S(2)}, u32[]{:S(2)}) async-start(bf16[8,192,256]{2,1,0:T(8,128)(2,1)} %bitcast.97), calls=%async_computation.1 | async-start | bytes 1572864 | tf_op jit(solution)/shard_map/all_to_all | solution.py:862
  162.1 39.0 %collective-permute-start.18 = (bf16[960,768]{1,0:T(8,128)(2,1)}, bf16[960,768]{1,0:T(8,128)(2,1)S(1)}, u32[]{:S(2)}, u32[]{:S(2)}) collective-permute-start(bf16[960,768]{1,0:T(8,128)(2,1)} %get-tuple-element.101), channel_id=1, source_target_pairs={{0,16},{16,0},{1,17},{17,1},{2,18},{18,2},{3,19},{19,3},{4,20},{20... | collective-permute-start | bytes 4423688 | tf_op jit(solution)/shard_map/weight_gradients/ppermute | solution.py:770
  173.1 27.9 %collective-permute-start.19 = (bf16[384,1536]{1,0:T(8,128)(2,1)}, bf16[384,1536]{1,0:T(8,128)(2,1)}, u32[]{:S(2)}, u32[]{:S(2)}) collective-permute-start(bf16[384,1536]{1,0:T(8,128)(2,1)} %get-tuple-element.97), channel_id=1, source_target_pairs={{0,1},{1,0},{2,3},{3,2},{4,5},{5,4},{6,7},{7,6},{8,9},{9,8},{10,11... | collective-permute-start | bytes 3538952 | tf_op jit(solution)/shard_map/weight_gradients/ppermute | solution.py:770
  204.9 21.3 %collective-permute-start.20 = (bf16[480,768]{1,0:T(8,128)(2,1)}, bf16[480,768]{1,0:T(8,128)(2,1)S(1)}, u32[]{:S(2)}, u32[]{:S(2)}) collective-permute-start(bf16[480,768]{1,0:T(8,128)(2,1)} %constant_dynamic-slice_fusion.5), channel_id=1, source_target_pairs={{0,1},{1,0},{2,3},{3,2},{4,5},{5,4},{6,7},{7,6},{8,9},{9,8},{10,11... | collective-permute-start | bytes 2211848 | tf_op jit(solution)/shard_map/weight_gradients/ppermute | solution.py:770
  239.0 27.5 %collective-permute-start.24 = (bf16[864,384]{1,0:T(8,128)(2,1)S(1)}, bf16[864,384]{1,0:T(8,128)(2,1)S(1)}, u32[]{:S(2)}, u32[]{:S(2)}) collective-permute-start(bf16[864,384]{1,0:T(8,128)(2,1)S(1)} %pad_maximum_fusion.2), channel_id=1, source_target_pairs={{0,4},{1,5},{2,6},{3,7},{4,0},{5,1},{6,2},{7,3},{8,12},{9,13},{10,... | collective-permute-start | bytes 1990664 | tf_op jit(solution)/shard_map/weight_gradients/ppermute | solution.py:770
  268.6 20.7 %collective-permute-start.30 = (bf16[2,2,256,384]{3,2,0,1:T(8,128)(2,1)}, bf16[2,2,256,384]{3,2,0,1:T(8,128)(2,1)}, u32[]{:S(2)}, u32[]{:S(2)}) collective-permute-start(bf16[2,2,256,384]{3,2,0,1:T(8,128)(2,1)} %bitcast.83), channel_id=1, source_target_pairs={{0,2},{1,3},{2,0},{3,1},{4,6},{5,7},{6,4},{7,5},{8,10},{9,11},{10,... | collective-permute-start | bytes 2359304 | tf_op jit(solution)/shard_map/first_round/ppermute | solution.py:770
  268.7 20.6 %collective-permute-start.26 = (bf16[384,384]{1,0:T(8,128)(2,1)S(1)}, bf16[384,384]{1,0:T(8,128)(2,1)S(1)}, u32[]{:S(2)}, u32[]{:S(2)}) collective-permute-start(bf16[384,384]{1,0:T(8,128)(2,1)S(1)} %split.7), channel_id=1, source_target_pairs={{0,16},{16,0},{1,17},{17,1},{2,18},{18,2},{3,19},{19,3},{4,20},{20... | collective-permute-start | bytes 884744 | tf_op jit(solution)/shard_map/first_round/ppermute | solution.py:770
  271.9 24.9 %collective-permute-start.25 = (bf16[480,384]{1,0:T(8,128)(2,1)S(1)}, bf16[480,384]{1,0:T(8,128)(2,1)}, u32[]{:S(2)}, u32[]{:S(2)}) collective-permute-start(bf16[480,384]{1,0:T(8,128)(2,1)S(1)} %split.6), channel_id=1, source_target_pairs={{0,2},{1,3},{2,0},{3,1},{4,6},{5,7},{6,4},{7,5},{8,10},{9,11},{10,... | collective-permute-start | bytes 1105928 | tf_op jit(solution)/shard_map/first_round/ppermute | solution.py:770
  275.9 20.8 %collective-permute-start.28 = (bf16[304,384]{1,0:T(8,128)(2,1)}, bf16[304,384]{1,0:T(8,128)(2,1)S(1)}, u32[]{:S(2)}, u32[]{:S(2)}) collective-permute-start(bf16[304,384]{1,0:T(8,128)(2,1)} %constant_dynamic-slice_fusion), channel_id=1, source_target_pairs={{0,16},{16,0},{1,17},{17,1},{2,18},{18,2},{3,19},{19,3},{4,20},{20... | collective-permute-start | bytes 700424 | tf_op jit(solution)/shard_map/first_round/ppermute | solution.py:770
  297.8 34.3 %collective-permute-start.32 = (bf16[480,768]{1,0:T(8,128)(2,1)S(1)}, bf16[480,768]{1,0:T(8,128)(2,1)S(1)}, u32[]{:S(2)}, u32[]{:S(2)}) collective-permute-start(bf16[480,768]{1,0:T(8,128)(2,1)S(1)} %pad_maximum_fusion.1.down_aa), channel_id=1, source_target_pairs={{0,16},{16,0},{1,17},{17,1},{2,18},{18,2},{3,19},{19,3},{4,20},{20... | collective-permute-start | bytes 2211848 | tf_op jit(solution)/shard_map/second_round/ppermute | solution.py:770
  301.1 31.1 %collective-permute-start.31 = (bf16[480,768]{1,0:T(8,128)(2,1)S(1)}, bf16[480,768]{1,0:T(8,128)(2,1)S(1)}, u32[]{:S(2)}, u32[]{:S(2)}) collective-permute-start(bf16[480,768]{1,0:T(8,128)(2,1)S(1)} %pad_maximum_fusion.1.down_aa), channel_id=1, source_target_pairs={{0,1},{1,0},{2,3},{3,2},{4,5},{5,4},{6,7},{7,6},{8,9},{9,8},{10,11... | collective-permute-start | bytes 2211848 | tf_op jit(solution)/shard_map/second_round/ppermute | solution.py:770
  304.0 23.2 %collective-permute-start.36 = (bf16[2,256,384]{2,1,0:T(8,128)(2,1)S(1)}, bf16[2,256,384]{2,1,0:T(8,128)(2,1)S(1)}, u32[]{:S(2)}, u32[]{:S(2)}) collective-permute-start(bf16[2,256,384]{2,1,0:T(8,128)(2,1)S(1)} %slice_bitcast_fusion.1), channel_id=1, source_target_pairs={{0,1},{1,0},{2,3},{3,2},{4,5},{5,4},{6,7},{7,6},{8,9},{9,8},{10,11... | collective-permute-start | bytes 1179656 | tf_op jit(solution)/shard_map/second_round/ppermute | solution.py:770
  304.7 27.4 %collective-permute-start.33 = (bf16[384,768]{1,0:T(8,128)(2,1)S(1)}, bf16[384,768]{1,0:T(8,128)(2,1)S(1)}, u32[]{:S(2)}, u32[]{:S(2)}) collective-permute-start(bf16[384,768]{1,0:T(8,128)(2,1)S(1)} %pad_maximum_fusion.3), channel_id=1, source_target_pairs={{0,2},{1,3},{2,0},{3,1},{4,6},{5,7},{6,4},{7,5},{8,10},{9,11},{10,... | collective-permute-start | bytes 1769480 | tf_op jit(solution)/shard_map/second_round/ppermute | solution.py:770
  339.8 40.7 %collective-permute-start.43 = (bf16[384,1536]{1,0:T(8,128)(2,1)S(1)}, bf16[384,1536]{1,0:T(8,128)(2,1)}, u32[]{:S(2)}, u32[]{:S(2)}) collective-permute-start(bf16[384,1536]{1,0:T(8,128)(2,1)S(1)} %pad_maximum_fusion.up_a), channel_id=1, source_target_pairs={{0,1},{1,0},{2,3},{3,2},{4,5},{5,4},{6,7},{7,6},{8,9},{9,8},{10,11... | collective-permute-start | bytes 3538952 | tf_op jit(solution)/shard_map/third_round/ppermute | solution.py:770
  341.3 18.6 %collective-permute-start.37 = (bf16[256,768]{1,0:T(8,128)(2,1)S(1)}, bf16[256,768]{1,0:T(8,128)(2,1)S(1)}, u32[]{:S(2)}, u32[]{:S(2)}) collective-permute-start(bf16[256,768]{1,0:T(8,128)(2,1)S(1)} %get-tuple-element.181), channel_id=1, source_target_pairs={{0,4},{1,5},{2,6},{3,7},{4,0},{5,1},{6,2},{7,3},{8,12},{9,13},{10,... | collective-permute-start | bytes 1179656 | tf_op jit(solution)/shard_map/third_round/ppermute | solution.py:770
  344.8 20.6 %collective-permute-start.40 = (bf16[2,304,384]{2,1,0:T(8,128)(2,1)S(1)}, bf16[2,304,384]{2,1,0:T(8,128)(2,1)S(1)}, u32[]{:S(2)}, u32[]{:S(2)}) collective-permute-start(bf16[2,304,384]{2,1,0:T(8,128)(2,1)S(1)} %pad_maximum_fusion.4.p00), channel_id=1, source_target_pairs={{0,16},{16,0},{1,17},{17,1},{2,18},{18,2},{3,19},{19,3},{4,20},{20... | collective-permute-start | bytes 1400840 | tf_op jit(solution)/shard_map/third_round/ppermute | solution.py:770
  357.8 22.8 %collective-permute-start.42 = (bf16[480,768]{1,0:T(8,128)(2,1)}, bf16[480,768]{1,0:T(8,128)(2,1)}, u32[]{:S(2)}, u32[]{:S(2)}) collective-permute-start(bf16[480,768]{1,0:T(8,128)(2,1)} %copy-done.21), channel_id=1, source_target_pairs={{0,16},{16,0},{1,17},{17,1},{2,18},{18,2},{3,19},{19,3},{4,20},{20... | collective-permute-start | bytes 2211848 | tf_op jit(solution)/shard_map/third_round/ppermute | solution.py:770
  (50 other events, 586.3 us)

commit v10 on v9

--- a/solution.py
+++ b/solution.py
@@ -831,16 +831,13 @@
         near = lax.dynamic_index_in_dim(mine, row, 0, keepdims=False)
         away = lax.dynamic_index_in_dim(mine, 1 - row, 0, keepdims=False)
         cut = local // 2
-        far = flip(away[:cut], "seq", 4), flip(away[cut:], "seq", 4)
-        one = flip(near, "seq", 1)
-        later, start = lax.optimization_barrier((near, far[0]))
-        far = start, far[1]
-        two = flip(later, "seq", 2)
-        slots = [(near,), (one,), (two,), (flip(two, "seq", 1),)]
-        one = tuple(flip(part, "seq", 1) for part in far)
-        two = tuple(flip(part, "seq", 2) for part in far)
-        three = flip(two[0], "seq", 1), flip(one[1], "seq", 2)
-        slots += [far, one, two, three]
+        far = flip(away, "seq", 4)
+
+        def spread(own):
+            one, two = flip(own, "seq", 1), flip(own, "seq", 2)
+            return [(own,), (one,), (two,), (flip(two[:cut], "seq", 1), flip(one[cut:], "seq", 2))]
+
+        slots = spread(near) + spread(far)
         spot = idx
     else:
         same_member = [[q * team + p for q in range(every)] for p in range(team)]
@@ -974,7 +971,7 @@
                 whole[:, 0], "seq", 0, 0, axis_index_groups=same_member, tiled=True
             ).reshape(every * local, width)
         downs.append(flip(downs[1], *x))
-        piece_z = flip(piece, *z)
+        piece_z, downs[3] = tie(flip(piece, *z), downs[3])
         pieces = [piece, piece_z, flip(piece, *x), flip(piece_z, *x)]
         ups = (up, flip(up, *y))
     grad_tokens = finish(x_home, grad_mid, back, g1)

time: 394 us -> 375 us (0.952)
  waiting for transfers between devices: 144 us -> 124 us
    ppermute x44 -> x42, waiting for transfers between devices: 129 us -> 106 us  [flip(): return lax.ppermute(value, axis, [(i, i ^ mask) for i in range(size)])]
    ppermute x44 -> x42, starting transfers between devices: 47.4 us -> 48.3 us  [flip(): return lax.ppermute(value, axis, [(i, i ^ mask) for i in range(size)])]
    unnamed x64 -> x70, local copies, waits for them, and re-layouts: 13.8 us -> 14.7 us
  transfers between devices with their start and end apart: 46 -> 44, of which waited for: 20 -> 17; matrix products, arithmetic and copies ran while one was open for 7% -> 7% of each run, Pallas kernels for 27% -> 28%
where the time goes in v10:
time: 375 us; the launch traced here: 371 us
  Pallas kernels  144 us (38%)
  waiting for transfers between devices  124 us (33%)
  starting transfers between devices  58.9 us (16%)
  local copies, waits for them, and re-layouts  27.1 us (7%)
  other arithmetic  15.7 us (4%)
    ppermute x42, waiting for transfers between devices, flip(): return lax.ppermute(value, axis, [(i, i ^ mask) for i in range(size)])  106 us
    ppermute x42, starting transfers between devices, flip(): return lax.ppermute(value, axis, [(i, i ^ mask) for i in range(size)])  48.3 us
    pallas_call x2, Pallas kernels, attend_back(): pl.pallas_call(functools.partial(attend_back_body, first, heads, hd), gri...  29.9 us
    pallas_call x1, Pallas kernels, ffn(): pl.pallas_call(body, grid_spec=pltpu.PrefetchScalarGridSpec(num_scalar_pr...  25.9 us
    all_to_all x2, waiting for transfers between devices, exchange(): return lax.all_to_all(value, 'seq', 0, 0, tiled=True)  18.7 us
    pallas_call x1, Pallas kernels, qkv_back(): pl.pallas_call(functools.partial(qkv_back_body, heads, hd), grid_spec=plt...  17.9 us
    unnamed x70, local copies, waits for them, and re-layouts  14.7 us
    pallas_call x2, Pallas kernels, down_out_grads(): pl.pallas_call(body, grid_spec=pltpu.PrefetchScalarGridSpec(num_scalar_pr...  13.8 us
  transfers between devices with their start and end apart: 44, of which 17 were waited for; matrix products, arithmetic and copies ran while one was open for 7% of the time, Pallas kernels for 28%

profile of v10, /device:TPU:0, one launch (start us, length us, event | category | flops | bytes accessed | tf_op | source)
XLA Modules:
  0.0 371.2 jit_solution(4200462824149215358)
XLA Ops:
  13.4 10.4 %collective-permute-done.4.refs_5_ = bf16[256,768]{1,0:T(8,128)(2,1)} collective-permute-done((bf16[256,768]{1,0:T(8,128)(2,1)S(1)}, bf16[256,768]{1,0:T(8,128)(2,1)}, u32[]{:S(2)}, u32[]{:S(2)}) %collective-permute-start.4) | collective-permute-done | bytes 393248 | tf_op jit(solution)/shard_map/ppermute | solution.py:770
  29.0 7.0 %collective-permute-done.6.refs_7_ = bf16[256,768]{1,0:T(8,128)(2,1)S(1)} collective-permute-done((bf16[256,768]{1,0:T(8,128)(2,1)}, bf16[256,768]{1,0:T(8,128)(2,1)S(1)}, u32[]{:S(2)}, u32[]{:S(2)}) %collective-permute-start.6) | collective-permute-done | bytes 393248 | tf_op jit(solution)/shard_map/ppermute | solution.py:770
  44.4 12.6 %qkv_forward.1 = (bf16[3,128,2048]{2,1,0:T(8,128)(2,1)}, bf16[3,2048,128]{2,1,0:T(8,128)(2,1)}, bf16[3,64,2048]{2,1,0:T(8,128)(2,1)}, bf16[3,2048,64]{2,1,0:T(8,...) custom-call(s32[6]{0:T(128)} %stack.46.meta, s32[2,8]{1,0:T(2,128)} %bitcast.108, ...), custom_call_target="tpu_custom_call" | custom-call | flops 4200000000 | bytes 1024 | tf_op jit(solution)/shard_map/forward_attention/qkv_forward/pallas_call | solution.py:108
  57.0 13.4 %attention_forward.1 = (bf16[8,192,256]{2,1,0:T(8,128)(2,1)}, f32[3,64,2048]{2,1,0:T(8,128)}, f32[3,1,2048]{2,1,0:T(1,128)}) custom-call(s32[6]{0:T(128)} %stack.46.meta, s32[2,8]{1,0:T(2,128)} %bitcast.109, bf16[3,128,2048]{2,1,0:T(8,128)(2,1)} %get-tuple-element.80.qt_ref.refs_0_, bf16[3,2048,128]{2,1,0:T(8,128)(2,1)} %get-tuple-element.81.ka_ref.refs_1_, ...), custom_call_target="tpu_custom_call" | custom-call | flops 8750000128 | bytes 1024 | tf_op jit(solution)/shard_map/forward_attention/attention_forward/pallas_call | solution.py:180
  70.4 6.2 %all-to-all-start = ((bf16[8,192,256]{2,1,0:T(8,128)(2,1)}), bf16[8,192,256]{2,1,0:T(8,128)(2,1)S(1)}, u32[]{:S(2)}, u32[]{:S(2)}) async-start(bf16[8,192,256]{2,1,0:T(8,128)(2,1)} %get-tuple-element.83), calls=%async_computation | async-start | bytes 1572864 | tf_op jit(solution)/shard_map/all_to_all | solution.py:859
  78.7 17.0 %all-to-all-done = bf16[8,192,256]{2,1,0:T(8,128)(2,1)S(1)} async-done(((bf16[8,192,256]{2,1,0:T(8,128)(2,1)}), bf16[8,192,256]{2,1,0:T(8,128)(2,1)S(1)}, u32[]{:S(2)}, u32[]{:S(2)}) %all-to-all-start) | async-done | bytes 786464 | tf_op jit(solution)/shard_map/all_to_all | solution.py:859
  96.6 25.9 %ffn_both_ways.1 = (bf16[512,768]{1,0:T(8,128)(2,1)}, f32[512,768]{1,0:T(8,128)}, bf16[512,768]{1,0:T(8,128)(2,1)}, bf16[768,512]{1,0:T(8,128)(2,1)}, bf16[512,3...) custom-call(s32[6]{0:T(128)} %stack.46.meta, ...), custom_call_target="tpu_custom_call" | custom-call | flops 8750000128 | bytes 1024 | tf_op jit(solution)/shard_map/feed_forward/ffn_both_ways/pallas_call | solution.py:525
  122.4 6.4 %down_out_gradient.2 = bf16[1920,768]{1,0:T(8,128)(2,1)} custom-call(s32[6]{0:T(128)} %stack.46.meta, bf16[512,3072]{1,0:T(8,128)(2,1)} %get-tuple-element.96.act_ref, bf16[512,768]{1,0:T(8,128)(2,1)} %bitcast.87, bf16[2,768,256]{2,1,0:T(8,128)(2,1)} %bitcast.84, bf16[512,768]{1,0:T(8,128)(2,1)} %get-tuple-element.97.gb_ref), custom_call_target="tpu_custom_call" | custom-call | flops 70000000 | bytes 1024 | tf_op jit(solution)/shard_map/weight_gradients/down_out_gradient/pallas_call | solution.py:678
  128.9 5.9 %up_gradient.2 = bf16[384,3072]{1,0:T(8,128)(2,1)} custom-call(s32[6]{0:T(128)} %stack.46.meta, bf16[768,512]{1,0:T(8,128)(2,1)} %get-tuple-element.92.h2_ref, bf16[512,3072]{1,0:T(8,128)(2,1)} %get-tuple-element.93.dup_ref), custom_call_target="tpu_custom_call" | custom-call | flops 70000000 | bytes 1024 | tf_op jit(solution)/shard_map/weight_gradients/up_gradient/pallas_call | solution.py:608
  141.3 7.3 %down_out_gradient.3 = (bf16[960,768]{1,0:T(8,128)(2,1)}, bf16[960,768]{1,0:T(8,128)(2,1)}) custom-call(s32[6]{0:T(128)} %stack.46.meta, bf16[512,3072]{1,0:T(8,128)(2,1)} %get-tuple-element.96.act_ref, bf16[512,768]{1,0:T(8,128)(2,1)} %bitcast.88, bf16[2,768,256]{2,1,0:T(8,128)(2,1)} %bitcast.85, bf16[512,768]{1,0:T(8,128)(2,1)} %get-tuple-element.97.gb_ref, ...), custom_call_target="tpu_custom_call" | custom-call | flops 70000000 | bytes 1024 | tf_op jit(solution)/shard_map/weight_gradients/down_out_gradient/pallas_call | solution.py:678
  150.1 6.6 %up_gradient.3 = (bf16[384,1536]{1,0:T(8,128)(2,1)}, bf16[384,1536]{1,0:T(8,128)(2,1)}) custom-call(s32[6]{0:T(128)} %stack.46.meta, bf16[768,512]{1,0:T(8,128)(2,1)} %get-tuple-element.92.h2_ref, bf16[512,3072]{1,0:T(8,128)(2,1)} %get-tuple-element.93.dup_ref, bf16[384,3072]{1,0:T(8,128)(2,1)} %collective-permute-done.14.rest_0_), custom_call_target="tpu_custom_call" | custom-call | flops 70000000 | bytes 1024 | tf_op jit(solution)/shard_map/weight_gradients/up_gradient/pallas_call | solution.py:608
  160.1 15.0 %attention_backward.2 = (f32[3,64,2048]{2,1,0:T(8,128)}, f32[3,64,2048]{2,1,0:T(8,128)}, f32[3,64,2048]{2,1,0:T(8,128)}) custom-call(s32[6]{0:T(128)} %stack.46.meta, s32[2,8]{1,0:T(2,128)} %bitcast.110, bf16[3,128,2048]{2,1,0:T(8,128)(2,1)} %get-tuple-element.80.qt_ref.refs_0_, bf16[3,2048,128]{2,1,0:T(8,128)(2,1)} %get-tuple-element.81.ka_ref.refs_1_, ...), custom_call_target="tpu_custom_call" | custom-call | flops 5249999872 | bytes 1024 | tf_op jit(solution)/shard_map/backward_attention/attention_backward/pallas_call | solution.py:255
  175.2 9.5 %collective-permute-done.17 = bf16[384,1536]{1,0:T(8,128)(2,1)} collective-permute-done((bf16[384,1536]{1,0:T(8,128)(2,1)}, bf16[384,1536]{1,0:T(8,128)(2,1)}, u32[]{:S(2)}, u32[]{:S(2)}) %collective-permute-start.17) | collective-permute-done | bytes 1179680 | tf_op jit(solution)/shard_map/weight_gradients/ppermute | solution.py:770
  193.8 14.9 %attention_backward.3 = (f32[3,64,2048]{2,1,0:T(8,128)}, f32[3,64,2048]{2,1,0:T(8,128)}, f32[3,64,2048]{2,1,0:T(8,128)}) custom-call(s32[6]{0:T(128)} %stack.46.meta, s32[2,8]{1,0:T(2,128)} %bitcast.111, bf16[3,128,2048]{2,1,0:T(8,128)(2,1)} %get-tuple-element.80.qt_ref.refs_0_, ...), custom_call_target="tpu_custom_call", output_to_operand_aliasing={{0}: (9, {})} | custom-call | flops 5249999872 | bytes 1024 | tf_op jit(solution)/shard_map/backward_attention/attention_backward/pallas_call | solution.py:255
  214.7 5.4 %collective-permute-done.21 = bf16[384,384]{1,0:T(8,128)(2,1)S(1)} collective-permute-done((bf16[384,384]{1,0:T(8,128)(2,1)S(1)}, bf16[384,384]{1,0:T(8,128)(2,1)S(1)}, u32[]{:S(2)}, u32[]{:S(2)}) %collective-permute-start.21) | collective-permute-done | bytes 294944 | tf_op jit(solution)/shard_map/weight_gradients/ppermute | solution.py:770
  226.3 17.9 %qkv_backward.1 = (bf16[8,256,384]{2,1,0:T(8,128)(2,1)}, bf16[8,256,384]{2,1,0:T(8,128)(2,1)}, bf16[608,768]{1,0:T(8,128)(2,1)}) custom-call(s32[6]{0:T(128)} %stack.46.meta, bf16[2048,768]{1,0:T(8,128)(2,1)} %get-tuple-element.86.x_ref, f32[3,64,2048]{2,1,0:T(8,128)} %get-tuple-element.117.refs_0_, f32[3,64,2048]{2,1,0:T(8,128)} %get-tuple-element.118.refs_1_, ...), custom_call_target="tpu_custom_call" | custom-call | flops 5950000128 | bytes 1024 | tf_op jit(solution)/shard_map/backward_attention/qkv_backward/pallas_call | solution.py:350
  261.9 12.8 %collective-permute-done.28 = bf16[2,2,256,384]{3,2,0,1:T(8,128)(2,1)} collective-permute-done((bf16[2,2,256,384]{3,2,0,1:T(8,128)(2,1)}, bf16[2,2,256,384]{3,2,0,1:T(8,128)(2,1)}, u32[]{:S(2)}, u32[]{:S(2)}) %collective-permute-start.28) | collective-permute-done | bytes 786464 | tf_op jit(solution)/shard_map/first_round/ppermute | solution.py:770
  274.6 7.4 %collective-permute-done.23 = bf16[480,384]{1,0:T(8,128)(2,1)} collective-permute-done((bf16[480,384]{1,0:T(8,128)(2,1)S(1)}, bf16[480,384]{1,0:T(8,128)(2,1)}, u32[]{:S(2)}, u32[]{:S(2)}) %collective-permute-start.23) | collective-permute-done | bytes 368672 | tf_op jit(solution)/shard_map/first_round/ppermute | solution.py:770
  292.4 6.2 %collective-permute-done.32 = bf16[304,384]{1,0:T(8,128)(2,1)S(1)} collective-permute-done((bf16[304,384]{1,0:T(8,128)(2,1)S(1)}, bf16[304,384]{1,0:T(8,128)(2,1)S(1)}, u32[]{:S(2)}, u32[]{:S(2)}) %collective-permute-start.32) | collective-permute-done | bytes 233504 | tf_op jit(solution)/shard_map/second_round/ppermute | solution.py:770
  298.7 12.2 %collective-permute-done.34 = bf16[2,256,384]{2,1,0:T(8,128)(2,1)S(1)} collective-permute-done((bf16[2,256,384]{2,1,0:T(8,128)(2,1)S(1)}, bf16[2,256,384]{2,1,0:T(8,128)(2,1)S(1)}, u32[]{:S(2)}, u32[]{:S(2)}) %collective-permute-start.34) | collective-permute-done | bytes 393248 | tf_op jit(solution)/shard_map/second_round/ppermute | solution.py:770
  310.9 5.8 %collective-permute-done.33 = bf16[2,256,384]{2,1,0:T(8,128)(2,1)S(1)} collective-permute-done((bf16[2,256,384]{2,1,0:T(8,128)(2,1)S(1)}, bf16[2,256,384]{2,1,0:T(8,128)(2,1)S(1)}, u32[]{:S(2)}, u32[]{:S(2)}) %collective-permute-start.33) | collective-permute-done | bytes 393248 | tf_op jit(solution)/shard_map/second_round/ppermute | solution.py:770
  328.6 13.4 %collective-permute-done.37.p01 = bf16[2,304,384]{2,1,0:T(8,128)(2,1)} collective-permute-done((bf16[2,304,384]{2,1,0:T(8,128)(2,1)S(1)}, bf16[2,304,384]{2,1,0:T(8,128)(2,1)}, u32[]{:S(2)}, u32[]{:S(2)}) %collective-permute-start.37) | collective-permute-done | bytes 466976 | tf_op jit(solution)/shard_map/third_round/ppermute | solution.py:770
  355.0 5.2 %first_projection_gradient.1 = (f32[384,2304]{1,0:T(8,128)}, f32[32,384]{1,0:T(8,128)}) custom-call(s32[6]{0:T(128)} %stack.46.meta, bf16[2,304,384]{2,1,0:T(8,128)(2,1)} %copy-done.10, bf16[2,304,384]{2,1,0:T(8,128)(2,1)} %collective-permute-done.37.p01, bf16[2,304,384]{2,1,0:T(8,128)(2,1)} %copy-done.27, bf16[2,304,384]{2,1,0:T(8,128)(2,1)} %collective-permute-done.40.p11), custom_call_target="tpu_custom_call" | custom-call | flops 1750000000 | bytes 1024 | tf_op jit(solution)/shard_map/first_projection_gradient/pallas_call | solution.py:417
  362.9 8.3 %weight_gradients.1 = (f32[1536,768]{1,0:T(8,128)}, f32[384,3072]{1,0:T(8,128)}, f32[384,768]{1,0:T(8,128)}) custom-call(s32[6]{0:T(128)} %stack.46.meta, bf16[480,768]{1,0:T(8,128)(2,1)} %copy-done.9, bf16[480,768]{1,0:T(8,128)(2,1)} %copy-done.23, bf16[480,768]{1,0:T(8,128)(2,1)} %copy-done.22, bf16[480,768]{1,0:T(8,128)(2,1)} %copy-done.24, ...), custom_call_target="tpu_custom_call" | custom-call | flops 2449999872 | bytes 1024 | tf_op jit(solution)/shard_map/weight_gradients/pallas_call | solution.py:722
  (198 shorter events, 117.3 us)
Async XLA Ops:
  1.9 21.9 %collective-permute-start.4 = (bf16[256,768]{1,0:T(8,128)(2,1)S(1)}, bf16[256,768]{1,0:T(8,128)(2,1)}, u32[]{:S(2)}, u32[]{:S(2)}) collective-permute-start(bf16[256,768]{1,0:T(8,128)(2,1)S(1)} %get-tuple-element.182), channel_id=1, source_target_pairs={{0,4},{1,5},{2,6},{3,7},{4,0},{5,1},{6,2},{7,3},{8,12},{9,13},{10,... | collective-permute-start | bytes 1179656 | tf_op jit(solution)/shard_map/ppermute | solution.py:770
  6.1 19.8 %collective-permute-start.1 = (bf16[256,768]{1,0:T(8,128)(2,1)S(1)}, bf16[256,768]{1,0:T(8,128)(2,1)S(1)}, u32[]{:S(2)}, u32[]{:S(2)}) collective-permute-start(bf16[256,768]{1,0:T(8,128)(2,1)S(1)} %get-tuple-element.183.refs_0_), channel_id=1, source_target_pairs={{0,2},{1,3},{2,0},{3,1},{4,6},{5,7},{6,4},{7,5},{8,10},{9,11},{10,... | collective-permute-start | bytes 1179656 | tf_op jit(solution)/shard_map/ppermute | solution.py:770
  7.6 18.9 %collective-permute-start = (bf16[256,768]{1,0:T(8,128)(2,1)S(1)}, bf16[256,768]{1,0:T(8,128)(2,1)}, u32[]{:S(2)}, u32[]{:S(2)}) collective-permute-start(bf16[256,768]{1,0:T(8,128)(2,1)S(1)} %get-tuple-element.183.refs_0_), channel_id=1, source_target_pairs={{0,1},{1,0},{2,3},{3,2},{4,5},{5,4},{6,7},{7,6},{8,9},{9,8},{10,11... | collective-permute-start | bytes 1179656 | tf_op jit(solution)/shard_map/ppermute | solution.py:770
  12.2 28.7 %collective-permute-start.9 = (bf16[384,576]{0,1:T(8,128)(2,1)S(1)}, bf16[384,576]{0,1:T(8,128)(2,1)S(1)}, u32[]{:S(2)}, u32[]{:S(2)}) collective-permute-start(bf16[384,576]{0,1:T(8,128)(2,1)S(1)} %bitcast.90), channel_id=1, source_target_pairs={{0,8},{8,0},{1,9},{9,1},{2,10},{10,2},{3,11},{11,3},{4,12},{12,4},... | collective-permute-start | bytes 1327112 | tf_op jit(solution)/shard_map/ppermute | solution.py:770
  40.9 37.8 %collective-permute-start.12 = (bf16[384,3072]{1,0:T(8,128)(2,1)}, bf16[384,3072]{1,0:T(8,128)(2,1)}, u32[]{:S(2)}, u32[]{:S(2)}) collective-permute-start(bf16[384,3072]{1,0:T(8,128)(2,1)} %refs_8_.1), channel_id=1, source_target_pairs={{0,8},{8,0},{1,9},{9,1},{2,10},{10,2},{3,11},{11,3},{4,12},{12,4},... | collective-permute-start | bytes 7077896 | tf_op jit(solution)/shard_map/ppermute | solution.py:770
  42.0 36.6 %collective-permute-start.13 = (bf16[1536,768]{1,0:T(8,128)(2,1)}, bf16[1536,768]{1,0:T(8,128)(2,1)}, u32[]{:S(2)}, u32[]{:S(2)}) collective-permute-start(bf16[1536,768]{1,0:T(8,128)(2,1)} %refs_10_.1), channel_id=1, source_target_pairs={{0,8},{8,0},{1,9},{9,1},{2,10},{10,2},{3,11},{11,3},{4,12},{12,4},... | collective-permute-start | bytes 7077896 | tf_op jit(solution)/shard_map/ppermute | solution.py:770
  70.4 25.3 %all-to-all-start = ((bf16[8,192,256]{2,1,0:T(8,128)(2,1)}), bf16[8,192,256]{2,1,0:T(8,128)(2,1)S(1)}, u32[]{:S(2)}, u32[]{:S(2)}) async-start(bf16[8,192,256]{2,1,0:T(8,128)(2,1)} %get-tuple-element.83), calls=%async_computation | async-start | bytes 1572864 | tf_op jit(solution)/shard_map/all_to_all | solution.py:859
  135.3 24.8 %all-to-all-start.1 = ((bf16[8,192,256]{2,1,0:T(8,128)(2,1)}), bf16[8,192,256]{2,1,0:T(8,128)(2,1)}, u32[]{:S(2)}, u32[]{:S(2)}) async-start(bf16[8,192,256]{2,1,0:T(8,128)(2,1)} %bitcast.95), calls=%async_computation.1 | async-start | bytes 1572864 | tf_op jit(solution)/shard_map/all_to_all | solution.py:859
  148.7 36.0 %collective-permute-start.16 = (bf16[960,768]{1,0:T(8,128)(2,1)}, bf16[960,768]{1,0:T(8,128)(2,1)S(1)}, u32[]{:S(2)}, u32[]{:S(2)}) collective-permute-start(bf16[960,768]{1,0:T(8,128)(2,1)} %get-tuple-element.99), channel_id=1, source_target_pairs={{0,16},{16,0},{1,17},{17,1},{2,18},{18,2},{3,19},{19,3},{4,20},{20... | collective-permute-start | bytes 4423688 | tf_op jit(solution)/shard_map/weight_gradients/ppermute | solution.py:770
  156.7 27.9 %collective-permute-start.17 = (bf16[384,1536]{1,0:T(8,128)(2,1)}, bf16[384,1536]{1,0:T(8,128)(2,1)}, u32[]{:S(2)}, u32[]{:S(2)}) collective-permute-start(bf16[384,1536]{1,0:T(8,128)(2,1)} %get-tuple-element.95), channel_id=1, source_target_pairs={{0,1},{1,0},{2,3},{3,2},{4,5},{5,4},{6,7},{7,6},{8,9},{9,8},{10,11... | collective-permute-start | bytes 3538952 | tf_op jit(solution)/shard_map/weight_gradients/ppermute | solution.py:770
  188.5 20.1 %collective-permute-start.18 = (bf16[480,768]{1,0:T(8,128)(2,1)}, bf16[480,768]{1,0:T(8,128)(2,1)S(1)}, u32[]{:S(2)}, u32[]{:S(2)}) collective-permute-start(bf16[480,768]{1,0:T(8,128)(2,1)} %constant_dynamic-slice_fusion.5), channel_id=1, source_target_pairs={{0,1},{1,0},{2,3},{3,2},{4,5},{5,4},{6,7},{7,6},{8,9},{9,8},{10,11... | collective-permute-start | bytes 2211848 | tf_op jit(solution)/shard_map/weight_gradients/ppermute | solution.py:770
  222.1 29.6 %collective-permute-start.22 = (bf16[864,384]{1,0:T(8,128)(2,1)S(1)}, bf16[864,384]{1,0:T(8,128)(2,1)S(1)}, u32[]{:S(2)}, u32[]{:S(2)}) collective-permute-start(bf16[864,384]{1,0:T(8,128)(2,1)S(1)} %pad_maximum_fusion.2), channel_id=1, source_target_pairs={{0,4},{1,5},{2,6},{3,7},{4,0},{5,1},{6,2},{7,3},{8,12},{9,13},{10,... | collective-permute-start | bytes 1990664 | tf_op jit(solution)/shard_map/weight_gradients/ppermute | solution.py:770
  253.9 20.7 %collective-permute-start.28 = (bf16[2,2,256,384]{3,2,0,1:T(8,128)(2,1)}, bf16[2,2,256,384]{3,2,0,1:T(8,128)(2,1)}, u32[]{:S(2)}, u32[]{:S(2)}) collective-permute-start(bf16[2,2,256,384]{3,2,0,1:T(8,128)(2,1)} %bitcast.81), channel_id=1, source_target_pairs={{0,2},{1,3},{2,0},{3,1},{4,6},{5,7},{6,4},{7,5},{8,10},{9,11},{10,... | collective-permute-start | bytes 2359304 | tf_op jit(solution)/shard_map/first_round/ppermute | solution.py:770
  254.2 20.4 %collective-permute-start.24 = (bf16[384,384]{1,0:T(8,128)(2,1)S(1)}, bf16[384,384]{1,0:T(8,128)(2,1)S(1)}, u32[]{:S(2)}, u32[]{:S(2)}) collective-permute-start(bf16[384,384]{1,0:T(8,128)(2,1)S(1)} %split.7), channel_id=1, source_target_pairs={{0,16},{16,0},{1,17},{17,1},{2,18},{18,2},{3,19},{19,3},{4,20},{20... | collective-permute-start | bytes 884744 | tf_op jit(solution)/shard_map/first_round/ppermute | solution.py:770
  255.5 26.5 %collective-permute-start.23 = (bf16[480,384]{1,0:T(8,128)(2,1)S(1)}, bf16[480,384]{1,0:T(8,128)(2,1)}, u32[]{:S(2)}, u32[]{:S(2)}) collective-permute-start(bf16[480,384]{1,0:T(8,128)(2,1)S(1)} %split.6), channel_id=1, source_target_pairs={{0,2},{1,3},{2,0},{3,1},{4,6},{5,7},{6,4},{7,5},{8,10},{9,11},{10,... | collective-permute-start | bytes 1105928 | tf_op jit(solution)/shard_map/first_round/ppermute | solution.py:770
  259.6 22.5 %collective-permute-start.26 = (bf16[304,384]{1,0:T(8,128)(2,1)}, bf16[304,384]{1,0:T(8,128)(2,1)S(1)}, u32[]{:S(2)}, u32[]{:S(2)}) collective-permute-start(bf16[304,384]{1,0:T(8,128)(2,1)} %constant_dynamic-slice_fusion), channel_id=1, source_target_pairs={{0,16},{16,0},{1,17},{17,1},{2,18},{18,2},{3,19},{19,3},{4,20},{20... | collective-permute-start | bytes 700424 | tf_op jit(solution)/shard_map/first_round/ppermute | solution.py:770
  283.1 33.6 %collective-permute-start.30 = (bf16[480,768]{1,0:T(8,128)(2,1)S(1)}, bf16[480,768]{1,0:T(8,128)(2,1)S(1)}, u32[]{:S(2)}, u32[]{:S(2)}) collective-permute-start(bf16[480,768]{1,0:T(8,128)(2,1)S(1)} %pad_maximum_fusion.1.down_aa), channel_id=1, source_target_pairs={{0,16},{16,0},{1,17},{17,1},{2,18},{18,2},{3,19},{19,3},{4,20},{20... | collective-permute-start | bytes 2211848 | tf_op jit(solution)/shard_map/second_round/ppermute | solution.py:770
  284.7 32.0 %collective-permute-start.29 = (bf16[480,768]{1,0:T(8,128)(2,1)S(1)}, bf16[480,768]{1,0:T(8,128)(2,1)S(1)}, u32[]{:S(2)}, u32[]{:S(2)}) collective-permute-start(bf16[480,768]{1,0:T(8,128)(2,1)S(1)} %pad_maximum_fusion.1.down_aa), channel_id=1, source_target_pairs={{0,1},{1,0},{2,3},{3,2},{4,5},{5,4},{6,7},{7,6},{8,9},{9,8},{10,11... | collective-permute-start | bytes 2211848 | tf_op jit(solution)/shard_map/second_round/ppermute | solution.py:770
  288.0 22.9 %collective-permute-start.34 = (bf16[2,256,384]{2,1,0:T(8,128)(2,1)S(1)}, bf16[2,256,384]{2,1,0:T(8,128)(2,1)S(1)}, u32[]{:S(2)}, u32[]{:S(2)}) collective-permute-start(bf16[2,256,384]{2,1,0:T(8,128)(2,1)S(1)} %slice_bitcast_fusion.1), channel_id=1, source_target_pairs={{0,1},{1,0},{2,3},{3,2},{4,5},{5,4},{6,7},{7,6},{8,9},{9,8},{10,11... | collective-permute-start | bytes 1179656 | tf_op jit(solution)/shard_map/second_round/ppermute | solution.py:770
  289.2 27.4 %collective-permute-start.31 = (bf16[384,768]{1,0:T(8,128)(2,1)S(1)}, bf16[384,768]{1,0:T(8,128)(2,1)S(1)}, u32[]{:S(2)}, u32[]{:S(2)}) collective-permute-start(bf16[384,768]{1,0:T(8,128)(2,1)S(1)} %pad_maximum_fusion.3), channel_id=1, source_target_pairs={{0,2},{1,3},{2,0},{3,1},{4,6},{5,7},{6,4},{7,5},{8,10},{9,11},{10,... | collective-permute-start | bytes 1769480 | tf_op jit(solution)/shard_map/second_round/ppermute | solution.py:770
  318.6 23.4 %collective-permute-start.38 = (bf16[480,768]{1,0:T(8,128)(2,1)S(1)}, bf16[480,768]{1,0:T(8,128)(2,1)S(1)}, u32[]{:S(2)}, u32[]{:S(2)}) collective-permute-start(bf16[480,768]{1,0:T(8,128)(2,1)S(1)} %collective-permute-done.29.down_ab), channel_id=1, source_target_pairs={{0,16},{16,0},{1,17},{17,1},{2,18},{18,2},{3,19},{19,3},{4,20},{20... | collective-permute-start | bytes 2211848 | tf_op jit(solution)/shard_map/third_round/ppermute | solution.py:770
  324.1 38.8 %collective-permute-start.41 = (bf16[384,1536]{1,0:T(8,128)(2,1)S(1)}, bf16[384,1536]{1,0:T(8,128)(2,1)}, u32[]{:S(2)}, u32[]{:S(2)}) collective-permute-start(bf16[384,1536]{1,0:T(8,128)(2,1)S(1)} %pad_maximum_fusion.up_a), channel_id=1, source_target_pairs={{0,1},{1,0},{2,3},{3,2},{4,5},{5,4},{6,7},{7,6},{8,9},{9,8},{10,11... | collective-permute-start | bytes 3538952 | tf_op jit(solution)/shard_map/third_round/ppermute | solution.py:770
  325.1 20.3 %collective-permute-start.35 = (bf16[256,768]{1,0:T(8,128)(2,1)S(1)}, bf16[256,768]{1,0:T(8,128)(2,1)S(1)}, u32[]{:S(2)}, u32[]{:S(2)}) collective-permute-start(bf16[256,768]{1,0:T(8,128)(2,1)S(1)} %get-tuple-element.181), channel_id=1, source_target_pairs={{0,4},{1,5},{2,6},{3,7},{4,0},{5,1},{6,2},{7,3},{8,12},{9,13},{10,... | collective-permute-start | bytes 1179656 | tf_op jit(solution)/shard_map/third_round/ppermute | solution.py:770
  327.8 23.0 %collective-permute-start.39 = (bf16[2,304,384]{2,1,0:T(8,128)(2,1)S(1)}, bf16[2,304,384]{2,1,0:T(8,128)(2,1)S(1)}, u32[]{:S(2)}, u32[]{:S(2)}) collective-permute-start(bf16[2,304,384]{2,1,0:T(8,128)(2,1)S(1)} %pad_maximum_fusion.4.p00), channel_id=1, source_target_pairs={{0,16},{16,0},{1,17},{17,1},{2,18},{18,2},{3,19},{19,3},{4,20},{20... | collective-permute-start | bytes 1400840 | tf_op jit(solution)/shard_map/third_round/ppermute | solution.py:770
  (51 other events, 427.1 us)

commit v11 on v10

--- a/solution.py
+++ b/solution.py
@@ -61,52 +61,78 @@
         xs.append(refs[:count])
         refs = refs[count:]
     w_ref, g_ref, b_ref, gq_ref, gk_ref = refs[:5]
-    qt_ref, ka_ref, kt_ref, v_ref, vt_ref, x_ref = refs[5:]
+    qt_ref, ka_ref, kt_ref, v_ref, vt_ref, x_ref, c = refs[-7:]
     wid = heads * hd
-    spot, row = meta[0], meta[1]
-    bounds = bounds_of(len_ref, row)
-    for s in range(8):
-        c = jnp.bitwise_xor(spot, s)
-        cols = pl.ds(pl.multiple_of(c * BLK, BLK), BLK)
-        x = jnp.concatenate([ref[...] for ref in xs[s]], axis=0) if len(xs[s]) > 1 else xs[s][0][...]
-        x_ref[cols, :] = x
-        hat, _ = norm_rows(x.astype(F32))
-        first = (hat * g_ref[...] + b_ref[...]).astype(BF16)
-        qkv = mm(w_ref[...], first, NT)
-        place = c * BLK + lax.broadcasted_iota(jnp.int32, (8, BLK), 1)
-        ident = jnp.zeros((8, BLK), jnp.int32)
-        place_k = c * BLK + lax.broadcasted_iota(jnp.int32, (BLK, 128), 0)
-        ident_k = jnp.zeros((BLK, 128), jnp.int32)
-        for bound in bounds:
-            ident = ident + (place >= bound).astype(jnp.int32)
-            ident_k = ident_k + (place_k >= bound).astype(jnp.int32)
-        which = lax.broadcasted_iota(jnp.int32, (8, BLK), 0)
-        hot = jnp.where((ident == which) & (which < len(bounds)), 16.0, 0.0)
-        hot = jnp.concatenate([hot, jnp.zeros((hd - 8, BLK), F32)], axis=0)
-        lane = lax.broadcasted_iota(jnp.int32, (BLK, 128), 1) - hd
-        hot_k = jnp.where((ident_k == lane) & (lane < len(bounds)), SHIFT / 16.0, 0.0)
-        for h in range(heads):
-            q, _ = norm_cols(qkv[h * hd : (h + 1) * hd])
-            k, _ = norm_cols(qkv[wid + h * hd : wid + (h + 1) * hd])
-            q = (q * gq_ref[...]).astype(BF16).astype(F32) * (hd**-0.5)
-            k = k * gk_ref[...]
-            v = qkv[2 * wid + h * hd : 2 * wid + (h + 1) * hd]
-            qt_ref[h, :, cols] = jnp.concatenate([q, hot], axis=0).astype(BF16)
-            kt_ref[h, :, cols] = k.astype(BF16)
-            vt_ref[h, :, cols] = v.astype(BF16)
-            both = jnp.transpose(jnp.concatenate([k, v], axis=0))
-            ka_ref[h, cols, :] = jnp.where(lane < 0, both, hot_k).astype(BF16)
-            v_ref[h, cols, :] = both[:, hd:].astype(BF16)
-
-
-def make_qkv(meta, lengths, slots, w_t, gain, bias, gq, gk, heads, hd):
-    length = 8 * sum(one.shape[0] for one in slots[0])
+    bounds = bounds_of(len_ref, meta[1])
+    for s in range(len(cuts)):
+
+        @pl.when(pl.program_id(0) == s)
+        def _():
+            at = 0
+            for ref in xs[s]:
+                x_ref[at : at + ref.shape[0], :] = ref[...]
+                at += ref.shape[0]
+
+    hat, _ = norm_rows(x_ref[...].astype(F32))
+    first = (hat * g_ref[...] + b_ref[...]).astype(BF16)
+    qkv = mm(w_ref[...], first, NT)
+    place = c * BLK + lax.broadcasted_iota(jnp.int32, (8, BLK), 1)
+    ident = jnp.zeros((8, BLK), jnp.int32)
+    place_k = c * BLK + lax.broadcasted_iota(jnp.int32, (BLK, 128), 0)
+    ident_k = jnp.zeros((BLK, 128), jnp.int32)
+    for bound in bounds:
+        ident = ident + (place >= bound).astype(jnp.int32)
+        ident_k = ident_k + (place_k >= bound).astype(jnp.int32)
+    which = lax.broadcasted_iota(jnp.int32, (8, BLK), 0)
+    hot = jnp.where((ident == which) & (which < len(bounds)), 16.0, 0.0)
+    hot = jnp.concatenate([hot, jnp.zeros((hd - 8, BLK), F32)], axis=0)
+    lane = lax.broadcasted_iota(jnp.int32, (BLK, 128), 1) - hd
+    hot_k = jnp.where((ident_k == lane) & (lane < len(bounds)), SHIFT / 16.0, 0.0)
+    for h in range(heads):
+        q, _ = norm_cols(qkv[h * hd : (h + 1) * hd])
+        k, _ = norm_cols(qkv[wid + h * hd : wid + (h + 1) * hd])
+        q = (q * gq_ref[...]).astype(BF16).astype(F32) * (hd**-0.5)
+        k = k * gk_ref[...]
+        v = qkv[2 * wid + h * hd : 2 * wid + (h + 1) * hd]
+        qt_ref[h] = jnp.concatenate([q, hot], axis=0).astype(BF16)
+        kt_ref[h] = k.astype(BF16)
+        vt_ref[h] = v.astype(BF16)
+        both = jnp.transpose(jnp.concatenate([k, v], axis=0))
+        ka_ref[h] = jnp.where(lane < 0, both, hot_k).astype(BF16)
+        v_ref[h] = both[:, hd:].astype(BF16)
+
+
+def make_qkv(meta, lengths, slots, w_t, gain, bias, gq, gk, heads, hd, before=None):
+    cuts = tuple(len(one) for one in slots)
+    blocks = 2 * len(cuts)
     width = slots[0][0].shape[1]
-    cuts = tuple(len(one) for one in slots)
-    smem = pl.BlockSpec(memory_space=pltpu.SMEM)
-    vmem = pl.BlockSpec(memory_space=pltpu.VMEM)
+    length = blocks * BLK
+    first = len(cuts) if before else 0
+    spot = lambda i, m: jnp.bitwise_xor(m[0], first + i)
+    whole = lambda value: pl.BlockSpec(value.shape, lambda i, m, n: (0,) * value.ndim)
+    operands = [*sum(slots, ()), w_t, gain, bias, gq, gk]
+    columns = lambda rows: pl.BlockSpec((heads, rows, BLK), lambda i, m, n: (0, 0, spot(i, m)))
+    lines = lambda size: pl.BlockSpec((heads, BLK, size), lambda i, m, n: (0, spot(i, m), 0))
+
+    def body(meta, len_ref, *refs):
+        qkv_body(heads, hd, cuts, meta, len_ref, *refs, spot(pl.program_id(0), meta))
+
+    more = list(before or ())
     return pl.pallas_call(
-        functools.partial(qkv_body, heads, hd, cuts),
+        body,
+        grid_spec=pltpu.PrefetchScalarGridSpec(
+            num_scalar_prefetch=2,
+            grid=(len(cuts),),
+            in_specs=[whole(value) for value in operands] + [pl.BlockSpec(memory_space=pl.ANY)] * len(more),
+            out_specs=(
+                columns(2 * hd),
+                lines(2 * hd),
+                columns(hd),
+                lines(hd),
+                columns(hd),
+                pl.BlockSpec((BLK, width), lambda i, m, n: (spot(i, m), 0)),
+            ),
+        ),
         out_shape=(
             jax.ShapeDtypeStruct((heads, 2 * hd, length), BF16),
             jax.ShapeDtypeStruct((heads, length, 2 * hd), BF16),
@@ -115,12 +141,11 @@
             jax.ShapeDtypeStruct((heads, hd, length), BF16),
             jax.ShapeDtypeStruct((length, width), BF16),
         ),
-        in_specs=[smem, smem] + [vmem] * (sum(cuts) + 5),
-        out_specs=(vmem,) * 6,
+        input_output_aliases={2 + len(operands) + k: k for k in range(len(more))},
         compiler_params=params(),
-        cost_estimate=cost(12),
+        cost_estimate=cost(6),
         name="qkv_forward",
-    )(meta, lengths, *sum(slots, ()), w_t, gain, bias, gq, gk)
+    )(meta, lengths, *operands, *more)
 
 
 def block_range(bounds, i):
@@ -696,50 +721,66 @@
     )(meta, act, dy, attn_t, gb, *([far] if own else []))
 
 
-def assemble(meta, downs, ups):
+def place(ref, value, swapped):
+    half = value.shape[1] // 2
+    lo, hi = value[:, :half].astype(F32), value[:, half:].astype(F32)
+    ref[:, :half] = jnp.where(swapped == 0, lo, hi)
+    ref[:, half:] = jnp.where(swapped == 0, hi, lo)
+
+
+def assemble_down(meta, downs):
     rows, width = downs[0].shape
     half = width // 2
     quarter = rows - half
-    hidden = ups[0].shape[1] * 2
-
-    def body(meta, down_aa, down_ab, down_ba, down_bb, up_a, up_b, down_ref, up_ref, out_ref):
+
+    def body(meta, down_aa, down_ab, down_ba, down_bb, down_ref, out_ref):
         i = pl.program_id(0)
-
-        def place(ref, value, swapped):
-            lo, hi = value[:, :half].astype(F32), value[:, half:].astype(F32)
-            ref[:, :half] = jnp.where(swapped == 0, lo, hi)
-            ref[:, half:] = jnp.where(swapped == 0, hi, lo)
-
         down_x, down_y = i // 2 == meta[3], lax.rem(i, 2) == meta[4]
         own_x = jnp.where(down_y, down_aa[...], down_ab[...])
         down = jnp.where(down_x, own_x, jnp.where(down_y, down_ba[...], down_bb[...]))
         place(down_ref, down[:half], meta[5])
         place(out_ref, down[half:], meta[5])
-        place(up_ref, jnp.where(i // 2 == meta[4], up_a[...], up_b[...]), meta[3])
-
-    down = pl.BlockSpec((rows, width), lambda i, m: (0, 0))
-    up = pl.BlockSpec((half, width), lambda i, m: (0, jnp.bitwise_xor(lax.rem(i, 2), m[5])))
+
     return pl.pallas_call(
         body,
         grid_spec=pltpu.PrefetchScalarGridSpec(
             num_scalar_prefetch=1,
             grid=(4,),
-            in_specs=[down, down, down, down, up, up],
+            in_specs=[pl.BlockSpec((rows, width), lambda i, m: (0, 0))] * 4,
             out_specs=(
                 pl.BlockSpec((half, width), lambda i, m: (i, 0)),
-                pl.BlockSpec((half, width), lambda i, m: (0, i)),
                 pl.BlockSpec((quarter, width), lambda i, m: (i, 0)),
             ),
         ),
         out_shape=(
             jax.ShapeDtypeStruct((4 * half, width), F32),
-            jax.ShapeDtypeStruct((half, hidden), F32),
             jax.ShapeDtypeStruct((half, width), F32),
         ),
         compiler_params=params(),
-        cost_estimate=cost(7),
-        name="weight_gradients",
-    )(meta, *downs, *ups)
+        cost_estimate=cost(4),
+        name="down_out_in_place",
+    )(meta, *downs)
+
+
+def assemble_up(meta, ups):
+    half, width = ups[0].shape[0], ups[0].shape[1] // 2
+
+    def body(meta, up_a, up_b, up_ref):
+        place(up_ref, jnp.where(pl.program_id(0) // 2 == meta[4], up_a[...], up_b[...]), meta[3])
+
+    return pl.pallas_call(
+        body,
+        grid_spec=pltpu.PrefetchScalarGridSpec(
+            num_scalar_prefetch=1,
+            grid=(4,),
+            in_specs=[pl.BlockSpec((half, width), lambda i, m: (0, jnp.bitwise_xor(lax.rem(i, 2), m[5])))] * 2,
+            out_specs=pl.BlockSpec((half, width), lambda i, m: (0, i)),
+        ),
+        out_shape=jax.ShapeDtypeStruct((half, 4 * width), F32),
+        compiler_params=params(),
+        cost_estimate=cost(4),
+        name="up_in_place",
+    )(meta, *ups)
 
 
 def finish_body(x_ref, gm_ref, back_ref, g_ref, out_ref):
@@ -852,7 +893,8 @@
     out_p, up_p, down_p = swap(out_weight), swap(up_weight), swap(down_weight)
 
     with jax.named_scope("forward_attention"):
-        qt, ka, kt, v, vt, x_row = make_qkv(meta, lengths, slots, w_t, g1, b1, gq, gk, heads, hd)
+        near = make_qkv(meta, lengths, slots[:4], w_t, g1, b1, gq, gk, heads, hd)
+        qt, ka, kt, v, vt, x_row = make_qkv(meta, lengths, slots[4:], w_t, g1, b1, gq, gk, heads, hd, near)
         attn, attn_f, logsum = attend(meta, lengths, qt, ka, vt, heads, hd)
 
     def exchange(value):
@@ -976,7 +1018,8 @@
         ups = (up, flip(up, *y))
     grad_tokens = finish(x_home, grad_mid, back, g1)
     grad_qkv, small = assemble_qkv(meta, pieces, heads, hd)
-    grad_down, grad_up, grad_out = assemble(meta, downs, ups)
+    grad_down, grad_out = assemble_down(meta, downs)
+    grad_up = assemble_up(meta, ups)
     cuts = [small[k] for k in range(4)] + [small[4, : hd // 2], small[5, : hd // 2]]
     shape = tokens.shape
     return (

time: 375 us -> 375 us (level)
  Pallas kernels: 144 us -> 153 us
  starting transfers between devices: 58.9 us -> 52.6 us
    ppermute x42, starting transfers between devices: 48.3 us -> 41.8 us  [flip(): return lax.ppermute(value, axis, [(i, i ^ mask) for i in range(size)])]
    pallas_call x2 -> x4, Pallas kernels: 20.8 us -> 27.2 us  [the longest x2 15.9 us: make_qkv(): pl.pallas_call(body, grid_spec=pltpu.PrefetchScalarGridSpec(num_scalar_pr...]
    ppermute x42, waiting for transfers between devices: 106 us -> 101 us  [flip(): return lax.ppermute(value, axis, [(i, i ^ mask) for i in range(size)])]
    unnamed x70 -> x74, local copies, waits for them, and re-layouts: 14.7 us -> 15.9 us
  transfers between devices with their start and end apart: 44 -> 44, of which waited for: 17 -> 17; matrix products, arithmetic and copies ran while one was open for 7% -> 8% of each run, Pallas kernels for 28% -> 31%
where the time goes in v11:
time: 375 us; the launch traced here: 374 us
  Pallas kernels  153 us (41%)
  waiting for transfers between devices  121 us (32%)
  starting transfers between devices  52.6 us (14%)
  local copies, waits for them, and re-layouts  29.1 us (8%)
  other arithmetic  17.5 us (5%)
    ppermute x42, waiting for transfers between devices, flip(): return lax.ppermute(value, axis, [(i, i ^ mask) for i in range(size)])  101 us
    ppermute x42, starting transfers between devices, flip(): return lax.ppermute(value, axis, [(i, i ^ mask) for i in range(size)])  41.8 us
    pallas_call x2, Pallas kernels, attend_back(): pl.pallas_call(functools.partial(attend_back_body, first, heads, hd), gri...  31.2 us
    pallas_call x1, Pallas kernels, ffn(): pl.pallas_call(body, grid_spec=pltpu.PrefetchScalarGridSpec(num_scalar_pr...  25.9 us
    all_to_all x2, waiting for transfers between devices, exchange(): return lax.all_to_all(value, 'seq', 0, 0, tiled=True)  19.7 us
    pallas_call x1, Pallas kernels, qkv_back(): pl.pallas_call(functools.partial(qkv_back_body, heads, hd), grid_spec=plt...  17.9 us
    pallas_call x2, Pallas kernels, make_qkv(): pl.pallas_call(body, grid_spec=pltpu.PrefetchScalarGridSpec(num_scalar_pr...  15.9 us
    unnamed x74, local copies, waits for them, and re-layouts  15.9 us
  transfers between devices with their start and end apart: 44, of which 17 were waited for; matrix products, arithmetic and copies ran while one was open for 8% of the time, Pallas kernels for 31%

profile of v11, /device:TPU:0, one launch (start us, length us, event | category | flops | bytes accessed | tf_op | source)
XLA Modules:
  0.0 374.0 jit_solution(2987061595319451339)
XLA Ops:
  13.4 10.3 %collective-permute-done.refs_0_ = bf16[256,768]{1,0:T(8,128)(2,1)S(1)} collective-permute-done((bf16[256,768]{1,0:T(8,128)(2,1)S(1)}, bf16[256,768]{1,0:T(8,128)(2,1)S(1)}, u32[]{:S(2)}, u32[]{:S(2)}) %collective-permute-start) | collective-permute-done | bytes 393248 | tf_op jit(solution)/shard_map/ppermute | solution.py:811
  40.9 7.9 %qkv_forward.2 = (bf16[3,128,2048]{2,1,0:T(8,128)(2,1)}, bf16[3,2048,128]{2,1,0:T(8,128)(2,1)}, bf16[3,64,2048]{2,1,0:T(8,128)(2,1)}, bf16[3,2048,64]{2,1,0:T(8,...) custom-call(s32[6]{0:T(128)} %stack.46.meta, s32[2,8]{1,0:T(2,128)} %bitcast.109, ...), custom_call_target="tpu_custom_call" | custom-call | flops 2100000000 | bytes 1024 | tf_op jit(solution)/shard_map/forward_attention/qkv_forward/pallas_call | solution.py:121
  49.6 7.9 %qkv_forward.3 = (bf16[3,128,2048]{2,1,0:T(8,128)(2,1)}, bf16[3,2048,128]{2,1,0:T(8,128)(2,1)}, bf16[3,64,2048]{2,1,0:T(8,128)(2,1)}, bf16[3,2048,64]{2,1,0:T(8,...) custom-call(s32[6]{0:T(128)} %stack.46.meta, ...), custom_call_target="tpu_custom_call", output_to_operand_aliasing={{0}: (12, {}), {1}: (13, {}), {2}: (14, {}), {3}: (15, {}),... | custom-call | flops 2100000000 | bytes 1024 | tf_op jit(solution)/shard_map/forward_attention/qkv_forward/pallas_call | solution.py:121
  57.6 14.3 %attention_forward.1 = (bf16[8,192,256]{2,1,0:T(8,128)(2,1)}, f32[3,64,2048]{2,1,0:T(8,128)}, f32[3,1,2048]{2,1,0:T(1,128)}) custom-call(s32[6]{0:T(128)} %stack.46.meta, s32[2,8]{1,0:T(2,128)} %bitcast.111, bf16[3,128,2048]{2,1,0:T(8,128)(2,1)} %get-tuple-element.91.qt_ref.refs_0_, bf16[3,2048,128]{2,1,0:T(8,128)(2,1)} %get-tuple-element.92.ka_ref.refs_1_, ...), custom_call_target="tpu_custom_call" | custom-call | flops 8750000128 | bytes 1024 | tf_op jit(solution)/shard_map/forward_attention/attention_forward/pallas_call | solution.py:205
  71.9 6.3 %all-to-all-start = ((bf16[8,192,256]{2,1,0:T(8,128)(2,1)}), bf16[8,192,256]{2,1,0:T(8,128)(2,1)S(1)}, u32[]{:S(2)}, u32[]{:S(2)}) async-start(bf16[8,192,256]{2,1,0:T(8,128)(2,1)} %get-tuple-element.94), calls=%async_computation | async-start | bytes 1572864 | tf_op jit(solution)/shard_map/all_to_all | solution.py:901
  80.3 16.9 %all-to-all-done = bf16[8,192,256]{2,1,0:T(8,128)(2,1)S(1)} async-done(((bf16[8,192,256]{2,1,0:T(8,128)(2,1)}), bf16[8,192,256]{2,1,0:T(8,128)(2,1)S(1)}, u32[]{:S(2)}, u32[]{:S(2)}) %all-to-all-start) | async-done | bytes 786464 | tf_op jit(solution)/shard_map/all_to_all | solution.py:901
  98.0 25.9 %ffn_both_ways.1 = (bf16[512,768]{1,0:T(8,128)(2,1)}, f32[512,768]{1,0:T(8,128)}, bf16[512,768]{1,0:T(8,128)(2,1)}, bf16[768,512]{1,0:T(8,128)(2,1)}, bf16[512,3...) custom-call(s32[6]{0:T(128)} %stack.46.meta, ...), custom_call_target="tpu_custom_call" | custom-call | flops 8750000128 | bytes 1024 | tf_op jit(solution)/shard_map/feed_forward/ffn_both_ways/pallas_call | solution.py:550
  124.0 6.4 %down_out_gradient.2 = bf16[1920,768]{1,0:T(8,128)(2,1)} custom-call(s32[6]{0:T(128)} %stack.46.meta, bf16[512,3072]{1,0:T(8,128)(2,1)} %get-tuple-element.107.act_ref, bf16[512,768]{1,0:T(8,128)(2,1)} %bitcast.87, bf16[2,768,256]{2,1,0:T(8,128)(2,1)} %bitcast.84, bf16[512,768]{1,0:T(8,128)(2,1)} %get-tuple-element.108.gb_ref), custom_call_target="tpu_custom_call" | custom-call | flops 70000000 | bytes 1024 | tf_op jit(solution)/shard_map/weight_gradients/down_out_gradient/pallas_call | solution.py:703
  130.4 5.9 %up_gradient.2 = bf16[384,3072]{1,0:T(8,128)(2,1)} custom-call(s32[6]{0:T(128)} %stack.46.meta, bf16[768,512]{1,0:T(8,128)(2,1)} %get-tuple-element.103.h2_ref, bf16[512,3072]{1,0:T(8,128)(2,1)} %get-tuple-element.104.dup_ref), custom_call_target="tpu_custom_call" | custom-call | flops 70000000 | bytes 1024 | tf_op jit(solution)/shard_map/weight_gradients/up_gradient/pallas_call | solution.py:633
  142.8 7.5 %down_out_gradient.3 = (bf16[960,768]{1,0:T(8,128)(2,1)}, bf16[960,768]{1,0:T(8,128)(2,1)}) custom-call(s32[6]{0:T(128)} %stack.46.meta, bf16[512,3072]{1,0:T(8,128)(2,1)} %get-tuple-element.107.act_ref, bf16[512,768]{1,0:T(8,128)(2,1)} %bitcast.88, bf16[2,768,256]{2,1,0:T(8,128)(2,1)} %bitcast.85, bf16[512,768]{1,0:T(8,128)(2,1)} %get-tuple-element.108.gb_ref, ...), custom_call_target="tpu_custom_call" | custom-call | flops 70000000 | bytes 1024 | tf_op jit(solution)/shard_map/weight_gradients/down_out_gradient/pallas_call | solution.py:703
  150.6 6.6 %up_gradient.3 = (bf16[384,1536]{1,0:T(8,128)(2,1)}, bf16[384,1536]{1,0:T(8,128)(2,1)}) custom-call(s32[6]{0:T(128)} %stack.46.meta, bf16[768,512]{1,0:T(8,128)(2,1)} %get-tuple-element.103.h2_ref, bf16[512,3072]{1,0:T(8,128)(2,1)} %get-tuple-element.104.dup_ref, bf16[384,3072]{1,0:T(8,128)(2,1)} %collective-permute-done.14.rest_0_), custom_call_target="tpu_custom_call" | custom-call | flops 70000000 | bytes 1024 | tf_op jit(solution)/shard_map/weight_gradients/up_gradient/pallas_call | solution.py:633
  161.6 14.0 %attention_backward.2 = (f32[3,64,2048]{2,1,0:T(8,128)}, f32[3,64,2048]{2,1,0:T(8,128)}, f32[3,64,2048]{2,1,0:T(8,128)}) custom-call(s32[6]{0:T(128)} %stack.46.meta, s32[2,8]{1,0:T(2,128)} %bitcast.112, bf16[3,128,2048]{2,1,0:T(8,128)(2,1)} %get-tuple-element.91.qt_ref.refs_0_, bf16[3,2048,128]{2,1,0:T(8,128)(2,1)} %get-tuple-element.92.ka_ref.refs_1_, ...), custom_call_target="tpu_custom_call" | custom-call | flops 5249999872 | bytes 1024 | tf_op jit(solution)/shard_map/backward_attention/attention_backward/pallas_call | solution.py:280
  175.6 9.5 %collective-permute-done.17 = bf16[384,1536]{1,0:T(8,128)(2,1)} collective-permute-done((bf16[384,1536]{1,0:T(8,128)(2,1)}, bf16[384,1536]{1,0:T(8,128)(2,1)}, u32[]{:S(2)}, u32[]{:S(2)}) %collective-permute-start.17) | collective-permute-done | bytes 1179680 | tf_op jit(solution)/shard_map/weight_gradients/ppermute | solution.py:811
  194.2 17.2 %attention_backward.3 = (f32[3,64,2048]{2,1,0:T(8,128)}, f32[3,64,2048]{2,1,0:T(8,128)}, f32[3,64,2048]{2,1,0:T(8,128)}) custom-call(s32[6]{0:T(128)} %stack.46.meta, s32[2,8]{1,0:T(2,128)} %bitcast.113, bf16[3,128,2048]{2,1,0:T(8,128)(2,1)} %get-tuple-element.91.qt_ref.refs_0_, ...), custom_call_target="tpu_custom_call", output_to_operand_aliasing={{0}: (9, {})} | custom-call | flops 5249999872 | bytes 1024 | tf_op jit(solution)/shard_map/backward_attention/attention_backward/pallas_call | solution.py:280
  216.0 7.0 %collective-permute-done.21 = bf16[384,384]{1,0:T(8,128)(2,1)S(1)} collective-permute-done((bf16[384,384]{1,0:T(8,128)(2,1)S(1)}, bf16[384,384]{1,0:T(8,128)(2,1)S(1)}, u32[]{:S(2)}, u32[]{:S(2)}) %collective-permute-start.21) | collective-permute-done | bytes 294944 | tf_op jit(solution)/shard_map/weight_gradients/ppermute | solution.py:811
  226.8 17.9 %qkv_backward.1 = (bf16[8,256,384]{2,1,0:T(8,128)(2,1)}, bf16[8,256,384]{2,1,0:T(8,128)(2,1)}, bf16[608,768]{1,0:T(8,128)(2,1)}) custom-call(s32[6]{0:T(128)} %stack.46.meta, bf16[2048,768]{1,0:T(8,128)(2,1)} %get-tuple-element.97.x_ref, f32[3,64,2048]{2,1,0:T(8,128)} %get-tuple-element.128.refs_0_, f32[3,64,2048]{2,1,0:T(8,128)} %get-tuple-element.129.refs_1_, ...), custom_call_target="tpu_custom_call" | custom-call | flops 5950000128 | bytes 1024 | tf_op jit(solution)/shard_map/backward_attention/qkv_backward/pallas_call | solution.py:375
  247.6 8.5 %collective-permute-done.22 = bf16[864,384]{1,0:T(8,128)(2,1)S(1)} collective-permute-done((bf16[864,384]{1,0:T(8,128)(2,1)S(1)}, bf16[864,384]{1,0:T(8,128)(2,1)S(1)}, u32[]{:S(2)}, u32[]{:S(2)}) %collective-permute-start.22) | collective-permute-done | bytes 663584 | tf_op jit(solution)/shard_map/weight_gradients/ppermute | solution.py:811
  266.7 12.3 %collective-permute-done.28 = bf16[2,2,256,384]{3,2,0,1:T(8,128)(2,1)} collective-permute-done((bf16[2,2,256,384]{3,2,0,1:T(8,128)(2,1)}, bf16[2,2,256,384]{3,2,0,1:T(8,128)(2,1)}, u32[]{:S(2)}, u32[]{:S(2)}) %collective-permute-start.28) | collective-permute-done | bytes 786464 | tf_op jit(solution)/shard_map/first_round/ppermute | solution.py:811
  279.0 7.4 %collective-permute-done.23 = bf16[480,384]{1,0:T(8,128)(2,1)} collective-permute-done((bf16[480,384]{1,0:T(8,128)(2,1)S(1)}, bf16[480,384]{1,0:T(8,128)(2,1)}, u32[]{:S(2)}, u32[]{:S(2)}) %collective-permute-start.23) | collective-permute-done | bytes 368672 | tf_op jit(solution)/shard_map/first_round/ppermute | solution.py:811
  301.8 12.3 %collective-permute-done.34 = bf16[2,256,384]{2,1,0:T(8,128)(2,1)S(1)} collective-permute-done((bf16[2,256,384]{2,1,0:T(8,128)(2,1)S(1)}, bf16[2,256,384]{2,1,0:T(8,128)(2,1)S(1)}, u32[]{:S(2)}, u32[]{:S(2)}) %collective-permute-start.34) | collective-permute-done | bytes 393248 | tf_op jit(solution)/shard_map/second_round/ppermute | solution.py:811
  314.1 6.4 %collective-permute-done.33 = bf16[2,256,384]{2,1,0:T(8,128)(2,1)S(1)} collective-permute-done((bf16[2,256,384]{2,1,0:T(8,128)(2,1)S(1)}, bf16[2,256,384]{2,1,0:T(8,128)(2,1)S(1)}, u32[]{:S(2)}, u32[]{:S(2)}) %collective-permute-start.33) | collective-permute-done | bytes 393248 | tf_op jit(solution)/shard_map/second_round/ppermute | solution.py:811
  332.7 12.2 %collective-permute-done.37.p01 = bf16[2,304,384]{2,1,0:T(8,128)(2,1)} collective-permute-done((bf16[2,304,384]{2,1,0:T(8,128)(2,1)S(1)}, bf16[2,304,384]{2,1,0:T(8,128)(2,1)}, u32[]{:S(2)}, u32[]{:S(2)}) %collective-permute-start.37) | collective-permute-done | bytes 466976 | tf_op jit(solution)/shard_map/third_round/ppermute | solution.py:811
  353.7 5.5 %down_out_in_place.1 = (f32[1536,768]{1,0:T(8,128)}, f32[384,768]{1,0:T(8,128)}) custom-call(s32[6]{0:T(128)} %stack.46.meta, bf16[480,768]{1,0:T(8,128)(2,1)} %copy-done.12, bf16[480,768]{1,0:T(8,128)(2,1)} %copy-done.27, bf16[480,768]{1,0:T(8,128)(2,1)} %copy-done.26, bf16[480,768]{1,0:T(8,128)(2,1)} %copy-done.28), custom_call_target="tpu_custom_call" | custom-call | flops 1400000000 | bytes 1024 | tf_op jit(solution)/shard_map/down_out_in_place/pallas_call | solution.py:744
  368.2 5.8 %up_in_place.1 = f32[384,3072]{1,0:T(8,128)} custom-call(s32[6]{0:T(128)} %stack.46.meta, bf16[384,1536]{1,0:T(8,128)(2,1)} %copy-done.1, bf16[384,1536]{1,0:T(8,128)(2,1)} %copy-done.6), custom_call_target="tpu_custom_call" | custom-call | flops 1400000000 | bytes 1024 | tf_op jit(solution)/shard_map/up_in_place/pallas_call | solution.py:771
  (204 shorter events, 120.7 us)
Async XLA Ops:
  1.9 21.8 %collective-permute-start = (bf16[256,768]{1,0:T(8,128)(2,1)S(1)}, bf16[256,768]{1,0:T(8,128)(2,1)S(1)}, u32[]{:S(2)}, u32[]{:S(2)}) collective-permute-start(bf16[256,768]{1,0:T(8,128)(2,1)S(1)} %get-tuple-element.193), channel_id=1, source_target_pairs={{0,4},{1,5},{2,6},{3,7},{4,0},{5,1},{6,2},{7,3},{8,12},{9,13},{10,... | collective-permute-start | bytes 1179656 | tf_op jit(solution)/shard_map/ppermute | solution.py:811
  6.0 19.8 %collective-permute-start.8 = (bf16[256,768]{1,0:T(8,128)(2,1)S(1)}, bf16[256,768]{1,0:T(8,128)(2,1)}, u32[]{:S(2)}, u32[]{:S(2)}) collective-permute-start(bf16[256,768]{1,0:T(8,128)(2,1)S(1)} %get-tuple-element.192.refs_0_), channel_id=1, source_target_pairs={{0,2},{1,3},{2,0},{3,1},{4,6},{5,7},{6,4},{7,5},{8,10},{9,11},{10,... | collective-permute-start | bytes 1179656 | tf_op jit(solution)/shard_map/ppermute | solution.py:811
  7.6 19.7 %collective-permute-start.7 = (bf16[256,768]{1,0:T(8,128)(2,1)S(1)}, bf16[256,768]{1,0:T(8,128)(2,1)}, u32[]{:S(2)}, u32[]{:S(2)}) collective-permute-start(bf16[256,768]{1,0:T(8,128)(2,1)S(1)} %get-tuple-element.192.refs_0_), channel_id=1, source_target_pairs={{0,1},{1,0},{2,3},{3,2},{4,5},{5,4},{6,7},{7,6},{8,9},{9,8},{10,11... | collective-permute-start | bytes 1179656 | tf_op jit(solution)/shard_map/ppermute | solution.py:811
  12.2 20.2 %collective-permute-start.5 = (bf16[384,576]{0,1:T(8,128)(2,1)S(1)}, bf16[384,576]{0,1:T(8,128)(2,1)S(1)}, u32[]{:S(2)}, u32[]{:S(2)}) collective-permute-start(bf16[384,576]{0,1:T(8,128)(2,1)S(1)} %bitcast.90), channel_id=1, source_target_pairs={{0,8},{8,0},{1,9},{9,1},{2,10},{10,2},{3,11},{11,3},{4,12},{12,4},... | collective-permute-start | bytes 1327112 | tf_op jit(solution)/shard_map/ppermute | solution.py:811
  32.4 47.9 %collective-permute-start.12 = (bf16[384,3072]{1,0:T(8,128)(2,1)}, bf16[384,3072]{1,0:T(8,128)(2,1)}, u32[]{:S(2)}, u32[]{:S(2)}) collective-permute-start(bf16[384,3072]{1,0:T(8,128)(2,1)} %refs_8_.1), channel_id=1, source_target_pairs={{0,8},{8,0},{1,9},{9,1},{2,10},{10,2},{3,11},{11,3},{4,12},{12,4},... | collective-permute-start | bytes 7077896 | tf_op jit(solution)/shard_map/ppermute | solution.py:811
  35.7 44.6 %collective-permute-start.13 = (bf16[1536,768]{1,0:T(8,128)(2,1)}, bf16[1536,768]{1,0:T(8,128)(2,1)}, u32[]{:S(2)}, u32[]{:S(2)}) collective-permute-start(bf16[1536,768]{1,0:T(8,128)(2,1)} %refs_10_.1), channel_id=1, source_target_pairs={{0,8},{8,0},{1,9},{9,1},{2,10},{10,2},{3,11},{11,3},{4,12},{12,4},... | collective-permute-start | bytes 7077896 | tf_op jit(solution)/shard_map/ppermute | solution.py:811
  71.9 25.3 %all-to-all-start = ((bf16[8,192,256]{2,1,0:T(8,128)(2,1)}), bf16[8,192,256]{2,1,0:T(8,128)(2,1)S(1)}, u32[]{:S(2)}, u32[]{:S(2)}) async-start(bf16[8,192,256]{2,1,0:T(8,128)(2,1)} %get-tuple-element.94), calls=%async_computation | async-start | bytes 1572864 | tf_op jit(solution)/shard_map/all_to_all | solution.py:901
  136.8 24.8 %all-to-all-start.1 = ((bf16[8,192,256]{2,1,0:T(8,128)(2,1)}), bf16[8,192,256]{2,1,0:T(8,128)(2,1)}, u32[]{:S(2)}, u32[]{:S(2)}) async-start(bf16[8,192,256]{2,1,0:T(8,128)(2,1)} %bitcast.95), calls=%async_computation.1 | async-start | bytes 1572864 | tf_op jit(solution)/shard_map/all_to_all | solution.py:901
  150.3 34.8 %collective-permute-start.16 = (bf16[960,768]{1,0:T(8,128)(2,1)}, bf16[960,768]{1,0:T(8,128)(2,1)S(1)}, u32[]{:S(2)}, u32[]{:S(2)}) collective-permute-start(bf16[960,768]{1,0:T(8,128)(2,1)} %get-tuple-element.110), channel_id=1, source_target_pairs={{0,16},{16,0},{1,17},{17,1},{2,18},{18,2},{3,19},{19,3},{4,20},{20... | collective-permute-start | bytes 4423688 | tf_op jit(solution)/shard_map/weight_gradients/ppermute | solution.py:811
  157.2 27.9 %collective-permute-start.17 = (bf16[384,1536]{1,0:T(8,128)(2,1)}, bf16[384,1536]{1,0:T(8,128)(2,1)}, u32[]{:S(2)}, u32[]{:S(2)}) collective-permute-start(bf16[384,1536]{1,0:T(8,128)(2,1)} %get-tuple-element.106), channel_id=1, source_target_pairs={{0,1},{1,0},{2,3},{3,2},{4,5},{5,4},{6,7},{7,6},{8,9},{9,8},{10,11... | collective-permute-start | bytes 3538952 | tf_op jit(solution)/shard_map/weight_gradients/ppermute | solution.py:811
  188.9 22.5 %collective-permute-start.18 = (bf16[480,768]{1,0:T(8,128)(2,1)}, bf16[480,768]{1,0:T(8,128)(2,1)S(1)}, u32[]{:S(2)}, u32[]{:S(2)}) collective-permute-start(bf16[480,768]{1,0:T(8,128)(2,1)} %constant_dynamic-slice_fusion.5), channel_id=1, source_target_pairs={{0,1},{1,0},{2,3},{3,2},{4,5},{5,4},{6,7},{7,6},{8,9},{9,8},{10,11... | collective-permute-start | bytes 2211848 | tf_op jit(solution)/shard_map/weight_gradients/ppermute | solution.py:811
  225.0 31.1 %collective-permute-start.22 = (bf16[864,384]{1,0:T(8,128)(2,1)S(1)}, bf16[864,384]{1,0:T(8,128)(2,1)S(1)}, u32[]{:S(2)}, u32[]{:S(2)}) collective-permute-start(bf16[864,384]{1,0:T(8,128)(2,1)S(1)} %pad_maximum_fusion.2), channel_id=1, source_target_pairs={{0,4},{1,5},{2,6},{3,7},{4,0},{5,1},{6,2},{7,3},{8,12},{9,13},{10,... | collective-permute-start | bytes 1990664 | tf_op jit(solution)/shard_map/weight_gradients/ppermute | solution.py:811
  247.2 19.5 %collective-permute-start.27 = (bf16[2,2,256,384]{3,2,0,1:T(8,128)(2,1)}, bf16[2,2,256,384]{3,2,0,1:T(8,128)(2,1)}, u32[]{:S(2)}, u32[]{:S(2)}) collective-permute-start(bf16[2,2,256,384]{3,2,0,1:T(8,128)(2,1)} %bitcast.82), channel_id=1, source_target_pairs={{0,1},{1,0},{2,3},{3,2},{4,5},{5,4},{6,7},{7,6},{8,9},{9,8},{10,11... | collective-permute-start | bytes 2359304 | tf_op jit(solution)/shard_map/first_round/ppermute | solution.py:811
  258.3 20.7 %collective-permute-start.28 = (bf16[2,2,256,384]{3,2,0,1:T(8,128)(2,1)}, bf16[2,2,256,384]{3,2,0,1:T(8,128)(2,1)}, u32[]{:S(2)}, u32[]{:S(2)}) collective-permute-start(bf16[2,2,256,384]{3,2,0,1:T(8,128)(2,1)} %bitcast.81), channel_id=1, source_target_pairs={{0,2},{1,3},{2,0},{3,1},{4,6},{5,7},{6,4},{7,5},{8,10},{9,11},{10,... | collective-permute-start | bytes 2359304 | tf_op jit(solution)/shard_map/first_round/ppermute | solution.py:811
  259.1 19.9 %collective-permute-start.24 = (bf16[384,384]{1,0:T(8,128)(2,1)S(1)}, bf16[384,384]{1,0:T(8,128)(2,1)S(1)}, u32[]{:S(2)}, u32[]{:S(2)}) collective-permute-start(bf16[384,384]{1,0:T(8,128)(2,1)S(1)} %split.7), channel_id=1, source_target_pairs={{0,16},{16,0},{1,17},{17,1},{2,18},{18,2},{3,19},{19,3},{4,20},{20... | collective-permute-start | bytes 884744 | tf_op jit(solution)/shard_map/first_round/ppermute | solution.py:811
  259.2 27.3 %collective-permute-start.23 = (bf16[480,384]{1,0:T(8,128)(2,1)S(1)}, bf16[480,384]{1,0:T(8,128)(2,1)}, u32[]{:S(2)}, u32[]{:S(2)}) collective-permute-start(bf16[480,384]{1,0:T(8,128)(2,1)S(1)} %split.6), channel_id=1, source_target_pairs={{0,2},{1,3},{2,0},{3,1},{4,6},{5,7},{6,4},{7,5},{8,10},{9,11},{10,... | collective-permute-start | bytes 1105928 | tf_op jit(solution)/shard_map/first_round/ppermute | solution.py:811
  262.5 23.9 %collective-permute-start.26 = (bf16[304,384]{1,0:T(8,128)(2,1)}, bf16[304,384]{1,0:T(8,128)(2,1)S(1)}, u32[]{:S(2)}, u32[]{:S(2)}) collective-permute-start(bf16[304,384]{1,0:T(8,128)(2,1)} %constant_dynamic-slice_fusion), channel_id=1, source_target_pairs={{0,16},{16,0},{1,17},{17,1},{2,18},{18,2},{3,19},{19,3},{4,20},{20... | collective-permute-start | bytes 700424 | tf_op jit(solution)/shard_map/first_round/ppermute | solution.py:811
  287.5 33.0 %collective-permute-start.30 = (bf16[480,768]{1,0:T(8,128)(2,1)S(1)}, bf16[480,768]{1,0:T(8,128)(2,1)S(1)}, u32[]{:S(2)}, u32[]{:S(2)}) collective-permute-start(bf16[480,768]{1,0:T(8,128)(2,1)S(1)} %pad_maximum_fusion.1.down_aa), channel_id=1, source_target_pairs={{0,16},{16,0},{1,17},{17,1},{2,18},{18,2},{3,19},{19,3},{4,20},{20... | collective-permute-start | bytes 2211848 | tf_op jit(solution)/shard_map/second_round/ppermute | solution.py:811
  287.6 32.9 %collective-permute-start.29 = (bf16[480,768]{1,0:T(8,128)(2,1)S(1)}, bf16[480,768]{1,0:T(8,128)(2,1)S(1)}, u32[]{:S(2)}, u32[]{:S(2)}) collective-permute-start(bf16[480,768]{1,0:T(8,128)(2,1)S(1)} %pad_maximum_fusion.1.down_aa), channel_id=1, source_target_pairs={{0,1},{1,0},{2,3},{3,2},{4,5},{5,4},{6,7},{7,6},{8,9},{9,8},{10,11... | collective-permute-start | bytes 2211848 | tf_op jit(solution)/shard_map/second_round/ppermute | solution.py:811
  292.0 22.1 %collective-permute-start.34 = (bf16[2,256,384]{2,1,0:T(8,128)(2,1)S(1)}, bf16[2,256,384]{2,1,0:T(8,128)(2,1)S(1)}, u32[]{:S(2)}, u32[]{:S(2)}) collective-permute-start(bf16[2,256,384]{2,1,0:T(8,128)(2,1)S(1)} %slice_bitcast_fusion.1), channel_id=1, source_target_pairs={{0,1},{1,0},{2,3},{3,2},{4,5},{5,4},{6,7},{7,6},{8,9},{9,8},{10,11... | collective-permute-start | bytes 1179656 | tf_op jit(solution)/shard_map/second_round/ppermute | solution.py:811
  293.7 26.8 %collective-permute-start.31 = (bf16[384,768]{1,0:T(8,128)(2,1)S(1)}, bf16[384,768]{1,0:T(8,128)(2,1)S(1)}, u32[]{:S(2)}, u32[]{:S(2)}) collective-permute-start(bf16[384,768]{1,0:T(8,128)(2,1)S(1)} %pad_maximum_fusion.3), channel_id=1, source_target_pairs={{0,2},{1,3},{2,0},{3,1},{4,6},{5,7},{6,4},{7,5},{8,10},{9,11},{10,... | collective-permute-start | bytes 1769480 | tf_op jit(solution)/shard_map/second_round/ppermute | solution.py:811
  321.4 23.5 %collective-permute-start.38 = (bf16[480,768]{1,0:T(8,128)(2,1)S(1)}, bf16[480,768]{1,0:T(8,128)(2,1)S(1)}, u32[]{:S(2)}, u32[]{:S(2)}) collective-permute-start(bf16[480,768]{1,0:T(8,128)(2,1)S(1)} %collective-permute-done.29.down_ab), channel_id=1, source_target_pairs={{0,16},{16,0},{1,17},{17,1},{2,18},{18,2},{3,19},{19,3},{4,20},{20... | collective-permute-start | bytes 2211848 | tf_op jit(solution)/shard_map/third_round/ppermute | solution.py:811
  330.5 36.7 %collective-permute-start.41 = (bf16[384,1536]{1,0:T(8,128)(2,1)S(1)}, bf16[384,1536]{1,0:T(8,128)(2,1)S(1)}, u32[]{:S(2)}, u32[]{:S(2)}) collective-permute-start(bf16[384,1536]{1,0:T(8,128)(2,1)S(1)} %pad_maximum_fusion.up_a), channel_id=1, source_target_pairs={{0,1},{1,0},{2,3},{3,2},{4,5},{5,4},{6,7},{7,6},{8,9},{9,8},{10,11... | collective-permute-start | bytes 3538952 | tf_op jit(solution)/shard_map/third_round/ppermute | solution.py:811
  331.0 28.3 %collective-permute-start.39 = (bf16[2,304,384]{2,1,0:T(8,128)(2,1)S(1)}, bf16[2,304,384]{2,1,0:T(8,128)(2,1)}, u32[]{:S(2)}, u32[]{:S(2)}) collective-permute-start(bf16[2,304,384]{2,1,0:T(8,128)(2,1)S(1)} %pad_maximum_fusion.4.p00), channel_id=1, source_target_pairs={{0,16},{16,0},{1,17},{17,1},{2,18},{18,2},{3,19},{19,3},{4,20},{20... | collective-permute-start | bytes 1400840 | tf_op jit(solution)/shard_map/third_round/ppermute | solution.py:811
  (53 other events, 440.0 us)

commit v12 on v11

--- a/solution.py
+++ b/solution.py
@@ -271,8 +271,9 @@
 
 def attend_back(meta, lengths, qt, ka, kt, v, of, ls, go, heads, hd, before=None):
     length = qt.shape[2]
-    count = length // BLK // 2
-    first = count if before else 0
+    split = (5 * length) // (8 * BLK)
+    first = split if before else 0
+    count = length // BLK - split if before else split
     smem = pl.BlockSpec(memory_space=pltpu.SMEM)
     whole = lambda *shape: pl.BlockSpec(shape, lambda i: (0, 0, 0))
     part = lambda *shape: pl.BlockSpec(shape, lambda i: (0, 0, first + i))
@@ -1014,12 +1015,14 @@
             ).reshape(every * local, width)
         downs.append(flip(downs[1], *x))
         piece_z, downs[3] = tie(flip(piece, *z), downs[3])
+        grad_down, grad_out = assemble_down(meta, downs)
+        piece_z, grad_down, grad_out = tie(piece_z, grad_down, grad_out)
         pieces = [piece, piece_z, flip(piece, *x), flip(piece_z, *x)]
         ups = (up, flip(up, *y))
     grad_tokens = finish(x_home, grad_mid, back, g1)
+    grad_up, grad_tokens = tie(assemble_up(meta, ups), grad_tokens)
+    pieces[3], grad_up = tie(pieces[3], grad_up)
     grad_qkv, small = assemble_qkv(meta, pieces, heads, hd)
-    grad_down, grad_out = assemble_down(meta, downs)
-    grad_up = assemble_up(meta, ups)
     cuts = [small[k] for k in range(4)] + [small[4, : hd // 2], small[5, : hd // 2]]
     shape = tokens.shape
     return (

time: 375 us -> 377 us (level)
  Pallas kernels: 153 us -> 144 us
  waiting for transfers between devices: 121 us -> 127 us
  starting transfers between devices: 52.6 us -> 58 us
    ppermute x42, waiting for transfers between devices: 101 us -> 110 us  [flip(): return lax.ppermute(value, axis, [(i, i ^ mask) for i in range(size)])]
    pallas_call x2, Pallas kernels: 31.2 us -> 25.3 us  [attend_back(): pl.pallas_call(functools.partial(attend_back_body, first, heads, hd), gri...]
    unnamed x74 -> x72, local copies, waits for them, and re-layouts: 15.9 us -> 14.7 us
  transfers between devices with their start and end apart: 44 -> 44, of which waited for: 17 -> 18; matrix products, arithmetic and copies ran while one was open for 8% -> 7% of each run, Pallas kernels for 31% -> 28%
where the time goes in v12:
time: 377 us; the launch traced here: 376 us
  Pallas kernels  144 us (38%)
  waiting for transfers between devices  127 us (34%)
  starting transfers between devices  58 us (15%)
  local copies, waits for them, and re-layouts  28.1 us (7%)
  other arithmetic  17.5 us (5%)
    ppermute x42, waiting for transfers between devices, flip(): return lax.ppermute(value, axis, [(i, i ^ mask) for i in range(size)])  110 us
    ppermute x42, starting transfers between devices, flip(): return lax.ppermute(value, axis, [(i, i ^ mask) for i in range(size)])  44.6 us
    pallas_call x1, Pallas kernels, ffn(): pl.pallas_call(body, grid_spec=pltpu.PrefetchScalarGridSpec(num_scalar_pr...  25.8 us
    pallas_call x2, Pallas kernels, attend_back(): pl.pallas_call(functools.partial(attend_back_body, first, heads, hd), gri...  25.3 us
    pallas_call x1, Pallas kernels, qkv_back(): pl.pallas_call(functools.partial(qkv_back_body, heads, hd), grid_spec=plt...  17.9 us
    all_to_all x2, waiting for transfers between devices, exchange(): return lax.all_to_all(value, 'seq', 0, 0, tiled=True)  17.7 us
    pallas_call x2, Pallas kernels, make_qkv(): pl.pallas_call(body, grid_spec=pltpu.PrefetchScalarGridSpec(num_scalar_pr...  15.9 us
    unnamed x72, local copies, waits for them, and re-layouts  14.7 us
  transfers between devices with their start and end apart: 44, of which 18 were waited for; matrix products, arithmetic and copies ran while one was open for 7% of the time, Pallas kernels for 28%

profile of v12, /device:TPU:0, one launch (start us, length us, event | category | flops | bytes accessed | tf_op | source)
XLA Modules:
  0.0 375.8 jit_solution(6871687934735685420)
XLA Ops:
  13.4 10.3 %collective-permute-done.refs_0_ = bf16[256,768]{1,0:T(8,128)(2,1)S(1)} collective-permute-done((bf16[256,768]{1,0:T(8,128)(2,1)S(1)}, bf16[256,768]{1,0:T(8,128)(2,1)S(1)}, u32[]{:S(2)}, u32[]{:S(2)}) %collective-permute-start) | collective-permute-done | bytes 393248 | tf_op jit(solution)/shard_map/ppermute | solution.py:812
  40.9 7.9 %qkv_forward.2 = (bf16[3,128,2048]{2,1,0:T(8,128)(2,1)}, bf16[3,2048,128]{2,1,0:T(8,128)(2,1)}, bf16[3,64,2048]{2,1,0:T(8,128)(2,1)}, bf16[3,2048,64]{2,1,0:T(8,...) custom-call(s32[6]{0:T(128)} %stack.46.meta, s32[2,8]{1,0:T(2,128)} %bitcast.109, ...), custom_call_target="tpu_custom_call" | custom-call | flops 2100000000 | bytes 1024 | tf_op jit(solution)/shard_map/forward_attention/qkv_forward/pallas_call | solution.py:121
  49.6 7.9 %qkv_forward.3 = (bf16[3,128,2048]{2,1,0:T(8,128)(2,1)}, bf16[3,2048,128]{2,1,0:T(8,128)(2,1)}, bf16[3,64,2048]{2,1,0:T(8,128)(2,1)}, bf16[3,2048,64]{2,1,0:T(8,...) custom-call(s32[6]{0:T(128)} %stack.46.meta, ...), custom_call_target="tpu_custom_call", output_to_operand_aliasing={{0}: (12, {}), {1}: (13, {}), {2}: (14, {}), {3}: (15, {}),... | custom-call | flops 2100000000 | bytes 1024 | tf_op jit(solution)/shard_map/forward_attention/qkv_forward/pallas_call | solution.py:121
  57.6 11.3 %attention_forward.1 = (bf16[8,192,256]{2,1,0:T(8,128)(2,1)}, f32[3,64,2048]{2,1,0:T(8,128)}, f32[3,1,2048]{2,1,0:T(1,128)}) custom-call(s32[6]{0:T(128)} %stack.46.meta, s32[2,8]{1,0:T(2,128)} %bitcast.111, bf16[3,128,2048]{2,1,0:T(8,128)(2,1)} %get-tuple-element.98.qt_ref.refs_0_, bf16[3,2048,128]{2,1,0:T(8,128)(2,1)} %get-tuple-element.99.ka_ref.refs_1_, ...), custom_call_target="tpu_custom_call" | custom-call | flops 8750000128 | bytes 1024 | tf_op jit(solution)/shard_map/forward_attention/attention_forward/pallas_call | solution.py:205
  68.8 9.0 %all-to-all-start = ((bf16[8,192,256]{2,1,0:T(8,128)(2,1)}), bf16[8,192,256]{2,1,0:T(8,128)(2,1)S(1)}, u32[]{:S(2)}, u32[]{:S(2)}) async-start(bf16[8,192,256]{2,1,0:T(8,128)(2,1)} %get-tuple-element.101), calls=%async_computation | async-start | bytes 1572864 | tf_op jit(solution)/shard_map/all_to_all | solution.py:902
  80.0 16.7 %all-to-all-done = bf16[8,192,256]{2,1,0:T(8,128)(2,1)S(1)} async-done(((bf16[8,192,256]{2,1,0:T(8,128)(2,1)}), bf16[8,192,256]{2,1,0:T(8,128)(2,1)S(1)}, u32[]{:S(2)}, u32[]{:S(2)}) %all-to-all-start) | async-done | bytes 786464 | tf_op jit(solution)/shard_map/all_to_all | solution.py:902
  97.5 25.8 %ffn_both_ways.1 = (bf16[512,768]{1,0:T(8,128)(2,1)}, f32[512,768]{1,0:T(8,128)}, bf16[512,768]{1,0:T(8,128)(2,1)}, bf16[768,512]{1,0:T(8,128)(2,1)}, bf16[512,3...) custom-call(s32[6]{0:T(128)} %stack.46.meta, ...), custom_call_target="tpu_custom_call" | custom-call | flops 8750000128 | bytes 1024 | tf_op jit(solution)/shard_map/feed_forward/ffn_both_ways/pallas_call | solution.py:551
  123.3 6.4 %down_out_gradient.2 = bf16[1920,768]{1,0:T(8,128)(2,1)} custom-call(s32[6]{0:T(128)} %stack.46.meta, bf16[512,3072]{1,0:T(8,128)(2,1)} %get-tuple-element.113.act_ref, bf16[512,768]{1,0:T(8,128)(2,1)} %bitcast.87, bf16[2,768,256]{2,1,0:T(8,128)(2,1)} %bitcast.84, bf16[512,768]{1,0:T(8,128)(2,1)} %get-tuple-element.114.gb_ref), custom_call_target="tpu_custom_call" | custom-call | flops 70000000 | bytes 1024 | tf_op jit(solution)/shard_map/weight_gradients/down_out_gradient/pallas_call | solution.py:704
  129.7 6.0 %up_gradient.2 = bf16[384,3072]{1,0:T(8,128)(2,1)} custom-call(s32[6]{0:T(128)} %stack.46.meta, bf16[768,512]{1,0:T(8,128)(2,1)} %get-tuple-element.109.h2_ref, bf16[512,3072]{1,0:T(8,128)(2,1)} %get-tuple-element.110.dup_ref), custom_call_target="tpu_custom_call" | custom-call | flops 70000000 | bytes 1024 | tf_op jit(solution)/shard_map/weight_gradients/up_gradient/pallas_call | solution.py:634
  142.2 7.5 %down_out_gradient.3 = (bf16[960,768]{1,0:T(8,128)(2,1)}, bf16[960,768]{1,0:T(8,128)(2,1)}) custom-call(s32[6]{0:T(128)} %stack.46.meta, bf16[512,3072]{1,0:T(8,128)(2,1)} %get-tuple-element.113.act_ref, bf16[512,768]{1,0:T(8,128)(2,1)} %bitcast.88, bf16[2,768,256]{2,1,0:T(8,128)(2,1)} %bitcast.85, bf16[512,768]{1,0:T(8,128)(2,1)} %get-tuple-element.114.gb_ref, ...), custom_call_target="tpu_custom_call" | custom-call | flops 70000000 | bytes 1024 | tf_op jit(solution)/shard_map/weight_gradients/down_out_gradient/pallas_call | solution.py:704
  151.7 6.6 %up_gradient.3 = (bf16[384,1536]{1,0:T(8,128)(2,1)}, bf16[384,1536]{1,0:T(8,128)(2,1)}) custom-call(s32[6]{0:T(128)} %stack.46.meta, bf16[768,512]{1,0:T(8,128)(2,1)} %get-tuple-element.109.h2_ref, bf16[512,3072]{1,0:T(8,128)(2,1)} %get-tuple-element.110.dup_ref, bf16[384,3072]{1,0:T(8,128)(2,1)} %collective-permute-done.14.rest_0_), custom_call_target="tpu_custom_call" | custom-call | flops 70000000 | bytes 1024 | tf_op jit(solution)/shard_map/weight_gradients/up_gradient/pallas_call | solution.py:634
  161.0 15.0 %attention_backward.2 = (f32[3,64,2048]{2,1,0:T(8,128)}, f32[3,64,2048]{2,1,0:T(8,128)}, f32[3,64,2048]{2,1,0:T(8,128)}) custom-call(s32[6]{0:T(128)} %stack.46.meta, s32[2,8]{1,0:T(2,128)} %bitcast.112, bf16[3,128,2048]{2,1,0:T(8,128)(2,1)} %get-tuple-element.98.qt_ref.refs_0_, bf16[3,2048,128]{2,1,0:T(8,128)(2,1)} %get-tuple-element.99.ka_ref.refs_1_, ...), custom_call_target="tpu_custom_call" | custom-call | flops 5249999872 | bytes 1024 | tf_op jit(solution)/shard_map/backward_attention/attention_backward/pallas_call | solution.py:281
  176.0 10.2 %collective-permute-done.17 = bf16[384,1536]{1,0:T(8,128)(2,1)} collective-permute-done((bf16[384,1536]{1,0:T(8,128)(2,1)}, bf16[384,1536]{1,0:T(8,128)(2,1)}, u32[]{:S(2)}, u32[]{:S(2)}) %collective-permute-start.17) | collective-permute-done | bytes 1179680 | tf_op jit(solution)/shard_map/weight_gradients/ppermute | solution.py:812
  195.3 10.3 %attention_backward.3 = (f32[3,64,2048]{2,1,0:T(8,128)}, f32[3,64,2048]{2,1,0:T(8,128)}, f32[3,64,2048]{2,1,0:T(8,128)}) custom-call(s32[6]{0:T(128)} %stack.46.meta, s32[2,8]{1,0:T(2,128)} %bitcast.113, bf16[3,128,2048]{2,1,0:T(8,128)(2,1)} %get-tuple-element.98.qt_ref.refs_0_, ...), custom_call_target="tpu_custom_call", output_to_operand_aliasing={{0}: (9, {})} | custom-call | flops 5249999872 | bytes 1024 | tf_op jit(solution)/shard_map/backward_attention/attention_backward/pallas_call | solution.py:281
  213.5 6.5 %collective-permute-done.21 = bf16[384,384]{1,0:T(8,128)(2,1)S(1)} collective-permute-done((bf16[384,384]{1,0:T(8,128)(2,1)S(1)}, bf16[384,384]{1,0:T(8,128)(2,1)S(1)}, u32[]{:S(2)}, u32[]{:S(2)}) %collective-permute-start.21) | collective-permute-done | bytes 294944 | tf_op jit(solution)/shard_map/weight_gradients/ppermute | solution.py:812
  223.9 17.9 %qkv_backward.1 = (bf16[8,256,384]{2,1,0:T(8,128)(2,1)}, bf16[8,256,384]{2,1,0:T(8,128)(2,1)}, bf16[608,768]{1,0:T(8,128)(2,1)}) custom-call(s32[6]{0:T(128)} %stack.46.meta, bf16[2048,768]{1,0:T(8,128)(2,1)} %get-tuple-element.103.x_ref, f32[3,64,2048]{2,1,0:T(8,128)} %get-tuple-element.134.refs_0_, f32[3,64,2048]{2,1,0:T(8,128)} %get-tuple-element.135.refs_1_, ...), custom_call_target="tpu_custom_call" | custom-call | flops 5950000128 | bytes 1024 | tf_op jit(solution)/shard_map/backward_attention/qkv_backward/pallas_call | solution.py:376
  245.3 6.4 %collective-permute-done.22 = bf16[864,384]{1,0:T(8,128)(2,1)S(1)} collective-permute-done((bf16[864,384]{1,0:T(8,128)(2,1)S(1)}, bf16[864,384]{1,0:T(8,128)(2,1)S(1)}, u32[]{:S(2)}, u32[]{:S(2)}) %collective-permute-start.22) | collective-permute-done | bytes 663584 | tf_op jit(solution)/shard_map/weight_gradients/ppermute | solution.py:812
  260.6 14.0 %collective-permute-done.28 = bf16[2,2,256,384]{3,2,0,1:T(8,128)(2,1)} collective-permute-done((bf16[2,2,256,384]{3,2,0,1:T(8,128)(2,1)}, bf16[2,2,256,384]{3,2,0,1:T(8,128)(2,1)}, u32[]{:S(2)}, u32[]{:S(2)}) %collective-permute-start.28) | collective-permute-done | bytes 786464 | tf_op jit(solution)/shard_map/first_round/ppermute | solution.py:812
  274.5 7.4 %collective-permute-done.24 = bf16[480,384]{1,0:T(8,128)(2,1)} collective-permute-done((bf16[480,384]{1,0:T(8,128)(2,1)S(1)}, bf16[480,384]{1,0:T(8,128)(2,1)}, u32[]{:S(2)}, u32[]{:S(2)}) %collective-permute-start.24) | collective-permute-done | bytes 368672 | tf_op jit(solution)/shard_map/first_round/ppermute | solution.py:812
  292.5 6.6 %collective-permute-done.32 = bf16[304,384]{1,0:T(8,128)(2,1)S(1)} collective-permute-done((bf16[304,384]{1,0:T(8,128)(2,1)S(1)}, bf16[304,384]{1,0:T(8,128)(2,1)S(1)}, u32[]{:S(2)}, u32[]{:S(2)}) %collective-permute-start.32) | collective-permute-done | bytes 233504 | tf_op jit(solution)/shard_map/second_round/ppermute | solution.py:812
  299.1 12.6 %collective-permute-done.34 = bf16[2,256,384]{2,1,0:T(8,128)(2,1)S(1)} collective-permute-done((bf16[2,256,384]{2,1,0:T(8,128)(2,1)S(1)}, bf16[2,256,384]{2,1,0:T(8,128)(2,1)S(1)}, u32[]{:S(2)}, u32[]{:S(2)}) %collective-permute-start.34) | collective-permute-done | bytes 393248 | tf_op jit(solution)/shard_map/second_round/ppermute | solution.py:812
  328.0 13.8 %collective-permute-done.38.p01 = bf16[2,304,384]{2,1,0:T(8,128)(2,1)} collective-permute-done((bf16[2,304,384]{2,1,0:T(8,128)(2,1)S(1)}, bf16[2,304,384]{2,1,0:T(8,128)(2,1)}, u32[]{:S(2)}, u32[]{:S(2)}) %collective-permute-start.38) | collective-permute-done | bytes 466976 | tf_op jit(solution)/shard_map/third_round/ppermute | solution.py:812
  341.9 5.5 %down_out_in_place.1 = (f32[1536,768]{1,0:T(8,128)}, f32[384,768]{1,0:T(8,128)}) custom-call(s32[6]{0:T(128)} %stack.46.meta, bf16[480,768]{1,0:T(8,128)(2,1)} %copy-done.12, bf16[480,768]{1,0:T(8,128)(2,1)} %copy-done.27, bf16[480,768]{1,0:T(8,128)(2,1)} %copy-done.26, bf16[480,768]{1,0:T(8,128)(2,1)} %collective-permute-done.39.down_bb), custom_call_target="tpu_custom_call" | custom-call | flops 1400000000 | bytes 1024 | tf_op jit(solution)/shard_map/third_round/down_out_in_place/pallas_call | solution.py:745
  357.0 5.8 %up_in_place.1 = f32[384,3072]{1,0:T(8,128)} custom-call(s32[6]{0:T(128)} %stack.46.meta, bf16[384,1536]{1,0:T(8,128)(2,1)} %copy-done.1, bf16[384,1536]{1,0:T(8,128)(2,1)} %copy-done.6), custom_call_target="tpu_custom_call" | custom-call | flops 1400000000 | bytes 1024 | tf_op jit(solution)/shard_map/up_in_place/pallas_call | solution.py:772
  (202 shorter events, 127.0 us)
Async XLA Ops:
  1.9 21.8 %collective-permute-start = (bf16[256,768]{1,0:T(8,128)(2,1)S(1)}, bf16[256,768]{1,0:T(8,128)(2,1)S(1)}, u32[]{:S(2)}, u32[]{:S(2)}) collective-permute-start(bf16[256,768]{1,0:T(8,128)(2,1)S(1)} %get-tuple-element.207), channel_id=1, source_target_pairs={{0,4},{1,5},{2,6},{3,7},{4,0},{5,1},{6,2},{7,3},{8,12},{9,13},{10,... | collective-permute-start | bytes 1179656 | tf_op jit(solution)/shard_map/ppermute | solution.py:812
  6.0 19.8 %collective-permute-start.8 = (bf16[256,768]{1,0:T(8,128)(2,1)S(1)}, bf16[256,768]{1,0:T(8,128)(2,1)}, u32[]{:S(2)}, u32[]{:S(2)}) collective-permute-start(bf16[256,768]{1,0:T(8,128)(2,1)S(1)} %get-tuple-element.206.refs_0_), channel_id=1, source_target_pairs={{0,2},{1,3},{2,0},{3,1},{4,6},{5,7},{6,4},{7,5},{8,10},{9,11},{10,... | collective-permute-start | bytes 1179656 | tf_op jit(solution)/shard_map/ppermute | solution.py:812
  7.6 19.7 %collective-permute-start.7 = (bf16[256,768]{1,0:T(8,128)(2,1)S(1)}, bf16[256,768]{1,0:T(8,128)(2,1)}, u32[]{:S(2)}, u32[]{:S(2)}) collective-permute-start(bf16[256,768]{1,0:T(8,128)(2,1)S(1)} %get-tuple-element.206.refs_0_), channel_id=1, source_target_pairs={{0,1},{1,0},{2,3},{3,2},{4,5},{5,4},{6,7},{7,6},{8,9},{9,8},{10,11... | collective-permute-start | bytes 1179656 | tf_op jit(solution)/shard_map/ppermute | solution.py:812
  12.2 20.2 %collective-permute-start.5 = (bf16[384,576]{0,1:T(8,128)(2,1)S(1)}, bf16[384,576]{0,1:T(8,128)(2,1)S(1)}, u32[]{:S(2)}, u32[]{:S(2)}) collective-permute-start(bf16[384,576]{0,1:T(8,128)(2,1)S(1)} %bitcast.90), channel_id=1, source_target_pairs={{0,8},{8,0},{1,9},{9,1},{2,10},{10,2},{3,11},{11,3},{4,12},{12,4},... | collective-permute-start | bytes 1327112 | tf_op jit(solution)/shard_map/ppermute | solution.py:812
  32.5 47.5 %collective-permute-start.12 = (bf16[384,3072]{1,0:T(8,128)(2,1)}, bf16[384,3072]{1,0:T(8,128)(2,1)}, u32[]{:S(2)}, u32[]{:S(2)}) collective-permute-start(bf16[384,3072]{1,0:T(8,128)(2,1)} %refs_8_.1), channel_id=1, source_target_pairs={{0,8},{8,0},{1,9},{9,1},{2,10},{10,2},{3,11},{11,3},{4,12},{12,4},... | collective-permute-start | bytes 7077896 | tf_op jit(solution)/shard_map/ppermute | solution.py:812
  35.7 44.3 %collective-permute-start.13 = (bf16[1536,768]{1,0:T(8,128)(2,1)}, bf16[1536,768]{1,0:T(8,128)(2,1)}, u32[]{:S(2)}, u32[]{:S(2)}) collective-permute-start(bf16[1536,768]{1,0:T(8,128)(2,1)} %refs_10_.1), channel_id=1, source_target_pairs={{0,8},{8,0},{1,9},{9,1},{2,10},{10,2},{3,11},{11,3},{4,12},{12,4},... | collective-permute-start | bytes 7077896 | tf_op jit(solution)/shard_map/ppermute | solution.py:812
  68.8 27.8 %all-to-all-start = ((bf16[8,192,256]{2,1,0:T(8,128)(2,1)}), bf16[8,192,256]{2,1,0:T(8,128)(2,1)S(1)}, u32[]{:S(2)}, u32[]{:S(2)}) async-start(bf16[8,192,256]{2,1,0:T(8,128)(2,1)} %get-tuple-element.101), calls=%async_computation | async-start | bytes 1572864 | tf_op jit(solution)/shard_map/all_to_all | solution.py:902
  136.2 24.8 %all-to-all-start.1 = ((bf16[8,192,256]{2,1,0:T(8,128)(2,1)}), bf16[8,192,256]{2,1,0:T(8,128)(2,1)}, u32[]{:S(2)}, u32[]{:S(2)}) async-start(bf16[8,192,256]{2,1,0:T(8,128)(2,1)} %bitcast.95), calls=%async_computation.1 | async-start | bytes 1572864 | tf_op jit(solution)/shard_map/all_to_all | solution.py:902
  149.7 36.5 %collective-permute-start.16 = (bf16[960,768]{1,0:T(8,128)(2,1)}, bf16[960,768]{1,0:T(8,128)(2,1)S(1)}, u32[]{:S(2)}, u32[]{:S(2)}) collective-permute-start(bf16[960,768]{1,0:T(8,128)(2,1)} %get-tuple-element.116), channel_id=1, source_target_pairs={{0,16},{16,0},{1,17},{17,1},{2,18},{18,2},{3,19},{19,3},{4,20},{20... | collective-permute-start | bytes 4423688 | tf_op jit(solution)/shard_map/weight_gradients/ppermute | solution.py:812
  158.3 27.9 %collective-permute-start.17 = (bf16[384,1536]{1,0:T(8,128)(2,1)}, bf16[384,1536]{1,0:T(8,128)(2,1)}, u32[]{:S(2)}, u32[]{:S(2)}) collective-permute-start(bf16[384,1536]{1,0:T(8,128)(2,1)} %get-tuple-element.112), channel_id=1, source_target_pairs={{0,1},{1,0},{2,3},{3,2},{4,5},{5,4},{6,7},{7,6},{8,9},{9,8},{10,11... | collective-permute-start | bytes 3538952 | tf_op jit(solution)/shard_map/weight_gradients/ppermute | solution.py:812
  190.0 17.7 %collective-permute-start.18 = (bf16[480,768]{1,0:T(8,128)(2,1)}, bf16[480,768]{1,0:T(8,128)(2,1)S(1)}, u32[]{:S(2)}, u32[]{:S(2)}) collective-permute-start(bf16[480,768]{1,0:T(8,128)(2,1)} %constant_dynamic-slice_fusion.5), channel_id=1, source_target_pairs={{0,1},{1,0},{2,3},{3,2},{4,5},{5,4},{6,7},{7,6},{8,9},{9,8},{10,11... | collective-permute-start | bytes 2211848 | tf_op jit(solution)/shard_map/weight_gradients/ppermute | solution.py:812
  222.0 29.7 %collective-permute-start.22 = (bf16[864,384]{1,0:T(8,128)(2,1)S(1)}, bf16[864,384]{1,0:T(8,128)(2,1)S(1)}, u32[]{:S(2)}, u32[]{:S(2)}) collective-permute-start(bf16[864,384]{1,0:T(8,128)(2,1)S(1)} %pad_maximum_fusion.2), channel_id=1, source_target_pairs={{0,4},{1,5},{2,6},{3,7},{4,0},{5,1},{6,2},{7,3},{8,12},{9,13},{10,... | collective-permute-start | bytes 1990664 | tf_op jit(solution)/shard_map/weight_gradients/ppermute | solution.py:812
  253.8 20.7 %collective-permute-start.28 = (bf16[2,2,256,384]{3,2,0,1:T(8,128)(2,1)}, bf16[2,2,256,384]{3,2,0,1:T(8,128)(2,1)}, u32[]{:S(2)}, u32[]{:S(2)}) collective-permute-start(bf16[2,2,256,384]{3,2,0,1:T(8,128)(2,1)} %bitcast.81), channel_id=1, source_target_pairs={{0,2},{1,3},{2,0},{3,1},{4,6},{5,7},{6,4},{7,5},{8,10},{9,11},{10,... | collective-permute-start | bytes 2359304 | tf_op jit(solution)/shard_map/first_round/ppermute | solution.py:812
  253.9 20.6 %collective-permute-start.25 = (bf16[384,384]{1,0:T(8,128)(2,1)S(1)}, bf16[384,384]{1,0:T(8,128)(2,1)S(1)}, u32[]{:S(2)}, u32[]{:S(2)}) collective-permute-start(bf16[384,384]{1,0:T(8,128)(2,1)S(1)} %split.7), channel_id=1, source_target_pairs={{0,16},{16,0},{1,17},{17,1},{2,18},{18,2},{3,19},{19,3},{4,20},{20... | collective-permute-start | bytes 884744 | tf_op jit(solution)/shard_map/first_round/ppermute | solution.py:812
  256.4 25.5 %collective-permute-start.24 = (bf16[480,384]{1,0:T(8,128)(2,1)S(1)}, bf16[480,384]{1,0:T(8,128)(2,1)}, u32[]{:S(2)}, u32[]{:S(2)}) collective-permute-start(bf16[480,384]{1,0:T(8,128)(2,1)S(1)} %split.6), channel_id=1, source_target_pairs={{0,2},{1,3},{2,0},{3,1},{4,6},{5,7},{6,4},{7,5},{8,10},{9,11},{10,... | collective-permute-start | bytes 1105928 | tf_op jit(solution)/shard_map/first_round/ppermute | solution.py:812
  260.5 21.5 %collective-permute-start.26 = (bf16[304,384]{1,0:T(8,128)(2,1)}, bf16[304,384]{1,0:T(8,128)(2,1)S(1)}, u32[]{:S(2)}, u32[]{:S(2)}) collective-permute-start(bf16[304,384]{1,0:T(8,128)(2,1)} %constant_dynamic-slice_fusion), channel_id=1, source_target_pairs={{0,16},{16,0},{1,17},{17,1},{2,18},{18,2},{3,19},{19,3},{4,20},{20... | collective-permute-start | bytes 700424 | tf_op jit(solution)/shard_map/first_round/ppermute | solution.py:812
  283.1 33.7 %collective-permute-start.30 = (bf16[480,768]{1,0:T(8,128)(2,1)S(1)}, bf16[480,768]{1,0:T(8,128)(2,1)S(1)}, u32[]{:S(2)}, u32[]{:S(2)}) collective-permute-start(bf16[480,768]{1,0:T(8,128)(2,1)S(1)} %pad_maximum_fusion.1.down_aa), channel_id=1, source_target_pairs={{0,16},{16,0},{1,17},{17,1},{2,18},{18,2},{3,19},{19,3},{4,20},{20... | collective-permute-start | bytes 2211848 | tf_op jit(solution)/shard_map/second_round/ppermute | solution.py:812
  285.6 31.2 %collective-permute-start.29 = (bf16[480,768]{1,0:T(8,128)(2,1)S(1)}, bf16[480,768]{1,0:T(8,128)(2,1)S(1)}, u32[]{:S(2)}, u32[]{:S(2)}) collective-permute-start(bf16[480,768]{1,0:T(8,128)(2,1)S(1)} %pad_maximum_fusion.1.down_aa), channel_id=1, source_target_pairs={{0,1},{1,0},{2,3},{3,2},{4,5},{5,4},{6,7},{7,6},{8,9},{9,8},{10,11... | collective-permute-start | bytes 2211848 | tf_op jit(solution)/shard_map/second_round/ppermute | solution.py:812
  288.3 23.4 %collective-permute-start.34 = (bf16[2,256,384]{2,1,0:T(8,128)(2,1)S(1)}, bf16[2,256,384]{2,1,0:T(8,128)(2,1)S(1)}, u32[]{:S(2)}, u32[]{:S(2)}) collective-permute-start(bf16[2,256,384]{2,1,0:T(8,128)(2,1)S(1)} %slice_bitcast_fusion.2), channel_id=1, source_target_pairs={{0,1},{1,0},{2,3},{3,2},{4,5},{5,4},{6,7},{7,6},{8,9},{9,8},{10,11... | collective-permute-start | bytes 1179656 | tf_op jit(solution)/shard_map/second_round/ppermute | solution.py:812
  289.3 27.4 %collective-permute-start.31 = (bf16[384,768]{1,0:T(8,128)(2,1)S(1)}, bf16[384,768]{1,0:T(8,128)(2,1)S(1)}, u32[]{:S(2)}, u32[]{:S(2)}) collective-permute-start(bf16[384,768]{1,0:T(8,128)(2,1)S(1)} %pad_maximum_fusion.3), channel_id=1, source_target_pairs={{0,2},{1,3},{2,0},{3,1},{4,6},{5,7},{6,4},{7,5},{8,10},{9,11},{10,... | collective-permute-start | bytes 1769480 | tf_op jit(solution)/shard_map/second_round/ppermute | solution.py:812
  318.1 23.8 %collective-permute-start.39 = (bf16[480,768]{1,0:T(8,128)(2,1)S(1)}, bf16[480,768]{1,0:T(8,128)(2,1)}, u32[]{:S(2)}, u32[]{:S(2)}) collective-permute-start(bf16[480,768]{1,0:T(8,128)(2,1)S(1)} %collective-permute-done.29.down_ab), channel_id=1, source_target_pairs={{0,16},{16,0},{1,17},{17,1},{2,18},{18,2},{3,19},{19,3},{4,20},{20... | collective-permute-start | bytes 2211848 | tf_op jit(solution)/shard_map/third_round/ppermute | solution.py:812
  323.6 32.4 %collective-permute-start.36 = (bf16[384,1536]{1,0:T(8,128)(2,1)S(1)}, bf16[384,1536]{1,0:T(8,128)(2,1)S(1)}, u32[]{:S(2)}, u32[]{:S(2)}) collective-permute-start(bf16[384,1536]{1,0:T(8,128)(2,1)S(1)} %pad_maximum_fusion.up_a), channel_id=1, source_target_pairs={{0,1},{1,0},{2,3},{3,2},{4,5},{5,4},{6,7},{7,6},{8,9},{9,8},{10,11... | collective-permute-start | bytes 3538952 | tf_op jit(solution)/shard_map/third_round/ppermute | solution.py:812
  325.9 23.6 %collective-permute-start.37 = (bf16[256,768]{1,0:T(8,128)(2,1)}, bf16[256,768]{1,0:T(8,128)(2,1)}, u32[]{:S(2)}, u32[]{:S(2)}) collective-permute-start(bf16[256,768]{1,0:T(8,128)(2,1)} %get-tuple-element.205), channel_id=1, source_target_pairs={{0,4},{1,5},{2,6},{3,7},{4,0},{5,1},{6,2},{7,3},{8,12},{9,13},{10,... | collective-permute-start | bytes 1179656 | tf_op jit(solution)/shard_map/third_round/ppermute | solution.py:812
  348.2 19.8 %collective-permute-start.40 = (bf16[2,304,384]{2,1,0:T(8,128)(2,1)S(1)}, bf16[2,304,384]{2,1,0:T(8,128)(2,1)}, u32[]{:S(2)}, u32[]{:S(2)}) collective-permute-start(bf16[2,304,384]{2,1,0:T(8,128)(2,1)S(1)} %pad_maximum_fusion.4.p00), channel_id=1, source_target_pairs={{0,16},{16,0},{1,17},{17,1},{2,18},{18,2},{3,19},{19,3},{4,20},{20... | collective-permute-start | bytes 1400840 | tf_op jit(solution)/shard_map/third_round/ppermute | solution.py:812
  (52 other events, 461.3 us)

commit v13 on v12

--- a/solution.py
+++ b/solution.py
@@ -1016,8 +1016,9 @@
         downs.append(flip(downs[1], *x))
         piece_z, downs[3] = tie(flip(piece, *z), downs[3])
         grad_down, grad_out = assemble_down(meta, downs)
-        piece_z, grad_down, grad_out = tie(piece_z, grad_down, grad_out)
-        pieces = [piece, piece_z, flip(piece, *x), flip(piece_z, *x)]
+        piece_x = flip(piece, *x)
+        piece_z, piece_x, grad_down, grad_out = tie(piece_z, piece_x, grad_down, grad_out)
+        pieces = [piece, piece_z, piece_x, flip(piece_z, *x)]
         ups = (up, flip(up, *y))
     grad_tokens = finish(x_home, grad_mid, back, g1)
     grad_up, grad_tokens = tie(assemble_up(meta, ups), grad_tokens)

time: 377 us -> 373 us (0.989)
  waiting for transfers between devices: 127 us -> 115 us
  starting transfers between devices: 58 us -> 62.1 us
    ppermute x42, waiting for transfers between devices: 110 us -> 102 us  [flip(): return lax.ppermute(value, axis, [(i, i ^ mask) for i in range(size)])]
    all_to_all x2, waiting for transfers between devices: 17.7 us -> 13.4 us  [exchange(): return lax.all_to_all(value, 'seq', 0, 0, tiled=True)]
    unnamed x72 -> x78, local copies, waits for them, and re-layouts: 14.7 us -> 17.1 us
  transfers between devices with their start and end apart: 44 -> 44, of which waited for: 18 -> 17; matrix products, arithmetic and copies ran while one was open for 7% -> 7% of each run, Pallas kernels for 28% -> 29%
where the time goes in v13:
time: 373 us; the launch traced here: 370 us
  Pallas kernels  144 us (39%)
  waiting for transfers between devices  115 us (31%)
  starting transfers between devices  62.1 us (17%)
  local copies, waits for them, and re-layouts  30.5 us (8%)
  other arithmetic  17.5 us (5%)
    ppermute x42, waiting for transfers between devices, flip(): return lax.ppermute(value, axis, [(i, i ^ mask) for i in range(size)])  102 us
    ppermute x42, starting transfers between devices, flip(): return lax.ppermute(value, axis, [(i, i ^ mask) for i in range(size)])  47.6 us
    pallas_call x1, Pallas kernels, ffn(): pl.pallas_call(body, grid_spec=pltpu.PrefetchScalarGridSpec(num_scalar_pr...  25.8 us
    pallas_call x2, Pallas kernels, attend_back(): pl.pallas_call(functools.partial(attend_back_body, first, heads, hd), gri...  25.3 us
    pallas_call x1, Pallas kernels, qkv_back(): pl.pallas_call(functools.partial(qkv_back_body, heads, hd), grid_spec=plt...  17.9 us
    unnamed x78, local copies, waits for them, and re-layouts  17.1 us
    pallas_call x2, Pallas kernels, make_qkv(): pl.pallas_call(body, grid_spec=pltpu.PrefetchScalarGridSpec(num_scalar_pr...  15.9 us
    all_to_all x2, starting transfers between devices, exchange(): return lax.all_to_all(value, 'seq', 0, 0, tiled=True)  14.4 us
  transfers between devices with their start and end apart: 44, of which 17 were waited for; matrix products, arithmetic and copies ran while one was open for 7% of the time, Pallas kernels for 29%

profile of v13, /device:TPU:0, one launch (start us, length us, event | category | flops | bytes accessed | tf_op | source)
XLA Modules:
  0.0 370.2 jit_solution(9063866073112273292)
XLA Ops:
  13.5 10.2 %collective-permute-done.refs_0_ = bf16[256,768]{1,0:T(8,128)(2,1)S(1)} collective-permute-done((bf16[256,768]{1,0:T(8,128)(2,1)S(1)}, bf16[256,768]{1,0:T(8,128)(2,1)S(1)}, u32[]{:S(2)}, u32[]{:S(2)}) %collective-permute-start) | collective-permute-done | bytes 393248 | tf_op jit(solution)/shard_map/ppermute | solution.py:812
  40.9 7.9 %qkv_forward.2 = (bf16[3,128,2048]{2,1,0:T(8,128)(2,1)}, bf16[3,2048,128]{2,1,0:T(8,128)(2,1)}, bf16[3,64,2048]{2,1,0:T(8,128)(2,1)}, bf16[3,2048,64]{2,1,0:T(8,...) custom-call(s32[6]{0:T(128)} %stack.46.meta, s32[2,8]{1,0:T(2,128)} %bitcast.109, ...), custom_call_target="tpu_custom_call" | custom-call | flops 2100000000 | bytes 1024 | tf_op jit(solution)/shard_map/forward_attention/qkv_forward/pallas_call | solution.py:121
  49.7 7.9 %qkv_forward.3 = (bf16[3,128,2048]{2,1,0:T(8,128)(2,1)}, bf16[3,2048,128]{2,1,0:T(8,128)(2,1)}, bf16[3,64,2048]{2,1,0:T(8,128)(2,1)}, bf16[3,2048,64]{2,1,0:T(8,...) custom-call(s32[6]{0:T(128)} %stack.46.meta, ...), custom_call_target="tpu_custom_call", output_to_operand_aliasing={{0}: (12, {}), {1}: (13, {}), {2}: (14, {}), {3}: (15, {}),... | custom-call | flops 2100000000 | bytes 1024 | tf_op jit(solution)/shard_map/forward_attention/qkv_forward/pallas_call | solution.py:121
  57.6 11.3 %attention_forward.1 = (bf16[8,192,256]{2,1,0:T(8,128)(2,1)}, f32[3,64,2048]{2,1,0:T(8,128)}, f32[3,1,2048]{2,1,0:T(1,128)}) custom-call(s32[6]{0:T(128)} %stack.46.meta, s32[2,8]{1,0:T(2,128)} %bitcast.111, bf16[3,128,2048]{2,1,0:T(8,128)(2,1)} %get-tuple-element.99.qt_ref.refs_0_, bf16[3,2048,128]{2,1,0:T(8,128)(2,1)} %get-tuple-element.100.ka_ref.refs_1_, ...), custom_call_target="tpu_custom_call" | custom-call | flops 8750000128 | bytes 1024 | tf_op jit(solution)/shard_map/forward_attention/attention_forward/pallas_call | solution.py:205
  68.9 10.0 %all-to-all-start = ((bf16[8,192,256]{2,1,0:T(8,128)(2,1)}), bf16[8,192,256]{2,1,0:T(8,128)(2,1)S(1)}, u32[]{:S(2)}, u32[]{:S(2)}) async-start(bf16[8,192,256]{2,1,0:T(8,128)(2,1)} %get-tuple-element.102), calls=%async_computation | async-start | bytes 1572864 | tf_op jit(solution)/shard_map/all_to_all | solution.py:902
  80.9 13.4 %all-to-all-done = bf16[8,192,256]{2,1,0:T(8,128)(2,1)S(1)} async-done(((bf16[8,192,256]{2,1,0:T(8,128)(2,1)}), bf16[8,192,256]{2,1,0:T(8,128)(2,1)S(1)}, u32[]{:S(2)}, u32[]{:S(2)}) %all-to-all-start) | async-done | bytes 786464 | tf_op jit(solution)/shard_map/all_to_all | solution.py:902
  95.2 25.8 %ffn_both_ways.1 = (bf16[512,768]{1,0:T(8,128)(2,1)}, f32[512,768]{1,0:T(8,128)}, bf16[512,768]{1,0:T(8,128)(2,1)}, bf16[768,512]{1,0:T(8,128)(2,1)}, bf16[512,3...) custom-call(s32[6]{0:T(128)} %stack.46.meta, ...), custom_call_target="tpu_custom_call" | custom-call | flops 8750000128 | bytes 1024 | tf_op jit(solution)/shard_map/feed_forward/ffn_both_ways/pallas_call | solution.py:551
  121.1 6.4 %down_out_gradient.2 = bf16[1920,768]{1,0:T(8,128)(2,1)} custom-call(s32[6]{0:T(128)} %stack.46.meta, bf16[512,3072]{1,0:T(8,128)(2,1)} %get-tuple-element.114.act_ref, bf16[512,768]{1,0:T(8,128)(2,1)} %bitcast.87, bf16[2,768,256]{2,1,0:T(8,128)(2,1)} %bitcast.84, bf16[512,768]{1,0:T(8,128)(2,1)} %get-tuple-element.115.gb_ref), custom_call_target="tpu_custom_call" | custom-call | flops 70000000 | bytes 1024 | tf_op jit(solution)/shard_map/weight_gradients/down_out_gradient/pallas_call | solution.py:704
  127.5 6.0 %up_gradient.2 = bf16[384,3072]{1,0:T(8,128)(2,1)} custom-call(s32[6]{0:T(128)} %stack.46.meta, bf16[768,512]{1,0:T(8,128)(2,1)} %get-tuple-element.110.h2_ref, bf16[512,3072]{1,0:T(8,128)(2,1)} %get-tuple-element.111.dup_ref), custom_call_target="tpu_custom_call" | custom-call | flops 70000000 | bytes 1024 | tf_op jit(solution)/shard_map/weight_gradients/up_gradient/pallas_call | solution.py:634
  140.0 7.4 %down_out_gradient.3 = (bf16[960,768]{1,0:T(8,128)(2,1)}, bf16[960,768]{1,0:T(8,128)(2,1)}) custom-call(s32[6]{0:T(128)} %stack.46.meta, bf16[512,3072]{1,0:T(8,128)(2,1)} %get-tuple-element.114.act_ref, bf16[512,768]{1,0:T(8,128)(2,1)} %bitcast.88, bf16[2,768,256]{2,1,0:T(8,128)(2,1)} %bitcast.85, bf16[512,768]{1,0:T(8,128)(2,1)} %get-tuple-element.115.gb_ref, ...), custom_call_target="tpu_custom_call" | custom-call | flops 70000000 | bytes 1024 | tf_op jit(solution)/shard_map/weight_gradients/down_out_gradient/pallas_call | solution.py:704
  151.1 6.6 %up_gradient.3 = (bf16[384,1536]{1,0:T(8,128)(2,1)}, bf16[384,1536]{1,0:T(8,128)(2,1)}) custom-call(s32[6]{0:T(128)} %stack.46.meta, bf16[768,512]{1,0:T(8,128)(2,1)} %get-tuple-element.110.h2_ref, bf16[512,3072]{1,0:T(8,128)(2,1)} %get-tuple-element.111.dup_ref, bf16[384,3072]{1,0:T(8,128)(2,1)} %collective-permute-done.14.rest_0_), custom_call_target="tpu_custom_call" | custom-call | flops 70000000 | bytes 1024 | tf_op jit(solution)/shard_map/weight_gradients/up_gradient/pallas_call | solution.py:634
  159.4 15.0 %attention_backward.2 = (f32[3,64,2048]{2,1,0:T(8,128)}, f32[3,64,2048]{2,1,0:T(8,128)}, f32[3,64,2048]{2,1,0:T(8,128)}) custom-call(s32[6]{0:T(128)} %stack.46.meta, s32[2,8]{1,0:T(2,128)} %bitcast.112, bf16[3,128,2048]{2,1,0:T(8,128)(2,1)} %get-tuple-element.99.qt_ref.refs_0_, bf16[3,2048,128]{2,1,0:T(8,128)(2,1)} %get-tuple-element.100.ka_ref.refs_1_, ...), custom_call_target="tpu_custom_call" | custom-call | flops 5249999872 | bytes 1024 | tf_op jit(solution)/shard_map/backward_attention/attention_backward/pallas_call | solution.py:281
  174.3 11.2 %collective-permute-done.17 = bf16[384,1536]{1,0:T(8,128)(2,1)} collective-permute-done((bf16[384,1536]{1,0:T(8,128)(2,1)}, bf16[384,1536]{1,0:T(8,128)(2,1)}, u32[]{:S(2)}, u32[]{:S(2)}) %collective-permute-start.17) | collective-permute-done | bytes 1179680 | tf_op jit(solution)/shard_map/weight_gradients/ppermute | solution.py:812
  194.7 10.3 %attention_backward.3 = (f32[3,64,2048]{2,1,0:T(8,128)}, f32[3,64,2048]{2,1,0:T(8,128)}, f32[3,64,2048]{2,1,0:T(8,128)}) custom-call(s32[6]{0:T(128)} %stack.46.meta, s32[2,8]{1,0:T(2,128)} %bitcast.113, bf16[3,128,2048]{2,1,0:T(8,128)(2,1)} %get-tuple-element.99.qt_ref.refs_0_, ...), custom_call_target="tpu_custom_call", output_to_operand_aliasing={{0}: (9, {})} | custom-call | flops 5249999872 | bytes 1024 | tf_op jit(solution)/shard_map/backward_attention/attention_backward/pallas_call | solution.py:281
  224.2 17.9 %qkv_backward.1 = (bf16[8,256,384]{2,1,0:T(8,128)(2,1)}, bf16[8,256,384]{2,1,0:T(8,128)(2,1)}, bf16[608,768]{1,0:T(8,128)(2,1)}) custom-call(s32[6]{0:T(128)} %stack.46.meta, bf16[2048,768]{1,0:T(8,128)(2,1)} %get-tuple-element.104.x_ref, f32[3,64,2048]{2,1,0:T(8,128)} %get-tuple-element.135.refs_0_, f32[3,64,2048]{2,1,0:T(8,128)} %get-tuple-element.136.refs_1_, ...), custom_call_target="tpu_custom_call" | custom-call | flops 5950000128 | bytes 1024 | tf_op jit(solution)/shard_map/backward_attention/qkv_backward/pallas_call | solution.py:376
  245.3 5.3 %collective-permute-done.22 = bf16[864,384]{1,0:T(8,128)(2,1)S(1)} collective-permute-done((bf16[864,384]{1,0:T(8,128)(2,1)S(1)}, bf16[864,384]{1,0:T(8,128)(2,1)S(1)}, u32[]{:S(2)}, u32[]{:S(2)}) %collective-permute-start.22) | collective-permute-done | bytes 663584 | tf_op jit(solution)/shard_map/weight_gradients/ppermute | solution.py:812
  259.5 14.0 %collective-permute-done.28 = bf16[2,2,256,384]{3,2,0,1:T(8,128)(2,1)} collective-permute-done((bf16[2,2,256,384]{3,2,0,1:T(8,128)(2,1)}, bf16[2,2,256,384]{3,2,0,1:T(8,128)(2,1)}, u32[]{:S(2)}, u32[]{:S(2)}) %collective-permute-start.28) | collective-permute-done | bytes 786464 | tf_op jit(solution)/shard_map/first_round/ppermute | solution.py:812
  273.5 7.4 %collective-permute-done.24 = bf16[480,384]{1,0:T(8,128)(2,1)} collective-permute-done((bf16[480,384]{1,0:T(8,128)(2,1)S(1)}, bf16[480,384]{1,0:T(8,128)(2,1)}, u32[]{:S(2)}, u32[]{:S(2)}) %collective-permute-start.24) | collective-permute-done | bytes 368672 | tf_op jit(solution)/shard_map/first_round/ppermute | solution.py:812
  289.5 6.6 %collective-permute-done.32 = bf16[304,384]{1,0:T(8,128)(2,1)S(1)} collective-permute-done((bf16[304,384]{1,0:T(8,128)(2,1)S(1)}, bf16[304,384]{1,0:T(8,128)(2,1)S(1)}, u32[]{:S(2)}, u32[]{:S(2)}) %collective-permute-start.32) | collective-permute-done | bytes 233504 | tf_op jit(solution)/shard_map/second_round/ppermute | solution.py:812
  296.1 12.5 %collective-permute-done.34 = bf16[2,256,384]{2,1,0:T(8,128)(2,1)S(1)} collective-permute-done((bf16[2,256,384]{2,1,0:T(8,128)(2,1)S(1)}, bf16[2,256,384]{2,1,0:T(8,128)(2,1)S(1)}, u32[]{:S(2)}, u32[]{:S(2)}) %collective-permute-start.34) | collective-permute-done | bytes 393248 | tf_op jit(solution)/shard_map/second_round/ppermute | solution.py:812
  326.5 13.3 %collective-permute-done.38.p01 = bf16[2,304,384]{2,1,0:T(8,128)(2,1)S(1)} collective-permute-done((bf16[2,304,384]{2,1,0:T(8,128)(2,1)S(1)}, bf16[2,304,384]{2,1,0:T(8,128)(2,1)S(1)}, u32[]{:S(2)}, u32[]{:S(2)}) %collective-permute-start.38) | collective-permute-done | bytes 466976 | tf_op jit(solution)/shard_map/third_round/ppermute | solution.py:812
  340.6 5.5 %down_out_in_place.1 = (f32[1536,768]{1,0:T(8,128)}, f32[384,768]{1,0:T(8,128)}) custom-call(s32[6]{0:T(128)} %stack.46.meta, bf16[480,768]{1,0:T(8,128)(2,1)} %copy-done.12, bf16[480,768]{1,0:T(8,128)(2,1)} %copy-done.27, bf16[480,768]{1,0:T(8,128)(2,1)} %copy-done.26, bf16[480,768]{1,0:T(8,128)(2,1)} %collective-permute-done.39.down_bb), custom_call_target="tpu_custom_call" | custom-call | flops 1400000000 | bytes 1024 | tf_op jit(solution)/shard_map/third_round/down_out_in_place/pallas_call | solution.py:745
  355.7 5.8 %up_in_place.1 = f32[384,3072]{1,0:T(8,128)} custom-call(s32[6]{0:T(128)} %stack.46.meta, bf16[384,1536]{1,0:T(8,128)(2,1)} %copy-done.1, bf16[384,1536]{1,0:T(8,128)(2,1)} %copy-done.6), custom_call_target="tpu_custom_call" | custom-call | flops 1400000000 | bytes 1024 | tf_op jit(solution)/shard_map/up_in_place/pallas_call | solution.py:772
  362.3 5.2 %first_projection_gradient.1 = (f32[384,2304]{1,0:T(8,128)}, f32[32,384]{1,0:T(8,128)}) custom-call(s32[6]{0:T(128)} %stack.46.meta, bf16[2,304,384]{2,1,0:T(8,128)(2,1)} %copy-done.13, bf16[2,304,384]{2,1,0:T(8,128)(2,1)} %copy-done.31, bf16[2,304,384]{2,1,0:T(8,128)(2,1)} %copy-done.30, bf16[2,304,384]{2,1,0:T(8,128)(2,1)} %copy-done.32), custom_call_target="tpu_custom_call" | custom-call | flops 1750000000 | bytes 1024 | tf_op jit(solution)/shard_map/first_projection_gradient/pallas_call | solution.py:443
  (208 shorter events, 125.8 us)
Async XLA Ops:
  1.9 21.8 %collective-permute-start = (bf16[256,768]{1,0:T(8,128)(2,1)S(1)}, bf16[256,768]{1,0:T(8,128)(2,1)S(1)}, u32[]{:S(2)}, u32[]{:S(2)}) collective-permute-start(bf16[256,768]{1,0:T(8,128)(2,1)S(1)} %get-tuple-element.209), channel_id=1, source_target_pairs={{0,4},{1,5},{2,6},{3,7},{4,0},{5,1},{6,2},{7,3},{8,12},{9,13},{10,... | collective-permute-start | bytes 1179656 | tf_op jit(solution)/shard_map/ppermute | solution.py:812
  6.0 19.8 %collective-permute-start.8 = (bf16[256,768]{1,0:T(8,128)(2,1)S(1)}, bf16[256,768]{1,0:T(8,128)(2,1)}, u32[]{:S(2)}, u32[]{:S(2)}) collective-permute-start(bf16[256,768]{1,0:T(8,128)(2,1)S(1)} %get-tuple-element.208.refs_0_), channel_id=1, source_target_pairs={{0,2},{1,3},{2,0},{3,1},{4,6},{5,7},{6,4},{7,5},{8,10},{9,11},{10,... | collective-permute-start | bytes 1179656 | tf_op jit(solution)/shard_map/ppermute | solution.py:812
  7.6 19.7 %collective-permute-start.7 = (bf16[256,768]{1,0:T(8,128)(2,1)S(1)}, bf16[256,768]{1,0:T(8,128)(2,1)}, u32[]{:S(2)}, u32[]{:S(2)}) collective-permute-start(bf16[256,768]{1,0:T(8,128)(2,1)S(1)} %get-tuple-element.208.refs_0_), channel_id=1, source_target_pairs={{0,1},{1,0},{2,3},{3,2},{4,5},{5,4},{6,7},{7,6},{8,9},{9,8},{10,11... | collective-permute-start | bytes 1179656 | tf_op jit(solution)/shard_map/ppermute | solution.py:812
  12.2 20.2 %collective-permute-start.5 = (bf16[384,576]{0,1:T(8,128)(2,1)S(1)}, bf16[384,576]{0,1:T(8,128)(2,1)S(1)}, u32[]{:S(2)}, u32[]{:S(2)}) collective-permute-start(bf16[384,576]{0,1:T(8,128)(2,1)S(1)} %bitcast.90), channel_id=1, source_target_pairs={{0,8},{8,0},{1,9},{9,1},{2,10},{10,2},{3,11},{11,3},{4,12},{12,4},... | collective-permute-start | bytes 1327112 | tf_op jit(solution)/shard_map/ppermute | solution.py:812
  32.4 48.5 %collective-permute-start.12 = (bf16[384,3072]{1,0:T(8,128)(2,1)}, bf16[384,3072]{1,0:T(8,128)(2,1)}, u32[]{:S(2)}, u32[]{:S(2)}) collective-permute-start(bf16[384,3072]{1,0:T(8,128)(2,1)} %refs_8_.1), channel_id=1, source_target_pairs={{0,8},{8,0},{1,9},{9,1},{2,10},{10,2},{3,11},{11,3},{4,12},{12,4},... | collective-permute-start | bytes 7077896 | tf_op jit(solution)/shard_map/ppermute | solution.py:812
  35.7 45.3 %collective-permute-start.13 = (bf16[1536,768]{1,0:T(8,128)(2,1)}, bf16[1536,768]{1,0:T(8,128)(2,1)}, u32[]{:S(2)}, u32[]{:S(2)}) collective-permute-start(bf16[1536,768]{1,0:T(8,128)(2,1)} %refs_10_.1), channel_id=1, source_target_pairs={{0,8},{8,0},{1,9},{9,1},{2,10},{10,2},{3,11},{11,3},{4,12},{12,4},... | collective-permute-start | bytes 7077896 | tf_op jit(solution)/shard_map/ppermute | solution.py:812
  68.9 25.5 %all-to-all-start = ((bf16[8,192,256]{2,1,0:T(8,128)(2,1)}), bf16[8,192,256]{2,1,0:T(8,128)(2,1)S(1)}, u32[]{:S(2)}, u32[]{:S(2)}) async-start(bf16[8,192,256]{2,1,0:T(8,128)(2,1)} %get-tuple-element.102), calls=%async_computation | async-start | bytes 1572864 | tf_op jit(solution)/shard_map/all_to_all | solution.py:902
  134.0 25.4 %all-to-all-start.1 = ((bf16[8,192,256]{2,1,0:T(8,128)(2,1)}), bf16[8,192,256]{2,1,0:T(8,128)(2,1)}, u32[]{:S(2)}, u32[]{:S(2)}) async-start(bf16[8,192,256]{2,1,0:T(8,128)(2,1)} %bitcast.95), calls=%async_computation.1 | async-start | bytes 1572864 | tf_op jit(solution)/shard_map/all_to_all | solution.py:902
  147.4 38.1 %collective-permute-start.16 = (bf16[960,768]{1,0:T(8,128)(2,1)}, bf16[960,768]{1,0:T(8,128)(2,1)S(1)}, u32[]{:S(2)}, u32[]{:S(2)}) collective-permute-start(bf16[960,768]{1,0:T(8,128)(2,1)} %get-tuple-element.117), channel_id=1, source_target_pairs={{0,16},{16,0},{1,17},{17,1},{2,18},{18,2},{3,19},{19,3},{4,20},{20... | collective-permute-start | bytes 4423688 | tf_op jit(solution)/shard_map/weight_gradients/ppermute | solution.py:812
  157.7 27.9 %collective-permute-start.17 = (bf16[384,1536]{1,0:T(8,128)(2,1)}, bf16[384,1536]{1,0:T(8,128)(2,1)}, u32[]{:S(2)}, u32[]{:S(2)}) collective-permute-start(bf16[384,1536]{1,0:T(8,128)(2,1)} %get-tuple-element.113), channel_id=1, source_target_pairs={{0,1},{1,0},{2,3},{3,2},{4,5},{5,4},{6,7},{7,6},{8,9},{9,8},{10,11... | collective-permute-start | bytes 3538952 | tf_op jit(solution)/shard_map/weight_gradients/ppermute | solution.py:812
  189.4 17.6 %collective-permute-start.18 = (bf16[480,768]{1,0:T(8,128)(2,1)}, bf16[480,768]{1,0:T(8,128)(2,1)S(1)}, u32[]{:S(2)}, u32[]{:S(2)}) collective-permute-start(bf16[480,768]{1,0:T(8,128)(2,1)} %constant_dynamic-slice_fusion.5), channel_id=1, source_target_pairs={{0,1},{1,0},{2,3},{3,2},{4,5},{5,4},{6,7},{7,6},{8,9},{9,8},{10,11... | collective-permute-start | bytes 2211848 | tf_op jit(solution)/shard_map/weight_gradients/ppermute | solution.py:812
  220.8 29.8 %collective-permute-start.22 = (bf16[864,384]{1,0:T(8,128)(2,1)S(1)}, bf16[864,384]{1,0:T(8,128)(2,1)S(1)}, u32[]{:S(2)}, u32[]{:S(2)}) collective-permute-start(bf16[864,384]{1,0:T(8,128)(2,1)S(1)} %pad_maximum_fusion.2), channel_id=1, source_target_pairs={{0,4},{1,5},{2,6},{3,7},{4,0},{5,1},{6,2},{7,3},{8,12},{9,13},{10,... | collective-permute-start | bytes 1990664 | tf_op jit(solution)/shard_map/weight_gradients/ppermute | solution.py:812
  252.7 20.7 %collective-permute-start.28 = (bf16[2,2,256,384]{3,2,0,1:T(8,128)(2,1)}, bf16[2,2,256,384]{3,2,0,1:T(8,128)(2,1)}, u32[]{:S(2)}, u32[]{:S(2)}) collective-permute-start(bf16[2,2,256,384]{3,2,0,1:T(8,128)(2,1)} %bitcast.81), channel_id=1, source_target_pairs={{0,2},{1,3},{2,0},{3,1},{4,6},{5,7},{6,4},{7,5},{8,10},{9,11},{10,... | collective-permute-start | bytes 2359304 | tf_op jit(solution)/shard_map/first_round/ppermute | solution.py:812
  252.8 20.6 %collective-permute-start.25 = (bf16[384,384]{1,0:T(8,128)(2,1)S(1)}, bf16[384,384]{1,0:T(8,128)(2,1)S(1)}, u32[]{:S(2)}, u32[]{:S(2)}) collective-permute-start(bf16[384,384]{1,0:T(8,128)(2,1)S(1)} %split.7), channel_id=1, source_target_pairs={{0,16},{16,0},{1,17},{17,1},{2,18},{18,2},{3,19},{19,3},{4,20},{20... | collective-permute-start | bytes 884744 | tf_op jit(solution)/shard_map/first_round/ppermute | solution.py:812
  253.2 27.7 %collective-permute-start.24 = (bf16[480,384]{1,0:T(8,128)(2,1)S(1)}, bf16[480,384]{1,0:T(8,128)(2,1)}, u32[]{:S(2)}, u32[]{:S(2)}) collective-permute-start(bf16[480,384]{1,0:T(8,128)(2,1)S(1)} %split.6), channel_id=1, source_target_pairs={{0,2},{1,3},{2,0},{3,1},{4,6},{5,7},{6,4},{7,5},{8,10},{9,11},{10,... | collective-permute-start | bytes 1105928 | tf_op jit(solution)/shard_map/first_round/ppermute | solution.py:812
  257.2 23.7 %collective-permute-start.26 = (bf16[304,384]{1,0:T(8,128)(2,1)}, bf16[304,384]{1,0:T(8,128)(2,1)S(1)}, u32[]{:S(2)}, u32[]{:S(2)}) collective-permute-start(bf16[304,384]{1,0:T(8,128)(2,1)} %constant_dynamic-slice_fusion), channel_id=1, source_target_pairs={{0,16},{16,0},{1,17},{17,1},{2,18},{18,2},{3,19},{19,3},{4,20},{20... | collective-permute-start | bytes 700424 | tf_op jit(solution)/shard_map/first_round/ppermute | solution.py:812
  282.0 31.8 %collective-permute-start.30 = (bf16[480,768]{1,0:T(8,128)(2,1)S(1)}, bf16[480,768]{1,0:T(8,128)(2,1)S(1)}, u32[]{:S(2)}, u32[]{:S(2)}) collective-permute-start(bf16[480,768]{1,0:T(8,128)(2,1)S(1)} %pad_maximum_fusion.1.down_aa), channel_id=1, source_target_pairs={{0,16},{16,0},{1,17},{17,1},{2,18},{18,2},{3,19},{19,3},{4,20},{20... | collective-permute-start | bytes 2211848 | tf_op jit(solution)/shard_map/second_round/ppermute | solution.py:812
  282.4 31.4 %collective-permute-start.29 = (bf16[480,768]{1,0:T(8,128)(2,1)S(1)}, bf16[480,768]{1,0:T(8,128)(2,1)S(1)}, u32[]{:S(2)}, u32[]{:S(2)}) collective-permute-start(bf16[480,768]{1,0:T(8,128)(2,1)S(1)} %pad_maximum_fusion.1.down_aa), channel_id=1, source_target_pairs={{0,1},{1,0},{2,3},{3,2},{4,5},{5,4},{6,7},{7,6},{8,9},{9,8},{10,11... | collective-permute-start | bytes 2211848 | tf_op jit(solution)/shard_map/second_round/ppermute | solution.py:812
  285.7 22.9 %collective-permute-start.34 = (bf16[2,256,384]{2,1,0:T(8,128)(2,1)S(1)}, bf16[2,256,384]{2,1,0:T(8,128)(2,1)S(1)}, u32[]{:S(2)}, u32[]{:S(2)}) collective-permute-start(bf16[2,256,384]{2,1,0:T(8,128)(2,1)S(1)} %slice_bitcast_fusion.2), channel_id=1, source_target_pairs={{0,1},{1,0},{2,3},{3,2},{4,5},{5,4},{6,7},{7,6},{8,9},{9,8},{10,11... | collective-permute-start | bytes 1179656 | tf_op jit(solution)/shard_map/second_round/ppermute | solution.py:812
  286.3 27.4 %collective-permute-start.31 = (bf16[384,768]{1,0:T(8,128)(2,1)S(1)}, bf16[384,768]{1,0:T(8,128)(2,1)S(1)}, u32[]{:S(2)}, u32[]{:S(2)}) collective-permute-start(bf16[384,768]{1,0:T(8,128)(2,1)S(1)} %pad_maximum_fusion.3), channel_id=1, source_target_pairs={{0,2},{1,3},{2,0},{3,1},{4,6},{5,7},{6,4},{7,5},{8,10},{9,11},{10,... | collective-permute-start | bytes 1769480 | tf_op jit(solution)/shard_map/second_round/ppermute | solution.py:812
  315.4 25.1 %collective-permute-start.39 = (bf16[480,768]{1,0:T(8,128)(2,1)S(1)}, bf16[480,768]{1,0:T(8,128)(2,1)}, u32[]{:S(2)}, u32[]{:S(2)}) collective-permute-start(bf16[480,768]{1,0:T(8,128)(2,1)S(1)} %collective-permute-done.29.down_ab), channel_id=1, source_target_pairs={{0,16},{16,0},{1,17},{17,1},{2,18},{18,2},{3,19},{19,3},{4,20},{20... | collective-permute-start | bytes 2211848 | tf_op jit(solution)/shard_map/third_round/ppermute | solution.py:812
  320.4 34.3 %collective-permute-start.36 = (bf16[384,1536]{1,0:T(8,128)(2,1)S(1)}, bf16[384,1536]{1,0:T(8,128)(2,1)S(1)}, u32[]{:S(2)}, u32[]{:S(2)}) collective-permute-start(bf16[384,1536]{1,0:T(8,128)(2,1)S(1)} %pad_maximum_fusion.up_a), channel_id=1, source_target_pairs={{0,1},{1,0},{2,3},{3,2},{4,5},{5,4},{6,7},{7,6},{8,9},{9,8},{10,11... | collective-permute-start | bytes 3538952 | tf_op jit(solution)/shard_map/third_round/ppermute | solution.py:812
  321.8 24.3 %collective-permute-start.40 = (bf16[2,304,384]{2,1,0:T(8,128)(2,1)S(1)}, bf16[2,304,384]{2,1,0:T(8,128)(2,1)S(1)}, u32[]{:S(2)}, u32[]{:S(2)}) collective-permute-start(bf16[2,304,384]{2,1,0:T(8,128)(2,1)S(1)} %pad_maximum_fusion.4.p00), channel_id=1, source_target_pairs={{0,16},{16,0},{1,17},{17,1},{2,18},{18,2},{3,19},{19,3},{4,20},{20... | collective-permute-start | bytes 1400840 | tf_op jit(solution)/shard_map/third_round/ppermute | solution.py:812
  324.2 23.9 %collective-permute-start.37 = (bf16[256,768]{1,0:T(8,128)(2,1)}, bf16[256,768]{1,0:T(8,128)(2,1)}, u32[]{:S(2)}, u32[]{:S(2)}) collective-permute-start(bf16[256,768]{1,0:T(8,128)(2,1)} %get-tuple-element.207), channel_id=1, source_target_pairs={{0,4},{1,5},{2,6},{3,7},{4,0},{5,1},{6,2},{7,3},{8,12},{9,13},{10,... | collective-permute-start | bytes 1179656 | tf_op jit(solution)/shard_map/third_round/ppermute | solution.py:812
  (55 other events, 434.9 us)
